TPU v7x, 32 devices: a whole 2x2x4 slice. The times are simulated.
32 devices in a mesh: rep: 2 (over y), head: 4 (over z), ctx: 4 (over x, core).
Axes of the slice: x: 2, y: 2, z: 4, core: 2. Of those that a mesh axis runs over, the one named last changes fastest.
Arguments:
- queries: bfloat16 [8, 512, 8192], P(('rep', 'ctx'), 'head'), parts along dimension 0, may hold values from -6 to 6
- keys: bfloat16 [8, 512, 8192], P(('rep', 'ctx'), 'head'), parts along dimension 0, may hold values from -6 to 6
- values: bfloat16 [8, 512, 8192], P(('rep', 'ctx'), 'head'), parts along dimension 0, may hold values from -6 to 6
- gain: float32 [8192], replicated, may hold values from 0.5 to 1.5
Outputs:
- normed: bfloat16 [8, 512, 8192], P(('rep', 'ctx'), 'head'), parts along dimension 0
There are 2 independent parts, one for each index of `rep`. A program takes and returns all parts, laid end to end along the dimension named above; an argument that names none is the same for every part. Nothing has to cross between parts.
All inputs are finite; a program needn't handle non-finite values.
Results may differ from a plain program's by a relative error of at most 0.0059.
Values may be sent and summed in bfloat16 or wider, within the bound.
No kernel may reach another device: no remote copies, remote signals or barrier semaphores. Data moves between devices by JAX's collectives and lax.ppermute only.
A program may use at most 128 MiB of HBM per device.

v0:
```python
import jax
import jax.numpy as jnp
from jax import lax
from jax.sharding import PartitionSpec as P

DH = 128


def entering(part, axis, combine, identity):
    place = lax.axis_index(axis)
    gathered = lax.all_gather(part, axis)
    state = jnp.zeros_like(part) + jnp.asarray(identity, part.dtype)

    def one(step, state):
        return combine(state, lax.dynamic_index_in_dim(gathered, step, 0, False))

    return lax.fori_loop(0, place, one, state)


def block_attention(query_blk, key_blk, value_blk, state_blk):
    length = query_blk.shape[-2]
    causal = jnp.arange(length)[:, None] >= jnp.arange(length)[None, :]
    scores = jnp.einsum(
        "...htd,...hsd->...hts", query_blk, key_blk, preferred_element_type=jnp.float32
    )
    scores = jnp.where(causal, scores, jnp.float32(0.0)).astype(jnp.bfloat16)
    local_part = jnp.einsum(
        "...hts,...hsd->...htd", scores, value_blk, preferred_element_type=jnp.float32
    )
    carried = jnp.einsum(
        "...htd,...hde->...hte", query_blk, state_blk, preferred_element_type=jnp.float32
    )
    return (local_part + carried).astype(jnp.bfloat16)


def activate(rows):
    return jax.nn.silu(rows.astype(jnp.float32)).astype(jnp.bfloat16)


def row_norm(attn, gain):
    wide = attn.astype(jnp.float32)
    mean_sq = jnp.mean(wide * wide, axis=1, keepdims=True)
    return (wide * lax.rsqrt(mean_sq + 1e-06) * gain[None, :]).astype(jnp.bfloat16)


def body(queries, keys, values, gain):
    tok_rows = queries.shape[1]
    width = queries.shape[2]
    q_rows = queries.reshape(tok_rows, width)
    k_rows = keys.reshape(tok_rows, width)
    v_rows = values.reshape(tok_rows, width)
    head_q, head_k, head_v = (
        lax.all_to_all(q_rows, "head", split_axis=1, concat_axis=0, tiled=True),
        lax.all_to_all(k_rows, "head", split_axis=1, concat_axis=0, tiled=True),
        lax.all_to_all(v_rows, "head", split_axis=1, concat_axis=0, tiled=True),
    )
    span = head_q.shape[0]
    local_cols = head_q.shape[1]
    local_heads = local_cols // DH
    blocks = span // tok_rows
    query_hb = activate(head_q).reshape(blocks, tok_rows, local_heads, DH).transpose(0, 2, 1, 3)
    key_hb = activate(head_k).reshape(blocks, tok_rows, local_heads, DH).transpose(0, 2, 1, 3)
    value_hb = head_v.reshape(blocks, tok_rows, local_heads, DH).transpose(0, 2, 1, 3)
    block_states = jnp.einsum(
        "bhtd,bhte->bhde", key_hb, value_hb, preferred_element_type=jnp.float32
    )
    stretch_total = jnp.sum(block_states, axis=0)
    earlier = entering(
        stretch_total, "ctx", lambda first, second: first + second, jnp.zeros_like(stretch_total)
    )
    running = jnp.cumsum(block_states, axis=0)
    within = jnp.concatenate([jnp.zeros_like(running[:1]), running[:-1]], axis=0)
    states = (earlier[None] + within).astype(jnp.bfloat16)
    attn = block_attention(query_hb, key_hb, value_hb, states)
    attn = attn.transpose(0, 2, 1, 3).reshape(span, local_cols)
    back = lax.all_to_all(attn, "head", split_axis=0, concat_axis=1, tiled=True)
    normed = row_norm(back, gain)
    return normed.reshape(1, tok_rows, width)


def solution(mesh):
    return jax.shard_map(
        body,
        mesh=mesh,
        in_specs=(
            P(("rep", "ctx"), "head", None),
            P(("rep", "ctx"), "head", None),
            P(("rep", "ctx"), "head", None),
            P(),
        ),
        out_specs=P(("rep", "ctx"), "head", None),
        check_vma=False,
    )
```

profile of v0, /device:TPU:0, one launch (start us, length us, event | category | flops | bytes accessed | tf_op | source)
XLA Modules:
  0.0 268.5 jit_solution(5377043979471332079)
XLA Ops:
  6.5 4.1 %copy.18 = bf16[1,128,8192]{1,2,0:T(8,128)(2,1)} copy(bf16[1,128,8192]{2,1,0:T(8,128)(2,1)} %param.7) | data formatting | bytes 4194304 | tf_op args[1]
  10.6 6.3 %all-to-all-start.1 = ((bf16[128,4,2048]{0,2,1:T(8,128)(2,1)}), bf16[128,4,2048]{0,2,1:T(8,128)(2,1)S(1)}, u32[]{:S(2)}, u32[]{:S(2)}) async-start(bf16[128,4,2048]{0,2,1:T(8,128)(2,1)} %bitcast.47), calls=%async_computation.1 | async-start | bytes 4194304 | tf_op jit(solution)/shard_map/all_to_all | solution.py:54
  16.9 4.1 %copy.31 = bf16[1,128,8192]{1,2,0:T(8,128)(2,1)} copy(bf16[1,128,8192]{2,1,0:T(8,128)(2,1)} %param.8) | data formatting | bytes 4194304 | tf_op jit(solution)/shard_map/all_to_all | solution.py:55
  21.0 44.1 %all-to-all-done.1 = bf16[128,4,2048]{0,2,1:T(8,128)(2,1)S(1)} async-done(((bf16[128,4,2048]{0,2,1:T(8,128)(2,1)}), bf16[128,4,2048]{0,2,1:T(8,128)(2,1)S(1)}, u32[]{:S(2)}, u32[]{:S(2)}) %all-to-all-start.1) | async-done | bytes 2097184 | tf_op jit(solution)/shard_map/all_to_all | solution.py:54
  65.1 4.4 %all-to-all-start.2 = ((bf16[128,4,2048]{0,2,1:T(8,128)(2,1)}), bf16[128,4,2048]{0,2,1:T(8,128)(2,1)}, u32[]{:S(2)}, u32[]{:S(2)}) async-start(bf16[128,4,2048]{0,2,1:T(8,128)(2,1)} %bitcast.46), calls=%async_computation.2 | async-start | bytes 4194304 | tf_op jit(solution)/shard_map/all_to_all | solution.py:55
  69.5 0.0 all-gather.3.cloned.1.call-start
  69.6 2.2 convert_element_type.92
  71.8 45.5 %all-to-all-done.2 = bf16[128,4,2048]{0,2,1:T(8,128)(2,1)} async-done(((bf16[128,4,2048]{0,2,1:T(8,128)(2,1)}), bf16[128,4,2048]{0,2,1:T(8,128)(2,1)}, u32[]{:S(2)}, u32[]{:S(2)}) %all-to-all-start.2) | async-done | bytes 2097184 | tf_op jit(solution)/shard_map/all_to_all | solution.py:55
  117.3 0.0 copy-start
  117.3 7.3 %fusion.13 = (f32[16,128,128]{2,1,0:T(8,128)}, f32[4,16,128,128]{3,2,1,0:T(8,128)}) fusion(bf16[4,16,128,128]{2,3,1,0:T(8,128)(2,1)} %bitcast.14, f32[4,128,16,128]{1,3,2,0:T(8,128)} %bitcast.51), kind=kOutput, calls=%fused_computation.19 | convolution fusion | flops 274464768 | bytes 11534336 | tf_op jit(solution)/shard_map/bhtd,bhte->bhde/dot_general | solution.py:64
  124.6 0.0 all-gather.3.cloned.1.call-update
  124.7 0.0 copy-done
  124.7 2.4 copy.17
  127.1 3.7 %all-to-all-start = ((bf16[128,4,2048]{0,2,1:T(8,128)(2,1)}), bf16[128,4,2048]{0,2,1:T(8,128)(2,1)S(1)}, u32[]{:S(2)}, u32[]{:S(2)}) async-start(bf16[128,4,2048]{0,2,1:T(8,128)(2,1)} %bitcast.45), calls=%async_computation | async-start | bytes 4194304 | tf_op jit(solution)/shard_map/all_to_all | solution.py:53
  130.8 3.3 %fusion.14 = f32[4,16,128,128]{3,2,1,0:T(8,128)S(1)} fusion(f32[4,16,128,128]{3,2,1,0:T(8,128)} %get-tuple-element.38), kind=kOutput, calls=%fused_computation.20 | output fusion | flops 3145728 | bytes 8388608 | tf_op jit(solution)/shard_map/jit(cumsum)/reduce_window_sum | solution.py:71
  134.1 2.0 slice.4
  136.1 42.3 %all-to-all-done = bf16[128,4,2048]{0,2,1:T(8,128)(2,1)S(1)} async-done(((bf16[128,4,2048]{0,2,1:T(8,128)(2,1)}), bf16[128,4,2048]{0,2,1:T(8,128)(2,1)S(1)}, u32[]{:S(2)}, u32[]{:S(2)}) %all-to-all-start) | async-done | bytes 2097184 | tf_op jit(solution)/shard_map/all_to_all | solution.py:53
  178.4 2.2 convert_element_type.91
  180.6 10.1 %fusion.8 = f32[4,16,128,128]{2,3,1,0:T(8,128)} fusion(bf16[4,16,128,128]{2,3,1,0:T(8,128)(2,1)} %bitcast.14, pred[128,128]{1,0:T(8,128)(4,1)S(1)} %iota_compare_fusion, f32[4,128,16,128]{1,3,2,0:T(8,128)} %bitcast.49, f32[4,128,16,128]{1,3,2,0:T(8,128)} %bitcast.52), kind=kOutput, calls=%fused_computation.14 | convolution fusion | flops 549453824 | bytes 14696448 | tf_op jit(solution)/shard_map/...hts,...hsd->...htd/dot_general | solution.py:27
  190.7 0.0 all-gather.3.cloned.1.call-done
  190.7 0.1 broadcast_in_dim.19
  190.8 6.2 %add_convert_fusion = bf16[4,16,128,128]{2,3,1,0:T(8,128)(2,1)S(1)} fusion(f32[4,16,128,128]{2,3,1,0:T(8,128)} %fusion.8, f32[3,16,128,128]{3,2,1,0:T(8,128)} %slice.4, f32[16,128,128]{2,1,0:T(8,128)S(1)} %get-tuple-element.28, f32[4,128,16,128]{1,3,2,0:T(8,128)} %bitcast.50), kind=kOutput, calls=%fused_computation.3 | convolution fusion | flops 277872640 | bytes 14680064 | tf_op jit(solution)/shard_map/...htd,...hde->...hte/dot_general | solution.py:30
  197.0 51.7 %all_to_all.55 = bf16[4,128,2048]{1,2,0:T(8,128)(2,1)S(1)} all-to-all(bf16[4,128,2048]{1,2,0:T(8,128)(2,1)S(1)} %bitcast.53), channel_id=1, replica_groups=mesh['rep'=2,'head'=4,'ctx'=4] {'head'}, dimensions={0} | all-to-all | bytes 4194304 | tf_op jit(solution)/shard_map/all_to_all | solution.py:76
  248.7 2.2 convert_element_type.93
  250.9 0.0 copy-start.1
  250.9 5.6 %copy.32 = f32[1,128,8192]{2,1,0:T(8,128)} copy(f32[1,128,8192]{1,2,0:T(8,128)} %bitcast.44) | data formatting | bytes 8388608 | tf_op jit(solution)/shard_map/convert_element_type | solution.py:41
  256.5 1.1 multiply_reduce_fusion
  257.6 0.0 copy-done.1
  257.6 4.0 %multiply_convert_fusion = bf16[1,128,8192]{2,1,0:T(8,128)(2,1)} fusion(f32[1,128,8192]{2,1,0:T(8,128)} %copy.32, f32[8192]{0:T(1024)S(1)} %copy-done.1, f32[128]{0:T(128)S(1)} %add_rsqrt_fusion), kind=kLoop, calls=%fused_computation.1 | loop fusion | flops 3145728 | bytes 6324736 | tf_op jit(solution)/shard_map/convert_element_type | solution.py:43
  (3 shorter events, 0.0 us)
Async XLA Ops:
  10.6 54.5 %all-to-all-start.1 = ((bf16[128,4,2048]{0,2,1:T(8,128)(2,1)}), bf16[128,4,2048]{0,2,1:T(8,128)(2,1)S(1)}, u32[]{:S(2)}, u32[]{:S(2)}) async-start(bf16[128,4,2048]{0,2,1:T(8,128)(2,1)} %bitcast.47), calls=%async_computation.1 | async-start | bytes 4194304 | tf_op jit(solution)/shard_map/all_to_all | solution.py:54
  65.1 52.2 %all-to-all-start.2 = ((bf16[128,4,2048]{0,2,1:T(8,128)(2,1)}), bf16[128,4,2048]{0,2,1:T(8,128)(2,1)}, u32[]{:S(2)}, u32[]{:S(2)}) async-start(bf16[128,4,2048]{0,2,1:T(8,128)(2,1)} %bitcast.46), calls=%async_computation.2 | async-start | bytes 4194304 | tf_op jit(solution)/shard_map/all_to_all | solution.py:55
  69.5 121.2 %all-gather.3.cloned.1.call-start = ((), (), s32[]{:S(2)}) async-start(), calls=%async_computation.4 | async-start | bytes 5242880 | tf_op jit(solution)/shard_map/all_gather | solution.py:11
  117.3 7.3 %copy-start = (bf16[1,128,8192]{2,1,0:T(8,128)(2,1)S(1)}, bf16[1,128,8192]{2,1,0:T(8,128)(2,1)}, u32[]{:S(2)}) copy-start(bf16[1,128,8192]{2,1,0:T(8,128)(2,1)} %param.6) | copy-start | bytes 6291460
  127.1 51.3 %all-to-all-start = ((bf16[128,4,2048]{0,2,1:T(8,128)(2,1)}), bf16[128,4,2048]{0,2,1:T(8,128)(2,1)S(1)}, u32[]{:S(2)}, u32[]{:S(2)}) async-start(bf16[128,4,2048]{0,2,1:T(8,128)(2,1)} %bitcast.45), calls=%async_computation | async-start | bytes 4194304 | tf_op jit(solution)/shard_map/all_to_all | solution.py:53
  250.9 6.7 %copy-start.1 = (f32[8192]{0:T(1024)S(1)}, f32[8192]{0:T(1024)}, u32[]{:S(2)}) copy-start(f32[8192]{0:T(1024)} %param.9) | copy-start | bytes 98308
Sparse Core Ops, SparseCore 0:
  124.8 33.5 all-gather.2
where the time goes:
time: 271 us; the launch traced here: 268 us
  waiting for transfers between devices  132 us (49%)
  blocking collectives  51.7 us (19%)
  matrix products  23.6 us (9%)
  local copies, waits for them, and re-layouts  18.3 us (7%)
  other arithmetic  15.1 us (6%)
  starting transfers between devices  14.5 us (5%)
  between operations  13.5 us (5%)
    all_to_all x1, blocking collectives, body(): back = lax.all_to_all(attn, 'head', split_axis=0, concat_axis=1, tiled=True)  51.7 us
    all_to_all x1, waiting for transfers between devices, body(): lax.all_to_all(v_rows, 'head', split_axis=1, concat_axis=0, tiled=True)  45.5 us
    all_to_all x1, waiting for transfers between devices, body(): lax.all_to_all(k_rows, 'head', split_axis=1, concat_axis=0, tiled=True)  44.1 us
    all_to_all x1, waiting for transfers between devices, body(): lax.all_to_all(q_rows, 'head', split_axis=1, concat_axis=0, tiled=True)  42.3 us
    dot_general x1, matrix products, block_attention(): jnp.einsum('...hts,...hsd->...htd', scores, value_blk, preferred_element_...  10.1 us
    dot_general x1, matrix products, body(): jnp.einsum('bhtd,bhte->bhde', key_hb, value_hb, preferred_element_type=jn...  7.31 us
    unnamed x6, local copies, waits for them, and re-layouts  6.5 us
    all_to_all x1, starting transfers between devices, body(): lax.all_to_all(k_rows, 'head', split_axis=1, concat_axis=0, tiled=True)  6.32 us
  transfers between devices with their start and end apart: 4, of which 3 were waited for; matrix products, arithmetic and copies ran while one was open for 10% of the time, Pallas kernels for 0%

commit v1 on v0

v1 whole, which is shorter than its diff:
```python
import functools

import jax
import jax.numpy as jnp
from jax import lax
from jax.experimental import pallas as pl
from jax.experimental.pallas import tpu as pltpu
from jax.sharding import PartitionSpec as P

DH = 128
F32 = jnp.float32
BF16 = jnp.bfloat16


def silu(x):
    x = x.astype(F32)
    return (x / (1.0 + jnp.exp(-x))).astype(BF16)


def kv_kernel(heads, k_ref, v_ref, c_ref):
    for h in range(heads):
        cols = slice(h * DH, (h + 1) * DH)
        ka = silu(k_ref[:, cols])
        c_ref[h] = lax.dot_general(
            ka, v_ref[:, cols], (((0,), (0,)), ((), ())), preferred_element_type=F32
        ).astype(BF16)


def kv_states(k_rows, v_rows, first, count, step):
    rows = k_rows.shape[0]
    base = first // step
    block = pl.BlockSpec((rows, step * DH), lambda i: (0, base + i))
    return pl.pallas_call(
        functools.partial(kv_kernel, step),
        grid=(count // step,),
        in_specs=[block, block],
        out_specs=pl.BlockSpec((step, DH, DH), lambda i: (i, 0, 0)),
        out_shape=jax.ShapeDtypeStruct((count, DH, DH), BF16),
        cost_estimate=pl.CostEstimate(
            flops=2 * count * rows * DH * DH,
            bytes_accessed=2 * count * DH * (2 * rows + DH),
            transcendentals=count * DH * rows,
        ),
        name="kv_states",
    )(k_rows, v_rows)


def local_kernel(heads, q_ref, k_ref, v_ref, qa_ref, part_ref):
    rows = q_ref.shape[0]
    causal = lax.broadcasted_iota(jnp.int32, (rows, rows), 0) >= lax.broadcasted_iota(
        jnp.int32, (rows, rows), 1
    )
    for h in range(heads):
        cols = slice(h * DH, (h + 1) * DH)
        qa = silu(q_ref[:, cols])
        ka = silu(k_ref[:, cols])
        scores = lax.dot_general(
            qa, ka, (((1,), (1,)), ((), ())), preferred_element_type=F32
        )
        scores = jnp.where(causal, scores, 0.0).astype(BF16)
        part_ref[:, cols] = jnp.dot(
            scores, v_ref[:, cols], preferred_element_type=F32
        )
        qa_ref[:, cols] = qa


def local_parts(q_rows, k_rows, v_rows, first, count, step):
    rows = q_rows.shape[0]
    base = first // step
    block = pl.BlockSpec((rows, step * DH), lambda i: (0, base + i))
    out = pl.BlockSpec((rows, step * DH), lambda i: (0, i))
    return pl.pallas_call(
        functools.partial(local_kernel, step),
        grid=(count // step,),
        in_specs=[block, block, block],
        out_specs=[out, out],
        out_shape=[
            jax.ShapeDtypeStruct((rows, count * DH), BF16),
            jax.ShapeDtypeStruct((rows, count * DH), F32),
        ],
        cost_estimate=pl.CostEstimate(
            flops=4 * count * rows * rows * DH,
            bytes_accessed=12 * count * DH * rows,
            transcendentals=2 * count * DH * rows,
        ),
        name="local_parts",
    )(q_rows, k_rows, v_rows)


def attend_kernel(heads, qa_ref, part_ref, in_ref, out_ref, f_ref, attn_ref, sq_ref):
    total = None
    for h in range(heads):
        cols = slice(h * DH, (h + 1) * DH)
        state = (
            in_ref[h].astype(F32) + out_ref[h].astype(F32) + f_ref[h].astype(F32)
        ).astype(BF16)
        carried = jnp.dot(qa_ref[:, cols], state, preferred_element_type=F32)
        attn = (part_ref[:, cols] + carried).astype(BF16)
        attn_ref[:, cols] = attn
        wide = attn.astype(F32)
        total = wide * wide if total is None else total + wide * wide
    sq_ref[...] = total


def attend(qa, part, inward, outward, early):
    rows, width = qa.shape
    heads = width // DH
    return pl.pallas_call(
        functools.partial(attend_kernel, heads),
        out_shape=[
            jax.ShapeDtypeStruct((rows, width), BF16),
            jax.ShapeDtypeStruct((rows, DH), F32),
        ],
        cost_estimate=pl.CostEstimate(
            flops=2 * heads * rows * DH * DH,
            bytes_accessed=8 * rows * width + 6 * heads * DH * DH,
            transcendentals=0,
        ),
        name="attend",
    )(qa, part, inward, outward, early)


def norm_kernel(sizes, *refs):
    n = len(sizes)
    attn_refs, sq_refs, gain_ref, out_ref = refs[:n], refs[n : 2 * n], refs[2 * n], refs[2 * n + 1]
    total = sq_refs[0][...]
    for ref in sq_refs[1:]:
        total = total + ref[...]
    mean_sq = jnp.sum(total, axis=1, keepdims=True) / sum(sizes)
    scale = lax.rsqrt(mean_sq + 1e-06)
    at = 0
    for ref, size in zip(attn_refs, sizes):
        for c in range(0, size, 512):
            wide = min(512, size - c)
            out_ref[0, :, at + c : at + c + wide] = (
                ref[:, c : c + wide].astype(F32) * scale * gain_ref[:, at + c : at + c + wide]
            ).astype(BF16)
        at += size


def row_norm(attns, squares, gain):
    rows = attns[0].shape[0]
    sizes = [a.shape[1] for a in attns]
    width = sum(sizes)
    return pl.pallas_call(
        functools.partial(norm_kernel, sizes),
        out_shape=jax.ShapeDtypeStruct((1, rows, width), BF16),
        cost_estimate=pl.CostEstimate(
            flops=3 * rows * width, bytes_accessed=4 * rows * width, transcendentals=0
        ),
        name="row_norm",
    )(*attns, *squares, gain.reshape(1, width))


def swap_halves(pairs):
    return pairs + [(b, a) for a, b in pairs]


def earlier_ctx(part, n_ctx):
    place = lax.axis_index("ctx")
    if n_ctx == 1:
        return jnp.zeros_like(part)
    if n_ctx % 2:
        total = jnp.zeros(part.shape, F32)
        for s in range(1, n_ctx):
            got = lax.ppermute(part, "ctx", [(i, i + s) for i in range(n_ctx - s)])
            total = total + got.astype(F32)
        return total.astype(BF16)
    couples = n_ctx // 2
    odd = place % 2 == 1
    partner = swap_halves([(2 * p, 2 * p + 1) for p in range(couples)])
    other = lax.ppermute(part, "ctx", partner)
    first = jnp.where(odd, other, jnp.zeros_like(other))
    if couples == 1:
        return first
    half = part.shape[0] // 2
    both = part.astype(F32) + other.astype(F32)
    mine = jnp.where(odd, both[half:], both[:half]).astype(BF16)
    before = jnp.zeros(mine.shape, F32)
    for s in range(1, couples):
        pairs = [(i, i + 2 * s) for i in range(n_ctx - 2 * s)]
        if 4 * s >= n_ctx:
            got = lax.ppermute(mine, "ctx", swap_halves(pairs))
            got = jnp.where(place >= 2 * s, got, jnp.zeros_like(got))
        else:
            got = lax.ppermute(mine, "ctx", pairs)
        before = before + got.astype(F32)
    before = before.astype(BF16)
    theirs = lax.ppermute(before, "ctx", partner)
    low = jnp.where(odd, theirs, before)
    high = jnp.where(odd, before, theirs)
    whole = jnp.concatenate([low, high], axis=0)
    return (whole.astype(F32) + first.astype(F32)).astype(BF16)


def add(*terms):
    total = terms[0].astype(F32)
    for term in terms[1:]:
        total = total + term.astype(F32)
    return total.astype(BF16)


def other_heads(early, upto, n_head):
    place = lax.axis_index("head")
    zero = jnp.zeros_like(early)
    if n_head == 1:
        return zero, zero
    if n_head % 2:
        lower, higher = zero, zero
        for _ in range(n_head - 1):
            lower = lax.ppermute(add(lower, upto), "head", [(i, i + 1) for i in range(n_head - 1)])
            higher = lax.ppermute(add(higher, early), "head", [(i + 1, i) for i in range(n_head - 1)])
        return lower, higher
    mid = n_head // 2
    left = place < mid
    mine = jnp.where(left, upto, early)
    mirror = jnp.where(left, early, upto)
    inward = None
    send = mine
    for t in range(mid - 1):
        got = lax.ppermute(send, "head", [(t, t + 1), (n_head - 1 - t, n_head - 2 - t)])
        inward = got if inward is None else inward + got
        send = add(inward, mine)
    outward = lax.ppermute(send, "head", [(mid - 1, mid), (mid, mid - 1)])
    for t in range(mid - 1, 0, -1):
        got = lax.ppermute(
            add(outward, mirror), "head", [(t, t - 1), (n_head - 1 - t, n_head - t)]
        )
        outward = outward + got
    return (zero if inward is None else inward), outward


def plan(heads):
    if heads % 16:
        return [[heads]]
    u = heads // 8
    return [[u], [2 * u], [2 * u, 2 * u, u]]


def body(n_head, n_ctx, queries, keys, values, gain):
    rows, width = queries.shape[1], queries.shape[2]
    q_rows = queries.reshape(rows, width)
    k_rows = keys.reshape(rows, width)
    v_rows = values.reshape(rows, width)
    heads = width // DH
    groups = plan(heads)
    step = heads if len(groups) == 1 else heads // 8
    attns, squares = [], []
    at = 0
    for sizes in groups:
        count = sum(sizes)
        own = kv_states(k_rows, v_rows, at, count, step)
        early = earlier_ctx(own, n_ctx)
        off = 0
        for size in sizes:
            e = early[off : off + size]
            upto = add(e, own[off : off + size])
            inward, outward = other_heads(e, upto, n_head)
            qa, part = local_parts(q_rows, k_rows, v_rows, at + off, size, step)
            attn, sq = attend(qa, part, inward, outward, e)
            attns.append(attn)
            squares.append(sq)
            off += size
        at += count
    return row_norm(attns, squares, gain)


def solution(mesh):
    n_head, n_ctx = mesh.shape["head"], mesh.shape["ctx"]
    return jax.shard_map(
        functools.partial(body, n_head, n_ctx),
        mesh=mesh,
        in_specs=(
            P(("rep", "ctx"), "head", None),
            P(("rep", "ctx"), "head", None),
            P(("rep", "ctx"), "head", None),
            P(),
        ),
        out_specs=P(("rep", "ctx"), "head", None),
        check_vma=False,
    )
```

time: 271 us -> 172 us (0.63)
  waiting for transfers between devices: 132 us -> 62.7 us
  blocking collectives: 51.7 us -> 0 us
  Pallas kernels: 0 us -> 47.8 us
  matrix products: 23.6 us -> 0 us
  starting transfers between devices: 14.5 us -> 36.9 us
  local copies, waits for them, and re-layouts: 18.3 us -> 1.58 us
  between operations: 13.5 us -> 0.45 us
  other arithmetic: 15.1 us -> 20.7 us
    all_to_all x3 -> x0, waiting for transfers between devices: 132 us -> none  [the longest x1 45.5 us: body(): lax.all_to_all(v_rows, 'head', split_axis=1, concat_axis=0, tiled=True)]
    ppermute x0 -> x24, waiting for transfers between devices: none -> 62.7 us  [the longest x5 26.8 us: other_heads(): lax.ppermute(send, 'head', [(t, t + 1), (n_head - 1 - t, n_head - 2 - t)])]
    all_to_all x1 -> x0, blocking collectives: 51.7 us -> none  [body(): back = lax.all_to_all(attn, 'head', split_axis=0, concat_axis=1, tiled=True)]
    pallas_call x0 -> x14, Pallas kernels: none -> 47.8 us  [the longest x5 20.7 us: local_parts(): pl.pallas_call(functools.partial(local_kernel, step), grid=(count // step...]
    ppermute x0 -> x24, starting transfers between devices: none -> 36.9 us  [the longest x5 20.8 us: other_heads(): lax.ppermute(send, 'head', [(t, t + 1), (n_head - 1 - t, n_head - 2 - t)])]
    dot_general x3 -> x0, matrix products: 23.6 us -> none  [the longest x1 10.1 us: block_attention(): jnp.einsum('...hts,...hsd->...htd', scores, value_blk, preferred_element_...]
    all_to_all x3 -> x0, starting transfers between devices: 14.4 us -> none  [the longest x1 6.32 us: body(): lax.all_to_all(k_rows, 'head', split_axis=1, concat_axis=0, tiled=True)]
    add x0 -> x8, other arithmetic: none -> 9.23 us  [the longest x5 7.51 us: other_heads(): outward = outward + got]
  transfers between devices with their start and end apart: 4 -> 24, of which waited for: 3 -> 8; matrix products, arithmetic and copies ran while one was open for 10% -> 11% of each run, Pallas kernels for 0% -> 21%
where the time goes in v1:
time: 172 us; the launch traced here: 170 us
  waiting for transfers between devices  62.7 us (36%)
  Pallas kernels  47.8 us (28%)
  starting transfers between devices  36.9 us (21%)
  other arithmetic  20.7 us (12%)
    ppermute x5, waiting for transfers between devices, other_heads(): lax.ppermute(send, 'head', [(t, t + 1), (n_head - 1 - t, n_head - 2 - t)])  26.8 us
    ppermute x3, waiting for transfers between devices, earlier_ctx(): got = lax.ppermute(mine, 'ctx', swap_halves(pairs))  23.7 us
    ppermute x5, starting transfers between devices, other_heads(): lax.ppermute(send, 'head', [(t, t + 1), (n_head - 1 - t, n_head - 2 - t)])  20.8 us
    pallas_call x5, Pallas kernels, local_parts(): pl.pallas_call(functools.partial(local_kernel, step), grid=(count // step...  20.7 us
    pallas_call x5, Pallas kernels, attend(): pl.pallas_call(functools.partial(attend_kernel, heads), out_shape=[jax.Sh...  13.9 us
    ppermute x5, waiting for transfers between devices, other_heads(): lax.ppermute(add(outward, mirror), 'head', [(t, t - 1), (n_head - 1 - t,...  12.2 us
    pallas_call x3, Pallas kernels, kv_states(): pl.pallas_call(functools.partial(kv_kernel, step), grid=(count // step,),...  9.63 us
    add x5, other arithmetic, other_heads(): outward = outward + got  7.51 us
  transfers between devices with their start and end apart: 24, of which 8 were waited for; matrix products, arithmetic and copies ran while one was open for 11% of the time, Pallas kernels for 21%

profile of v1, /device:TPU:0, one launch (start us, length us, event | category | flops | bytes accessed | tf_op | source)
XLA Modules:
  0.0 170.2 jit_solution(7755623012521211527)
XLA Ops:
  0.0 2.1 %kv_states.3 = bf16[8,128,128]{2,1,0:T(8,128)(2,1)} custom-call(bf16[128,8192]{1,0:T(8,128)(2,1)} %bitcast.4, bf16[128,8192]{1,0:T(8,128)(2,1)} %bitcast.12), custom_call_target="tpu_custom_call" | custom-call | flops 33554432 | bytes 786432 | tf_op jit(solution)/shard_map/kv_states/pallas_call | solution.py:33
  2.5 5.1 %kv_states.5 = bf16[40,128,128]{2,1,0:T(8,128)(2,1)} custom-call(bf16[128,8192]{1,0:T(8,128)(2,1)} %bitcast.5, bf16[128,8192]{1,0:T(8,128)(2,1)} %bitcast.13), custom_call_target="tpu_custom_call" | custom-call | flops 167772160 | bytes 3932160 | tf_op jit(solution)/shard_map/kv_states/pallas_call | solution.py:33
  7.7 2.5 %kv_states.4 = bf16[16,128,128]{2,1,0:T(8,128)(2,1)} custom-call(bf16[128,8192]{1,0:T(8,128)(2,1)} %bitcast.6, bf16[128,8192]{1,0:T(8,128)(2,1)} %bitcast.14), custom_call_target="tpu_custom_call" | custom-call | flops 67108864 | bytes 1572864 | tf_op jit(solution)/shard_map/kv_states/pallas_call | solution.py:33
  12.0 2.5 %collective-permute-start.1 = (bf16[4,128,128]{2,1,0:T(8,128)(2,1)}, bf16[4,128,128]{2,1,0:T(8,128)(2,1)S(1)}, u32[]{:S(2)}, u32[]{:S(2)}) collective-permute-start(bf16[4,128,128]{2,1,0:T(8,128)(2,1)} %fusion.14), channel_id=1, source_target_pairs={{0,2},{1,3},{2,0},{3,1},{4,6},{5,7},{6,4},{7,5},{8,10},{9,11},{10,... | collective-permute-start | bytes 393224 | tf_op jit(solution)/shard_map/ppermute | solution.py:183
  14.6 4.3 %collective-permute-done.1 = bf16[4,128,128]{2,1,0:T(8,128)(2,1)S(1)} collective-permute-done((bf16[4,128,128]{2,1,0:T(8,128)(2,1)}, bf16[4,128,128]{2,1,0:T(8,128)(2,1)S(1)}, u32[]{:S(2)}, u32[]{:S(2)}) %collective-permute-start.1) | collective-permute-done | bytes 131104 | tf_op jit(solution)/shard_map/ppermute | solution.py:183
  22.2 1.7 %collective-permute-start.13 = (bf16[20,128,128]{2,1,0:T(8,128)(2,1)}, bf16[20,128,128]{2,1,0:T(8,128)(2,1)}, u32[]{:S(2)}, u32[]{:S(2)}) collective-permute-start(bf16[20,128,128]{2,1,0:T(8,128)(2,1)} %fusion), channel_id=1, source_target_pairs={{0,2},{1,3},{2,0},{3,1},{4,6},{5,7},{6,4},{7,5},{8,10},{9,11},{10,... | collective-permute-start | bytes 1966088 | tf_op jit(solution)/shard_map/ppermute | solution.py:183
  25.9 19.3 %collective-permute-done.7 = bf16[8,128,128]{2,1,0:T(8,128)(2,1)} collective-permute-done((bf16[8,128,128]{2,1,0:T(8,128)(2,1)}, bf16[8,128,128]{2,1,0:T(8,128)(2,1)}, u32[]{:S(2)}, u32[]{:S(2)}) %collective-permute-start.7) | collective-permute-done | bytes 262176 | tf_op jit(solution)/shard_map/ppermute | solution.py:183
  46.2 3.7 %collective-permute-start.3 = (bf16[8,128,128]{2,1,0:T(8,128)(2,1)S(1)}, bf16[8,128,128]{2,1,0:T(8,128)(2,1)S(1)}, u32[]{:S(2)}, u32[]{:S(2)}) collective-permute-start(bf16[8,128,128]{2,1,0:T(8,128)(2,1)S(1)} %get-tuple-element.47), channel_id=1, source_target_pairs={{0,4},{12,8},{1,5},{13,9},{2,6},{14,10},{3,7},{15,11},{16,20},{28,... | collective-permute-start | bytes 786440 | tf_op jit(solution)/shard_map/ppermute | solution.py:221
  55.0 1.6 collective-permute-done.3.in_ref
  57.3 7.2 %collective-permute-start.15 = (bf16[16,128,128]{2,1,0:T(8,128)(2,1)S(1)}, bf16[16,128,128]{2,1,0:T(8,128)(2,1)S(1)}, u32[]{:S(2)}, u32[]{:S(2)}) collective-permute-start(bf16[16,128,128]{2,1,0:T(8,128)(2,1)S(1)} %get-tuple-element.52), channel_id=1, source_target_pairs={{0,4},{12,8},{1,5},{13,9},{2,6},{14,10},{3,7},{15,11},{16,20},{28,... | collective-permute-start | bytes 1572872 | tf_op jit(solution)/shard_map/ppermute | solution.py:221
  64.6 3.2 %collective-permute-done.9.in_ref = bf16[16,128,128]{2,1,0:T(8,128)(2,1)S(1)} collective-permute-done((bf16[16,128,128]{2,1,0:T(8,128)(2,1)S(1)}, bf16[16,128,128]{2,1,0:T(8,128)(2,1)S(1)}, u32[]{:S(2)}, u32[]{:S(2)}) %collective-permute-start.9) | collective-permute-done | bytes 524320 | tf_op jit(solution)/shard_map/ppermute | solution.py:221
  68.7 10.3 %collective-permute-done.18.in_ref = bf16[16,128,128]{2,1,0:T(8,128)(2,1)S(1)} collective-permute-done((bf16[16,128,128]{2,1,0:T(8,128)(2,1)S(1)}, bf16[16,128,128]{2,1,0:T(8,128)(2,1)S(1)}, u32[]{:S(2)}, u32[]{:S(2)}) %collective-permute-start.18) | collective-permute-done | bytes 524320 | tf_op jit(solution)/shard_map/ppermute | solution.py:221
  79.9 9.4 %collective-permute-done.15.in_ref = bf16[16,128,128]{2,1,0:T(8,128)(2,1)S(1)} collective-permute-done((bf16[16,128,128]{2,1,0:T(8,128)(2,1)S(1)}, bf16[16,128,128]{2,1,0:T(8,128)(2,1)S(1)}, u32[]{:S(2)}, u32[]{:S(2)}) %collective-permute-start.15) | collective-permute-done | bytes 524320 | tf_op jit(solution)/shard_map/ppermute | solution.py:221
  91.8 7.2 %collective-permute-start.21 = (bf16[8,128,128]{2,1,0:T(8,128)(2,1)S(1)}, bf16[8,128,128]{2,1,0:T(8,128)(2,1)S(1)}, u32[]{:S(2)}, u32[]{:S(2)}) collective-permute-start(bf16[8,128,128]{2,1,0:T(8,128)(2,1)S(1)} %get-tuple-element.54), channel_id=1, source_target_pairs={{0,4},{12,8},{1,5},{13,9},{2,6},{14,10},{3,7},{15,11},{16,20},{28,... | collective-permute-start | bytes 786440 | tf_op jit(solution)/shard_map/ppermute | solution.py:221
  101.4 2.2 %collective-permute-done.21.in_ref = bf16[8,128,128]{2,1,0:T(8,128)(2,1)S(1)} collective-permute-done((bf16[8,128,128]{2,1,0:T(8,128)(2,1)S(1)}, bf16[8,128,128]{2,1,0:T(8,128)(2,1)S(1)}, u32[]{:S(2)}, u32[]{:S(2)}) %collective-permute-start.21) | collective-permute-done | bytes 262176 | tf_op jit(solution)/shard_map/ppermute | solution.py:221
  104.4 1.5 add_convert_fusion.1
  110.8 1.5 collective-permute-start.23
  112.2 3.3 %local_parts.9 = (bf16[128,1024]{1,0:T(8,128)(2,1)}, f32[128,1024]{1,0:T(8,128)}) custom-call(bf16[128,8192]{1,0:T(8,128)(2,1)} %bitcast.20, bf16[128,8192]{1,0:T(8,128)(2,1)} %bitcast.7, bf16[128,8192]{1,0:T(8,128)(2,1)} %bitcast.15), custom_call_target="tpu_custom_call" | custom-call | flops 67108864 | bytes 1572864 | tf_op jit(solution)/shard_map/local_parts/pallas_call | solution.py:72
  115.5 3.3 %local_parts.5 = (bf16[128,1024]{1,0:T(8,128)(2,1)}, f32[128,1024]{1,0:T(8,128)}) custom-call(bf16[128,8192]{1,0:T(8,128)(2,1)} %bitcast.21, bf16[128,8192]{1,0:T(8,128)(2,1)} %bitcast.8, bf16[128,8192]{1,0:T(8,128)(2,1)} %bitcast.16), custom_call_target="tpu_custom_call" | custom-call | flops 67108864 | bytes 1572864 | tf_op jit(solution)/shard_map/local_parts/pallas_call | solution.py:72
  118.8 4.7 %local_parts.8 = (bf16[128,2048]{1,0:T(8,128)(2,1)}, f32[128,2048]{1,0:T(8,128)}) custom-call(bf16[128,8192]{1,0:T(8,128)(2,1)} %bitcast.22, bf16[128,8192]{1,0:T(8,128)(2,1)} %bitcast.9, bf16[128,8192]{1,0:T(8,128)(2,1)} %bitcast.17), custom_call_target="tpu_custom_call" | custom-call | flops 134217728 | bytes 3145728 | tf_op jit(solution)/shard_map/local_parts/pallas_call | solution.py:72
  123.5 4.7 %local_parts.7 = (bf16[128,2048]{1,0:T(8,128)(2,1)}, f32[128,2048]{1,0:T(8,128)}) custom-call(bf16[128,8192]{1,0:T(8,128)(2,1)} %bitcast.23, bf16[128,8192]{1,0:T(8,128)(2,1)} %bitcast.10, bf16[128,8192]{1,0:T(8,128)(2,1)} %bitcast.18), custom_call_target="tpu_custom_call" | custom-call | flops 134217728 | bytes 3145728 | tf_op jit(solution)/shard_map/local_parts/pallas_call | solution.py:72
  128.2 4.7 %local_parts.6 = (bf16[128,2048]{1,0:T(8,128)(2,1)}, f32[128,2048]{1,0:T(8,128)}) custom-call(bf16[128,8192]{1,0:T(8,128)(2,1)} %bitcast.24, bf16[128,8192]{1,0:T(8,128)(2,1)} %bitcast.11, bf16[128,8192]{1,0:T(8,128)(2,1)} %bitcast.19), custom_call_target="tpu_custom_call" | custom-call | flops 134217728 | bytes 3145728 | tf_op jit(solution)/shard_map/local_parts/pallas_call | solution.py:72
  132.9 12.2 %collective-permute-done.5 = bf16[8,128,128]{2,1,0:T(8,128)(2,1)S(1)} collective-permute-done((bf16[8,128,128]{2,1,0:T(8,128)(2,1)}, bf16[8,128,128]{2,1,0:T(8,128)(2,1)S(1)}, u32[]{:S(2)}, u32[]{:S(2)}) %collective-permute-start.5) | collective-permute-done | bytes 262176 | tf_op jit(solution)/shard_map/ppermute | solution.py:226
  145.9 2.3 %attend.5 = (bf16[128,1024]{1,0:T(8,128)(2,1)}, f32[128,128]{1,0:T(8,128)}) custom-call(bf16[128,1024]{1,0:T(8,128)(2,1)} %get-tuple-element.25.qa_ref, f32[128,1024]{1,0:T(8,128)} %get-tuple-element.26.part_ref, bf16[8,128,128]{2,1,0:T(8,128)(2,1)} %copy-done.10, bf16[8,128,128]{2,1,0:T(8,128)(2,1)} %add.90.out_ref, bf16[8,128,128]{2,1,0:T(8,128)(2,1)} %copy-done.4), custom_call_target="tpu_custom_call" | custom-call | flops 33554432 | bytes 1835008 | tf_op jit(solution)/shard_map/attend/pallas_call | solution.py:108
  148.2 2.0 %add.96.out_ref = bf16[16,128,128]{2,1,0:T(8,128)(2,1)} add(bf16[16,128,128]{2,1,0:T(8,128)(2,1)S(1)} %copy-done.6, bf16[16,128,128]{2,1,0:T(8,128)(2,1)} %collective-permute-done.11) | non-fusion elementwise | flops 262144 | bytes 1572864 | tf_op jit(solution)/shard_map/add | solution.py:229
  150.2 3.1 %attend.6 = (bf16[128,2048]{1,0:T(8,128)(2,1)}, f32[128,128]{1,0:T(8,128)}) custom-call(bf16[128,2048]{1,0:T(8,128)(2,1)} %get-tuple-element.28.qa_ref, f32[128,2048]{1,0:T(8,128)} %get-tuple-element.29.part_ref, bf16[16,128,128]{2,1,0:T(8,128)(2,1)} %copy-done.9, bf16[16,128,128]{2,1,0:T(8,128)(2,1)} %add.96.out_ref, bf16[16,128,128]{2,1,0:T(8,128)(2,1)} %copy-done.2), custom_call_target="tpu_custom_call" | custom-call | flops 67108864 | bytes 3670016 | tf_op jit(solution)/shard_map/attend/pallas_call | solution.py:108
  154.1 2.4 %attend.9 = (bf16[128,1024]{1,0:T(8,128)(2,1)}, f32[128,128]{1,0:T(8,128)}) custom-call(bf16[128,1024]{1,0:T(8,128)(2,1)} %get-tuple-element.37.qa_ref, f32[128,1024]{1,0:T(8,128)} %get-tuple-element.38.part_ref, bf16[8,128,128]{2,1,0:T(8,128)(2,1)} %copy-done.11, bf16[8,128,128]{2,1,0:T(8,128)(2,1)} %add.110.out_ref, ...), custom_call_target="tpu_custom_call" | custom-call | flops 33554432 | bytes 1835008 | tf_op jit(solution)/shard_map/attend/pallas_call | solution.py:108
  156.5 2.0 %add.106.out_ref = bf16[16,128,128]{2,1,0:T(8,128)(2,1)} add(bf16[16,128,128]{2,1,0:T(8,128)(2,1)S(1)} %collective-permute-done.19, bf16[16,128,128]{2,1,0:T(8,128)(2,1)} %collective-permute-done.20) | non-fusion elementwise | flops 262144 | bytes 1572864 | tf_op jit(solution)/shard_map/add | solution.py:229
  158.5 2.0 %add.102.out_ref = bf16[16,128,128]{2,1,0:T(8,128)(2,1)} add(bf16[16,128,128]{2,1,0:T(8,128)(2,1)S(1)} %collective-permute-done.16, bf16[16,128,128]{2,1,0:T(8,128)(2,1)} %collective-permute-done.17) | non-fusion elementwise | flops 262144 | bytes 1572864 | tf_op jit(solution)/shard_map/add | solution.py:229
  160.4 3.1 %attend.8 = (bf16[128,2048]{1,0:T(8,128)(2,1)}, f32[128,128]{1,0:T(8,128)}) custom-call(bf16[128,2048]{1,0:T(8,128)(2,1)} %get-tuple-element.34.qa_ref, f32[128,2048]{1,0:T(8,128)} %get-tuple-element.35.part_ref, bf16[16,128,128]{2,1,0:T(8,128)(2,1)} %copy-done.7, bf16[16,128,128]{2,1,0:T(8,128)(2,1)} %add.106.out_ref, ...), custom_call_target="tpu_custom_call" | custom-call | flops 67108864 | bytes 3670016 | tf_op jit(solution)/shard_map/attend/pallas_call | solution.py:108
  163.5 3.1 %attend.7 = (bf16[128,2048]{1,0:T(8,128)(2,1)}, f32[128,128]{1,0:T(8,128)}) custom-call(bf16[128,2048]{1,0:T(8,128)(2,1)} %get-tuple-element.31.qa_ref, f32[128,2048]{1,0:T(8,128)} %get-tuple-element.32.part_ref, bf16[16,128,128]{2,1,0:T(8,128)(2,1)} %copy-done.8, bf16[16,128,128]{2,1,0:T(8,128)(2,1)} %add.102.out_ref, ...), custom_call_target="tpu_custom_call" | custom-call | flops 67108864 | bytes 3670016 | tf_op jit(solution)/shard_map/attend/pallas_call | solution.py:108
  166.6 3.6 %row_norm.1 = bf16[1,128,8192]{2,1,0:T(8,128)(2,1)} custom-call(bf16[128,1024]{1,0:T(8,128)(2,1)} %get-tuple-element.27.refs_0_, bf16[128,2048]{1,0:T(8,128)(2,1)} %get-tuple-element.30.refs_1_, bf16[128,2048]{1,0:T(8,128)(2,1)} %get-tuple-element.33.refs_2_, bf16[128,2048]{1,0:T(8,128)(2,1)} %get-tuple-element.36.refs_3_, ...), custom_call_target="tpu_custom_call" | custom-call | flops 3145728 | bytes 4194304 | tf_op jit(solution)/shard_map/row_norm/pallas_call | solution.py:145
  (97 shorter events, 27.9 us)
Async XLA Ops:
  2.1 8.5 %collective-permute-start = (bf16[8,128,128]{2,1,0:T(8,128)(2,1)}, bf16[8,128,128]{2,1,0:T(8,128)(2,1)S(1)}, u32[]{:S(2)}, u32[]{:S(2)}) collective-permute-start(bf16[8,128,128]{2,1,0:T(8,128)(2,1)} %kv_states.3), channel_id=1, source_target_pairs={{0,1},{2,3},{1,0},{3,2},{4,5},{6,7},{5,4},{7,6},{8,9},{10,11},{9,8... | collective-permute-start | bytes 786440 | tf_op jit(solution)/shard_map/ppermute | solution.py:172
  7.6 13.2 %collective-permute-start.12 = (bf16[40,128,128]{2,1,0:T(8,128)(2,1)}, bf16[40,128,128]{2,1,0:T(8,128)(2,1)S(1)}, u32[]{:S(2)}, u32[]{:S(2)}) collective-permute-start(bf16[40,128,128]{2,1,0:T(8,128)(2,1)} %kv_states.5), channel_id=1, source_target_pairs={{0,1},{2,3},{1,0},{3,2},{4,5},{6,7},{5,4},{7,6},{8,9},{10,11},{9,8... | collective-permute-start | bytes 3932168 | tf_op jit(solution)/shard_map/ppermute | solution.py:172
  10.1 9.4 %collective-permute-start.6 = (bf16[16,128,128]{2,1,0:T(8,128)(2,1)}, bf16[16,128,128]{2,1,0:T(8,128)(2,1)}, u32[]{:S(2)}, u32[]{:S(2)}) collective-permute-start(bf16[16,128,128]{2,1,0:T(8,128)(2,1)} %kv_states.4), channel_id=1, source_target_pairs={{0,1},{2,3},{1,0},{3,2},{4,5},{6,7},{5,4},{7,6},{8,9},{10,11},{9,8... | collective-permute-start | bytes 1572872 | tf_op jit(solution)/shard_map/ppermute | solution.py:172
  12.0 6.9 %collective-permute-start.1 = (bf16[4,128,128]{2,1,0:T(8,128)(2,1)}, bf16[4,128,128]{2,1,0:T(8,128)(2,1)S(1)}, u32[]{:S(2)}, u32[]{:S(2)}) collective-permute-start(bf16[4,128,128]{2,1,0:T(8,128)(2,1)} %fusion.14), channel_id=1, source_target_pairs={{0,2},{1,3},{2,0},{3,1},{4,6},{5,7},{6,4},{7,5},{8,10},{9,11},{10,... | collective-permute-start | bytes 393224 | tf_op jit(solution)/shard_map/ppermute | solution.py:183
  19.6 5.4 %collective-permute-start.2 = (bf16[4,128,128]{2,1,0:T(8,128)(2,1)}, bf16[4,128,128]{2,1,0:T(8,128)(2,1)}, u32[]{:S(2)}, u32[]{:S(2)}) collective-permute-start(bf16[4,128,128]{2,1,0:T(8,128)(2,1)} %broadcast_select_fusion.6), channel_id=1, source_target_pairs={{0,1},{2,3},{1,0},{3,2},{4,5},{6,7},{5,4},{7,6},{8,9},{10,11},{9,8... | collective-permute-start | bytes 393224 | tf_op jit(solution)/shard_map/ppermute | solution.py:189
  22.2 23.2 %collective-permute-start.13 = (bf16[20,128,128]{2,1,0:T(8,128)(2,1)}, bf16[20,128,128]{2,1,0:T(8,128)(2,1)}, u32[]{:S(2)}, u32[]{:S(2)}) collective-permute-start(bf16[20,128,128]{2,1,0:T(8,128)(2,1)} %fusion), channel_id=1, source_target_pairs={{0,2},{1,3},{2,0},{3,1},{4,6},{5,7},{6,4},{7,5},{8,10},{9,11},{10,... | collective-permute-start | bytes 1966088 | tf_op jit(solution)/shard_map/ppermute | solution.py:183
  24.6 20.6 %collective-permute-start.7 = (bf16[8,128,128]{2,1,0:T(8,128)(2,1)}, bf16[8,128,128]{2,1,0:T(8,128)(2,1)}, u32[]{:S(2)}, u32[]{:S(2)}) collective-permute-start(bf16[8,128,128]{2,1,0:T(8,128)(2,1)} %fusion.9), channel_id=1, source_target_pairs={{0,2},{1,3},{2,0},{3,1},{4,6},{5,7},{6,4},{7,5},{8,10},{9,11},{10,... | collective-permute-start | bytes 786440 | tf_op jit(solution)/shard_map/ppermute | solution.py:183
  24.9 21.1 %copy-start.13 = (bf16[8,128,128]{2,1,0:T(8,128)(2,1)S(1)}, bf16[8,128,128]{2,1,0:T(8,128)(2,1)}, u32[]{:S(2)}) copy-start(bf16[8,128,128]{2,1,0:T(8,128)(2,1)} %copy-done.12) | copy-start | bytes 786436
  45.3 4.6 %collective-permute-start.8 = (bf16[8,128,128]{2,1,0:T(8,128)(2,1)S(1)}, bf16[8,128,128]{2,1,0:T(8,128)(2,1)S(1)}, u32[]{:S(2)}, u32[]{:S(2)}) collective-permute-start(bf16[8,128,128]{2,1,0:T(8,128)(2,1)S(1)} %broadcast_select_fusion.3), channel_id=1, source_target_pairs={{0,1},{2,3},{1,0},{3,2},{4,5},{6,7},{5,4},{7,6},{8,9},{10,11},{9,8... | collective-permute-start | bytes 786440 | tf_op jit(solution)/shard_map/ppermute | solution.py:189
  45.4 6.2 %collective-permute-start.14 = (bf16[20,128,128]{2,1,0:T(8,128)(2,1)S(1)}, bf16[20,128,128]{2,1,0:T(8,128)(2,1)S(1)}, u32[]{:S(2)}, u32[]{:S(2)}) collective-permute-start(bf16[20,128,128]{2,1,0:T(8,128)(2,1)S(1)} %broadcast_select_fusion), channel_id=1, source_target_pairs={{0,1},{2,3},{1,0},{3,2},{4,5},{6,7},{5,4},{7,6},{8,9},{10,11},{9,8... | collective-permute-start | bytes 1966088 | tf_op jit(solution)/shard_map/ppermute | solution.py:189
  46.1 62.3 %copy-start.4 = (bf16[8,128,128]{2,1,0:T(8,128)(2,1)}, bf16[8,128,128]{2,1,0:T(8,128)(2,1)S(1)}, u32[]{:S(2)}) copy-start(bf16[8,128,128]{2,1,0:T(8,128)(2,1)S(1)} %get-tuple-element.48.f_ref) | copy-start | bytes 786436
  46.2 10.4 %collective-permute-start.3 = (bf16[8,128,128]{2,1,0:T(8,128)(2,1)S(1)}, bf16[8,128,128]{2,1,0:T(8,128)(2,1)S(1)}, u32[]{:S(2)}, u32[]{:S(2)}) collective-permute-start(bf16[8,128,128]{2,1,0:T(8,128)(2,1)S(1)} %get-tuple-element.47), channel_id=1, source_target_pairs={{0,4},{12,8},{1,5},{13,9},{2,6},{14,10},{3,7},{15,11},{16,20},{28,... | collective-permute-start | bytes 786440 | tf_op jit(solution)/shard_map/ppermute | solution.py:221
  50.3 48.7 %copy-start.2 = (bf16[16,128,128]{2,1,0:T(8,128)(2,1)}, bf16[16,128,128]{2,1,0:T(8,128)(2,1)S(1)}, u32[]{:S(2)}) copy-start(bf16[16,128,128]{2,1,0:T(8,128)(2,1)S(1)} %get-tuple-element.46.f_ref) | copy-start | bytes 1572868
  50.3 17.5 %collective-permute-start.9 = (bf16[16,128,128]{2,1,0:T(8,128)(2,1)S(1)}, bf16[16,128,128]{2,1,0:T(8,128)(2,1)S(1)}, u32[]{:S(2)}, u32[]{:S(2)}) collective-permute-start(bf16[16,128,128]{2,1,0:T(8,128)(2,1)S(1)} %get-tuple-element.45), channel_id=1, source_target_pairs={{0,4},{12,8},{1,5},{13,9},{2,6},{14,10},{3,7},{15,11},{16,20},{28,... | collective-permute-start | bytes 1572872 | tf_op jit(solution)/shard_map/ppermute | solution.py:221
  53.7 25.4 %collective-permute-start.18 = (bf16[16,128,128]{2,1,0:T(8,128)(2,1)S(1)}, bf16[16,128,128]{2,1,0:T(8,128)(2,1)S(1)}, u32[]{:S(2)}, u32[]{:S(2)}) collective-permute-start(bf16[16,128,128]{2,1,0:T(8,128)(2,1)S(1)} %get-tuple-element.51), channel_id=1, source_target_pairs={{0,4},{12,8},{1,5},{13,9},{2,6},{14,10},{3,7},{15,11},{16,20},{28,... | collective-permute-start | bytes 1572872 | tf_op jit(solution)/shard_map/ppermute | solution.py:221
  56.6 22.6 %copy-start.10 = (bf16[8,128,128]{2,1,0:T(8,128)(2,1)}, bf16[8,128,128]{2,1,0:T(8,128)(2,1)S(1)}, u32[]{:S(2)}) copy-start(bf16[8,128,128]{2,1,0:T(8,128)(2,1)S(1)} %collective-permute-done.3.in_ref) | copy-start | bytes 786436
  56.6 51.8 %collective-permute-start.4 = (bf16[8,128,128]{2,1,0:T(8,128)(2,1)S(1)}, bf16[8,128,128]{2,1,0:T(8,128)(2,1)S(1)}, u32[]{:S(2)}, u32[]{:S(2)}) collective-permute-start(bf16[8,128,128]{2,1,0:T(8,128)(2,1)S(1)} %add_convert_fusion.14), channel_id=1, source_target_pairs={{4,8},{8,4},{5,9},{9,5},{6,10},{10,6},{7,11},{11,7},{20,24},{24,20... | collective-permute-start | bytes 786440 | tf_op jit(solution)/shard_map/ppermute | solution.py:224
  57.3 32.0 %collective-permute-start.15 = (bf16[16,128,128]{2,1,0:T(8,128)(2,1)S(1)}, bf16[16,128,128]{2,1,0:T(8,128)(2,1)S(1)}, u32[]{:S(2)}, u32[]{:S(2)}) collective-permute-start(bf16[16,128,128]{2,1,0:T(8,128)(2,1)S(1)} %get-tuple-element.52), channel_id=1, source_target_pairs={{0,4},{12,8},{1,5},{13,9},{2,6},{14,10},{3,7},{15,11},{16,20},{28,... | collective-permute-start | bytes 1572872 | tf_op jit(solution)/shard_map/ppermute | solution.py:221
  67.8 11.4 %copy-start.9 = (bf16[16,128,128]{2,1,0:T(8,128)(2,1)}, bf16[16,128,128]{2,1,0:T(8,128)(2,1)S(1)}, u32[]{:S(2)}) copy-start(bf16[16,128,128]{2,1,0:T(8,128)(2,1)S(1)} %collective-permute-done.9.in_ref) | copy-start | bytes 1572868
  68.0 31.0 %collective-permute-start.10 = (bf16[16,128,128]{2,1,0:T(8,128)(2,1)S(1)}, bf16[16,128,128]{2,1,0:T(8,128)(2,1)S(1)}, u32[]{:S(2)}, u32[]{:S(2)}) collective-permute-start(bf16[16,128,128]{2,1,0:T(8,128)(2,1)S(1)} %add_convert_fusion.8), channel_id=1, source_target_pairs={{4,8},{8,4},{5,9},{9,5},{6,10},{10,6},{7,11},{11,7},{20,24},{24,20... | collective-permute-start | bytes 1572872 | tf_op jit(solution)/shard_map/ppermute | solution.py:224
  79.0 11.3 %copy-start.7 = (bf16[16,128,128]{2,1,0:T(8,128)(2,1)}, bf16[16,128,128]{2,1,0:T(8,128)(2,1)S(1)}, u32[]{:S(2)}) copy-start(bf16[16,128,128]{2,1,0:T(8,128)(2,1)S(1)} %collective-permute-done.18.in_ref) | copy-start | bytes 1572868
  79.2 25.2 %collective-permute-start.19 = (bf16[16,128,128]{2,1,0:T(8,128)(2,1)S(1)}, bf16[16,128,128]{2,1,0:T(8,128)(2,1)S(1)}, u32[]{:S(2)}, u32[]{:S(2)}) collective-permute-start(bf16[16,128,128]{2,1,0:T(8,128)(2,1)S(1)} %add_convert_fusion.2), channel_id=1, source_target_pairs={{4,8},{8,4},{5,9},{9,5},{6,10},{10,6},{7,11},{11,7},{20,24},{24,20... | collective-permute-start | bytes 1572872 | tf_op jit(solution)/shard_map/ppermute | solution.py:224
  90.3 14.1 %collective-permute-start.16 = (bf16[16,128,128]{2,1,0:T(8,128)(2,1)S(1)}, bf16[16,128,128]{2,1,0:T(8,128)(2,1)S(1)}, u32[]{:S(2)}, u32[]{:S(2)}) collective-permute-start(bf16[16,128,128]{2,1,0:T(8,128)(2,1)S(1)} %add_convert_fusion.5), channel_id=1, source_target_pairs={{4,8},{8,4},{5,9},{9,5},{6,10},{10,6},{7,11},{11,7},{20,24},{24,20... | collective-permute-start | bytes 1572872 | tf_op jit(solution)/shard_map/ppermute | solution.py:224
  91.8 11.8 %collective-permute-start.21 = (bf16[8,128,128]{2,1,0:T(8,128)(2,1)S(1)}, bf16[8,128,128]{2,1,0:T(8,128)(2,1)S(1)}, u32[]{:S(2)}, u32[]{:S(2)}) collective-permute-start(bf16[8,128,128]{2,1,0:T(8,128)(2,1)S(1)} %get-tuple-element.54), channel_id=1, source_target_pairs={{0,4},{12,8},{1,5},{13,9},{2,6},{14,10},{3,7},{15,11},{16,20},{28,... | collective-permute-start | bytes 786440 | tf_op jit(solution)/shard_map/ppermute | solution.py:221
  100.1 48.2 %collective-permute-start.11 = (bf16[16,128,128]{2,1,0:T(8,128)(2,1)}, bf16[16,128,128]{2,1,0:T(8,128)(2,1)}, u32[]{:S(2)}, u32[]{:S(2)}) collective-permute-start(bf16[16,128,128]{2,1,0:T(8,128)(2,1)} %add_convert_fusion.7), channel_id=1, source_target_pairs={{4,0},{8,12},{5,1},{9,13},{6,2},{10,14},{7,3},{11,15},{20,16},{24,... | collective-permute-start | bytes 1572872 | tf_op jit(solution)/shard_map/ppermute | solution.py:226
  103.7 6.9 %collective-permute-start.22 = (bf16[8,128,128]{2,1,0:T(8,128)(2,1)S(1)}, bf16[8,128,128]{2,1,0:T(8,128)(2,1)S(1)}, u32[]{:S(2)}, u32[]{:S(2)}) collective-permute-start(bf16[8,128,128]{2,1,0:T(8,128)(2,1)S(1)} %add_convert_fusion.11), channel_id=1, source_target_pairs={{4,8},{8,4},{5,9},{9,5},{6,10},{10,6},{7,11},{11,7},{20,24},{24,20... | collective-permute-start | bytes 786440 | tf_op jit(solution)/shard_map/ppermute | solution.py:224
  105.9 50.6 %collective-permute-start.20 = (bf16[16,128,128]{2,1,0:T(8,128)(2,1)}, bf16[16,128,128]{2,1,0:T(8,128)(2,1)}, u32[]{:S(2)}, u32[]{:S(2)}) collective-permute-start(bf16[16,128,128]{2,1,0:T(8,128)(2,1)} %get-tuple-element.49), channel_id=1, source_target_pairs={{4,0},{8,12},{5,1},{9,13},{6,2},{10,14},{7,3},{11,15},{20,16},{24,... | collective-permute-start | bytes 1572872 | tf_op jit(solution)/shard_map/ppermute | solution.py:226
  107.1 51.3 %collective-permute-start.17 = (bf16[16,128,128]{2,1,0:T(8,128)(2,1)}, bf16[16,128,128]{2,1,0:T(8,128)(2,1)}, u32[]{:S(2)}, u32[]{:S(2)}) collective-permute-start(bf16[16,128,128]{2,1,0:T(8,128)(2,1)} %get-tuple-element.50), channel_id=1, source_target_pairs={{4,0},{8,12},{5,1},{9,13},{6,2},{10,14},{7,3},{11,15},{20,16},{24,... | collective-permute-start | bytes 1572872 | tf_op jit(solution)/shard_map/ppermute | solution.py:226
  109.3 35.8 %collective-permute-start.5 = (bf16[8,128,128]{2,1,0:T(8,128)(2,1)}, bf16[8,128,128]{2,1,0:T(8,128)(2,1)S(1)}, u32[]{:S(2)}, u32[]{:S(2)}) collective-permute-start(bf16[8,128,128]{2,1,0:T(8,128)(2,1)} %add_convert_fusion.13), channel_id=1, source_target_pairs={{4,0},{8,12},{5,1},{9,13},{6,2},{10,14},{7,3},{11,15},{20,16},{24,... | collective-permute-start | bytes 786440 | tf_op jit(solution)/shard_map/ppermute | solution.py:226
  110.8 42.6 %collective-permute-start.23 = (bf16[8,128,128]{2,1,0:T(8,128)(2,1)S(1)}, bf16[8,128,128]{2,1,0:T(8,128)(2,1)S(1)}, u32[]{:S(2)}, u32[]{:S(2)}) collective-permute-start(bf16[8,128,128]{2,1,0:T(8,128)(2,1)S(1)} %add_convert_fusion.10), channel_id=1, source_target_pairs={{4,0},{8,12},{5,1},{9,13},{6,2},{10,14},{7,3},{11,15},{20,16},{24,... | collective-permute-start | bytes 786440 | tf_op jit(solution)/shard_map/ppermute | solution.py:226
  128.2 16.9 %copy-start.15 = (bf16[8,128,128]{2,1,0:T(8,128)(2,1)S(1)}, bf16[8,128,128]{2,1,0:T(8,128)(2,1)}, u32[]{:S(2)}) copy-start(bf16[8,128,128]{2,1,0:T(8,128)(2,1)} %copy-done.14) | copy-start | bytes 786436
  132.9 15.3 %copy-start.6 = (bf16[16,128,128]{2,1,0:T(8,128)(2,1)S(1)}, bf16[16,128,128]{2,1,0:T(8,128)(2,1)}, u32[]{:S(2)}) copy-start(bf16[16,128,128]{2,1,0:T(8,128)(2,1)} %copy-done.5) | copy-start | bytes 1572868
  (10 other events, 41.4 us)

commit v2 on v0

v2 whole, which is shorter than its diff:
```python
import functools

import jax
import jax.numpy as jnp
from jax import lax
from jax.experimental import pallas as pl
from jax.experimental.pallas import tpu as pltpu
from jax.sharding import PartitionSpec as P

DH = 128
F32 = jnp.float32
BF16 = jnp.bfloat16
VMEM_LIMIT = 8 << 20
VMEM = pl.BlockSpec(memory_space=pltpu.VMEM)
ANY = pl.BlockSpec(memory_space=pl.ANY)


def silu(x):
    x = x.astype(F32)
    return (x * (0.5 * jnp.tanh(0.5 * x) + 0.5)).astype(BF16)


def call(kernel, name, operands, outs, after):
    n_in, n_after = len(operands), len(after)

    def run(*refs):
        kernel(refs[:n_in], refs[n_in + n_after :])

    return pl.pallas_call(
        run,
        in_specs=[VMEM] * n_in + [ANY] * n_after,
        out_specs=[VMEM] * len(outs),
        out_shape=outs,
        compiler_params=pltpu.CompilerParams(vmem_limit_bytes=VMEM_LIMIT),
        cost_estimate=pl.CostEstimate(flops=1, bytes_accessed=1, transcendentals=0),
        name=name,
    )(*operands, *after)


def head_cols(h):
    return slice(h * DH, (h + 1) * DH)


def states_of(count, rows, kind=BF16):
    return jax.ShapeDtypeStruct((count, rows, DH), kind)


def kv_states(k_rows, v_rows, first, count, after):
    rows = k_rows.shape[0]

    def kernel(ins, outs):
        k_ref, v_ref = ins
        c_ref, ka_ref = outs
        for h in range(count):
            ka = silu(k_ref[:, head_cols(first + h)])
            ka_ref[:, head_cols(h)] = ka
            c_ref[h] = lax.dot_general(
                ka, v_ref[:, head_cols(first + h)], (((0,), (0,)), ((), ())),
                preferred_element_type=F32,
            ).astype(BF16)

    outs = [states_of(count, DH), jax.ShapeDtypeStruct((rows, count * DH), BF16)]
    return call(
        kernel, "kv_states", [k_rows, v_rows], outs, after
    )


def places_block():
    odd = lax.rem(lax.axis_index("ctx"), 2)
    along = lax.axis_index("head")
    rows = lax.broadcasted_iota(jnp.int32, (8, DH), 0)
    left = jnp.where(along < 2, 1, 0)
    outer = jnp.where((along == 0) | (along == 3), 1, 0)
    value = jnp.where(rows == 0, odd, jnp.where(rows == 1, left, outer))
    return value.astype(F32)


def first_kv_states(k_rows, v_rows, count):
    rows = k_rows.shape[0]

    def kernel(k_ref, v_ref, c_ref, ka_ref, m_ref):
        m_ref[...] = places_block()
        for h in range(count):
            ka = silu(k_ref[:, head_cols(h)])
            ka_ref[:, head_cols(h)] = ka
            c_ref[h] = lax.dot_general(
                ka, v_ref[:, head_cols(h)], (((0,), (0,)), ((), ())),
                preferred_element_type=F32,
            ).astype(BF16)

    block = pl.BlockSpec((rows, count * DH), lambda i: (0, 0))
    return pl.pallas_call(
        kernel,
        grid=(1,),
        in_specs=[block, block],
        out_specs=[VMEM, VMEM, VMEM],
        out_shape=[
            states_of(count, DH),
            jax.ShapeDtypeStruct((rows, count * DH), BF16),
            jax.ShapeDtypeStruct((8, DH), F32),
        ],
        compiler_params=pltpu.CompilerParams(vmem_limit_bytes=VMEM_LIMIT),
        cost_estimate=pl.CostEstimate(
            flops=2 * count * rows * DH * DH,
            bytes_accessed=8 * count * rows * DH,
            transcendentals=count * rows * DH,
        ),
        name="first_kv_states",
    )(k_rows, v_rows)


def early_states(other, parts, sizes, after):
    half = other.shape[0] // 2

    def kernel(ins, outs):
        place = lax.axis_index("ctx")
        odd, later = lax.rem(place, 2) == 1, place >= 2
        at = 0
        for f_ref, size in zip(outs, sizes):
            for h in range(size):
                g = at + h
                early = jnp.where(odd, ins[0][g].astype(F32), 0.0)
                if parts:
                    a, b = (ins[1], ins[2]) if g < half else (ins[2], ins[1])
                    i = g if g < half else g - half
                    before = jnp.where(odd, b[i].astype(F32), a[i].astype(F32))
                    early = early + jnp.where(later, before, 0.0)
                f_ref[h] = early.astype(BF16)
            at += size

    outs = [states_of(size, DH) for size in sizes]
    return call(kernel, "early_states", [other, *parts], outs, after)


def total(*terms):
    out = terms[0].astype(F32)
    for term in terms[1:]:
        out = out + term.astype(F32)
    return out


def local_scores(q_rows, ka, first, ka_first, count, after):
    rows = q_rows.shape[0]

    def kernel(ins, outs):
        q_ref, ka_ref = ins
        causal = lax.broadcasted_iota(jnp.int32, (rows, rows), 0) >= lax.broadcasted_iota(
            jnp.int32, (rows, rows), 1
        )
        for h in range(count):
            qa = silu(q_ref[:, head_cols(first + h)])
            scores = lax.dot_general(
                qa, ka_ref[:, head_cols(ka_first + h)], (((1,), (1,)), ((), ())),
                preferred_element_type=F32,
            )
            at = h * (rows + DH)
            outs[0][:, at : at + rows] = jnp.where(causal, scores, 0.0).astype(BF16)
            outs[0][:, at + rows : at + rows + DH] = qa

    out = jax.ShapeDtypeStruct((rows, count * (rows + DH)), BF16)
    return call(
        kernel, "local_scores", [q_rows, ka], [out], after
    )[0]


def attend_head(both_ref, v, terms, h, rows):
    at = h * (rows + DH)
    state = terms[0][h].astype(F32)
    for ref in terms[1:]:
        state = state + ref[h].astype(F32)
    right = jnp.concatenate([v, state.astype(BF16)], axis=0)
    return jnp.dot(
        both_ref[:, at : at + rows + DH], right, preferred_element_type=F32
    ).astype(BF16)


def attend(both, v_rows, first, terms, after):
    rows = both.shape[0]
    count = both.shape[1] // (rows + DH)

    def kernel(ins, outs):
        both_ref, v_ref, terms = ins[0], ins[1], ins[2:]
        total = None
        for h in range(count):
            attn = attend_head(both_ref, v_ref[:, head_cols(first + h)], terms, h, rows)
            outs[0][:, head_cols(h)] = attn
            wide = attn.astype(F32)
            total = wide * wide if total is None else total + wide * wide
        outs[1][...] = total

    outs = [
        jax.ShapeDtypeStruct((rows, count * DH), BF16),
        jax.ShapeDtypeStruct((rows, DH), F32),
    ]
    return call(
        kernel, "attend", [both, v_rows, *terms], outs, after
    )


def last_attend(both, v_rows, first, terms, attns, squares, gain):
    rows, width = v_rows.shape
    count = both.shape[1] // (rows + DH)
    n_terms, n = len(terms), len(attns)
    starts, at = [], 0
    for a in attns:
        starts.append(at)
        at += a.shape[1]

    def kernel(ins, outs):
        both_ref, v_ref = ins[0], ins[1]
        terms = ins[2 : 2 + n_terms]
        attn_refs = ins[2 + n_terms : 2 + n_terms + n]
        sq_refs = ins[2 + n_terms + n : 2 + n_terms + 2 * n]
        gain_ref, out_ref = ins[-1], outs[0]
        total = None
        for ref in sq_refs:
            total = ref[...] if total is None else total + ref[...]
        last = []
        for h in range(count):
            attn = attend_head(both_ref, v_ref[:, head_cols(first + h)], terms, h, rows)
            last.append(attn)
            wide = attn.astype(F32)
            total = wide * wide if total is None else total + wide * wide
        mean_sq = jnp.sum(total, axis=1, keepdims=True) / width
        scale = jnp.broadcast_to(lax.rsqrt(mean_sq + 1e-06), (rows, DH))
        for ref, start in zip(attn_refs, starts):
            for h in range(ref.shape[1] // DH):
                cols = slice(start + h * DH, start + (h + 1) * DH)
                out_ref[0, :, cols] = (
                    ref[:, head_cols(h)].astype(F32) * scale * gain_ref[:, cols]
                ).astype(BF16)
        for h in range(count):
            cols = head_cols(first + h)
            out_ref[0, :, cols] = (
                last[h].astype(F32) * scale * gain_ref[:, cols]
            ).astype(BF16)

    out = jax.ShapeDtypeStruct((1, rows, width), BF16)
    return call(
        kernel, "last_attend",
        [both, v_rows, *terms, *attns, *squares, gain.reshape(1, width)], [out], [],
    )[0]


def held(x, after):
    return lax.optimization_barrier((x, *after))[0]


def both_ways(pairs):
    return pairs + [(b, a) for a, b in pairs]


class Group:
    def __init__(self, n_ctx, first, sizes):
        self.n_ctx = n_ctx
        self.first, self.sizes, self.count = first, sizes, sum(sizes)
        self.partner = both_ways([(2 * p, 2 * p + 1) for p in range(n_ctx // 2)])
        self.got = []

    def begin(self, own, ka, odd):
        self.own, self.ka, self.odd = own, ka, odd
        if self.n_ctx % 2 == 0:
            self.other = lax.ppermute(own, "ctx", self.partner)
        return [own]

    def cross(self, after):
        n = self.n_ctx
        if n == 2 or n % 2:
            return after
        half = self.count // 2
        own, other = self.own, held(self.other, after)
        mine = jnp.where(
            self.odd, total(own[half:], other[half:]), total(own[:half], other[:half])
        ).astype(BF16)
        for s in range(1, n // 2):
            pairs = [(i, i + 2 * s) for i in range(n - 2 * s)]
            self.got.append(lax.ppermute(mine, "ctx", both_ways(pairs) if n == 4 else pairs))
        return [mine]

    def spread(self, after):
        n = self.n_ctx
        if n == 2 or n % 2:
            return after
        got = self.got[0] if n == 4 else total(*self.got).astype(BF16)
        self.got = [held(got, after)]
        self.theirs = lax.ppermute(self.got[0], "ctx", self.partner)
        return self.got

    def finish(self, after):
        n = self.n_ctx
        parts = []
        if n == 1:
            return [jnp.zeros_like(self.own)]
        if n % 2:
            got = [
                lax.ppermute(self.own, "ctx", [(i, i + s) for i in range(n - s)])
                for s in range(1, n)
            ]
            return [total(*got).astype(BF16)]
        if n > 2:
            parts = [self.got[0], self.theirs]
        return early_states(self.other, parts, self.sizes, after)


def whole_chain(n_head, own, early):
    upto = total(early, own)
    early = early.astype(F32)
    left = lax.axis_index("head") < n_head // 2
    if n_head == 1:
        return early.astype(BF16)
    if n_head % 2:
        lower = higher = jnp.zeros_like(own)
        for _ in range(n_head - 1):
            lower = lax.ppermute(
                total(lower, upto).astype(BF16), "head", [(i, i + 1) for i in range(n_head - 1)]
            )
            higher = lax.ppermute(
                total(higher, early).astype(BF16), "head", [(i + 1, i) for i in range(n_head - 1)]
            )
        return total(early, lower, higher).astype(BF16)
    mid = n_head // 2
    mine, mirror = jnp.where(left, upto, early), jnp.where(left, early, upto)
    inward = jnp.zeros_like(own)
    for t in range(mid - 1):
        inward = inward + lax.ppermute(
            total(inward, mine).astype(BF16), "head", [(t, t + 1), (n_head - 1 - t, n_head - 2 - t)]
        )
    outward = lax.ppermute(total(inward, mine).astype(BF16), "head", both_ways([(mid - 1, mid)]))
    for t in range(mid - 1, 0, -1):
        outward = outward + lax.ppermute(
            total(outward, mirror).astype(BF16), "head", [(t, t - 1), (n_head - 1 - t, n_head - t)]
        )
    return total(early, inward, outward).astype(BF16)


SKEW = 3


class Four:
    def __init__(self, n_ctx, n, masks):
        self.n, self.n_ctx = n, n_ctx
        self.left, self.outer = masks[1] > 0, masks[2] > 0
        self.own, self.early, self.a, self.b = {}, {}, {}, {}
        at = lambda z, c: z * n_ctx + c
        self.swap = both_ways([(1, 2)])
        if n_ctx % 2 == 0:
            self.swap = both_ways(
                [(at(1, c), at(2, c)) for c in range(n_ctx)]
                + [(at(z, c), at(z, c + 1)) for z in (0, 3) for c in range(0, n_ctx, 2)]
            )

    def mine(self, c):
        f = self.early[c].astype(F32)
        return f + jnp.where(self.left, self.own[c].astype(F32), 0.0)

    def mirror(self, c):
        f = self.early[c].astype(F32)
        return f + jnp.where(self.left, 0.0, self.own[c].astype(F32))

    def side(self, t, after):
        inwards, outwards = t < self.n, t >= SKEW
        c = t - SKEW
        if outwards:
            out = total(self.b[c], self.mirror(c))
        if inwards and outwards:
            send = jnp.where(self.outer, self.mine(t), out)
        else:
            send = self.mine(t) if inwards else out
        send = held(send.astype(BF16), after)
        self.a[t] = lax.ppermute(send, "head", both_ways([(0, 1), (3, 2)]))
        return [send]

    def middle(self, t, after):
        send = held(total(self.a[t], self.mine(t)).astype(BF16), after)
        axes = ("head", "ctx") if self.n_ctx % 2 == 0 else "head"
        self.b[t] = lax.ppermute(send, axes, self.swap)
        return [send]

    def state(self, c, after):
        got = jnp.where(
            self.outer, self.a[c + SKEW].astype(F32), total(self.a[c], self.b[c])
        )
        return held((got + self.early[c].astype(F32)).astype(BF16), after)


def plan(heads, n_head):
    if n_head != 4 or heads % 16:
        return [[heads]]
    u = heads // 8
    return [[u], [u], [u, u], [u, u, u, u]]


def body(n_head, n_ctx, queries, keys, values, gain):
    rows, width = queries.shape[1], queries.shape[2]
    q_rows = queries.reshape(rows, width)
    k_rows = keys.reshape(rows, width)
    v_rows = values.reshape(rows, width)
    heads = width // DH
    groups, chunks = [], []
    for sizes in plan(heads, n_head):
        g = Group(n_ctx, len(chunks) and sum(c[2] for c in chunks), sizes)
        groups.append(g)
        for i, size in enumerate(sizes):
            chunks.append((g, g.first + sum(sizes[:i]), size))
    n = len(chunks)
    both, states, attns, squares = {}, {}, {}, {}

    masks = None

    def kv(g, after):
        odd = masks[0] > 0 if masks is not None else lax.axis_index("ctx") % 2 == 1
        return g.begin(*kv_states(k_rows, v_rows, g.first, g.count, after), odd)

    def scores(c, after):
        g, first, size = chunks[c]
        both[c] = local_scores(q_rows, g.ka, first, first - g.first, size, after)
        return [both[c]]

    def attention(c, after):
        attns[c], squares[c] = attend(both[c], v_rows, chunks[c][1], [states[c]], after)
        return [squares[c]]

    if n == 1:
        g = groups[0]
        clock = kv(g, [])
        clock = g.cross(clock)
        clock = g.spread(clock)
        early = g.finish(clock)[0]
        states[0] = whole_chain(n_head, g.own, early)
        scores(0, [])
    else:
        def ready(g, after):
            early = g.finish(after)
            at = 0
            for c in range(n):
                if chunks[c][0] is g:
                    four.early[c] = early[at]
                    first = chunks[c][1] - g.first
                    four.own[c] = g.own[first : first + chunks[c][2]]
                    at += 1
            return [early[0]]

        g0, g1, g2, g3 = groups
        own, ka, masks = first_kv_states(k_rows, v_rows, g0.count)
        four = Four(n_ctx, n, masks)
        clock = g0.begin(own, ka, masks[0] > 0)
        clock = kv(g1, clock)
        clock = g0.cross(clock)
        clock = kv(g2, clock)
        clock = g1.cross(clock)
        clock = kv(g3, clock)
        clock = scores(0, clock)
        clock = g0.spread(clock)
        clock = g2.cross(clock)
        clock = ready(g0, clock)
        clock = four.side(0, clock)
        clock = scores(1, clock)
        clock = g1.spread(clock)
        clock = g3.cross(clock)
        clock = ready(g1, clock)
        clock = four.side(1, clock)
        clock = scores(2, clock)
        clock = four.middle(0, clock)
        clock = g2.spread(clock)
        clock = scores(3, clock)
        clock = ready(g2, clock)
        for t in range(2, n + SKEW):
            clock = four.side(t, clock)
            if t + 2 < n:
                clock = scores(t + 2, clock)
            c = t - 1 - SKEW
            if c >= 0:
                states[c] = four.state(c, clock)
                clock = attention(c, [states[c]])
            if t == 2:
                clock = g3.spread(clock)
                clock = ready(g3, clock)
            if t - 1 < n:
                clock = four.middle(t - 1, clock)
            if 0 <= t - 2 < n:
                clock = [held(four.b[t - 2], clock)]
                four.b[t - 2] = clock[0]
        states[n - 1] = four.state(n - 1, clock)
    return last_attend(
        both[n - 1], v_rows, chunks[n - 1][1], [states[n - 1]],
        [attns[c] for c in range(n - 1)], [squares[c] for c in range(n - 1)], gain,
    )


def solution(mesh):
    n_head, n_ctx = mesh.shape["head"], mesh.shape["ctx"]
    return jax.shard_map(
        functools.partial(body, n_head, n_ctx),
        mesh=mesh,
        in_specs=(
            P(("rep", "ctx"), "head", None),
            P(("rep", "ctx"), "head", None),
            P(("rep", "ctx"), "head", None),
            P(),
        ),
        out_specs=P(("rep", "ctx"), "head", None),
        check_vma=False,
    )
```

time: 271 us -> 117 us (0.43)
  waiting for transfers between devices: 132 us -> 60.4 us
  blocking collectives: 51.7 us -> 0 us
  matrix products: 23.6 us -> 0 us
  starting transfers between devices: 14.5 us -> 37.4 us
  local copies, waits for them, and re-layouts: 18.3 us -> 3.64 us
  between operations: 13.5 us -> 0.5 us
  other arithmetic: 15.1 us -> 4.88 us
  Pallas kernels: 0 us -> 10.2 us
    all_to_all x3 -> x0, waiting for transfers between devices: 132 us -> none  [the longest x1 45.5 us: body(): lax.all_to_all(v_rows, 'head', split_axis=1, concat_axis=0, tiled=True)]
    ppermute x0 -> x31, waiting for transfers between devices: none -> 60.4 us  [the longest x11 48.4 us: side(): self.a[t] = lax.ppermute(send, 'head', both_ways([(0, 1), (3, 2)]))]
    all_to_all x1 -> x0, blocking collectives: 51.7 us -> none  [body(): back = lax.all_to_all(attn, 'head', split_axis=0, concat_axis=1, tiled=True)]
    ppermute x0 -> x31, starting transfers between devices: none -> 37.4 us  [the longest x11 29.1 us: side(): self.a[t] = lax.ppermute(send, 'head', both_ways([(0, 1), (3, 2)]))]
    dot_general x3 -> x0, matrix products: 23.6 us -> none  [the longest x1 10.1 us: block_attention(): jnp.einsum('...hts,...hsd->...htd', scores, value_blk, preferred_element_...]
    all_to_all x3 -> x0, starting transfers between devices: 14.4 us -> none  [the longest x1 6.32 us: body(): lax.all_to_all(k_rows, 'head', split_axis=1, concat_axis=0, tiled=True)]
    pallas_call x0 -> x24, Pallas kernels: none -> 10.2 us  [the longest x23 9.88 us: call(): pl.pallas_call(run, in_specs=[VMEM] * n_in + [ANY] * n_after, out_specs=[...]
    convert_element_type x4 -> x19, other arithmetic: 10.7 us -> 4.88 us  [the longest x9 1.88 us: side(): send = held(send.astype(BF16), after)]
  transfers between devices with their start and end apart: 4 -> 31, of which waited for: 3 -> 14; matrix products, arithmetic and copies ran while one was open for 10% -> 4% of each run, Pallas kernels for 0% -> 6%
where the time goes in v2:
time: 117 us
  waiting for transfers between devices  60.4 us (52%)
  starting transfers between devices  37.4 us (32%)
  Pallas kernels  10.2 us (9%)
  other arithmetic  4.88 us (4%)
  local copies, waits for them, and re-layouts  3.64 us (3%)
    ppermute x11, waiting for transfers between devices, side(): self.a[t] = lax.ppermute(send, 'head', both_ways([(0, 1), (3, 2)]))  48.4 us
    ppermute x11, starting transfers between devices, side(): self.a[t] = lax.ppermute(send, 'head', both_ways([(0, 1), (3, 2)]))  29.1 us
    ppermute x4, waiting for transfers between devices, cross(): lax.ppermute(mine, 'ctx', both_ways(pairs) if n == 4 else pairs)  10.3 us
    pallas_call x23, Pallas kernels, call(): pl.pallas_call(run, in_specs=[VMEM] * n_in + [ANY] * n_after, out_specs=[...  9.88 us
    ppermute x4, starting transfers between devices, cross(): lax.ppermute(mine, 'ctx', both_ways(pairs) if n == 4 else pairs)  6.12 us
    unnamed x12, local copies, waits for them, and re-layouts  3.64 us
  transfers between devices with their start and end apart: 31, of which 14 were waited for; matrix products, arithmetic and copies ran while one was open for 4% of the time, Pallas kernels for 6%

profile of v2, /device:TPU:0, one launch (start us, length us, event | category | flops | bytes accessed | tf_op | source)
XLA Modules:
  0.0 117.1 jit_solution(1398051076833921876)
XLA Ops:
  0.0 1.6 %copy-done = bf16[1,128,8192]{2,1,0:T(8,128)(2,1)S(1)} copy-done((bf16[1,128,8192]{2,1,0:T(8,128)(2,1)S(1)}, bf16[1,128,8192]{2,1,0:T(8,128)(2,1)}, u32[]{:S(2)}) %copy-start) | copy-done | bytes 2097176
  1.6 1.6 %copy-done.3 = bf16[1,128,8192]{2,1,0:T(8,128)(2,1)S(1)} copy-done((bf16[1,128,8192]{2,1,0:T(8,128)(2,1)S(1)}, bf16[1,128,8192]{2,1,0:T(8,128)(2,1)}, u32[]{:S(2)}) %copy-start.3) | copy-done | bytes 2097176
  4.5 0.7 collective-permute-done.1.refs_0_
  6.4 0.9 kv_states.5
  7.9 2.9 %collective-permute-start.4 = (bf16[4,128,128]{2,1,0:T(8,128)(2,1)S(1)}, bf16[4,128,128]{2,1,0:T(8,128)(2,1)S(1)}, u32[]{:S(2)}, u32[]{:S(2)}) collective-permute-start(bf16[4,128,128]{2,1,0:T(8,128)(2,1)S(1)} %select_convert_fusion.2.refs_2_), channel_id=1, source_target_pairs={{0,2},{1,3},{2,0},{3,1},{4,6},{5,7},{6,4},{7,5},{8,10},{9,11},{10,... | collective-permute-start | bytes 393224 | tf_op jit(solution)/shard_map/ppermute | solution.py:277
  11.2 3.9 %collective-permute-done.4.refs_1_ = bf16[4,128,128]{2,1,0:T(8,128)(2,1)S(1)} collective-permute-done((bf16[4,128,128]{2,1,0:T(8,128)(2,1)S(1)}, bf16[4,128,128]{2,1,0:T(8,128)(2,1)S(1)}, u32[]{:S(2)}, u32[]{:S(2)}) %collective-permute-start.4) | collective-permute-done | bytes 131104 | tf_op jit(solution)/shard_map/ppermute | solution.py:277
  15.3 2.1 %collective-permute-start.8 = (bf16[8,128,128]{2,1,0:T(8,128)(2,1)S(1)}, bf16[8,128,128]{2,1,0:T(8,128)(2,1)S(1)}, u32[]{:S(2)}, u32[]{:S(2)}) collective-permute-start(bf16[8,128,128]{2,1,0:T(8,128)(2,1)S(1)} %fusion.17.refs_3_), channel_id=1, source_target_pairs={{0,2},{1,3},{2,0},{3,1},{4,6},{5,7},{6,4},{7,5},{8,10},{9,11},{10,... | collective-permute-start | bytes 786440 | tf_op jit(solution)/shard_map/ppermute | solution.py:277
  17.7 1.6 %collective-permute-start.9 = (bf16[8,128,128]{2,1,0:T(8,128)(2,1)S(1)}, bf16[8,128,128]{2,1,0:T(8,128)(2,1)S(1)}, u32[]{:S(2)}, u32[]{:S(2)}) collective-permute-start(bf16[8,128,128]{2,1,0:T(8,128)(2,1)S(1)} %fusion.34.refs_2_), channel_id=1, source_target_pairs={{0,4},{12,8},{4,0},{8,12},{1,5},{13,9},{5,1},{9,13},{2,6},{14,10},... | collective-permute-start | bytes 786440 | tf_op jit(solution)/shard_map/ppermute | solution.py:370
  20.1 1.0 collective-permute-done.10.refs_2_
  21.2 5.0 %collective-permute-done.9 = bf16[8,128,128]{2,1,0:T(8,128)(2,1)S(1)} collective-permute-done((bf16[8,128,128]{2,1,0:T(8,128)(2,1)S(1)}, bf16[8,128,128]{2,1,0:T(8,128)(2,1)S(1)}, u32[]{:S(2)}, u32[]{:S(2)}) %collective-permute-start.9) | collective-permute-done | bytes 262176 | tf_op jit(solution)/shard_map/ppermute | solution.py:370
  26.8 1.6 %collective-permute-start.15 = (bf16[8,128,128]{2,1,0:T(8,128)(2,1)S(1)}, bf16[8,128,128]{2,1,0:T(8,128)(2,1)S(1)}, u32[]{:S(2)}, u32[]{:S(2)}) collective-permute-start(bf16[8,128,128]{2,1,0:T(8,128)(2,1)S(1)} %get-tuple-element.93.refs_2_), channel_id=1, source_target_pairs={{0,4},{12,8},{4,0},{8,12},{1,5},{13,9},{5,1},{9,13},{2,6},{14,10},... | collective-permute-start | bytes 786440 | tf_op jit(solution)/shard_map/ppermute | solution.py:370
  28.4 1.0 collective-permute-start.7
  30.1 5.4 %collective-permute-done.15 = bf16[8,128,128]{2,1,0:T(8,128)(2,1)S(1)} collective-permute-done((bf16[8,128,128]{2,1,0:T(8,128)(2,1)S(1)}, bf16[8,128,128]{2,1,0:T(8,128)(2,1)S(1)}, u32[]{:S(2)}, u32[]{:S(2)}) %collective-permute-start.15) | collective-permute-done | bytes 262176 | tf_op jit(solution)/shard_map/ppermute | solution.py:370
  36.1 6.4 %collective-permute-done.7.refs_1_.refs_3_ = bf16[16,128,128]{2,1,0:T(8,128)(2,1)S(1)} collective-permute-done((bf16[16,128,128]{2,1,0:T(8,128)(2,1)S(1)}, bf16[16,128,128]{2,1,0:T(8,128)(2,1)S(1)}, u32[]{:S(2)}, u32[]{:S(2)}) %collective-permute-start.7) | collective-permute-done | bytes 524320 | tf_op jit(solution)/shard_map/ppermute | solution.py:277
  43.0 2.6 %collective-permute-start.13 = (bf16[8,128,128]{2,1,0:T(8,128)(2,1)S(1)}, bf16[8,128,128]{2,1,0:T(8,128)(2,1)S(1)}, u32[]{:S(2)}, u32[]{:S(2)}) collective-permute-start(bf16[8,128,128]{2,1,0:T(8,128)(2,1)S(1)} %get-tuple-element.97.refs_2_), channel_id=1, source_target_pairs={{0,4},{12,8},{4,0},{8,12},{1,5},{13,9},{5,1},{9,13},{2,6},{14,10},... | collective-permute-start | bytes 786440 | tf_op jit(solution)/shard_map/ppermute | solution.py:370
  46.4 6.5 %collective-permute-start.17 = (bf16[8,128,128]{2,1,0:T(8,128)(2,1)S(1)}, bf16[8,128,128]{2,1,0:T(8,128)(2,1)S(1)}, u32[]{:S(2)}, u32[]{:S(2)}) collective-permute-start(bf16[8,128,128]{2,1,0:T(8,128)(2,1)S(1)} %fusion.4.refs_2_), channel_id=1, source_target_pairs={{0,4},{12,8},{4,0},{8,12},{1,5},{13,9},{5,1},{9,13},{2,6},{14,10},... | collective-permute-start | bytes 786440 | tf_op jit(solution)/shard_map/ppermute | solution.py:370
  53.2 6.1 %collective-permute-done.17 = bf16[8,128,128]{2,1,0:T(8,128)(2,1)S(1)} collective-permute-done((bf16[8,128,128]{2,1,0:T(8,128)(2,1)S(1)}, bf16[8,128,128]{2,1,0:T(8,128)(2,1)S(1)}, u32[]{:S(2)}, u32[]{:S(2)}) %collective-permute-start.17) | collective-permute-done | bytes 262176 | tf_op jit(solution)/shard_map/ppermute | solution.py:370
  60.0 3.3 %collective-permute-start.19 = (bf16[8,128,128]{2,1,0:T(8,128)(2,1)S(1)}, bf16[8,128,128]{2,1,0:T(8,128)(2,1)S(1)}, u32[]{:S(2)}, u32[]{:S(2)}) collective-permute-start(bf16[8,128,128]{2,1,0:T(8,128)(2,1)S(1)} %fusion.6.refs_2_), channel_id=1, source_target_pairs={{0,4},{12,8},{4,0},{8,12},{1,5},{13,9},{5,1},{9,13},{2,6},{14,10},... | collective-permute-start | bytes 786440 | tf_op jit(solution)/shard_map/ppermute | solution.py:370
  64.0 4.7 %collective-permute-done.19 = bf16[8,128,128]{2,1,0:T(8,128)(2,1)S(1)} collective-permute-done((bf16[8,128,128]{2,1,0:T(8,128)(2,1)S(1)}, bf16[8,128,128]{2,1,0:T(8,128)(2,1)S(1)}, u32[]{:S(2)}, u32[]{:S(2)}) %collective-permute-start.19) | collective-permute-done | bytes 262176 | tf_op jit(solution)/shard_map/ppermute | solution.py:370
  69.6 2.0 %collective-permute-start.21 = (bf16[8,128,128]{2,1,0:T(8,128)(2,1)S(1)}, bf16[8,128,128]{2,1,0:T(8,128)(2,1)S(1)}, u32[]{:S(2)}, u32[]{:S(2)}) collective-permute-start(bf16[8,128,128]{2,1,0:T(8,128)(2,1)S(1)} %get-tuple-element.112.refs_2_), channel_id=1, source_target_pairs={{0,4},{12,8},{4,0},{8,12},{1,5},{13,9},{5,1},{9,13},{2,6},{14,10},... | collective-permute-start | bytes 786440 | tf_op jit(solution)/shard_map/ppermute | solution.py:370
  72.2 2.5 %collective-permute-start.25 = (bf16[8,128,128]{2,1,0:T(8,128)(2,1)S(1)}, bf16[8,128,128]{2,1,0:T(8,128)(2,1)S(1)}, u32[]{:S(2)}, u32[]{:S(2)}) collective-permute-start(bf16[8,128,128]{2,1,0:T(8,128)(2,1)S(1)} %fusion.10), channel_id=1, source_target_pairs={{0,4},{12,8},{4,0},{8,12},{1,5},{13,9},{5,1},{9,13},{2,6},{14,10},... | collective-permute-start | bytes 786440 | tf_op jit(solution)/shard_map/ppermute | solution.py:370
  74.7 4.1 %collective-permute-done.21 = bf16[8,128,128]{2,1,0:T(8,128)(2,1)S(1)} collective-permute-done((bf16[8,128,128]{2,1,0:T(8,128)(2,1)S(1)}, bf16[8,128,128]{2,1,0:T(8,128)(2,1)S(1)}, u32[]{:S(2)}, u32[]{:S(2)}) %collective-permute-start.21) | collective-permute-done | bytes 262176 | tf_op jit(solution)/shard_map/ppermute | solution.py:370
  78.7 3.1 %collective-permute-done.25 = bf16[8,128,128]{2,1,0:T(8,128)(2,1)S(1)} collective-permute-done((bf16[8,128,128]{2,1,0:T(8,128)(2,1)S(1)}, bf16[8,128,128]{2,1,0:T(8,128)(2,1)S(1)}, u32[]{:S(2)}, u32[]{:S(2)}) %collective-permute-start.25) | collective-permute-done | bytes 262176 | tf_op jit(solution)/shard_map/ppermute | solution.py:370
  81.8 0.7 fusion.32
  83.1 3.1 %collective-permute-start.23 = (bf16[8,128,128]{2,1,0:T(8,128)(2,1)S(1)}, bf16[8,128,128]{2,1,0:T(8,128)(2,1)S(1)}, u32[]{:S(2)}, u32[]{:S(2)}) collective-permute-start(bf16[8,128,128]{2,1,0:T(8,128)(2,1)S(1)} %fusion.12), channel_id=1, source_target_pairs={{0,4},{12,8},{4,0},{8,12},{1,5},{13,9},{5,1},{9,13},{2,6},{14,10},... | collective-permute-start | bytes 786440 | tf_op jit(solution)/shard_map/ppermute | solution.py:370
  86.6 5.2 %collective-permute-done.23 = bf16[8,128,128]{2,1,0:T(8,128)(2,1)S(1)} collective-permute-done((bf16[8,128,128]{2,1,0:T(8,128)(2,1)S(1)}, bf16[8,128,128]{2,1,0:T(8,128)(2,1)S(1)}, u32[]{:S(2)}, u32[]{:S(2)}) %collective-permute-start.23) | collective-permute-done | bytes 262176 | tf_op jit(solution)/shard_map/ppermute | solution.py:370
  93.0 3.9 %collective-permute-start.30 = (bf16[8,128,128]{2,1,0:T(8,128)(2,1)S(1)}, bf16[8,128,128]{2,1,0:T(8,128)(2,1)S(1)}, u32[]{:S(2)}, u32[]{:S(2)}) collective-permute-start(bf16[8,128,128]{2,1,0:T(8,128)(2,1)S(1)} %fusion.14), channel_id=1, source_target_pairs={{0,4},{12,8},{4,0},{8,12},{1,5},{13,9},{5,1},{9,13},{2,6},{14,10},... | collective-permute-start | bytes 786440 | tf_op jit(solution)/shard_map/ppermute | solution.py:370
  96.9 7.1 %collective-permute-done.30 = bf16[8,128,128]{2,1,0:T(8,128)(2,1)S(1)} collective-permute-done((bf16[8,128,128]{2,1,0:T(8,128)(2,1)S(1)}, bf16[8,128,128]{2,1,0:T(8,128)(2,1)S(1)}, u32[]{:S(2)}, u32[]{:S(2)}) %collective-permute-start.30) | collective-permute-done | bytes 262176 | tf_op jit(solution)/shard_map/ppermute | solution.py:370
  104.1 3.3 %collective-permute-done.27 = bf16[8,128,128]{2,1,0:T(8,128)(2,1)S(1)} collective-permute-done((bf16[8,128,128]{2,1,0:T(8,128)(2,1)S(1)}, bf16[8,128,128]{2,1,0:T(8,128)(2,1)S(1)}, u32[]{:S(2)}, u32[]{:S(2)}) %collective-permute-start.27) | collective-permute-done | bytes 262176 | tf_op jit(solution)/shard_map/ppermute | solution.py:370
  108.2 1.8 %collective-permute-start.29 = (bf16[8,128,128]{2,1,0:T(8,128)(2,1)S(1)}, bf16[8,128,128]{2,1,0:T(8,128)(2,1)S(1)}, u32[]{:S(2)}, u32[]{:S(2)}) collective-permute-start(bf16[8,128,128]{2,1,0:T(8,128)(2,1)S(1)} %fusion.15), channel_id=1, source_target_pairs={{0,4},{12,8},{4,0},{8,12},{1,5},{13,9},{5,1},{9,13},{2,6},{14,10},... | collective-permute-start | bytes 786440 | tf_op jit(solution)/shard_map/ppermute | solution.py:370
  110.3 4.3 %collective-permute-done.29 = bf16[8,128,128]{2,1,0:T(8,128)(2,1)S(1)} collective-permute-done((bf16[8,128,128]{2,1,0:T(8,128)(2,1)S(1)}, bf16[8,128,128]{2,1,0:T(8,128)(2,1)S(1)}, u32[]{:S(2)}, u32[]{:S(2)}) %collective-permute-start.29) | collective-permute-done | bytes 262176 | tf_op jit(solution)/shard_map/ppermute | solution.py:370
  114.8 2.4 %last_attend.1 = bf16[1,128,8192]{2,1,0:T(8,128)(2,1)} custom-call(bf16[128,2048]{1,0:T(8,128)(2,1)S(1)} %local_scores.15.refs_0_, bf16[128,8192]{1,0:T(8,128)(2,1)S(1)} %bitcast.21, bf16[8,128,128]{2,1,0:T(8,128)(2,1)S(1)} %fusion.25.refs_2_, bf16[128,1024]{1,0:T(8,128)(2,1)S(1)} %get-tuple-element.142.refs_3_, ...), custom_call_target="tpu_custom_call" | custom-call | flops 1 | bytes 1 | tf_op jit(solution)/shard_map/last_attend/pallas_call | solution.py:29
  (86 shorter events, 13.9 us)
Async XLA Ops:
  3.6 1.7 %collective-permute-start.1 = (bf16[8,128,128]{2,1,0:T(8,128)(2,1)S(1)}, bf16[8,128,128]{2,1,0:T(8,128)(2,1)S(1)}, u32[]{:S(2)}, u32[]{:S(2)}) collective-permute-start(bf16[8,128,128]{2,1,0:T(8,128)(2,1)S(1)} %get-tuple-element.78.refs_2_), channel_id=1, source_target_pairs={{0,1},{2,3},{1,0},{3,2},{4,5},{6,7},{5,4},{7,6},{8,9},{10,11},{9,8... | collective-permute-start | bytes 786440 | tf_op jit(solution)/shard_map/ppermute | solution.py:263
  4.4 1.9 %collective-permute-start = (bf16[8,128,128]{2,1,0:T(8,128)(2,1)S(1)}, bf16[8,128,128]{2,1,0:T(8,128)(2,1)S(1)}, u32[]{:S(2)}, u32[]{:S(2)}) collective-permute-start(bf16[8,128,128]{2,1,0:T(8,128)(2,1)S(1)} %get-tuple-element.79), channel_id=1, source_target_pairs={{0,1},{2,3},{1,0},{3,2},{4,5},{6,7},{5,4},{7,6},{8,9},{10,11},{9,8... | collective-permute-start | bytes 786440 | tf_op jit(solution)/shard_map/ppermute | solution.py:263
  7.3 12.4 %collective-permute-start.2 = (bf16[32,128,128]{2,1,0:T(8,128)(2,1)S(1)}, bf16[32,128,128]{2,1,0:T(8,128)(2,1)S(1)}, u32[]{:S(2)}, u32[]{:S(2)}) collective-permute-start(bf16[32,128,128]{2,1,0:T(8,128)(2,1)S(1)} %get-tuple-element.84.refs_2_), channel_id=1, source_target_pairs={{0,1},{2,3},{1,0},{3,2},{4,5},{6,7},{5,4},{7,6},{8,9},{10,11},{9,8... | collective-permute-start | bytes 3145736 | tf_op jit(solution)/shard_map/ppermute | solution.py:263
  7.9 7.3 %collective-permute-start.6 = (bf16[16,128,128]{2,1,0:T(8,128)(2,1)S(1)}, bf16[16,128,128]{2,1,0:T(8,128)(2,1)S(1)}, u32[]{:S(2)}, u32[]{:S(2)}) collective-permute-start(bf16[16,128,128]{2,1,0:T(8,128)(2,1)S(1)} %get-tuple-element.81), channel_id=1, source_target_pairs={{0,1},{2,3},{1,0},{3,2},{4,5},{6,7},{5,4},{7,6},{8,9},{10,11},{9,8... | collective-permute-start | bytes 1572872 | tf_op jit(solution)/shard_map/ppermute | solution.py:263
  7.9 7.2 %collective-permute-start.4 = (bf16[4,128,128]{2,1,0:T(8,128)(2,1)S(1)}, bf16[4,128,128]{2,1,0:T(8,128)(2,1)S(1)}, u32[]{:S(2)}, u32[]{:S(2)}) collective-permute-start(bf16[4,128,128]{2,1,0:T(8,128)(2,1)S(1)} %select_convert_fusion.2.refs_2_), channel_id=1, source_target_pairs={{0,2},{1,3},{2,0},{3,1},{4,6},{5,7},{6,4},{7,5},{8,10},{9,11},{10,... | collective-permute-start | bytes 393224 | tf_op jit(solution)/shard_map/ppermute | solution.py:277
  10.9 8.8 %collective-permute-start.3 = (bf16[4,128,128]{2,1,0:T(8,128)(2,1)S(1)}, bf16[4,128,128]{2,1,0:T(8,128)(2,1)S(1)}, u32[]{:S(2)}, u32[]{:S(2)}) collective-permute-start(bf16[4,128,128]{2,1,0:T(8,128)(2,1)S(1)} %select_convert_fusion.1.refs_2_), channel_id=1, source_target_pairs={{0,2},{1,3},{2,0},{3,1},{4,6},{5,7},{6,4},{7,5},{8,10},{9,11},{10,... | collective-permute-start | bytes 393224 | tf_op jit(solution)/shard_map/ppermute | solution.py:277
  15.2 2.3 %collective-permute-start.5 = (bf16[4,128,128]{2,1,0:T(8,128)(2,1)S(1)}, bf16[4,128,128]{2,1,0:T(8,128)(2,1)S(1)}, u32[]{:S(2)}, u32[]{:S(2)}) collective-permute-start(bf16[4,128,128]{2,1,0:T(8,128)(2,1)S(1)} %collective-permute-done.4.refs_1_), channel_id=1, source_target_pairs={{0,1},{2,3},{1,0},{3,2},{4,5},{6,7},{5,4},{7,6},{8,9},{10,11},{9,8... | collective-permute-start | bytes 393224 | tf_op jit(solution)/shard_map/ppermute | solution.py:286
  15.3 11.4 %collective-permute-start.8 = (bf16[8,128,128]{2,1,0:T(8,128)(2,1)S(1)}, bf16[8,128,128]{2,1,0:T(8,128)(2,1)S(1)}, u32[]{:S(2)}, u32[]{:S(2)}) collective-permute-start(bf16[8,128,128]{2,1,0:T(8,128)(2,1)S(1)} %fusion.17.refs_3_), channel_id=1, source_target_pairs={{0,2},{1,3},{2,0},{3,1},{4,6},{5,7},{6,4},{7,5},{8,10},{9,11},{10,... | collective-permute-start | bytes 786440 | tf_op jit(solution)/shard_map/ppermute | solution.py:277
  17.7 8.5 %collective-permute-start.9 = (bf16[8,128,128]{2,1,0:T(8,128)(2,1)S(1)}, bf16[8,128,128]{2,1,0:T(8,128)(2,1)S(1)}, u32[]{:S(2)}, u32[]{:S(2)}) collective-permute-start(bf16[8,128,128]{2,1,0:T(8,128)(2,1)S(1)} %fusion.34.refs_2_), channel_id=1, source_target_pairs={{0,4},{12,8},{4,0},{8,12},{1,5},{13,9},{5,1},{9,13},{2,6},{14,10},... | collective-permute-start | bytes 786440 | tf_op jit(solution)/shard_map/ppermute | solution.py:370
  19.6 1.4 %collective-permute-start.10 = (bf16[4,128,128]{2,1,0:T(8,128)(2,1)S(1)}, bf16[4,128,128]{2,1,0:T(8,128)(2,1)S(1)}, u32[]{:S(2)}, u32[]{:S(2)}) collective-permute-start(bf16[4,128,128]{2,1,0:T(8,128)(2,1)S(1)} %collective-permute-done.3.refs_1_), channel_id=1, source_target_pairs={{0,1},{2,3},{1,0},{3,2},{4,5},{6,7},{5,4},{7,6},{8,9},{10,11},{9,8... | collective-permute-start | bytes 393224 | tf_op jit(solution)/shard_map/ppermute | solution.py:286
  26.7 3.1 %collective-permute-start.11 = (bf16[8,128,128]{2,1,0:T(8,128)(2,1)S(1)}, bf16[8,128,128]{2,1,0:T(8,128)(2,1)S(1)}, u32[]{:S(2)}, u32[]{:S(2)}) collective-permute-start(bf16[8,128,128]{2,1,0:T(8,128)(2,1)S(1)} %collective-permute-done.8.refs_2_.refs_1_), channel_id=1, source_target_pairs={{0,1},{2,3},{1,0},{3,2},{4,5},{6,7},{5,4},{7,6},{8,9},{10,11},{9,8... | collective-permute-start | bytes 786440 | tf_op jit(solution)/shard_map/ppermute | solution.py:286
  26.8 8.7 %collective-permute-start.15 = (bf16[8,128,128]{2,1,0:T(8,128)(2,1)S(1)}, bf16[8,128,128]{2,1,0:T(8,128)(2,1)S(1)}, u32[]{:S(2)}, u32[]{:S(2)}) collective-permute-start(bf16[8,128,128]{2,1,0:T(8,128)(2,1)S(1)} %get-tuple-element.93.refs_2_), channel_id=1, source_target_pairs={{0,4},{12,8},{4,0},{8,12},{1,5},{13,9},{5,1},{9,13},{2,6},{14,10},... | collective-permute-start | bytes 786440 | tf_op jit(solution)/shard_map/ppermute | solution.py:370
  28.4 14.0 %collective-permute-start.7 = (bf16[16,128,128]{2,1,0:T(8,128)(2,1)S(1)}, bf16[16,128,128]{2,1,0:T(8,128)(2,1)S(1)}, u32[]{:S(2)}, u32[]{:S(2)}) collective-permute-start(bf16[16,128,128]{2,1,0:T(8,128)(2,1)S(1)} %select_convert_fusion.refs_3_), channel_id=1, source_target_pairs={{0,2},{1,3},{2,0},{3,1},{4,6},{5,7},{6,4},{7,5},{8,10},{9,11},{10,... | collective-permute-start | bytes 1572872 | tf_op jit(solution)/shard_map/ppermute | solution.py:277
  42.4 3.2 %collective-permute-start.12 = (bf16[16,128,128]{2,1,0:T(8,128)(2,1)S(1)}, bf16[16,128,128]{2,1,0:T(8,128)(2,1)S(1)}, u32[]{:S(2)}, u32[]{:S(2)}) collective-permute-start(bf16[16,128,128]{2,1,0:T(8,128)(2,1)S(1)} %collective-permute-done.7.refs_1_.refs_3_), channel_id=1, source_target_pairs={{0,1},{2,3},{1,0},{3,2},{4,5},{6,7},{5,4},{7,6},{8,9},{10,11},{9,8... | collective-permute-start | bytes 1572872 | tf_op jit(solution)/shard_map/ppermute | solution.py:286
  42.4 3.7 %collective-permute-start.14 = (bf16[8,128,128]{2,1,0:T(8,128)(2,1)S(1)}, bf16[8,128,128]{2,1,0:T(8,128)(2,1)S(1)}, u32[]{:S(2)}, u32[]{:S(2)}) collective-permute-start(bf16[8,128,128]{2,1,0:T(8,128)(2,1)S(1)} %get-tuple-element.94), channel_id=1, source_target_pairs={{4,8},{5,9},{6,10},{7,11},{0,1},{2,3},{12,13},{14,15},{8,4},{9,5},... | collective-permute-start | bytes 786440 | tf_op jit(solution)/shard_map/ppermute | solution.py:376
  43.0 10.2 %collective-permute-start.13 = (bf16[8,128,128]{2,1,0:T(8,128)(2,1)S(1)}, bf16[8,128,128]{2,1,0:T(8,128)(2,1)S(1)}, u32[]{:S(2)}, u32[]{:S(2)}) collective-permute-start(bf16[8,128,128]{2,1,0:T(8,128)(2,1)S(1)} %get-tuple-element.97.refs_2_), channel_id=1, source_target_pairs={{0,4},{12,8},{4,0},{8,12},{1,5},{13,9},{5,1},{9,13},{2,6},{14,10},... | collective-permute-start | bytes 786440 | tf_op jit(solution)/shard_map/ppermute | solution.py:370
  46.4 12.9 %collective-permute-start.17 = (bf16[8,128,128]{2,1,0:T(8,128)(2,1)S(1)}, bf16[8,128,128]{2,1,0:T(8,128)(2,1)S(1)}, u32[]{:S(2)}, u32[]{:S(2)}) collective-permute-start(bf16[8,128,128]{2,1,0:T(8,128)(2,1)S(1)} %fusion.4.refs_2_), channel_id=1, source_target_pairs={{0,4},{12,8},{4,0},{8,12},{1,5},{13,9},{5,1},{9,13},{2,6},{14,10},... | collective-permute-start | bytes 786440 | tf_op jit(solution)/shard_map/ppermute | solution.py:370
  52.8 6.9 %collective-permute-start.18 = (bf16[8,128,128]{2,1,0:T(8,128)(2,1)S(1)}, bf16[8,128,128]{2,1,0:T(8,128)(2,1)S(1)}, u32[]{:S(2)}, u32[]{:S(2)}) collective-permute-start(bf16[8,128,128]{2,1,0:T(8,128)(2,1)S(1)} %get-tuple-element.102), channel_id=1, source_target_pairs={{4,8},{5,9},{6,10},{7,11},{0,1},{2,3},{12,13},{14,15},{8,4},{9,5},... | collective-permute-start | bytes 786440 | tf_op jit(solution)/shard_map/ppermute | solution.py:376
  59.7 4.3 %collective-permute-start.16 = (bf16[8,128,128]{2,1,0:T(8,128)(2,1)S(1)}, bf16[8,128,128]{2,1,0:T(8,128)(2,1)S(1)}, u32[]{:S(2)}, u32[]{:S(2)}) collective-permute-start(bf16[8,128,128]{2,1,0:T(8,128)(2,1)S(1)} %get-tuple-element.105), channel_id=1, source_target_pairs={{4,8},{5,9},{6,10},{7,11},{0,1},{2,3},{12,13},{14,15},{8,4},{9,5},... | collective-permute-start | bytes 786440 | tf_op jit(solution)/shard_map/ppermute | solution.py:376
  60.0 8.8 %collective-permute-start.19 = (bf16[8,128,128]{2,1,0:T(8,128)(2,1)S(1)}, bf16[8,128,128]{2,1,0:T(8,128)(2,1)S(1)}, u32[]{:S(2)}, u32[]{:S(2)}) collective-permute-start(bf16[8,128,128]{2,1,0:T(8,128)(2,1)S(1)} %fusion.6.refs_2_), channel_id=1, source_target_pairs={{0,4},{12,8},{4,0},{8,12},{1,5},{13,9},{5,1},{9,13},{2,6},{14,10},... | collective-permute-start | bytes 786440 | tf_op jit(solution)/shard_map/ppermute | solution.py:370
  63.9 8.0 %collective-permute-start.22 = (bf16[8,128,128]{2,1,0:T(8,128)(2,1)S(1)}, bf16[8,128,128]{2,1,0:T(8,128)(2,1)S(1)}, u32[]{:S(2)}, u32[]{:S(2)}) collective-permute-start(bf16[8,128,128]{2,1,0:T(8,128)(2,1)S(1)} %get-tuple-element.110), channel_id=1, source_target_pairs={{4,8},{5,9},{6,10},{7,11},{0,1},{2,3},{12,13},{14,15},{8,4},{9,5},... | collective-permute-start | bytes 786440 | tf_op jit(solution)/shard_map/ppermute | solution.py:376
  69.6 9.2 %collective-permute-start.21 = (bf16[8,128,128]{2,1,0:T(8,128)(2,1)S(1)}, bf16[8,128,128]{2,1,0:T(8,128)(2,1)S(1)}, u32[]{:S(2)}, u32[]{:S(2)}) collective-permute-start(bf16[8,128,128]{2,1,0:T(8,128)(2,1)S(1)} %get-tuple-element.112.refs_2_), channel_id=1, source_target_pairs={{0,4},{12,8},{4,0},{8,12},{1,5},{13,9},{5,1},{9,13},{2,6},{14,10},... | collective-permute-start | bytes 786440 | tf_op jit(solution)/shard_map/ppermute | solution.py:370
  72.2 9.6 %collective-permute-start.25 = (bf16[8,128,128]{2,1,0:T(8,128)(2,1)S(1)}, bf16[8,128,128]{2,1,0:T(8,128)(2,1)S(1)}, u32[]{:S(2)}, u32[]{:S(2)}) collective-permute-start(bf16[8,128,128]{2,1,0:T(8,128)(2,1)S(1)} %fusion.10), channel_id=1, source_target_pairs={{0,4},{12,8},{4,0},{8,12},{1,5},{13,9},{5,1},{9,13},{2,6},{14,10},... | collective-permute-start | bytes 786440 | tf_op jit(solution)/shard_map/ppermute | solution.py:370
  74.7 8.2 %collective-permute-start.20 = (bf16[8,128,128]{2,1,0:T(8,128)(2,1)S(1)}, bf16[8,128,128]{2,1,0:T(8,128)(2,1)S(1)}, u32[]{:S(2)}, u32[]{:S(2)}) collective-permute-start(bf16[8,128,128]{2,1,0:T(8,128)(2,1)S(1)} %get-tuple-element.116), channel_id=1, source_target_pairs={{4,8},{5,9},{6,10},{7,11},{0,1},{2,3},{12,13},{14,15},{8,4},{9,5},... | collective-permute-start | bytes 786440 | tf_op jit(solution)/shard_map/ppermute | solution.py:376
  82.8 3.8 %collective-permute-start.24 = (bf16[8,128,128]{2,1,0:T(8,128)(2,1)S(1)}, bf16[8,128,128]{2,1,0:T(8,128)(2,1)S(1)}, u32[]{:S(2)}, u32[]{:S(2)}) collective-permute-start(bf16[8,128,128]{2,1,0:T(8,128)(2,1)S(1)} %get-tuple-element.122), channel_id=1, source_target_pairs={{4,8},{5,9},{6,10},{7,11},{0,1},{2,3},{12,13},{14,15},{8,4},{9,5},... | collective-permute-start | bytes 786440 | tf_op jit(solution)/shard_map/ppermute | solution.py:376
  83.1 8.8 %collective-permute-start.23 = (bf16[8,128,128]{2,1,0:T(8,128)(2,1)S(1)}, bf16[8,128,128]{2,1,0:T(8,128)(2,1)S(1)}, u32[]{:S(2)}, u32[]{:S(2)}) collective-permute-start(bf16[8,128,128]{2,1,0:T(8,128)(2,1)S(1)} %fusion.12), channel_id=1, source_target_pairs={{0,4},{12,8},{4,0},{8,12},{1,5},{13,9},{5,1},{9,13},{2,6},{14,10},... | collective-permute-start | bytes 786440 | tf_op jit(solution)/shard_map/ppermute | solution.py:370
  86.5 6.3 %collective-permute-start.28 = (bf16[8,128,128]{2,1,0:T(8,128)(2,1)S(1)}, bf16[8,128,128]{2,1,0:T(8,128)(2,1)S(1)}, u32[]{:S(2)}, u32[]{:S(2)}) collective-permute-start(bf16[8,128,128]{2,1,0:T(8,128)(2,1)S(1)} %get-tuple-element.127), channel_id=1, source_target_pairs={{4,8},{5,9},{6,10},{7,11},{0,1},{2,3},{12,13},{14,15},{8,4},{9,5},... | collective-permute-start | bytes 786440 | tf_op jit(solution)/shard_map/ppermute | solution.py:376
  93.0 11.1 %collective-permute-start.30 = (bf16[8,128,128]{2,1,0:T(8,128)(2,1)S(1)}, bf16[8,128,128]{2,1,0:T(8,128)(2,1)S(1)}, u32[]{:S(2)}, u32[]{:S(2)}) collective-permute-start(bf16[8,128,128]{2,1,0:T(8,128)(2,1)S(1)} %fusion.14), channel_id=1, source_target_pairs={{0,4},{12,8},{4,0},{8,12},{1,5},{13,9},{5,1},{9,13},{2,6},{14,10},... | collective-permute-start | bytes 786440 | tf_op jit(solution)/shard_map/ppermute | solution.py:370
  96.9 10.5 %collective-permute-start.27 = (bf16[8,128,128]{2,1,0:T(8,128)(2,1)S(1)}, bf16[8,128,128]{2,1,0:T(8,128)(2,1)S(1)}, u32[]{:S(2)}, u32[]{:S(2)}) collective-permute-start(bf16[8,128,128]{2,1,0:T(8,128)(2,1)S(1)} %get-tuple-element.129), channel_id=1, source_target_pairs={{0,4},{12,8},{4,0},{8,12},{1,5},{13,9},{5,1},{9,13},{2,6},{14,10},... | collective-permute-start | bytes 786440 | tf_op jit(solution)/shard_map/ppermute | solution.py:370
  96.9 11.1 %collective-permute-start.26 = (bf16[8,128,128]{2,1,0:T(8,128)(2,1)S(1)}, bf16[8,128,128]{2,1,0:T(8,128)(2,1)S(1)}, u32[]{:S(2)}, u32[]{:S(2)}) collective-permute-start(bf16[8,128,128]{2,1,0:T(8,128)(2,1)S(1)} %get-tuple-element.132), channel_id=1, source_target_pairs={{4,8},{5,9},{6,10},{7,11},{0,1},{2,3},{12,13},{14,15},{8,4},{9,5},... | collective-permute-start | bytes 786440 | tf_op jit(solution)/shard_map/ppermute | solution.py:376
  108.2 6.4 %collective-permute-start.29 = (bf16[8,128,128]{2,1,0:T(8,128)(2,1)S(1)}, bf16[8,128,128]{2,1,0:T(8,128)(2,1)S(1)}, u32[]{:S(2)}, u32[]{:S(2)}) collective-permute-start(bf16[8,128,128]{2,1,0:T(8,128)(2,1)S(1)} %fusion.15), channel_id=1, source_target_pairs={{0,4},{12,8},{4,0},{8,12},{1,5},{13,9},{5,1},{9,13},{2,6},{14,10},... | collective-permute-start | bytes 786440 | tf_op jit(solution)/shard_map/ppermute | solution.py:370
  110.0 4.8 %copy-start.5 = (f32[8192]{0:T(1024)S(1)}, f32[8192]{0:T(1024)}, u32[]{:S(2)}) copy-start(f32[8192]{0:T(1024)} %param.7) | copy-start | bytes 98308
  (5 other events, 11.7 us)

commit v3 on v2

--- a/solution.py
+++ b/solution.py
@@ -11,6 +11,7 @@
 F32 = jnp.float32
 BF16 = jnp.bfloat16
 VMEM_LIMIT = 8 << 20
+COST = 2 * 10**9
 VMEM = pl.BlockSpec(memory_space=pltpu.VMEM)
 ANY = pl.BlockSpec(memory_space=pl.ANY)
 
@@ -32,7 +33,7 @@
         out_specs=[VMEM] * len(outs),
         out_shape=outs,
         compiler_params=pltpu.CompilerParams(vmem_limit_bytes=VMEM_LIMIT),
-        cost_estimate=pl.CostEstimate(flops=1, bytes_accessed=1, transcendentals=0),
+        cost_estimate=pl.CostEstimate(flops=COST, bytes_accessed=1, transcendentals=0),
         name=name,
     )(*operands, *after)
 
@@ -66,12 +67,14 @@
 
 
 def places_block():
-    odd = lax.rem(lax.axis_index("ctx"), 2)
+    place = lax.axis_index("ctx")
+    odd = lax.rem(place, 2)
+    later = jnp.where(place >= 2, 1, 0)
     along = lax.axis_index("head")
     rows = lax.broadcasted_iota(jnp.int32, (8, DH), 0)
     left = jnp.where(along < 2, 1, 0)
     outer = jnp.where((along == 0) | (along == 3), 1, 0)
-    value = jnp.where(rows == 0, odd, jnp.where(rows == 1, left, outer))
+    value = jnp.where(rows == 0, odd, jnp.where(rows == 1, left, jnp.where(rows == 2, outer, later)))
     return value.astype(F32)
 
 
@@ -109,29 +112,6 @@
     )(k_rows, v_rows)
 
 
-def early_states(other, parts, sizes, after):
-    half = other.shape[0] // 2
-
-    def kernel(ins, outs):
-        place = lax.axis_index("ctx")
-        odd, later = lax.rem(place, 2) == 1, place >= 2
-        at = 0
-        for f_ref, size in zip(outs, sizes):
-            for h in range(size):
-                g = at + h
-                early = jnp.where(odd, ins[0][g].astype(F32), 0.0)
-                if parts:
-                    a, b = (ins[1], ins[2]) if g < half else (ins[2], ins[1])
-                    i = g if g < half else g - half
-                    before = jnp.where(odd, b[i].astype(F32), a[i].astype(F32))
-                    early = early + jnp.where(later, before, 0.0)
-                f_ref[h] = early.astype(BF16)
-            at += size
-
-    outs = [states_of(size, DH) for size in sizes]
-    return call(kernel, "early_states", [other, *parts], outs, after)
-
-
 def total(*terms):
     out = terms[0].astype(F32)
     for term in terms[1:]:
@@ -139,7 +119,7 @@
     return out
 
 
-def local_scores(q_rows, ka, first, ka_first, count, after):
+def local_scores(q_rows, ka, ka_first, first, count, after):
     rows = q_rows.shape[0]
 
     def kernel(ins, outs):
@@ -250,56 +230,18 @@
     return pairs + [(b, a) for a, b in pairs]
 
 
-class Group:
-    def __init__(self, n_ctx, first, sizes):
-        self.n_ctx = n_ctx
-        self.first, self.sizes, self.count = first, sizes, sum(sizes)
-        self.partner = both_ways([(2 * p, 2 * p + 1) for p in range(n_ctx // 2)])
-        self.got = []
-
-    def begin(self, own, ka, odd):
-        self.own, self.ka, self.odd = own, ka, odd
-        if self.n_ctx % 2 == 0:
-            self.other = lax.ppermute(own, "ctx", self.partner)
-        return [own]
-
-    def cross(self, after):
-        n = self.n_ctx
-        if n == 2 or n % 2:
-            return after
-        half = self.count // 2
-        own, other = self.own, held(self.other, after)
-        mine = jnp.where(
-            self.odd, total(own[half:], other[half:]), total(own[:half], other[:half])
-        ).astype(BF16)
-        for s in range(1, n // 2):
-            pairs = [(i, i + 2 * s) for i in range(n - 2 * s)]
-            self.got.append(lax.ppermute(mine, "ctx", both_ways(pairs) if n == 4 else pairs))
-        return [mine]
-
-    def spread(self, after):
-        n = self.n_ctx
-        if n == 2 or n % 2:
-            return after
-        got = self.got[0] if n == 4 else total(*self.got).astype(BF16)
-        self.got = [held(got, after)]
-        self.theirs = lax.ppermute(self.got[0], "ctx", self.partner)
-        return self.got
-
-    def finish(self, after):
-        n = self.n_ctx
-        parts = []
-        if n == 1:
-            return [jnp.zeros_like(self.own)]
-        if n % 2:
-            got = [
-                lax.ppermute(self.own, "ctx", [(i, i + s) for i in range(n - s)])
-                for s in range(1, n)
-            ]
-            return [total(*got).astype(BF16)]
-        if n > 2:
-            parts = [self.got[0], self.theirs]
-        return early_states(self.other, parts, self.sizes, after)
+def before_ctx(n_ctx, own):
+    odd = lax.axis_index("ctx") % 2 == 1
+    before = jnp.zeros(own.shape, F32)
+    if n_ctx % 2:
+        for s in range(1, n_ctx):
+            before = total(before, lax.ppermute(own, "ctx", [(i, i + s) for i in range(n_ctx - s)]))
+        return before.astype(BF16)
+    other = lax.ppermute(own, "ctx", both_ways([(i, i + 1) for i in range(0, n_ctx, 2)]))
+    couple = total(own, other).astype(BF16)
+    for s in range(2, n_ctx, 2):
+        before = total(before, lax.ppermute(couple, "ctx", [(i, i + s) for i in range(n_ctx - s)]))
+    return (before + jnp.where(odd, other.astype(F32), 0.0)).astype(BF16)
 
 
 def whole_chain(n_head, own, early):
@@ -336,30 +278,41 @@
 SKEW = 3
 
 
-class Four:
-    def __init__(self, n_ctx, n, masks):
-        self.n, self.n_ctx = n, n_ctx
-        self.left, self.outer = masks[1] > 0, masks[2] > 0
-        self.own, self.early, self.a, self.b = {}, {}, {}, {}
-        at = lambda z, c: z * n_ctx + c
-        self.swap = both_ways([(1, 2)])
-        if n_ctx % 2 == 0:
-            self.swap = both_ways(
-                [(at(1, c), at(2, c)) for c in range(n_ctx)]
-                + [(at(z, c), at(z, c + 1)) for z in (0, 3) for c in range(0, n_ctx, 2)]
-            )
+class Scan:
+    def __init__(self, n, masks):
+        self.n = n
+        self.odd, self.left, self.outer, self.later = (masks[i] > 0 for i in range(4))
+        self.own, self.other, self.x, self.a, self.b = {}, {}, {}, {}, {}
+        self.couples = both_ways([(0, 1), (2, 3)])
+        at = lambda z, c: 4 * z + c
+        self.swap = both_ways(
+            [(at(1, c), at(2, c)) for c in range(4)]
+            + [(at(z, c), at(z, c + 1)) for z in (0, 3) for c in (0, 2)]
+        )
+
+    def begin(self, own):
+        return lax.ppermute(own, "ctx", self.couples)
+
+    def cross(self, c, after):
+        send = held(total(self.own[c], self.other[c]).astype(BF16), after)
+        self.x[c] = lax.ppermute(send, "ctx", both_ways([(0, 2), (1, 3)]))
+        return [send]
+
+    def early(self, c):
+        couple = jnp.where(self.odd, self.other[c].astype(F32), 0.0)
+        return couple + jnp.where(self.later, self.x[c].astype(F32), 0.0)
 
     def mine(self, c):
-        f = self.early[c].astype(F32)
-        return f + jnp.where(self.left, self.own[c].astype(F32), 0.0)
+        return self.early(c) + jnp.where(self.left, self.own[c].astype(F32), 0.0)
 
     def mirror(self, c):
-        f = self.early[c].astype(F32)
-        return f + jnp.where(self.left, 0.0, self.own[c].astype(F32))
+        return self.early(c) + jnp.where(self.left, 0.0, self.own[c].astype(F32))
 
     def side(self, t, after):
         inwards, outwards = t < self.n, t >= SKEW
         c = t - SKEW
+        if inwards:
+            self.arrived(self.x, t, after)
         if outwards:
             out = total(self.b[c], self.mirror(c))
         if inwards and outwards:
@@ -371,23 +324,21 @@
         return [send]
 
     def middle(self, t, after):
+        self.arrived(self.a, t, after)
         send = held(total(self.a[t], self.mine(t)).astype(BF16), after)
-        axes = ("head", "ctx") if self.n_ctx % 2 == 0 else "head"
-        self.b[t] = lax.ppermute(send, axes, self.swap)
+        self.b[t] = lax.ppermute(send, ("head", "ctx"), self.swap)
         return [send]
 
+    def arrived(self, table, c, after):
+        table[c] = held(table[c], after)
+        return [table[c]]
+
     def state(self, c, after):
+        self.arrived(self.a, c + SKEW, after)
         got = jnp.where(
             self.outer, self.a[c + SKEW].astype(F32), total(self.a[c], self.b[c])
         )
-        return held((got + self.early[c].astype(F32)).astype(BF16), after)
-
-
-def plan(heads, n_head):
-    if n_head != 4 or heads % 16:
-        return [[heads]]
-    u = heads // 8
-    return [[u], [u], [u, u], [u, u, u, u]]
+        return held((got + self.early(c)).astype(BF16), after)
 
 
 def body(n_head, n_ctx, queries, keys, values, gain):
@@ -396,93 +347,66 @@
     k_rows = keys.reshape(rows, width)
     v_rows = values.reshape(rows, width)
     heads = width // DH
-    groups, chunks = [], []
-    for sizes in plan(heads, n_head):
-        g = Group(n_ctx, len(chunks) and sum(c[2] for c in chunks), sizes)
-        groups.append(g)
-        for i, size in enumerate(sizes):
-            chunks.append((g, g.first + sum(sizes[:i]), size))
-    n = len(chunks)
-    both, states, attns, squares = {}, {}, {}, {}
-
-    masks = None
-
-    def kv(g, after):
-        odd = masks[0] > 0 if masks is not None else lax.axis_index("ctx") % 2 == 1
-        return g.begin(*kv_states(k_rows, v_rows, g.first, g.count, after), odd)
+    if n_head != 4 or n_ctx != 4 or heads % 8:
+        own, ka = kv_states(k_rows, v_rows, 0, heads, [])
+        state = whole_chain(n_head, own, before_ctx(n_ctx, own))
+        both = local_scores(q_rows, ka, 0, 0, heads, [])
+        return last_attend(both, v_rows, 0, [state], [], [], gain)
+
+    n = 8
+    size = heads // n
+    both, states, attns, squares, ka = {}, {}, {}, {}, {}
+
+    own, keys_active, masks = first_kv_states(k_rows, v_rows, size)
+    scan = Scan(n, masks)
+
+    def begin(first, count, own, keys_active):
+        other = scan.begin(own)
+        for i in range(count):
+            c = first + i
+            cut = slice(i * size, (i + 1) * size)
+            scan.own[c], scan.other[c] = own[cut], other[cut]
+            ka[c] = (keys_active, i * size)
+        return [own]
+
+    def kv(first, count, after):
+        return begin(
+            first, count, *kv_states(k_rows, v_rows, first * size, count * size, after)
+        )
 
     def scores(c, after):
-        g, first, size = chunks[c]
-        both[c] = local_scores(q_rows, g.ka, first, first - g.first, size, after)
+        both[c] = local_scores(q_rows, *ka[c], c * size, size, after)
         return [both[c]]
 
     def attention(c, after):
-        attns[c], squares[c] = attend(both[c], v_rows, chunks[c][1], [states[c]], after)
+        attns[c], squares[c] = attend(both[c], v_rows, c * size, [states[c]], after)
         return [squares[c]]
 
-    if n == 1:
-        g = groups[0]
-        clock = kv(g, [])
-        clock = g.cross(clock)
-        clock = g.spread(clock)
-        early = g.finish(clock)[0]
-        states[0] = whole_chain(n_head, g.own, early)
-        scores(0, [])
-    else:
-        def ready(g, after):
-            early = g.finish(after)
-            at = 0
-            for c in range(n):
-                if chunks[c][0] is g:
-                    four.early[c] = early[at]
-                    first = chunks[c][1] - g.first
-                    four.own[c] = g.own[first : first + chunks[c][2]]
-                    at += 1
-            return [early[0]]
-
-        g0, g1, g2, g3 = groups
-        own, ka, masks = first_kv_states(k_rows, v_rows, g0.count)
-        four = Four(n_ctx, n, masks)
-        clock = g0.begin(own, ka, masks[0] > 0)
-        clock = kv(g1, clock)
-        clock = g0.cross(clock)
-        clock = kv(g2, clock)
-        clock = g1.cross(clock)
-        clock = kv(g3, clock)
-        clock = scores(0, clock)
-        clock = g0.spread(clock)
-        clock = g2.cross(clock)
-        clock = ready(g0, clock)
-        clock = four.side(0, clock)
-        clock = scores(1, clock)
-        clock = g1.spread(clock)
-        clock = g3.cross(clock)
-        clock = ready(g1, clock)
-        clock = four.side(1, clock)
-        clock = scores(2, clock)
-        clock = four.middle(0, clock)
-        clock = g2.spread(clock)
-        clock = scores(3, clock)
-        clock = ready(g2, clock)
-        for t in range(2, n + SKEW):
-            clock = four.side(t, clock)
-            if t + 2 < n:
-                clock = scores(t + 2, clock)
-            c = t - 1 - SKEW
-            if c >= 0:
-                states[c] = four.state(c, clock)
-                clock = attention(c, [states[c]])
-            if t == 2:
-                clock = g3.spread(clock)
-                clock = ready(g3, clock)
-            if t - 1 < n:
-                clock = four.middle(t - 1, clock)
-            if 0 <= t - 2 < n:
-                clock = [held(four.b[t - 2], clock)]
-                four.b[t - 2] = clock[0]
-        states[n - 1] = four.state(n - 1, clock)
+    clock = begin(0, 1, own, keys_active)
+    clock = kv(1, 1, clock)
+    clock = scan.cross(0, clock)
+    clock = scan.cross(1, clock)
+    clock = kv(2, 2, clock)
+    clock = kv(4, 4, clock)
+    clock = scores(0, clock)
+    clock = scores(1, clock)
+    for t in range(n + SKEW):
+        clock = scan.side(t, clock)
+        if t + 2 < n:
+            clock = scores(t + 2, clock)
+        if 0 <= t - 1 < n:
+            clock = scan.middle(t - 1, clock)
+        if t + 2 < n:
+            clock = scan.cross(t + 2, clock)
+        c = t - 1 - SKEW
+        if c >= 0:
+            states[c] = scan.state(c, clock)
+            clock = attention(c, [states[c]])
+        if 0 <= t - 2 < n:
+            clock = scan.arrived(scan.b, t - 2, clock)
+    states[n - 1] = scan.state(n - 1, clock)
     return last_attend(
-        both[n - 1], v_rows, chunks[n - 1][1], [states[n - 1]],
+        both[n - 1], v_rows, (n - 1) * size, [states[n - 1]],
         [attns[c] for c in range(n - 1)], [squares[c] for c in range(n - 1)], gain,
     )
 

time: 117 us -> 87.6 us (0.75)
  waiting for transfers between devices: 60.4 us -> 31.5 us
  other arithmetic: 4.88 us -> 6.67 us
    ppermute x11, waiting for transfers between devices: 48.4 us -> 17.7 us  [side(): self.a[t] = lax.ppermute(send, 'head', both_ways([(0, 1), (3, 2)]))]
    ppermute x11, starting transfers between devices: 29.1 us -> 22.6 us  [side(): self.a[t] = lax.ppermute(send, 'head', both_ways([(0, 1), (3, 2)]))]
    ppermute x20, starting transfers between devices: 8.3 us -> 13.8 us  [the longest x8 12.1 us: cross(): self.x[c] = lax.ppermute(send, 'ctx', both_ways([(0, 2), (1, 3)]))]
    convert_element_type x6 -> x14, other arithmetic: 1.17 us -> 3.01 us  [the longest x8 1.7 us: state(): return held((got + self.early(c)).astype(BF16), after)]
    ppermute x20, waiting for transfers between devices: 12 us -> 13.8 us  [the longest x8 13 us: cross(): self.x[c] = lax.ppermute(send, 'ctx', both_ways([(0, 2), (1, 3)]))]
    pallas_call x23 -> x19, Pallas kernels: 9.88 us -> 8.73 us  [call(): pl.pallas_call(run, in_specs=[VMEM] * n_in + [ANY] * n_after, out_specs=[...]
  transfers between devices with their start and end apart: 31 -> 31, of which waited for: 14 -> 16; matrix products, arithmetic and copies ran while one was open for 4% -> 7% of each run, Pallas kernels for 6% -> 7%
where the time goes in v3:
time: 87.6 us; the launch traced here: 87.4 us
  starting transfers between devices  36.4 us (42%)
  waiting for transfers between devices  31.5 us (36%)
  Pallas kernels  9.08 us (10%)
  other arithmetic  6.67 us (8%)
  local copies, waits for them, and re-layouts  3.21 us (4%)
    ppermute x11, starting transfers between devices, side(): self.a[t] = lax.ppermute(send, 'head', both_ways([(0, 1), (3, 2)]))  22.6 us
    ppermute x11, waiting for transfers between devices, side(): self.a[t] = lax.ppermute(send, 'head', both_ways([(0, 1), (3, 2)]))  17.7 us
    ppermute x8, waiting for transfers between devices, cross(): self.x[c] = lax.ppermute(send, 'ctx', both_ways([(0, 2), (1, 3)]))  13 us
    ppermute x8, starting transfers between devices, cross(): self.x[c] = lax.ppermute(send, 'ctx', both_ways([(0, 2), (1, 3)]))  12.1 us
    pallas_call x19, Pallas kernels, call(): pl.pallas_call(run, in_specs=[VMEM] * n_in + [ANY] * n_after, out_specs=[...  8.73 us
    unnamed x12, local copies, waits for them, and re-layouts  3.21 us
    convert_element_type x9, other arithmetic, side(): send = held(send.astype(BF16), after)  2.1 us
  transfers between devices with their start and end apart: 31, of which 16 were waited for; matrix products, arithmetic and copies ran while one was open for 7% of the time, Pallas kernels for 7%

profile of v3, /device:TPU:0, one launch (start us, length us, event | category | flops | bytes accessed | tf_op | source)
XLA Modules:
  0.0 87.4 jit_solution(11065133123200495084)
XLA Ops:
  0.0 1.6 %copy-done = bf16[1,128,8192]{2,1,0:T(8,128)(2,1)S(1)} copy-done((bf16[1,128,8192]{2,1,0:T(8,128)(2,1)S(1)}, bf16[1,128,8192]{2,1,0:T(8,128)(2,1)}, u32[]{:S(2)}) %copy-start) | copy-done | bytes 2097176
  1.6 1.6 %copy-done.2 = bf16[1,128,8192]{2,1,0:T(8,128)(2,1)S(1)} copy-done((bf16[1,128,8192]{2,1,0:T(8,128)(2,1)S(1)}, bf16[1,128,8192]{2,1,0:T(8,128)(2,1)}, u32[]{:S(2)}) %copy-start.2) | copy-done | bytes 2097176
  5.3 2.9 %collective-permute-start.4 = (bf16[8,128,128]{2,1,0:T(8,128)(2,1)S(1)}, bf16[8,128,128]{2,1,0:T(8,128)(2,1)S(1)}, u32[]{:S(2)}, u32[]{:S(2)}) collective-permute-start(bf16[8,128,128]{2,1,0:T(8,128)(2,1)S(1)} %fusion.46), channel_id=1, source_target_pairs={{0,2},{1,3},{2,0},{3,1},{4,6},{5,7},{6,4},{7,5},{8,10},{9,11},{10,... | collective-permute-start | bytes 786440 | tf_op jit(solution)/shard_map/ppermute | solution.py:298
  9.5 0.9 %kv_states.5 = (bf16[32,128,128]{2,1,0:T(8,128)(2,1)S(1)}, bf16[128,4096]{1,0:T(8,128)(2,1)S(1)}) custom-call(bf16[128,8192]{1,0:T(8,128)(2,1)S(1)} %bitcast.15, bf16[128,8192]{1,0:T(8,128)(2,1)S(1)} %bitcast.19, bf16[16,128,128]{2,1,0:T(8,128)(2,1)S(1)} %get-tuple-element.99.refs_2_), custom_call_target="tpu_custom_call" | custom-call | flops 2000000000 | bytes 1 | tf_op jit(solution)/shard_map/kv_states/pallas_call | solution.py:30
  11.5 3.8 %collective-permute-done.4 = bf16[8,128,128]{2,1,0:T(8,128)(2,1)S(1)} collective-permute-done((bf16[8,128,128]{2,1,0:T(8,128)(2,1)S(1)}, bf16[8,128,128]{2,1,0:T(8,128)(2,1)S(1)}, u32[]{:S(2)}, u32[]{:S(2)}) %collective-permute-start.4) | collective-permute-done | bytes 262176 | tf_op jit(solution)/shard_map/ppermute | solution.py:298
  15.5 2.2 %collective-permute-start.6 = (bf16[8,128,128]{2,1,0:T(8,128)(2,1)S(1)}, bf16[8,128,128]{2,1,0:T(8,128)(2,1)S(1)}, u32[]{:S(2)}, u32[]{:S(2)}) collective-permute-start(bf16[8,128,128]{2,1,0:T(8,128)(2,1)S(1)} %fusion.68.refs_2_), channel_id=1, source_target_pairs={{0,4},{12,8},{4,0},{8,12},{1,5},{13,9},{5,1},{9,13},{2,6},{14,10},... | collective-permute-start | bytes 786440 | tf_op jit(solution)/shard_map/ppermute | solution.py:323
  18.2 1.6 %collective-permute-start.5 = (bf16[8,128,128]{2,1,0:T(8,128)(2,1)S(1)}, bf16[8,128,128]{2,1,0:T(8,128)(2,1)S(1)}, u32[]{:S(2)}, u32[]{:S(2)}) collective-permute-start(bf16[8,128,128]{2,1,0:T(8,128)(2,1)S(1)} %get-tuple-element.108), channel_id=1, source_target_pairs={{0,2},{1,3},{2,0},{3,1},{4,6},{5,7},{6,4},{7,5},{8,10},{9,11},{10,... | collective-permute-start | bytes 786440 | tf_op jit(solution)/shard_map/ppermute | solution.py:298
  19.7 1.2 %collective-permute-done.7 = bf16[8,128,128]{2,1,0:T(8,128)(2,1)S(1)} collective-permute-done((bf16[8,128,128]{2,1,0:T(8,128)(2,1)S(1)}, bf16[8,128,128]{2,1,0:T(8,128)(2,1)S(1)}, u32[]{:S(2)}, u32[]{:S(2)}) %collective-permute-start.7) | collective-permute-done | bytes 262176 | tf_op jit(solution)/shard_map/ppermute | solution.py:298
  21.4 2.2 %collective-permute-start.11 = (bf16[8,128,128]{2,1,0:T(8,128)(2,1)S(1)}, bf16[8,128,128]{2,1,0:T(8,128)(2,1)S(1)}, u32[]{:S(2)}, u32[]{:S(2)}) collective-permute-start(bf16[8,128,128]{2,1,0:T(8,128)(2,1)S(1)} %fusion.69.refs_2_), channel_id=1, source_target_pairs={{0,4},{12,8},{4,0},{8,12},{1,5},{13,9},{5,1},{9,13},{2,6},{14,10},... | collective-permute-start | bytes 786440 | tf_op jit(solution)/shard_map/ppermute | solution.py:323
  23.9 1.6 %collective-permute-start.9 = (bf16[8,128,128]{2,1,0:T(8,128)(2,1)S(1)}, bf16[8,128,128]{2,1,0:T(8,128)(2,1)S(1)}, u32[]{:S(2)}, u32[]{:S(2)}) collective-permute-start(bf16[8,128,128]{2,1,0:T(8,128)(2,1)S(1)} %get-tuple-element.113), channel_id=1, source_target_pairs={{0,2},{1,3},{2,0},{3,1},{4,6},{5,7},{6,4},{7,5},{8,10},{9,11},{10,... | collective-permute-start | bytes 786440 | tf_op jit(solution)/shard_map/ppermute | solution.py:298
  26.2 2.5 %collective-permute-start.8 = (bf16[8,128,128]{2,1,0:T(8,128)(2,1)S(1)}, bf16[8,128,128]{2,1,0:T(8,128)(2,1)S(1)}, u32[]{:S(2)}, u32[]{:S(2)}) collective-permute-start(bf16[8,128,128]{2,1,0:T(8,128)(2,1)S(1)} %fusion.67.refs_2_), channel_id=1, source_target_pairs={{0,4},{12,8},{4,0},{8,12},{1,5},{13,9},{5,1},{9,13},{2,6},{14,10},... | collective-permute-start | bytes 786440 | tf_op jit(solution)/shard_map/ppermute | solution.py:323
  29.6 1.6 %collective-permute-start.15 = (bf16[8,128,128]{2,1,0:T(8,128)(2,1)S(1)}, bf16[8,128,128]{2,1,0:T(8,128)(2,1)S(1)}, u32[]{:S(2)}, u32[]{:S(2)}) collective-permute-start(bf16[8,128,128]{2,1,0:T(8,128)(2,1)S(1)} %get-tuple-element.118), channel_id=1, source_target_pairs={{0,2},{1,3},{2,0},{3,1},{4,6},{5,7},{6,4},{7,5},{8,10},{9,11},{10,... | collective-permute-start | bytes 786440 | tf_op jit(solution)/shard_map/ppermute | solution.py:298
  31.2 1.5 %collective-permute-done.9 = bf16[8,128,128]{2,1,0:T(8,128)(2,1)S(1)} collective-permute-done((bf16[8,128,128]{2,1,0:T(8,128)(2,1)S(1)}, bf16[8,128,128]{2,1,0:T(8,128)(2,1)S(1)}, u32[]{:S(2)}, u32[]{:S(2)}) %collective-permute-start.9) | collective-permute-done | bytes 262176 | tf_op jit(solution)/shard_map/ppermute | solution.py:298
  33.0 1.7 %collective-permute-start.14 = (bf16[8,128,128]{2,1,0:T(8,128)(2,1)S(1)}, bf16[8,128,128]{2,1,0:T(8,128)(2,1)S(1)}, u32[]{:S(2)}, u32[]{:S(2)}) collective-permute-start(bf16[8,128,128]{2,1,0:T(8,128)(2,1)S(1)} %fusion.9.refs_2_), channel_id=1, source_target_pairs={{0,4},{12,8},{4,0},{8,12},{1,5},{13,9},{5,1},{9,13},{2,6},{14,10},... | collective-permute-start | bytes 786440 | tf_op jit(solution)/shard_map/ppermute | solution.py:323
  36.2 2.1 %collective-permute-done.15 = bf16[8,128,128]{2,1,0:T(8,128)(2,1)S(1)} collective-permute-done((bf16[8,128,128]{2,1,0:T(8,128)(2,1)S(1)}, bf16[8,128,128]{2,1,0:T(8,128)(2,1)S(1)}, u32[]{:S(2)}, u32[]{:S(2)}) %collective-permute-start.15) | collective-permute-done | bytes 262176 | tf_op jit(solution)/shard_map/ppermute | solution.py:298
  38.8 1.0 %collective-permute-start.17 = (bf16[8,128,128]{2,1,0:T(8,128)(2,1)S(1)}, bf16[8,128,128]{2,1,0:T(8,128)(2,1)S(1)}, u32[]{:S(2)}, u32[]{:S(2)}) collective-permute-start(bf16[8,128,128]{2,1,0:T(8,128)(2,1)S(1)} %get-tuple-element.127.refs_2_), channel_id=1, source_target_pairs={{0,4},{12,8},{4,0},{8,12},{1,5},{13,9},{5,1},{9,13},{2,6},{14,10},... | collective-permute-start | bytes 786440 | tf_op jit(solution)/shard_map/ppermute | solution.py:323
  41.1 1.6 %collective-permute-start.21 = (bf16[8,128,128]{2,1,0:T(8,128)(2,1)S(1)}, bf16[8,128,128]{2,1,0:T(8,128)(2,1)S(1)}, u32[]{:S(2)}, u32[]{:S(2)}) collective-permute-start(bf16[8,128,128]{2,1,0:T(8,128)(2,1)S(1)} %get-tuple-element.130), channel_id=1, source_target_pairs={{0,2},{1,3},{2,0},{3,1},{4,6},{5,7},{6,4},{7,5},{8,10},{9,11},{10,... | collective-permute-start | bytes 786440 | tf_op jit(solution)/shard_map/ppermute | solution.py:298
  43.2 1.3 %collective-permute-done.12 = bf16[8,128,128]{2,1,0:T(8,128)(2,1)S(1)} collective-permute-done((bf16[8,128,128]{2,1,0:T(8,128)(2,1)S(1)}, bf16[8,128,128]{2,1,0:T(8,128)(2,1)S(1)}, u32[]{:S(2)}, u32[]{:S(2)}) %collective-permute-start.12) | collective-permute-done | bytes 262176 | tf_op jit(solution)/shard_map/ppermute | solution.py:298
  45.0 2.2 %collective-permute-start.20 = (bf16[8,128,128]{2,1,0:T(8,128)(2,1)S(1)}, bf16[8,128,128]{2,1,0:T(8,128)(2,1)S(1)}, u32[]{:S(2)}, u32[]{:S(2)}) collective-permute-start(bf16[8,128,128]{2,1,0:T(8,128)(2,1)S(1)} %get-tuple-element.136.refs_2_), channel_id=1, source_target_pairs={{0,4},{12,8},{4,0},{8,12},{1,5},{13,9},{5,1},{9,13},{2,6},{14,10},... | collective-permute-start | bytes 786440 | tf_op jit(solution)/shard_map/ppermute | solution.py:323
  47.7 1.6 %collective-permute-start.18 = (bf16[8,128,128]{2,1,0:T(8,128)(2,1)S(1)}, bf16[8,128,128]{2,1,0:T(8,128)(2,1)S(1)}, u32[]{:S(2)}, u32[]{:S(2)}) collective-permute-start(bf16[8,128,128]{2,1,0:T(8,128)(2,1)S(1)} %get-tuple-element.139), channel_id=1, source_target_pairs={{0,2},{1,3},{2,0},{3,1},{4,6},{5,7},{6,4},{7,5},{8,10},{9,11},{10,... | collective-permute-start | bytes 786440 | tf_op jit(solution)/shard_map/ppermute | solution.py:298
  50.8 1.8 %collective-permute-start.25 = (bf16[8,128,128]{2,1,0:T(8,128)(2,1)S(1)}, bf16[8,128,128]{2,1,0:T(8,128)(2,1)S(1)}, u32[]{:S(2)}, u32[]{:S(2)}) collective-permute-start(bf16[8,128,128]{2,1,0:T(8,128)(2,1)S(1)} %fusion.22), channel_id=1, source_target_pairs={{0,4},{12,8},{4,0},{8,12},{1,5},{13,9},{5,1},{9,13},{2,6},{14,10},... | collective-permute-start | bytes 786440 | tf_op jit(solution)/shard_map/ppermute | solution.py:323
  53.4 1.9 %collective-permute-done.18 = bf16[8,128,128]{2,1,0:T(8,128)(2,1)S(1)} collective-permute-done((bf16[8,128,128]{2,1,0:T(8,128)(2,1)S(1)}, bf16[8,128,128]{2,1,0:T(8,128)(2,1)S(1)}, u32[]{:S(2)}, u32[]{:S(2)}) %collective-permute-start.18) | collective-permute-done | bytes 262176 | tf_op jit(solution)/shard_map/ppermute | solution.py:298
  55.6 3.3 %collective-permute-done.25 = bf16[8,128,128]{2,1,0:T(8,128)(2,1)S(1)} collective-permute-done((bf16[8,128,128]{2,1,0:T(8,128)(2,1)S(1)}, bf16[8,128,128]{2,1,0:T(8,128)(2,1)S(1)}, u32[]{:S(2)}, u32[]{:S(2)}) %collective-permute-start.25) | collective-permute-done | bytes 262176 | tf_op jit(solution)/shard_map/ppermute | solution.py:323
  59.2 2.1 %collective-permute-start.23 = (bf16[8,128,128]{2,1,0:T(8,128)(2,1)S(1)}, bf16[8,128,128]{2,1,0:T(8,128)(2,1)S(1)}, u32[]{:S(2)}, u32[]{:S(2)}) collective-permute-start(bf16[8,128,128]{2,1,0:T(8,128)(2,1)S(1)} %fusion.26), channel_id=1, source_target_pairs={{0,4},{12,8},{4,0},{8,12},{1,5},{13,9},{5,1},{9,13},{2,6},{14,10},... | collective-permute-start | bytes 786440 | tf_op jit(solution)/shard_map/ppermute | solution.py:323
  62.2 1.7 %collective-permute-start.27 = (bf16[8,128,128]{2,1,0:T(8,128)(2,1)S(1)}, bf16[8,128,128]{2,1,0:T(8,128)(2,1)S(1)}, u32[]{:S(2)}, u32[]{:S(2)}) collective-permute-start(bf16[8,128,128]{2,1,0:T(8,128)(2,1)S(1)} %fusion.29), channel_id=1, source_target_pairs={{0,4},{12,8},{4,0},{8,12},{1,5},{13,9},{5,1},{9,13},{2,6},{14,10},... | collective-permute-start | bytes 786440 | tf_op jit(solution)/shard_map/ppermute | solution.py:323
  63.9 4.5 %collective-permute-done.23 = bf16[8,128,128]{2,1,0:T(8,128)(2,1)S(1)} collective-permute-done((bf16[8,128,128]{2,1,0:T(8,128)(2,1)S(1)}, bf16[8,128,128]{2,1,0:T(8,128)(2,1)S(1)}, u32[]{:S(2)}, u32[]{:S(2)}) %collective-permute-start.23) | collective-permute-done | bytes 262176 | tf_op jit(solution)/shard_map/ppermute | solution.py:323
  69.4 2.3 %collective-permute-start.30 = (bf16[8,128,128]{2,1,0:T(8,128)(2,1)S(1)}, bf16[8,128,128]{2,1,0:T(8,128)(2,1)S(1)}, u32[]{:S(2)}, u32[]{:S(2)}) collective-permute-start(bf16[8,128,128]{2,1,0:T(8,128)(2,1)S(1)} %fusion.35), channel_id=1, source_target_pairs={{0,4},{12,8},{4,0},{8,12},{1,5},{13,9},{5,1},{9,13},{2,6},{14,10},... | collective-permute-start | bytes 786440 | tf_op jit(solution)/shard_map/ppermute | solution.py:323
  71.8 2.3 %collective-permute-done.27 = bf16[8,128,128]{2,1,0:T(8,128)(2,1)S(1)} collective-permute-done((bf16[8,128,128]{2,1,0:T(8,128)(2,1)S(1)}, bf16[8,128,128]{2,1,0:T(8,128)(2,1)S(1)}, u32[]{:S(2)}, u32[]{:S(2)}) %collective-permute-start.27) | collective-permute-done | bytes 262176 | tf_op jit(solution)/shard_map/ppermute | solution.py:323
  74.7 2.7 %collective-permute-start.29 = (bf16[8,128,128]{2,1,0:T(8,128)(2,1)S(1)}, bf16[8,128,128]{2,1,0:T(8,128)(2,1)S(1)}, u32[]{:S(2)}, u32[]{:S(2)}) collective-permute-start(bf16[8,128,128]{2,1,0:T(8,128)(2,1)S(1)} %fusion.39), channel_id=1, source_target_pairs={{0,4},{12,8},{4,0},{8,12},{1,5},{13,9},{5,1},{9,13},{2,6},{14,10},... | collective-permute-start | bytes 786440 | tf_op jit(solution)/shard_map/ppermute | solution.py:323
  77.4 2.2 %collective-permute-done.30 = bf16[8,128,128]{2,1,0:T(8,128)(2,1)S(1)} collective-permute-done((bf16[8,128,128]{2,1,0:T(8,128)(2,1)S(1)}, bf16[8,128,128]{2,1,0:T(8,128)(2,1)S(1)}, u32[]{:S(2)}, u32[]{:S(2)}) %collective-permute-start.30) | collective-permute-done | bytes 262176 | tf_op jit(solution)/shard_map/ppermute | solution.py:323
  80.2 4.6 %collective-permute-done.29 = bf16[8,128,128]{2,1,0:T(8,128)(2,1)S(1)} collective-permute-done((bf16[8,128,128]{2,1,0:T(8,128)(2,1)S(1)}, bf16[8,128,128]{2,1,0:T(8,128)(2,1)S(1)}, u32[]{:S(2)}, u32[]{:S(2)}) %collective-permute-start.29) | collective-permute-done | bytes 262176 | tf_op jit(solution)/shard_map/ppermute | solution.py:323
  85.0 2.3 %last_attend.1 = bf16[1,128,8192]{2,1,0:T(8,128)(2,1)} custom-call(bf16[128,2048]{1,0:T(8,128)(2,1)S(1)} %local_scores.15.refs_0_, bf16[128,8192]{1,0:T(8,128)(2,1)S(1)} %bitcast.27, bf16[8,128,128]{2,1,0:T(8,128)(2,1)S(1)} %fusion.42.refs_2_, bf16[128,1024]{1,0:T(8,128)(2,1)S(1)} %get-tuple-element.178.refs_3_, ...), custom_call_target="tpu_custom_call" | custom-call | flops 2000000000 | bytes 1 | tf_op jit(solution)/shard_map/last_attend/pallas_call | solution.py:30
  (94 shorter events, 18.5 us)
Async XLA Ops:
  3.5 5.3 %copy-start.1 = (bf16[1,128,8192]{2,1,0:T(8,128)(2,1)S(1)}, bf16[1,128,8192]{2,1,0:T(8,128)(2,1)}, u32[]{:S(2)}) copy-start(bf16[1,128,8192]{2,1,0:T(8,128)(2,1)} %param.5) | copy-start | bytes 6291460
  3.6 1.7 %collective-permute-start.1 = (bf16[8,128,128]{2,1,0:T(8,128)(2,1)S(1)}, bf16[8,128,128]{2,1,0:T(8,128)(2,1)S(1)}, u32[]{:S(2)}, u32[]{:S(2)}) collective-permute-start(bf16[8,128,128]{2,1,0:T(8,128)(2,1)S(1)} %get-tuple-element.95.refs_2_), channel_id=1, source_target_pairs={{0,1},{2,3},{1,0},{3,2},{4,5},{6,7},{5,4},{7,6},{8,9},{10,11},{9,8... | collective-permute-start | bytes 786440 | tf_op jit(solution)/shard_map/ppermute | solution.py:294
  4.4 3.8 %collective-permute-start = (bf16[8,128,128]{2,1,0:T(8,128)(2,1)S(1)}, bf16[8,128,128]{2,1,0:T(8,128)(2,1)S(1)}, u32[]{:S(2)}, u32[]{:S(2)}) collective-permute-start(bf16[8,128,128]{2,1,0:T(8,128)(2,1)S(1)} %get-tuple-element.96), channel_id=1, source_target_pairs={{0,1},{2,3},{1,0},{3,2},{4,5},{6,7},{5,4},{7,6},{8,9},{10,11},{9,8... | collective-permute-start | bytes 786440 | tf_op jit(solution)/shard_map/ppermute | solution.py:294
  5.3 10.0 %collective-permute-start.4 = (bf16[8,128,128]{2,1,0:T(8,128)(2,1)S(1)}, bf16[8,128,128]{2,1,0:T(8,128)(2,1)S(1)}, u32[]{:S(2)}, u32[]{:S(2)}) collective-permute-start(bf16[8,128,128]{2,1,0:T(8,128)(2,1)S(1)} %fusion.46), channel_id=1, source_target_pairs={{0,2},{1,3},{2,0},{3,1},{4,6},{5,7},{6,4},{7,5},{8,10},{9,11},{10,... | collective-permute-start | bytes 786440 | tf_op jit(solution)/shard_map/ppermute | solution.py:298
  8.3 12.6 %collective-permute-start.7 = (bf16[8,128,128]{2,1,0:T(8,128)(2,1)S(1)}, bf16[8,128,128]{2,1,0:T(8,128)(2,1)S(1)}, u32[]{:S(2)}, u32[]{:S(2)}) collective-permute-start(bf16[8,128,128]{2,1,0:T(8,128)(2,1)S(1)} %fusion.43.refs_2_), channel_id=1, source_target_pairs={{0,2},{1,3},{2,0},{3,1},{4,6},{5,7},{6,4},{7,5},{8,10},{9,11},{10,... | collective-permute-start | bytes 786440 | tf_op jit(solution)/shard_map/ppermute | solution.py:298
  9.3 8.7 %collective-permute-start.3 = (bf16[16,128,128]{2,1,0:T(8,128)(2,1)S(1)}, bf16[16,128,128]{2,1,0:T(8,128)(2,1)S(1)}, u32[]{:S(2)}, u32[]{:S(2)}) collective-permute-start(bf16[16,128,128]{2,1,0:T(8,128)(2,1)S(1)} %get-tuple-element.99.refs_2_), channel_id=1, source_target_pairs={{0,1},{2,3},{1,0},{3,2},{4,5},{6,7},{5,4},{7,6},{8,9},{10,11},{9,8... | collective-permute-start | bytes 1572872 | tf_op jit(solution)/shard_map/ppermute | solution.py:294
  10.4 19.0 %collective-permute-start.2 = (bf16[32,128,128]{2,1,0:T(8,128)(2,1)S(1)}, bf16[32,128,128]{2,1,0:T(8,128)(2,1)S(1)}, u32[]{:S(2)}, u32[]{:S(2)}) collective-permute-start(bf16[32,128,128]{2,1,0:T(8,128)(2,1)S(1)} %get-tuple-element.102.refs_2_), channel_id=1, source_target_pairs={{0,1},{2,3},{1,0},{3,2},{4,5},{6,7},{5,4},{7,6},{8,9},{10,11},{9,8... | collective-permute-start | bytes 3145736 | tf_op jit(solution)/shard_map/ppermute | solution.py:294
  15.5 8.1 %collective-permute-start.6 = (bf16[8,128,128]{2,1,0:T(8,128)(2,1)S(1)}, bf16[8,128,128]{2,1,0:T(8,128)(2,1)S(1)}, u32[]{:S(2)}, u32[]{:S(2)}) collective-permute-start(bf16[8,128,128]{2,1,0:T(8,128)(2,1)S(1)} %fusion.68.refs_2_), channel_id=1, source_target_pairs={{0,4},{12,8},{4,0},{8,12},{1,5},{13,9},{5,1},{9,13},{2,6},{14,10},... | collective-permute-start | bytes 786440 | tf_op jit(solution)/shard_map/ppermute | solution.py:323
  18.2 7.9 %collective-permute-start.5 = (bf16[8,128,128]{2,1,0:T(8,128)(2,1)S(1)}, bf16[8,128,128]{2,1,0:T(8,128)(2,1)S(1)}, u32[]{:S(2)}, u32[]{:S(2)}) collective-permute-start(bf16[8,128,128]{2,1,0:T(8,128)(2,1)S(1)} %get-tuple-element.108), channel_id=1, source_target_pairs={{0,2},{1,3},{2,0},{3,1},{4,6},{5,7},{6,4},{7,5},{8,10},{9,11},{10,... | collective-permute-start | bytes 786440 | tf_op jit(solution)/shard_map/ppermute | solution.py:298
  21.4 7.7 %collective-permute-start.11 = (bf16[8,128,128]{2,1,0:T(8,128)(2,1)S(1)}, bf16[8,128,128]{2,1,0:T(8,128)(2,1)S(1)}, u32[]{:S(2)}, u32[]{:S(2)}) collective-permute-start(bf16[8,128,128]{2,1,0:T(8,128)(2,1)S(1)} %fusion.69.refs_2_), channel_id=1, source_target_pairs={{0,4},{12,8},{4,0},{8,12},{1,5},{13,9},{5,1},{9,13},{2,6},{14,10},... | collective-permute-start | bytes 786440 | tf_op jit(solution)/shard_map/ppermute | solution.py:323
  23.8 7.3 %collective-permute-start.10 = (bf16[8,128,128]{2,1,0:T(8,128)(2,1)S(1)}, bf16[8,128,128]{2,1,0:T(8,128)(2,1)S(1)}, u32[]{:S(2)}, u32[]{:S(2)}) collective-permute-start(bf16[8,128,128]{2,1,0:T(8,128)(2,1)S(1)} %fusion.5), channel_id=1, source_target_pairs={{4,8},{5,9},{6,10},{7,11},{0,1},{2,3},{12,13},{14,15},{8,4},{9,5},... | collective-permute-start | bytes 786440 | tf_op jit(solution)/shard_map/ppermute | solution.py:329
  23.9 8.7 %collective-permute-start.9 = (bf16[8,128,128]{2,1,0:T(8,128)(2,1)S(1)}, bf16[8,128,128]{2,1,0:T(8,128)(2,1)S(1)}, u32[]{:S(2)}, u32[]{:S(2)}) collective-permute-start(bf16[8,128,128]{2,1,0:T(8,128)(2,1)S(1)} %get-tuple-element.113), channel_id=1, source_target_pairs={{0,2},{1,3},{2,0},{3,1},{4,6},{5,7},{6,4},{7,5},{8,10},{9,11},{10,... | collective-permute-start | bytes 786440 | tf_op jit(solution)/shard_map/ppermute | solution.py:298
  26.2 8.8 %collective-permute-start.8 = (bf16[8,128,128]{2,1,0:T(8,128)(2,1)S(1)}, bf16[8,128,128]{2,1,0:T(8,128)(2,1)S(1)}, u32[]{:S(2)}, u32[]{:S(2)}) collective-permute-start(bf16[8,128,128]{2,1,0:T(8,128)(2,1)S(1)} %fusion.67.refs_2_), channel_id=1, source_target_pairs={{0,4},{12,8},{4,0},{8,12},{1,5},{13,9},{5,1},{9,13},{2,6},{14,10},... | collective-permute-start | bytes 786440 | tf_op jit(solution)/shard_map/ppermute | solution.py:323
  29.4 6.9 %collective-permute-start.16 = (bf16[8,128,128]{2,1,0:T(8,128)(2,1)S(1)}, bf16[8,128,128]{2,1,0:T(8,128)(2,1)S(1)}, u32[]{:S(2)}, u32[]{:S(2)}) collective-permute-start(bf16[8,128,128]{2,1,0:T(8,128)(2,1)S(1)} %fusion.7), channel_id=1, source_target_pairs={{4,8},{5,9},{6,10},{7,11},{0,1},{2,3},{12,13},{14,15},{8,4},{9,5},... | collective-permute-start | bytes 786440 | tf_op jit(solution)/shard_map/ppermute | solution.py:329
  29.6 8.8 %collective-permute-start.15 = (bf16[8,128,128]{2,1,0:T(8,128)(2,1)S(1)}, bf16[8,128,128]{2,1,0:T(8,128)(2,1)S(1)}, u32[]{:S(2)}, u32[]{:S(2)}) collective-permute-start(bf16[8,128,128]{2,1,0:T(8,128)(2,1)S(1)} %get-tuple-element.118), channel_id=1, source_target_pairs={{0,2},{1,3},{2,0},{3,1},{4,6},{5,7},{6,4},{7,5},{8,10},{9,11},{10,... | collective-permute-start | bytes 786440 | tf_op jit(solution)/shard_map/ppermute | solution.py:298
  33.0 7.9 %collective-permute-start.14 = (bf16[8,128,128]{2,1,0:T(8,128)(2,1)S(1)}, bf16[8,128,128]{2,1,0:T(8,128)(2,1)S(1)}, u32[]{:S(2)}, u32[]{:S(2)}) collective-permute-start(bf16[8,128,128]{2,1,0:T(8,128)(2,1)S(1)} %fusion.9.refs_2_), channel_id=1, source_target_pairs={{0,4},{12,8},{4,0},{8,12},{1,5},{13,9},{5,1},{9,13},{2,6},{14,10},... | collective-permute-start | bytes 786440 | tf_op jit(solution)/shard_map/ppermute | solution.py:323
  35.2 8.0 %collective-permute-start.13 = (bf16[8,128,128]{2,1,0:T(8,128)(2,1)S(1)}, bf16[8,128,128]{2,1,0:T(8,128)(2,1)S(1)}, u32[]{:S(2)}, u32[]{:S(2)}) collective-permute-start(bf16[8,128,128]{2,1,0:T(8,128)(2,1)S(1)} %fusion.10), channel_id=1, source_target_pairs={{4,8},{5,9},{6,10},{7,11},{0,1},{2,3},{12,13},{14,15},{8,4},{9,5},... | collective-permute-start | bytes 786440 | tf_op jit(solution)/shard_map/ppermute | solution.py:329
  35.3 9.2 %collective-permute-start.12 = (bf16[8,128,128]{2,1,0:T(8,128)(2,1)S(1)}, bf16[8,128,128]{2,1,0:T(8,128)(2,1)S(1)}, u32[]{:S(2)}, u32[]{:S(2)}) collective-permute-start(bf16[8,128,128]{2,1,0:T(8,128)(2,1)S(1)} %get-tuple-element.124), channel_id=1, source_target_pairs={{0,2},{1,3},{2,0},{3,1},{4,6},{5,7},{6,4},{7,5},{8,10},{9,11},{10,... | collective-permute-start | bytes 786440 | tf_op jit(solution)/shard_map/ppermute | solution.py:298
  38.8 8.7 %collective-permute-start.17 = (bf16[8,128,128]{2,1,0:T(8,128)(2,1)S(1)}, bf16[8,128,128]{2,1,0:T(8,128)(2,1)S(1)}, u32[]{:S(2)}, u32[]{:S(2)}) collective-permute-start(bf16[8,128,128]{2,1,0:T(8,128)(2,1)S(1)} %get-tuple-element.127.refs_2_), channel_id=1, source_target_pairs={{0,4},{12,8},{4,0},{8,12},{1,5},{13,9},{5,1},{9,13},{2,6},{14,10},... | collective-permute-start | bytes 786440 | tf_op jit(solution)/shard_map/ppermute | solution.py:323
  41.1 9.3 %collective-permute-start.21 = (bf16[8,128,128]{2,1,0:T(8,128)(2,1)S(1)}, bf16[8,128,128]{2,1,0:T(8,128)(2,1)S(1)}, u32[]{:S(2)}, u32[]{:S(2)}) collective-permute-start(bf16[8,128,128]{2,1,0:T(8,128)(2,1)S(1)} %get-tuple-element.130), channel_id=1, source_target_pairs={{0,2},{1,3},{2,0},{3,1},{4,6},{5,7},{6,4},{7,5},{8,10},{9,11},{10,... | collective-permute-start | bytes 786440 | tf_op jit(solution)/shard_map/ppermute | solution.py:298
  42.7 7.1 %collective-permute-start.22 = (bf16[8,128,128]{2,1,0:T(8,128)(2,1)S(1)}, bf16[8,128,128]{2,1,0:T(8,128)(2,1)S(1)}, u32[]{:S(2)}, u32[]{:S(2)}) collective-permute-start(bf16[8,128,128]{2,1,0:T(8,128)(2,1)S(1)} %add_convert_fusion.4), channel_id=1, source_target_pairs={{4,8},{5,9},{6,10},{7,11},{0,1},{2,3},{12,13},{14,15},{8,4},{9,5},... | collective-permute-start | bytes 786440 | tf_op jit(solution)/shard_map/ppermute | solution.py:329
  45.0 7.7 %collective-permute-start.20 = (bf16[8,128,128]{2,1,0:T(8,128)(2,1)S(1)}, bf16[8,128,128]{2,1,0:T(8,128)(2,1)S(1)}, u32[]{:S(2)}, u32[]{:S(2)}) collective-permute-start(bf16[8,128,128]{2,1,0:T(8,128)(2,1)S(1)} %get-tuple-element.136.refs_2_), channel_id=1, source_target_pairs={{0,4},{12,8},{4,0},{8,12},{1,5},{13,9},{5,1},{9,13},{2,6},{14,10},... | collective-permute-start | bytes 786440 | tf_op jit(solution)/shard_map/ppermute | solution.py:323
  47.7 7.6 %collective-permute-start.18 = (bf16[8,128,128]{2,1,0:T(8,128)(2,1)S(1)}, bf16[8,128,128]{2,1,0:T(8,128)(2,1)S(1)}, u32[]{:S(2)}, u32[]{:S(2)}) collective-permute-start(bf16[8,128,128]{2,1,0:T(8,128)(2,1)S(1)} %get-tuple-element.139), channel_id=1, source_target_pairs={{0,2},{1,3},{2,0},{3,1},{4,6},{5,7},{6,4},{7,5},{8,10},{9,11},{10,... | collective-permute-start | bytes 786440 | tf_op jit(solution)/shard_map/ppermute | solution.py:298
  49.2 4.2 %collective-permute-start.19 = (bf16[8,128,128]{2,1,0:T(8,128)(2,1)S(1)}, bf16[8,128,128]{2,1,0:T(8,128)(2,1)S(1)}, u32[]{:S(2)}, u32[]{:S(2)}) collective-permute-start(bf16[8,128,128]{2,1,0:T(8,128)(2,1)S(1)} %add_convert_fusion.3), channel_id=1, source_target_pairs={{4,8},{5,9},{6,10},{7,11},{0,1},{2,3},{12,13},{14,15},{8,4},{9,5},... | collective-permute-start | bytes 786440 | tf_op jit(solution)/shard_map/ppermute | solution.py:329
  50.8 8.2 %collective-permute-start.25 = (bf16[8,128,128]{2,1,0:T(8,128)(2,1)S(1)}, bf16[8,128,128]{2,1,0:T(8,128)(2,1)S(1)}, u32[]{:S(2)}, u32[]{:S(2)}) collective-permute-start(bf16[8,128,128]{2,1,0:T(8,128)(2,1)S(1)} %fusion.22), channel_id=1, source_target_pairs={{0,4},{12,8},{4,0},{8,12},{1,5},{13,9},{5,1},{9,13},{2,6},{14,10},... | collective-permute-start | bytes 786440 | tf_op jit(solution)/shard_map/ppermute | solution.py:323
  52.8 9.2 %collective-permute-start.24 = (bf16[8,128,128]{2,1,0:T(8,128)(2,1)S(1)}, bf16[8,128,128]{2,1,0:T(8,128)(2,1)S(1)}, u32[]{:S(2)}, u32[]{:S(2)}) collective-permute-start(bf16[8,128,128]{2,1,0:T(8,128)(2,1)S(1)} %add_convert_fusion.2), channel_id=1, source_target_pairs={{4,8},{5,9},{6,10},{7,11},{0,1},{2,3},{12,13},{14,15},{8,4},{9,5},... | collective-permute-start | bytes 786440 | tf_op jit(solution)/shard_map/ppermute | solution.py:329
  59.1 10.1 %collective-permute-start.28 = (bf16[8,128,128]{2,1,0:T(8,128)(2,1)S(1)}, bf16[8,128,128]{2,1,0:T(8,128)(2,1)S(1)}, u32[]{:S(2)}, u32[]{:S(2)}) collective-permute-start(bf16[8,128,128]{2,1,0:T(8,128)(2,1)S(1)} %add_convert_fusion.1), channel_id=1, source_target_pairs={{4,8},{5,9},{6,10},{7,11},{0,1},{2,3},{12,13},{14,15},{8,4},{9,5},... | collective-permute-start | bytes 786440 | tf_op jit(solution)/shard_map/ppermute | solution.py:329
  59.2 9.2 %collective-permute-start.23 = (bf16[8,128,128]{2,1,0:T(8,128)(2,1)S(1)}, bf16[8,128,128]{2,1,0:T(8,128)(2,1)S(1)}, u32[]{:S(2)}, u32[]{:S(2)}) collective-permute-start(bf16[8,128,128]{2,1,0:T(8,128)(2,1)S(1)} %fusion.26), channel_id=1, source_target_pairs={{0,4},{12,8},{4,0},{8,12},{1,5},{13,9},{5,1},{9,13},{2,6},{14,10},... | collective-permute-start | bytes 786440 | tf_op jit(solution)/shard_map/ppermute | solution.py:323
  62.2 11.8 %collective-permute-start.27 = (bf16[8,128,128]{2,1,0:T(8,128)(2,1)S(1)}, bf16[8,128,128]{2,1,0:T(8,128)(2,1)S(1)}, u32[]{:S(2)}, u32[]{:S(2)}) collective-permute-start(bf16[8,128,128]{2,1,0:T(8,128)(2,1)S(1)} %fusion.29), channel_id=1, source_target_pairs={{0,4},{12,8},{4,0},{8,12},{1,5},{13,9},{5,1},{9,13},{2,6},{14,10},... | collective-permute-start | bytes 786440 | tf_op jit(solution)/shard_map/ppermute | solution.py:323
  68.6 5.9 %collective-permute-start.26 = (bf16[8,128,128]{2,1,0:T(8,128)(2,1)S(1)}, bf16[8,128,128]{2,1,0:T(8,128)(2,1)S(1)}, u32[]{:S(2)}, u32[]{:S(2)}) collective-permute-start(bf16[8,128,128]{2,1,0:T(8,128)(2,1)S(1)} %add_convert_fusion), channel_id=1, source_target_pairs={{4,8},{5,9},{6,10},{7,11},{0,1},{2,3},{12,13},{14,15},{8,4},{9,5},... | collective-permute-start | bytes 786440 | tf_op jit(solution)/shard_map/ppermute | solution.py:329
  69.4 10.2 %collective-permute-start.30 = (bf16[8,128,128]{2,1,0:T(8,128)(2,1)S(1)}, bf16[8,128,128]{2,1,0:T(8,128)(2,1)S(1)}, u32[]{:S(2)}, u32[]{:S(2)}) collective-permute-start(bf16[8,128,128]{2,1,0:T(8,128)(2,1)S(1)} %fusion.35), channel_id=1, source_target_pairs={{0,4},{12,8},{4,0},{8,12},{1,5},{13,9},{5,1},{9,13},{2,6},{14,10},... | collective-permute-start | bytes 786440 | tf_op jit(solution)/shard_map/ppermute | solution.py:323
  74.7 10.0 %collective-permute-start.29 = (bf16[8,128,128]{2,1,0:T(8,128)(2,1)S(1)}, bf16[8,128,128]{2,1,0:T(8,128)(2,1)S(1)}, u32[]{:S(2)}, u32[]{:S(2)}) collective-permute-start(bf16[8,128,128]{2,1,0:T(8,128)(2,1)S(1)} %fusion.39), channel_id=1, source_target_pairs={{0,4},{12,8},{4,0},{8,12},{1,5},{13,9},{5,1},{9,13},{2,6},{14,10},... | collective-permute-start | bytes 786440 | tf_op jit(solution)/shard_map/ppermute | solution.py:323
  (5 other events, 15.2 us)

commit v4 on v3

v4 whole, which is shorter than its diff:
```python
import functools

import jax
import jax.numpy as jnp
from jax import lax
from jax.experimental import pallas as pl
from jax.experimental.pallas import tpu as pltpu
from jax.sharding import PartitionSpec as P

DH = 128
F32 = jnp.float32
BF16 = jnp.bfloat16
VMEM_LIMIT = 8 << 20
PART = 4
COST = 2 * 10**9
VMEM = pl.BlockSpec(memory_space=pltpu.VMEM)
ANY = pl.BlockSpec(memory_space=pl.ANY)


def silu(x):
    x = x.astype(F32)
    return (x * (0.5 * jnp.tanh(0.5 * x) + 0.5)).astype(BF16)


def call(kernel, name, operands, outs, after):
    n_in, n_after = len(operands), len(after)

    def run(*refs):
        kernel(refs[:n_in], refs[n_in + n_after :])

    return pl.pallas_call(
        run,
        in_specs=[VMEM] * n_in + [ANY] * n_after,
        out_specs=[VMEM] * len(outs),
        out_shape=outs,
        compiler_params=pltpu.CompilerParams(vmem_limit_bytes=VMEM_LIMIT),
        cost_estimate=pl.CostEstimate(flops=COST, bytes_accessed=1, transcendentals=0),
        name=name,
    )(*operands, *after)


def head_cols(h):
    return slice(h * DH, (h + 1) * DH)


def states_of(count, rows, kind=BF16):
    return jax.ShapeDtypeStruct((count, rows, DH), kind)


def conditions():
    place, along = lax.axis_index("ctx"), lax.axis_index("head")
    outer = (along == 0) | (along == 3)
    return {
        "odd": lax.rem(place, 2) == 1,
        "even": lax.rem(place, 2) == 0,
        "later": place >= 2,
        "left": along < 2,
        "right": along >= 2,
        "outer": outer,
        "inner": jnp.logical_not(outer),
    }


def term_sum(refs, terms, held, h):
    out = None
    for ref, (_, first, wanted) in zip(refs, terms):
        x = ref[first + h].astype(F32)
        if wanted:
            x = jnp.where(held[wanted], x, 0.0)
        out = x if out is None else out + x
    return out


def combine(name, count, chunks, after):
    starts = [sum(len(c) for c in chunks[:i]) for i in range(len(chunks))]

    def kernel(ins, outs):
        held = Held()
        for i, terms in enumerate(chunks):
            for h in range(count):
                outs[0][i * count + h] = term_sum(ins[starts[i] :], terms, held, h).astype(BF16)

    arrays = [t[0] for terms in chunks for t in terms]
    return call(kernel, name, arrays, [states_of(count * len(chunks), DH)], after)[0]


class Held:
    def __init__(self):
        self.base, self.known = conditions(), {}

    def __getitem__(self, wanted):
        if wanted not in self.known:
            out = self.base[wanted[0]]
            for name in wanted[1:]:
                out = out & self.base[name]
            self.known[wanted] = out
        return self.known[wanted]


def kv_states(k_rows, v_rows, first, count, after, limit=VMEM_LIMIT):
    rows = k_rows.shape[0]
    n_after = len(after)

    def run(*refs):
        k_hbm, v_hbm = refs[:2]
        outs = refs[2 + n_after : -3]
        k_ref, v_ref, sem = refs[-3:]
        parts = count // PART
        copies = []
        for i in range(parts):
            cols = pl.ds((first + i * PART) * DH, PART * DH)
            to = pl.ds(i * PART * DH, PART * DH)
            for j, (hbm_ref, ref) in enumerate(((k_hbm, k_ref), (v_hbm, v_ref))):
                copy = pltpu.make_async_copy(hbm_ref.at[:, cols], ref.at[:, to], sem.at[2 * i + j])
                copy.start()
                copies.append(copy)
        for h in range(count):
            if h % PART == 0:
                copies[2 * (h // PART)].wait()
                copies[2 * (h // PART) + 1].wait()
            ka = silu(k_ref[:, head_cols(h)])
            outs[1][:, head_cols(h)] = ka
            outs[0][h] = lax.dot_general(
                ka, v_ref[:, head_cols(h)], (((0,), (0,)), ((), ())),
                preferred_element_type=F32,
            ).astype(BF16)

    outs = [states_of(count, DH), jax.ShapeDtypeStruct((rows, count * DH), BF16)]
    hbm = pl.BlockSpec(memory_space=pltpu.HBM)
    block = pltpu.VMEM((rows, count * DH), BF16)
    return pl.pallas_call(
        run,
        in_specs=[hbm, hbm] + [ANY] * n_after,
        out_specs=[VMEM] * len(outs),
        out_shape=outs,
        scratch_shapes=[block, block, pltpu.SemaphoreType.DMA((2 * (count // PART),))],
        compiler_params=pltpu.CompilerParams(vmem_limit_bytes=limit),
        cost_estimate=pl.CostEstimate(flops=10**6, bytes_accessed=1, transcendentals=0),
        name="kv_states",
    )(k_rows, v_rows, *after)


def local_scores(q_rows, ka, ka_first, first, count, after):
    rows = q_rows.shape[0]

    def kernel(ins, outs):
        q_ref, ka_ref = ins
        causal = lax.broadcasted_iota(jnp.int32, (rows, rows), 0) >= lax.broadcasted_iota(
            jnp.int32, (rows, rows), 1
        )
        for h in range(count):
            qa = silu(q_ref[:, head_cols(first + h)])
            scores = lax.dot_general(
                qa, ka_ref[:, head_cols(ka_first + h)], (((1,), (1,)), ((), ())),
                preferred_element_type=F32,
            )
            at = h * (rows + DH)
            outs[0][:, at : at + rows] = jnp.where(causal, scores, 0.0).astype(BF16)
            outs[0][:, at + rows : at + rows + DH] = qa

    out = jax.ShapeDtypeStruct((rows, count * (rows + DH)), BF16)
    return call(
        kernel, "local_scores", [q_rows, ka], [out], after
    )[0]


def attend_head(both_ref, v, state, h, rows):
    at = h * (rows + DH)
    right = jnp.concatenate([v, state.astype(BF16)], axis=0)
    return jnp.dot(
        both_ref[:, at : at + rows + DH], right, preferred_element_type=F32
    ).astype(BF16)


def attend(both, v_rows, first, terms, after):
    rows = both.shape[0]
    count = both.shape[1] // (rows + DH)

    def kernel(ins, outs):
        both_ref, v_ref, refs = ins[0], ins[1], ins[2:]
        held = Held()
        squares = None
        for h in range(count):
            state = term_sum(refs, terms, held, h)
            attn = attend_head(both_ref, v_ref[:, head_cols(first + h)], state, h, rows)
            outs[0][:, head_cols(h)] = attn
            wide = attn.astype(F32)
            squares = wide * wide if squares is None else squares + wide * wide
        outs[1][...] = squares

    outs = [
        jax.ShapeDtypeStruct((rows, count * DH), BF16),
        jax.ShapeDtypeStruct((rows, DH), F32),
    ]
    return call(kernel, "attend", [both, v_rows, *(t[0] for t in terms)], outs, after)


def last_attend(both, v_rows, first, terms, attns, squares, gain):
    rows, width = v_rows.shape
    count = both.shape[1] // (rows + DH)
    n_terms, n = len(terms), len(attns)
    starts = [0]
    for a in attns:
        starts.append(starts[-1] + a.shape[1])

    def kernel(*refs):
        both_ref, v_ref = refs[:2]
        term_refs = refs[2 : 2 + n_terms]
        attn_refs = refs[2 + n_terms : 2 + n_terms + n]
        sq_refs = refs[2 + n_terms + n : 2 + n_terms + 2 * n]
        gain_ref, out_hbm, done_ref, sem = refs[2 + n_terms + 2 * n :]
        held = Held()
        squares = None
        last = []
        for h in range(count):
            state = term_sum(term_refs, terms, held, h)
            attn = attend_head(both_ref, v_ref[:, head_cols(first + h)], state, h, rows)
            last.append(attn)
            wide = attn.astype(F32)
            squares = wide * wide if squares is None else squares + wide * wide
        for ref in sq_refs:
            squares = squares + ref[...]
        mean_sq = jnp.sum(squares, axis=1, keepdims=True) / width
        scale = jnp.broadcast_to(lax.rsqrt(mean_sq + 1e-06), (rows, DH))
        copies = []
        for i, start in enumerate(starts):
            wide = count * DH if i == n else attn_refs[i].shape[1]
            for h in range(wide // DH):
                cols = slice(start + h * DH, start + (h + 1) * DH)
                attn = last[h] if i == n else attn_refs[i][:, head_cols(h)]
                done_ref[:, cols] = (attn.astype(F32) * scale * gain_ref[:, cols]).astype(BF16)
            part = pl.ds(start, wide)
            copy = pltpu.make_async_copy(
                done_ref.at[:, part], out_hbm.at[0, :, part], sem.at[i]
            )
            copy.start()
            copies.append(copy)
        for copy in copies:
            copy.wait()

    operands = [both, v_rows, *(t[0] for t in terms), *attns, *squares, gain.reshape(1, width)]
    return pl.pallas_call(
        kernel,
        in_specs=[VMEM] * len(operands),
        out_specs=pl.BlockSpec(memory_space=pltpu.HBM),
        out_shape=jax.ShapeDtypeStruct((1, rows, width), BF16),
        scratch_shapes=[pltpu.VMEM((rows, width), BF16), pltpu.SemaphoreType.DMA((n + 1,))],
        compiler_params=pltpu.CompilerParams(vmem_limit_bytes=VMEM_LIMIT),
        cost_estimate=pl.CostEstimate(flops=COST, bytes_accessed=1, transcendentals=0),
        name="last_attend",
    )(*operands)


def total(*terms):
    out = terms[0].astype(F32)
    for term in terms[1:]:
        out = out + term.astype(F32)
    return out


def both_ways(pairs):
    return pairs + [(b, a) for a, b in pairs]


def before_ctx(n_ctx, own):
    odd = lax.axis_index("ctx") % 2 == 1
    before = jnp.zeros(own.shape, F32)
    if n_ctx % 2:
        for s in range(1, n_ctx):
            before = total(before, lax.ppermute(own, "ctx", [(i, i + s) for i in range(n_ctx - s)]))
        return before.astype(BF16)
    other = lax.ppermute(own, "ctx", both_ways([(i, i + 1) for i in range(0, n_ctx, 2)]))
    couple = total(own, other).astype(BF16)
    for s in range(2, n_ctx, 2):
        before = total(before, lax.ppermute(couple, "ctx", [(i, i + s) for i in range(n_ctx - s)]))
    return (before + jnp.where(odd, other.astype(F32), 0.0)).astype(BF16)


def whole_chain(n_head, own, early):
    upto = total(early, own)
    early = early.astype(F32)
    left = lax.axis_index("head") < n_head // 2
    if n_head == 1:
        return early.astype(BF16)
    if n_head % 2:
        lower = higher = jnp.zeros_like(own)
        for _ in range(n_head - 1):
            lower = lax.ppermute(
                total(lower, upto).astype(BF16), "head", [(i, i + 1) for i in range(n_head - 1)]
            )
            higher = lax.ppermute(
                total(higher, early).astype(BF16), "head", [(i + 1, i) for i in range(n_head - 1)]
            )
        return total(early, lower, higher).astype(BF16)
    mid = n_head // 2
    mine, mirror = jnp.where(left, upto, early), jnp.where(left, early, upto)
    inward = jnp.zeros_like(own)
    for t in range(mid - 1):
        inward = inward + lax.ppermute(
            total(inward, mine).astype(BF16), "head", [(t, t + 1), (n_head - 1 - t, n_head - 2 - t)]
        )
    outward = lax.ppermute(total(inward, mine).astype(BF16), "head", both_ways([(mid - 1, mid)]))
    for t in range(mid - 1, 0, -1):
        outward = outward + lax.ppermute(
            total(outward, mirror).astype(BF16), "head", [(t, t - 1), (n_head - 1 - t, n_head - t)]
        )
    return total(early, inward, outward).astype(BF16)


SKEW = 3
LATE = 2


def also(terms, *wanted):
    return [(array, first, (*had, *wanted)) for array, first, had in terms]


class Scan:
    def __init__(self, n, size):
        self.n, self.size = n, size
        self.own, self.other, self.x, self.a, self.b = {}, {}, {}, {}, {}
        self.couples = both_ways([(0, 1), (2, 3)])
        self.across = both_ways([(0, 2), (1, 3)])
        at = lambda z, c: 4 * z + c
        self.swap = both_ways(
            [(at(1, c), at(2, c)) for c in range(4)]
            + [(at(z, c), at(z, c + 1)) for z in (0, 3) for c in (0, 2)]
        )

    def begin(self, first, own):
        other = lax.ppermute(own, "ctx", self.couples)
        for i in range(own.shape[0] // self.size):
            self.own[first + i] = (own, i * self.size)
            self.other[first + i] = (other, i * self.size)

    def cross(self, c, after):
        terms = [(*self.own[c], ()), (*self.other[c], ())]
        send = combine("cross_sum", self.size, [terms], after)
        self.x[c] = (lax.ppermute(send, "ctx", self.across), 0)
        return [send]

    def early(self, c):
        return [(*self.other[c], ("odd",)), (*self.x[c], ("later",))]

    def to_right(self, c):
        if c < LATE:
            return [(*self.own[c], ()), (*self.other[c], ("odd",))]
        return [*self.early(c), (*self.own[c], ())]

    def to_left(self, c):
        if c < LATE:
            return [(*self.other[c], ()), (*self.own[c], ("even",))]
        return self.early(c)

    def mine(self, c):
        if c < LATE:
            return [*also(self.to_right(c), "left"), *also(self.to_left(c), "right")]
        return [*self.early(c), (*self.own[c], ("left",))]

    def mirror(self, c):
        if c < LATE:
            return [*also(self.to_left(c), "left"), *also(self.to_right(c), "right")]
        return [*self.early(c), (*self.own[c], ("right",))]

    def side(self, t, after):
        inwards, outwards = t < self.n, t >= SKEW
        c = t - SKEW
        terms = []
        if inwards:
            terms += also(self.mine(t), *(("outer",) if outwards else ()))
        if outwards:
            terms += also([*self.mirror(c), (*self.b[c], ())], *(("inner",) if inwards else ()))
        send = combine("side_sum", self.size, [terms], after)
        self.a[t] = (lax.ppermute(send, "head", both_ways([(0, 1), (3, 2)])), 0)
        return [send]

    def middle(self, t, after):
        send = combine("middle_sum", self.size, [[*self.mine(t), (*self.a[t], ())]], after)
        self.b[t] = (lax.ppermute(send, ("head", "ctx"), self.swap), 0)
        return [send]

    def lower(self, c):
        return [
            (*self.a[c], ("left", "inner")),
            (*self.b[c], ("right", "inner")),
            (*self.a[c + SKEW], ("right", "outer")),
        ]

    def higher(self, c):
        return [
            (*self.b[c], ("left", "inner")),
            (*self.a[c + SKEW], ("left", "outer")),
            (*self.a[c], ("right", "inner")),
        ]

    def late_cross(self, after):
        chunks = []
        for c in range(LATE):
            whole = [*self.lower(c), (*self.own[c], ()), (*self.other[c], ())]
            chunks.append([*also(self.higher(c), "even"), *also(whole, "odd")])
        send = combine("late_sum", self.size, chunks, after)
        self.late = lax.ppermute(send, "ctx", self.across)
        return [send]

    def late_swap(self, after):
        self.late = lax.optimization_barrier((self.late, *after))[0]
        self.late_other = lax.ppermute(self.late, "ctx", self.couples)

    def state(self, c):
        if c < LATE:
            at = c * self.size
            return [
                *self.lower(c),
                *also([*self.higher(c), (*self.other[c], ())], "odd"),
                (self.late, at, ("later",)),
                (self.late_other, at, ("later",)),
            ]
        return [
            *self.early(c),
            (*self.a[c], ("inner",)),
            (*self.b[c], ("inner",)),
            (*self.a[c + SKEW], ("outer",)),
        ]


def body(n_head, n_ctx, queries, keys, values, gain):
    rows, width = queries.shape[1], queries.shape[2]
    q_rows = queries.reshape(rows, width)
    k_rows = keys.reshape(rows, width)
    v_rows = values.reshape(rows, width)
    heads = width // DH
    if n_head != 4 or n_ctx != 4 or heads % 16:
        own, ka = kv_states(k_rows, v_rows, 0, heads, [])
        state = whole_chain(n_head, own, before_ctx(n_ctx, own))
        both = local_scores(q_rows, ka, 0, 0, heads, [])
        return last_attend(both, v_rows, 0, [(state, 0, ())], [], [], gain)

    n = 8
    size = heads // n
    both, attns, squares, ka = {}, {}, {}, {}
    scan = Scan(n, size)

    def kv(first, count, after, limit=VMEM_LIMIT):
        own, active = kv_states(k_rows, v_rows, first * size, count * size, after, limit)
        scan.begin(first, own)
        for i in range(count):
            ka[first + i] = (active, i * size)
        return [own]

    def scores(c, after):
        both[c] = local_scores(q_rows, *ka[c], c * size, size, after)
        return [both[c]]

    def attention(c, after):
        attns[c], squares[c] = attend(both[c], v_rows, c * size, scan.state(c), after)
        return [squares[c]]

    fill = {
        1: [0], 2: [1], 3: [2], 4: [3], 5: [4], 6: [5], 7: [6], 8: [7],
    }
    clock = kv(0, 2, [], 61 * 10**6)
    clock = kv(2, 2, clock, 60 * 10**6)
    for t in range(n + SKEW):
        clock = scan.side(t, clock)
        if t == 1:
            clock = kv(4, 4, clock)
        for c in fill.get(t, []):
            clock = scores(c, clock)
        if t > n:
            clock = attention(t - n - 1 + LATE, clock)
        if 0 <= t - 1 < n:
            clock = scan.middle(t - 1, clock)
        if t + 2 < n:
            clock = scan.cross(t + 2, clock)
        if t + 2 == n:
            clock = scan.late_cross(clock)
        if t == n + 1:
            scan.late_swap(clock)
    for c in [*range(LATE + 2, n - 2), *range(LATE), n - 2]:
        clock = attention(c, clock)
    return last_attend(
        both[n - 1], v_rows, (n - 1) * size, scan.state(n - 1),
        [attns[c] for c in range(n - 1)], [squares[c] for c in range(n - 1)], gain,
    )


def solution(mesh):
    n_head, n_ctx = mesh.shape["head"], mesh.shape["ctx"]
    return jax.shard_map(
        functools.partial(body, n_head, n_ctx),
        mesh=mesh,
        in_specs=(
            P(("rep", "ctx"), "head", None),
            P(("rep", "ctx"), "head", None),
            P(("rep", "ctx"), "head", None),
            P(),
        ),
        out_specs=P(("rep", "ctx"), "head", None),
        check_vma=False,
    )
```

time: 87.6 us -> 78.3 us (0.89)
  waiting for transfers between devices: 31.5 us -> 14.3 us
  Pallas kernels: 9.08 us -> 22.5 us
  other arithmetic: 6.67 us -> 0 us
  starting transfers between devices: 36.4 us -> 39.4 us
  local copies, waits for them, and re-layouts: 3.21 us -> 1.09 us
    ppermute x31 -> x30, waiting for transfers between devices: 31.5 us -> 14.3 us  [the longest x11 7.51 us: side(): self.a[t] = (lax.ppermute(send, 'head', both_ways([(0, 1), (3, 2)])), 0)]
    pallas_call x1 -> x4, Pallas kernels: 0.34 us -> 10.4 us  [the longest x3 8.32 us: kv_states(): pl.pallas_call(run, in_specs=[hbm, hbm] + [ANY] * n_after, out_specs=[VME...]
    convert_element_type x31 -> x0, other arithmetic: 6.66 us -> none  [the longest x9 2.1 us: side(): send = held(send.astype(BF16), after)]
    pallas_call x19 -> x41, Pallas kernels: 8.73 us -> 12.1 us  [call(): pl.pallas_call(run, in_specs=[VMEM] * n_in + [ANY] * n_after, out_specs=[...]
    ppermute x31 -> x30, starting transfers between devices: 36.4 us -> 39.4 us  [the longest x11 27.3 us: side(): self.a[t] = (lax.ppermute(send, 'head', both_ways([(0, 1), (3, 2)])), 0)]
    unnamed x12 -> x18, local copies, waits for them, and re-layouts: 3.21 us -> 1.09 us
  transfers between devices with their start and end apart: 31 -> 30, of which waited for: 16 -> 8; matrix products, arithmetic and copies ran while one was open for 7% -> 0% of each run, Pallas kernels for 7% -> 23%
where the time goes in v4:
time: 78.3 us; the launch traced here: 78.1 us
  starting transfers between devices  39.4 us (50%)
  Pallas kernels  22.5 us (29%)
  waiting for transfers between devices  14.3 us (18%)
  local copies, waits for them, and re-layouts  1.09 us (1%)
    ppermute x11, starting transfers between devices, side(): self.a[t] = (lax.ppermute(send, 'head', both_ways([(0, 1), (3, 2)])), 0)  27.3 us
    pallas_call x41, Pallas kernels, call(): pl.pallas_call(run, in_specs=[VMEM] * n_in + [ANY] * n_after, out_specs=[...  12.1 us
    ppermute x6, starting transfers between devices, cross(): self.x[c] = (lax.ppermute(send, 'ctx', self.across), 0)  9.13 us
    pallas_call x3, Pallas kernels, kv_states(): pl.pallas_call(run, in_specs=[hbm, hbm] + [ANY] * n_after, out_specs=[VME...  8.32 us
    ppermute x11, waiting for transfers between devices, side(): self.a[t] = (lax.ppermute(send, 'head', both_ways([(0, 1), (3, 2)])), 0)  7.51 us
    ppermute x6, waiting for transfers between devices, cross(): self.x[c] = (lax.ppermute(send, 'ctx', self.across), 0)  6.76 us
    pallas_call x1, Pallas kernels, last_attend(): pl.pallas_call(kernel, in_specs=[VMEM] * len(operands), out_specs=pl.Bloc...  2.04 us
  transfers between devices with their start and end apart: 30, of which 8 were waited for; matrix products, arithmetic and copies ran while one was open for 0% of the time, Pallas kernels for 23%

profile of v4, /device:TPU:0, one launch (start us, length us, event | category | flops | bytes accessed | tf_op | source)
XLA Modules:
  0.0 78.1 jit_solution(4123877572708730352)
XLA Ops:
  0.0 2.8 %kv_states.3 = (bf16[16,128,128]{2,1,0:T(8,128)(2,1)}, bf16[128,2048]{1,0:T(8,128)(2,1)}) custom-call(bf16[128,8192]{1,0:T(8,128)(2,1)} %bitcast.15, bf16[128,8192]{1,0:T(8,128)(2,1)} %bitcast.4), custom_call_target="tpu_custom_call" | custom-call | flops 1000000 | bytes 1 | tf_op jit(solution)/shard_map/kv_states/pallas_call | solution.py:131
  3.3 2.9 %kv_states.4 = (bf16[16,128,128]{2,1,0:T(8,128)(2,1)}, bf16[128,2048]{1,0:T(8,128)(2,1)}) custom-call(bf16[128,8192]{1,0:T(8,128)(2,1)} %bitcast.16, bf16[128,8192]{1,0:T(8,128)(2,1)} %bitcast.5, bf16[16,128,128]{2,1,0:T(8,128)(2,1)} %get-tuple-element.26.refs_2_.refs_0_.refs_3_.refs_4_.refs_5_.refs_6_.refs_14_), custom_call_target="tpu_custom_call" | custom-call | flops 1000000 | bytes 1 | tf_op jit(solution)/shard_map/kv_states/pallas_call | solution.py:131
  6.4 1.0 %copy-done.5 = bf16[16,128,128]{2,1,0:T(8,128)(2,1)S(1)} copy-done((bf16[16,128,128]{2,1,0:T(8,128)(2,1)S(1)}, bf16[16,128,128]{2,1,0:T(8,128)(2,1)}, u32[]{:S(2)}) %copy-start.5) | copy-done | bytes 524312
  7.6 3.1 %collective-permute-start.4 = (bf16[8,128,128]{2,1,0:T(8,128)(2,1)S(1)}, bf16[8,128,128]{2,1,0:T(8,128)(2,1)S(1)}, u32[]{:S(2)}, u32[]{:S(2)}) collective-permute-start(bf16[8,128,128]{2,1,0:T(8,128)(2,1)S(1)} %side_sum.11.refs_2_), channel_id=1, source_target_pairs={{0,4},{12,8},{4,0},{8,12},{1,5},{13,9},{5,1},{9,13},{2,6},{14,10},... | collective-permute-start | bytes 786440 | tf_op jit(solution)/shard_map/ppermute | solution.py:374
  10.8 1.6 %collective-permute-start.3 = (bf16[8,128,128]{2,1,0:T(8,128)(2,1)S(1)}, bf16[8,128,128]{2,1,0:T(8,128)(2,1)S(1)}, u32[]{:S(2)}, u32[]{:S(2)}) collective-permute-start(bf16[8,128,128]{2,1,0:T(8,128)(2,1)S(1)} %cross_sum.6.refs_4_), channel_id=1, source_target_pairs={{0,2},{1,3},{2,0},{3,1},{4,6},{5,7},{6,4},{7,5},{8,10},{9,11},{10,... | collective-permute-start | bytes 786440 | tf_op jit(solution)/shard_map/ppermute | solution.py:339
  13.1 2.6 %kv_states.5 = (bf16[32,128,128]{2,1,0:T(8,128)(2,1)S(1)}, bf16[128,4096]{1,0:T(8,128)(2,1)S(1)}) custom-call(bf16[128,8192]{1,0:T(8,128)(2,1)S(1)} %bitcast.17, bf16[128,8192]{1,0:T(8,128)(2,1)S(1)} %bitcast.6, bf16[8,128,128]{2,1,0:T(8,128)(2,1)S(1)} %side_sum.12.refs_2_), custom_call_target="tpu_custom_call" | custom-call | flops 1000000 | bytes 1 | tf_op jit(solution)/shard_map/kv_states/pallas_call | solution.py:131
  16.2 1.6 %collective-permute-done.4.refs_4_.refs_2_.refs_3_.refs_7_ = bf16[8,128,128]{2,1,0:T(8,128)(2,1)S(1)} collective-permute-done((bf16[8,128,128]{2,1,0:T(8,128)(2,1)S(1)}, bf16[8,128,128]{2,1,0:T(8,128)(2,1)S(1)}, u32[]{:S(2)}, u32[]{:S(2)}) %collective-permute-start.4) | collective-permute-done | bytes 262176 | tf_op jit(solution)/shard_map/ppermute | solution.py:374
  18.2 2.0 %collective-permute-start.6 = (bf16[8,128,128]{2,1,0:T(8,128)(2,1)S(1)}, bf16[8,128,128]{2,1,0:T(8,128)(2,1)S(1)}, u32[]{:S(2)}, u32[]{:S(2)}) collective-permute-start(bf16[8,128,128]{2,1,0:T(8,128)(2,1)S(1)} %cross_sum.7.refs_3_), channel_id=1, source_target_pairs={{0,2},{1,3},{2,0},{3,1},{4,6},{5,7},{6,4},{7,5},{8,10},{9,11},{10,... | collective-permute-start | bytes 786440 | tf_op jit(solution)/shard_map/ppermute | solution.py:339
  20.4 3.2 %collective-permute-start.5 = (bf16[8,128,128]{2,1,0:T(8,128)(2,1)S(1)}, bf16[8,128,128]{2,1,0:T(8,128)(2,1)S(1)}, u32[]{:S(2)}, u32[]{:S(2)}) collective-permute-start(bf16[8,128,128]{2,1,0:T(8,128)(2,1)S(1)} %side_sum.13.refs_2_), channel_id=1, source_target_pairs={{0,4},{12,8},{4,0},{8,12},{1,5},{13,9},{5,1},{9,13},{2,6},{14,10},... | collective-permute-start | bytes 786440 | tf_op jit(solution)/shard_map/ppermute | solution.py:374
  24.3 1.5 %collective-permute-start.12 = (bf16[8,128,128]{2,1,0:T(8,128)(2,1)S(1)}, bf16[8,128,128]{2,1,0:T(8,128)(2,1)S(1)}, u32[]{:S(2)}, u32[]{:S(2)}) collective-permute-start(bf16[8,128,128]{2,1,0:T(8,128)(2,1)S(1)} %cross_sum.8.refs_8_), channel_id=1, source_target_pairs={{0,2},{1,3},{2,0},{3,1},{4,6},{5,7},{6,4},{7,5},{8,10},{9,11},{10,... | collective-permute-start | bytes 786440 | tf_op jit(solution)/shard_map/ppermute | solution.py:339
  25.9 1.3 %collective-permute-done.6.refs_1_.refs_4_.refs_3_ = bf16[8,128,128]{2,1,0:T(8,128)(2,1)S(1)} collective-permute-done((bf16[8,128,128]{2,1,0:T(8,128)(2,1)S(1)}, bf16[8,128,128]{2,1,0:T(8,128)(2,1)S(1)}, u32[]{:S(2)}, u32[]{:S(2)}) %collective-permute-start.6) | collective-permute-done | bytes 262176 | tf_op jit(solution)/shard_map/ppermute | solution.py:339
  27.6 1.8 %collective-permute-start.11 = (bf16[8,128,128]{2,1,0:T(8,128)(2,1)S(1)}, bf16[8,128,128]{2,1,0:T(8,128)(2,1)S(1)}, u32[]{:S(2)}, u32[]{:S(2)}) collective-permute-start(bf16[8,128,128]{2,1,0:T(8,128)(2,1)S(1)} %side_sum.14.refs_2_), channel_id=1, source_target_pairs={{0,4},{12,8},{4,0},{8,12},{1,5},{13,9},{5,1},{9,13},{2,6},{14,10},... | collective-permute-start | bytes 786440 | tf_op jit(solution)/shard_map/ppermute | solution.py:374
  30.1 0.9 %collective-permute-start.9 = (bf16[8,128,128]{2,1,0:T(8,128)(2,1)S(1)}, bf16[8,128,128]{2,1,0:T(8,128)(2,1)S(1)}, u32[]{:S(2)}, u32[]{:S(2)}) collective-permute-start(bf16[8,128,128]{2,1,0:T(8,128)(2,1)S(1)} %cross_sum.9.refs_8_), channel_id=1, source_target_pairs={{0,2},{1,3},{2,0},{3,1},{4,6},{5,7},{6,4},{7,5},{8,10},{9,11},{10,... | collective-permute-start | bytes 786440 | tf_op jit(solution)/shard_map/ppermute | solution.py:339
  31.0 2.1 %collective-permute-done.12.refs_1_.refs_4_.refs_3_ = bf16[8,128,128]{2,1,0:T(8,128)(2,1)S(1)} collective-permute-done((bf16[8,128,128]{2,1,0:T(8,128)(2,1)S(1)}, bf16[8,128,128]{2,1,0:T(8,128)(2,1)S(1)}, u32[]{:S(2)}, u32[]{:S(2)}) %collective-permute-start.12) | collective-permute-done | bytes 262176 | tf_op jit(solution)/shard_map/ppermute | solution.py:339
  33.5 2.0 %collective-permute-start.17 = (bf16[8,128,128]{2,1,0:T(8,128)(2,1)S(1)}, bf16[8,128,128]{2,1,0:T(8,128)(2,1)S(1)}, u32[]{:S(2)}, u32[]{:S(2)}) collective-permute-start(bf16[8,128,128]{2,1,0:T(8,128)(2,1)S(1)} %side_sum.15.refs_2_), channel_id=1, source_target_pairs={{0,4},{12,8},{4,0},{8,12},{1,5},{13,9},{5,1},{9,13},{2,6},{14,10},... | collective-permute-start | bytes 786440 | tf_op jit(solution)/shard_map/ppermute | solution.py:374
  36.2 1.5 %collective-permute-start.15 = (bf16[8,128,128]{2,1,0:T(8,128)(2,1)S(1)}, bf16[8,128,128]{2,1,0:T(8,128)(2,1)S(1)}, u32[]{:S(2)}, u32[]{:S(2)}) collective-permute-start(bf16[8,128,128]{2,1,0:T(8,128)(2,1)S(1)} %cross_sum.10.refs_7_), channel_id=1, source_target_pairs={{0,2},{1,3},{2,0},{3,1},{4,6},{5,7},{6,4},{7,5},{8,10},{9,11},{10,... | collective-permute-start | bytes 786440 | tf_op jit(solution)/shard_map/ppermute | solution.py:339
  37.8 1.1 %collective-permute-done.9.refs_1_.refs_3_ = bf16[8,128,128]{2,1,0:T(8,128)(2,1)S(1)} collective-permute-done((bf16[8,128,128]{2,1,0:T(8,128)(2,1)S(1)}, bf16[8,128,128]{2,1,0:T(8,128)(2,1)S(1)}, u32[]{:S(2)}, u32[]{:S(2)}) %collective-permute-start.9) | collective-permute-done | bytes 262176 | tf_op jit(solution)/shard_map/ppermute | solution.py:339
  39.2 2.0 %collective-permute-start.14 = (bf16[8,128,128]{2,1,0:T(8,128)(2,1)S(1)}, bf16[8,128,128]{2,1,0:T(8,128)(2,1)S(1)}, u32[]{:S(2)}, u32[]{:S(2)}) collective-permute-start(bf16[8,128,128]{2,1,0:T(8,128)(2,1)S(1)} %side_sum.16.refs_2_), channel_id=1, source_target_pairs={{0,4},{12,8},{4,0},{8,12},{1,5},{13,9},{5,1},{9,13},{2,6},{14,10},... | collective-permute-start | bytes 786440 | tf_op jit(solution)/shard_map/ppermute | solution.py:374
  41.9 1.6 %collective-permute-start.20 = (bf16[8,128,128]{2,1,0:T(8,128)(2,1)S(1)}, bf16[8,128,128]{2,1,0:T(8,128)(2,1)S(1)}, u32[]{:S(2)}, u32[]{:S(2)}) collective-permute-start(bf16[8,128,128]{2,1,0:T(8,128)(2,1)S(1)} %cross_sum.11.refs_7_), channel_id=1, source_target_pairs={{0,2},{1,3},{2,0},{3,1},{4,6},{5,7},{6,4},{7,5},{8,10},{9,11},{10,... | collective-permute-start | bytes 786440 | tf_op jit(solution)/shard_map/ppermute | solution.py:339
  43.4 1.6 %collective-permute-done.15.refs_1_.refs_3_ = bf16[8,128,128]{2,1,0:T(8,128)(2,1)S(1)} collective-permute-done((bf16[8,128,128]{2,1,0:T(8,128)(2,1)S(1)}, bf16[8,128,128]{2,1,0:T(8,128)(2,1)S(1)}, u32[]{:S(2)}, u32[]{:S(2)}) %collective-permute-start.15) | collective-permute-done | bytes 262176 | tf_op jit(solution)/shard_map/ppermute | solution.py:339
  45.3 1.6 %collective-permute-start.19 = (bf16[8,128,128]{2,1,0:T(8,128)(2,1)S(1)}, bf16[8,128,128]{2,1,0:T(8,128)(2,1)S(1)}, u32[]{:S(2)}, u32[]{:S(2)}) collective-permute-start(bf16[8,128,128]{2,1,0:T(8,128)(2,1)S(1)} %side_sum.17.refs_2_), channel_id=1, source_target_pairs={{0,4},{12,8},{4,0},{8,12},{1,5},{13,9},{5,1},{9,13},{2,6},{14,10},... | collective-permute-start | bytes 786440 | tf_op jit(solution)/shard_map/ppermute | solution.py:374
  47.5 0.8 %late_sum.1.refs_7_ = bf16[16,128,128]{2,1,0:T(8,128)(2,1)S(1)} custom-call(bf16[8,128,128]{2,1,0:T(8,128)(2,1)S(1)} %collective-permute-done.7.refs_7_.refs_0_.refs_4_.refs_3_.refs_5_, bf16[8,128,128]{2,1,0:T(8,128)(2,1)S(1)} %collective-permute-done.11.refs_3_.refs_1_.refs_5_.refs_4_.refs_6_, ...), custom_call_target="tpu_custom_call" | custom-call | flops 2000000000 | bytes 1 | tf_op jit(solution)/shard_map/late_sum/pallas_call | solution.py:31
  48.4 1.6 %collective-permute-start.26 = (bf16[16,128,128]{2,1,0:T(8,128)(2,1)S(1)}, bf16[16,128,128]{2,1,0:T(8,128)(2,1)S(1)}, u32[]{:S(2)}, u32[]{:S(2)}) collective-permute-start(bf16[16,128,128]{2,1,0:T(8,128)(2,1)S(1)} %late_sum.1.refs_7_), channel_id=1, source_target_pairs={{0,2},{1,3},{2,0},{3,1},{4,6},{5,7},{6,4},{7,5},{8,10},{9,11},{10,... | collective-permute-start | bytes 1572872 | tf_op jit(solution)/shard_map/ppermute | solution.py:402
  50.0 0.7 collective-permute-done.20.refs_1_.refs_3_
  51.0 2.6 %collective-permute-start.22 = (bf16[8,128,128]{2,1,0:T(8,128)(2,1)S(1)}, bf16[8,128,128]{2,1,0:T(8,128)(2,1)S(1)}, u32[]{:S(2)}, u32[]{:S(2)}) collective-permute-start(bf16[8,128,128]{2,1,0:T(8,128)(2,1)S(1)} %side_sum.18.refs_2_), channel_id=1, source_target_pairs={{0,4},{12,8},{4,0},{8,12},{1,5},{13,9},{5,1},{9,13},{2,6},{14,10},... | collective-permute-start | bytes 786440 | tf_op jit(solution)/shard_map/ppermute | solution.py:374
  54.7 2.5 %collective-permute-start.28 = (bf16[8,128,128]{2,1,0:T(8,128)(2,1)S(1)}, bf16[8,128,128]{2,1,0:T(8,128)(2,1)S(1)}, u32[]{:S(2)}, u32[]{:S(2)}) collective-permute-start(bf16[8,128,128]{2,1,0:T(8,128)(2,1)S(1)} %side_sum.19.refs_2_), channel_id=1, source_target_pairs={{0,4},{12,8},{4,0},{8,12},{1,5},{13,9},{5,1},{9,13},{2,6},{14,10},... | collective-permute-start | bytes 786440 | tf_op jit(solution)/shard_map/ppermute | solution.py:374
  57.2 2.9 %collective-permute-done.22.refs_3_.refs_6_.refs_4_ = bf16[8,128,128]{2,1,0:T(8,128)(2,1)S(1)} collective-permute-done((bf16[8,128,128]{2,1,0:T(8,128)(2,1)S(1)}, bf16[8,128,128]{2,1,0:T(8,128)(2,1)S(1)}, u32[]{:S(2)}, u32[]{:S(2)}) %collective-permute-start.22) | collective-permute-done | bytes 262176 | tf_op jit(solution)/shard_map/ppermute | solution.py:374
  60.6 2.9 %collective-permute-start.29 = (bf16[8,128,128]{2,1,0:T(8,128)(2,1)S(1)}, bf16[8,128,128]{2,1,0:T(8,128)(2,1)S(1)}, u32[]{:S(2)}, u32[]{:S(2)}) collective-permute-start(bf16[8,128,128]{2,1,0:T(8,128)(2,1)S(1)} %side_sum.20.refs_7_), channel_id=1, source_target_pairs={{0,4},{12,8},{4,0},{8,12},{1,5},{13,9},{5,1},{9,13},{2,6},{14,10},... | collective-permute-start | bytes 786440 | tf_op jit(solution)/shard_map/ppermute | solution.py:374
  64.2 5.3 %collective-permute-start.25 = (bf16[8,128,128]{2,1,0:T(8,128)(2,1)S(1)}, bf16[8,128,128]{2,1,0:T(8,128)(2,1)S(1)}, u32[]{:S(2)}, u32[]{:S(2)}) collective-permute-start(bf16[8,128,128]{2,1,0:T(8,128)(2,1)S(1)} %side_sum.21.refs_7_), channel_id=1, source_target_pairs={{0,4},{12,8},{4,0},{8,12},{1,5},{13,9},{5,1},{9,13},{2,6},{14,10},... | collective-permute-start | bytes 786440 | tf_op jit(solution)/shard_map/ppermute | solution.py:374
  69.9 0.7 attend.9
  72.9 3.0 %collective-permute-done.25.refs_6_ = bf16[8,128,128]{2,1,0:T(8,128)(2,1)S(1)} collective-permute-done((bf16[8,128,128]{2,1,0:T(8,128)(2,1)S(1)}, bf16[8,128,128]{2,1,0:T(8,128)(2,1)S(1)}, u32[]{:S(2)}, u32[]{:S(2)}) %collective-permute-start.25) | collective-permute-done | bytes 262176 | tf_op jit(solution)/shard_map/ppermute | solution.py:374
  75.8 2.0 %last_attend.1 = bf16[1,128,8192]{2,1,0:T(8,128)(2,1)} custom-call(bf16[128,2048]{1,0:T(8,128)(2,1)S(1)} %local_scores.15.refs_4_.refs_0_, bf16[128,8192]{1,0:T(8,128)(2,1)S(1)} %bitcast.14, bf16[32,128,128]{2,1,0:T(8,128)(2,1)S(1)} %collective-permute-done.2.refs_1_.refs_0_.refs_3_.refs_2_, ...), custom_call_target="tpu_custom_call" | custom-call | flops 2000000000 | bytes 1 | tf_op jit(solution)/shard_map/last_attend/pallas_call | solution.py:242
  (91 shorter events, 12.6 us)
Async XLA Ops:
  2.8 3.6 %copy-start.2 = (bf16[16,128,128]{2,1,0:T(8,128)(2,1)S(1)}, bf16[16,128,128]{2,1,0:T(8,128)(2,1)}, u32[]{:S(2)}) copy-start(bf16[16,128,128]{2,1,0:T(8,128)(2,1)} %get-tuple-element.26.refs_2_.refs_0_.refs_3_.refs_4_.refs_5_.refs_6_.refs_14_) | copy-start | bytes 1572868
  2.8 3.6 %collective-permute-start = (bf16[16,128,128]{2,1,0:T(8,128)(2,1)}, bf16[16,128,128]{2,1,0:T(8,128)(2,1)S(1)}, u32[]{:S(2)}, u32[]{:S(2)}) collective-permute-start(bf16[16,128,128]{2,1,0:T(8,128)(2,1)} %get-tuple-element.26.refs_2_.refs_0_.refs_3_.refs_4_.refs_5_.refs_6_.refs_14_), channel_id=1, source_target_pairs={{0,1},{2,3},{1,0},{3,2},{4,5},{6,7},{5,4},{7,6},{8,9},{10,11},{9,8... | collective-permute-start | bytes 1572872 | tf_op jit(solution)/shard_map/ppermute | solution.py:331
  6.2 4.5 %collective-permute-start.1 = (bf16[16,128,128]{2,1,0:T(8,128)(2,1)}, bf16[16,128,128]{2,1,0:T(8,128)(2,1)S(1)}, u32[]{:S(2)}, u32[]{:S(2)}) collective-permute-start(bf16[16,128,128]{2,1,0:T(8,128)(2,1)} %get-tuple-element.27.refs_4_.refs_0_.refs_2_.refs_5_), channel_id=1, source_target_pairs={{0,1},{2,3},{1,0},{3,2},{4,5},{6,7},{5,4},{7,6},{8,9},{10,11},{9,8... | collective-permute-start | bytes 1572872 | tf_op jit(solution)/shard_map/ppermute | solution.py:331
  7.6 10.2 %collective-permute-start.4 = (bf16[8,128,128]{2,1,0:T(8,128)(2,1)S(1)}, bf16[8,128,128]{2,1,0:T(8,128)(2,1)S(1)}, u32[]{:S(2)}, u32[]{:S(2)}) collective-permute-start(bf16[8,128,128]{2,1,0:T(8,128)(2,1)S(1)} %side_sum.11.refs_2_), channel_id=1, source_target_pairs={{0,4},{12,8},{4,0},{8,12},{1,5},{13,9},{5,1},{9,13},{2,6},{14,10},... | collective-permute-start | bytes 786440 | tf_op jit(solution)/shard_map/ppermute | solution.py:374
  10.8 9.5 %collective-permute-start.3 = (bf16[8,128,128]{2,1,0:T(8,128)(2,1)S(1)}, bf16[8,128,128]{2,1,0:T(8,128)(2,1)S(1)}, u32[]{:S(2)}, u32[]{:S(2)}) collective-permute-start(bf16[8,128,128]{2,1,0:T(8,128)(2,1)S(1)} %cross_sum.6.refs_4_), channel_id=1, source_target_pairs={{0,2},{1,3},{2,0},{3,1},{4,6},{5,7},{6,4},{7,5},{8,10},{9,11},{10,... | collective-permute-start | bytes 786440 | tf_op jit(solution)/shard_map/ppermute | solution.py:339
  12.6 11.3 %collective-permute-start.8 = (bf16[8,128,128]{2,1,0:T(8,128)(2,1)S(1)}, bf16[8,128,128]{2,1,0:T(8,128)(2,1)S(1)}, u32[]{:S(2)}, u32[]{:S(2)}) collective-permute-start(bf16[8,128,128]{2,1,0:T(8,128)(2,1)S(1)} %side_sum.12.refs_2_), channel_id=1, source_target_pairs={{0,4},{12,8},{4,0},{8,12},{1,5},{13,9},{5,1},{9,13},{2,6},{14,10},... | collective-permute-start | bytes 786440 | tf_op jit(solution)/shard_map/ppermute | solution.py:374
  15.8 8.5 %collective-permute-start.2 = (bf16[32,128,128]{2,1,0:T(8,128)(2,1)S(1)}, bf16[32,128,128]{2,1,0:T(8,128)(2,1)S(1)}, u32[]{:S(2)}, u32[]{:S(2)}) collective-permute-start(bf16[32,128,128]{2,1,0:T(8,128)(2,1)S(1)} %get-tuple-element.29.refs_2_.refs_0_.refs_5_), channel_id=1, source_target_pairs={{0,1},{2,3},{1,0},{3,2},{4,5},{6,7},{5,4},{7,6},{8,9},{10,11},{9,8... | collective-permute-start | bytes 3145736 | tf_op jit(solution)/shard_map/ppermute | solution.py:331
  18.0 9.2 %collective-permute-start.7 = (bf16[8,128,128]{2,1,0:T(8,128)(2,1)S(1)}, bf16[8,128,128]{2,1,0:T(8,128)(2,1)S(1)}, u32[]{:S(2)}, u32[]{:S(2)}) collective-permute-start(bf16[8,128,128]{2,1,0:T(8,128)(2,1)S(1)} %middle_sum.8.refs_2_), channel_id=1, source_target_pairs={{4,8},{5,9},{6,10},{7,11},{0,1},{2,3},{12,13},{14,15},{8,4},{9,5},... | collective-permute-start | bytes 786440 | tf_op jit(solution)/shard_map/ppermute | solution.py:379
  18.2 9.0 %collective-permute-start.6 = (bf16[8,128,128]{2,1,0:T(8,128)(2,1)S(1)}, bf16[8,128,128]{2,1,0:T(8,128)(2,1)S(1)}, u32[]{:S(2)}, u32[]{:S(2)}) collective-permute-start(bf16[8,128,128]{2,1,0:T(8,128)(2,1)S(1)} %cross_sum.7.refs_3_), channel_id=1, source_target_pairs={{0,2},{1,3},{2,0},{3,1},{4,6},{5,7},{6,4},{7,5},{8,10},{9,11},{10,... | collective-permute-start | bytes 786440 | tf_op jit(solution)/shard_map/ppermute | solution.py:339
  20.4 9.3 %collective-permute-start.5 = (bf16[8,128,128]{2,1,0:T(8,128)(2,1)S(1)}, bf16[8,128,128]{2,1,0:T(8,128)(2,1)S(1)}, u32[]{:S(2)}, u32[]{:S(2)}) collective-permute-start(bf16[8,128,128]{2,1,0:T(8,128)(2,1)S(1)} %side_sum.13.refs_2_), channel_id=1, source_target_pairs={{0,4},{12,8},{4,0},{8,12},{1,5},{13,9},{5,1},{9,13},{2,6},{14,10},... | collective-permute-start | bytes 786440 | tf_op jit(solution)/shard_map/ppermute | solution.py:374
  24.2 6.8 %collective-permute-start.13 = (bf16[8,128,128]{2,1,0:T(8,128)(2,1)S(1)}, bf16[8,128,128]{2,1,0:T(8,128)(2,1)S(1)}, u32[]{:S(2)}, u32[]{:S(2)}) collective-permute-start(bf16[8,128,128]{2,1,0:T(8,128)(2,1)S(1)} %middle_sum.9.refs_2_), channel_id=1, source_target_pairs={{4,8},{5,9},{6,10},{7,11},{0,1},{2,3},{12,13},{14,15},{8,4},{9,5},... | collective-permute-start | bytes 786440 | tf_op jit(solution)/shard_map/ppermute | solution.py:379
  24.3 5.1 %copy-start.7 = (bf16[128,2048]{1,0:T(8,128)(2,1)S(1)}, bf16[128,2048]{1,0:T(8,128)(2,1)}, u32[]{:S(2)}) copy-start(bf16[128,2048]{1,0:T(8,128)(2,1)} %get-tuple-element.31.refs_1_) | copy-start | bytes 1572868
  24.3 8.8 %collective-permute-start.12 = (bf16[8,128,128]{2,1,0:T(8,128)(2,1)S(1)}, bf16[8,128,128]{2,1,0:T(8,128)(2,1)S(1)}, u32[]{:S(2)}, u32[]{:S(2)}) collective-permute-start(bf16[8,128,128]{2,1,0:T(8,128)(2,1)S(1)} %cross_sum.8.refs_8_), channel_id=1, source_target_pairs={{0,2},{1,3},{2,0},{3,1},{4,6},{5,7},{6,4},{7,5},{8,10},{9,11},{10,... | collective-permute-start | bytes 786440 | tf_op jit(solution)/shard_map/ppermute | solution.py:339
  27.6 8.2 %collective-permute-start.11 = (bf16[8,128,128]{2,1,0:T(8,128)(2,1)S(1)}, bf16[8,128,128]{2,1,0:T(8,128)(2,1)S(1)}, u32[]{:S(2)}, u32[]{:S(2)}) collective-permute-start(bf16[8,128,128]{2,1,0:T(8,128)(2,1)S(1)} %side_sum.14.refs_2_), channel_id=1, source_target_pairs={{0,4},{12,8},{4,0},{8,12},{1,5},{13,9},{5,1},{9,13},{2,6},{14,10},... | collective-permute-start | bytes 786440 | tf_op jit(solution)/shard_map/ppermute | solution.py:374
  29.9 8.9 %collective-permute-start.10 = (bf16[8,128,128]{2,1,0:T(8,128)(2,1)S(1)}, bf16[8,128,128]{2,1,0:T(8,128)(2,1)S(1)}, u32[]{:S(2)}, u32[]{:S(2)}) collective-permute-start(bf16[8,128,128]{2,1,0:T(8,128)(2,1)S(1)} %middle_sum.10.refs_2_), channel_id=1, source_target_pairs={{4,8},{5,9},{6,10},{7,11},{0,1},{2,3},{12,13},{14,15},{8,4},{9,5},... | collective-permute-start | bytes 786440 | tf_op jit(solution)/shard_map/ppermute | solution.py:379
  30.1 8.8 %collective-permute-start.9 = (bf16[8,128,128]{2,1,0:T(8,128)(2,1)S(1)}, bf16[8,128,128]{2,1,0:T(8,128)(2,1)S(1)}, u32[]{:S(2)}, u32[]{:S(2)}) collective-permute-start(bf16[8,128,128]{2,1,0:T(8,128)(2,1)S(1)} %cross_sum.9.refs_8_), channel_id=1, source_target_pairs={{0,2},{1,3},{2,0},{3,1},{4,6},{5,7},{6,4},{7,5},{8,10},{9,11},{10,... | collective-permute-start | bytes 786440 | tf_op jit(solution)/shard_map/ppermute | solution.py:339
  33.5 8.0 %collective-permute-start.17 = (bf16[8,128,128]{2,1,0:T(8,128)(2,1)S(1)}, bf16[8,128,128]{2,1,0:T(8,128)(2,1)S(1)}, u32[]{:S(2)}, u32[]{:S(2)}) collective-permute-start(bf16[8,128,128]{2,1,0:T(8,128)(2,1)S(1)} %side_sum.15.refs_2_), channel_id=1, source_target_pairs={{0,4},{12,8},{4,0},{8,12},{1,5},{13,9},{5,1},{9,13},{2,6},{14,10},... | collective-permute-start | bytes 786440 | tf_op jit(solution)/shard_map/ppermute | solution.py:374
  36.1 8.9 %collective-permute-start.16 = (bf16[8,128,128]{2,1,0:T(8,128)(2,1)S(1)}, bf16[8,128,128]{2,1,0:T(8,128)(2,1)S(1)}, u32[]{:S(2)}, u32[]{:S(2)}) collective-permute-start(bf16[8,128,128]{2,1,0:T(8,128)(2,1)S(1)} %middle_sum.11.refs_2_), channel_id=1, source_target_pairs={{4,8},{5,9},{6,10},{7,11},{0,1},{2,3},{12,13},{14,15},{8,4},{9,5},... | collective-permute-start | bytes 786440 | tf_op jit(solution)/shard_map/ppermute | solution.py:379
  36.2 8.8 %collective-permute-start.15 = (bf16[8,128,128]{2,1,0:T(8,128)(2,1)S(1)}, bf16[8,128,128]{2,1,0:T(8,128)(2,1)S(1)}, u32[]{:S(2)}, u32[]{:S(2)}) collective-permute-start(bf16[8,128,128]{2,1,0:T(8,128)(2,1)S(1)} %cross_sum.10.refs_7_), channel_id=1, source_target_pairs={{0,2},{1,3},{2,0},{3,1},{4,6},{5,7},{6,4},{7,5},{8,10},{9,11},{10,... | collective-permute-start | bytes 786440 | tf_op jit(solution)/shard_map/ppermute | solution.py:339
  39.2 8.0 %collective-permute-start.14 = (bf16[8,128,128]{2,1,0:T(8,128)(2,1)S(1)}, bf16[8,128,128]{2,1,0:T(8,128)(2,1)S(1)}, u32[]{:S(2)}, u32[]{:S(2)}) collective-permute-start(bf16[8,128,128]{2,1,0:T(8,128)(2,1)S(1)} %side_sum.16.refs_2_), channel_id=1, source_target_pairs={{0,4},{12,8},{4,0},{8,12},{1,5},{13,9},{5,1},{9,13},{2,6},{14,10},... | collective-permute-start | bytes 786440 | tf_op jit(solution)/shard_map/ppermute | solution.py:374
  41.7 8.9 %collective-permute-start.21 = (bf16[8,128,128]{2,1,0:T(8,128)(2,1)S(1)}, bf16[8,128,128]{2,1,0:T(8,128)(2,1)S(1)}, u32[]{:S(2)}, u32[]{:S(2)}) collective-permute-start(bf16[8,128,128]{2,1,0:T(8,128)(2,1)S(1)} %middle_sum.12.refs_2_), channel_id=1, source_target_pairs={{4,8},{5,9},{6,10},{7,11},{0,1},{2,3},{12,13},{14,15},{8,4},{9,5},... | collective-permute-start | bytes 786440 | tf_op jit(solution)/shard_map/ppermute | solution.py:379
  41.9 8.8 %collective-permute-start.20 = (bf16[8,128,128]{2,1,0:T(8,128)(2,1)S(1)}, bf16[8,128,128]{2,1,0:T(8,128)(2,1)S(1)}, u32[]{:S(2)}, u32[]{:S(2)}) collective-permute-start(bf16[8,128,128]{2,1,0:T(8,128)(2,1)S(1)} %cross_sum.11.refs_7_), channel_id=1, source_target_pairs={{0,2},{1,3},{2,0},{3,1},{4,6},{5,7},{6,4},{7,5},{8,10},{9,11},{10,... | collective-permute-start | bytes 786440 | tf_op jit(solution)/shard_map/ppermute | solution.py:339
  45.3 8.5 %collective-permute-start.19 = (bf16[8,128,128]{2,1,0:T(8,128)(2,1)S(1)}, bf16[8,128,128]{2,1,0:T(8,128)(2,1)S(1)}, u32[]{:S(2)}, u32[]{:S(2)}) collective-permute-start(bf16[8,128,128]{2,1,0:T(8,128)(2,1)S(1)} %side_sum.17.refs_2_), channel_id=1, source_target_pairs={{0,4},{12,8},{4,0},{8,12},{1,5},{13,9},{5,1},{9,13},{2,6},{14,10},... | collective-permute-start | bytes 786440 | tf_op jit(solution)/shard_map/ppermute | solution.py:374
  47.5 6.7 %collective-permute-start.18 = (bf16[8,128,128]{2,1,0:T(8,128)(2,1)S(1)}, bf16[8,128,128]{2,1,0:T(8,128)(2,1)S(1)}, u32[]{:S(2)}, u32[]{:S(2)}) collective-permute-start(bf16[8,128,128]{2,1,0:T(8,128)(2,1)S(1)} %middle_sum.13.refs_16_), channel_id=1, source_target_pairs={{4,8},{5,9},{6,10},{7,11},{0,1},{2,3},{12,13},{14,15},{8,4},{9,5},... | collective-permute-start | bytes 786440 | tf_op jit(solution)/shard_map/ppermute | solution.py:379
  48.4 15.5 %collective-permute-start.26 = (bf16[16,128,128]{2,1,0:T(8,128)(2,1)S(1)}, bf16[16,128,128]{2,1,0:T(8,128)(2,1)S(1)}, u32[]{:S(2)}, u32[]{:S(2)}) collective-permute-start(bf16[16,128,128]{2,1,0:T(8,128)(2,1)S(1)} %late_sum.1.refs_7_), channel_id=1, source_target_pairs={{0,2},{1,3},{2,0},{3,1},{4,6},{5,7},{6,4},{7,5},{8,10},{9,11},{10,... | collective-permute-start | bytes 1572872 | tf_op jit(solution)/shard_map/ppermute | solution.py:402
  51.0 9.1 %collective-permute-start.22 = (bf16[8,128,128]{2,1,0:T(8,128)(2,1)S(1)}, bf16[8,128,128]{2,1,0:T(8,128)(2,1)S(1)}, u32[]{:S(2)}, u32[]{:S(2)}) collective-permute-start(bf16[8,128,128]{2,1,0:T(8,128)(2,1)S(1)} %side_sum.18.refs_2_), channel_id=1, source_target_pairs={{0,4},{12,8},{4,0},{8,12},{1,5},{13,9},{5,1},{9,13},{2,6},{14,10},... | collective-permute-start | bytes 786440 | tf_op jit(solution)/shard_map/ppermute | solution.py:374
  54.1 6.3 %collective-permute-start.24 = (bf16[8,128,128]{2,1,0:T(8,128)(2,1)S(1)}, bf16[8,128,128]{2,1,0:T(8,128)(2,1)S(1)}, u32[]{:S(2)}, u32[]{:S(2)}) collective-permute-start(bf16[8,128,128]{2,1,0:T(8,128)(2,1)S(1)} %middle_sum.14.refs_4_), channel_id=1, source_target_pairs={{4,8},{5,9},{6,10},{7,11},{0,1},{2,3},{12,13},{14,15},{8,4},{9,5},... | collective-permute-start | bytes 786440 | tf_op jit(solution)/shard_map/ppermute | solution.py:379
  54.7 15.9 %collective-permute-start.28 = (bf16[8,128,128]{2,1,0:T(8,128)(2,1)S(1)}, bf16[8,128,128]{2,1,0:T(8,128)(2,1)S(1)}, u32[]{:S(2)}, u32[]{:S(2)}) collective-permute-start(bf16[8,128,128]{2,1,0:T(8,128)(2,1)S(1)} %side_sum.19.refs_2_), channel_id=1, source_target_pairs={{0,4},{12,8},{4,0},{8,12},{1,5},{13,9},{5,1},{9,13},{2,6},{14,10},... | collective-permute-start | bytes 786440 | tf_op jit(solution)/shard_map/ppermute | solution.py:374
  60.3 3.7 %collective-permute-start.23 = (bf16[8,128,128]{2,1,0:T(8,128)(2,1)S(1)}, bf16[8,128,128]{2,1,0:T(8,128)(2,1)S(1)}, u32[]{:S(2)}, u32[]{:S(2)}) collective-permute-start(bf16[8,128,128]{2,1,0:T(8,128)(2,1)S(1)} %middle_sum.15.refs_4_), channel_id=1, source_target_pairs={{4,8},{5,9},{6,10},{7,11},{0,1},{2,3},{12,13},{14,15},{8,4},{9,5},... | collective-permute-start | bytes 786440 | tf_op jit(solution)/shard_map/ppermute | solution.py:379
  60.6 11.8 %collective-permute-start.29 = (bf16[8,128,128]{2,1,0:T(8,128)(2,1)S(1)}, bf16[8,128,128]{2,1,0:T(8,128)(2,1)S(1)}, u32[]{:S(2)}, u32[]{:S(2)}) collective-permute-start(bf16[8,128,128]{2,1,0:T(8,128)(2,1)S(1)} %side_sum.20.refs_7_), channel_id=1, source_target_pairs={{0,4},{12,8},{4,0},{8,12},{1,5},{13,9},{5,1},{9,13},{2,6},{14,10},... | collective-permute-start | bytes 786440 | tf_op jit(solution)/shard_map/ppermute | solution.py:374
  63.9 7.2 %collective-permute-start.27 = (bf16[16,128,128]{2,1,0:T(8,128)(2,1)S(1)}, bf16[16,128,128]{2,1,0:T(8,128)(2,1)S(1)}, u32[]{:S(2)}, u32[]{:S(2)}) collective-permute-start(bf16[16,128,128]{2,1,0:T(8,128)(2,1)S(1)} %collective-permute-done.26.refs_9_), channel_id=1, source_target_pairs={{0,1},{2,3},{1,0},{3,2},{4,5},{6,7},{5,4},{7,6},{8,9},{10,11},{9,8... | collective-permute-start | bytes 1572872 | tf_op jit(solution)/shard_map/ppermute | solution.py:407
  64.2 11.6 %collective-permute-start.25 = (bf16[8,128,128]{2,1,0:T(8,128)(2,1)S(1)}, bf16[8,128,128]{2,1,0:T(8,128)(2,1)S(1)}, u32[]{:S(2)}, u32[]{:S(2)}) collective-permute-start(bf16[8,128,128]{2,1,0:T(8,128)(2,1)S(1)} %side_sum.21.refs_7_), channel_id=1, source_target_pairs={{0,4},{12,8},{4,0},{8,12},{1,5},{13,9},{5,1},{9,13},{2,6},{14,10},... | collective-permute-start | bytes 786440 | tf_op jit(solution)/shard_map/ppermute | solution.py:374
  (7 other events, 17.6 us)

commit v5 on v4

--- a/solution.py
+++ b/solution.py
@@ -11,7 +11,7 @@
 F32 = jnp.float32
 BF16 = jnp.bfloat16
 VMEM_LIMIT = 8 << 20
-PART = 4
+EARLY = 10**6
 COST = 2 * 10**9
 VMEM = pl.BlockSpec(memory_space=pltpu.VMEM)
 ANY = pl.BlockSpec(memory_space=pl.ANY)
@@ -22,7 +22,7 @@
     return (x * (0.5 * jnp.tanh(0.5 * x) + 0.5)).astype(BF16)
 
 
-def call(kernel, name, operands, outs, after):
+def call(kernel, name, operands, outs, after, cost=COST):
     n_in, n_after = len(operands), len(after)
 
     def run(*refs):
@@ -34,7 +34,7 @@
         out_specs=[VMEM] * len(outs),
         out_shape=outs,
         compiler_params=pltpu.CompilerParams(vmem_limit_bytes=VMEM_LIMIT),
-        cost_estimate=pl.CostEstimate(flops=COST, bytes_accessed=1, transcendentals=0),
+        cost_estimate=pl.CostEstimate(flops=cost, bytes_accessed=1, transcendentals=0),
         name=name,
     )(*operands, *after)
 
@@ -71,7 +71,7 @@
     return out
 
 
-def combine(name, count, chunks, after):
+def combine(name, count, chunks, after, cost=COST):
     starts = [sum(len(c) for c in chunks[:i]) for i in range(len(chunks))]
 
     def kernel(ins, outs):
@@ -81,7 +81,7 @@
                 outs[0][i * count + h] = term_sum(ins[starts[i] :], terms, held, h).astype(BF16)
 
     arrays = [t[0] for terms in chunks for t in terms]
-    return call(kernel, name, arrays, [states_of(count * len(chunks), DH)], after)[0]
+    return call(kernel, name, arrays, [states_of(count * len(chunks), DH)], after, cost)[0]
 
 
 class Held:
@@ -97,47 +97,20 @@
         return self.known[wanted]
 
 
-def kv_states(k_rows, v_rows, first, count, after, limit=VMEM_LIMIT):
+def kv_states(k_rows, v_rows, first, count, after):
     rows = k_rows.shape[0]
-    n_after = len(after)
-
-    def run(*refs):
-        k_hbm, v_hbm = refs[:2]
-        outs = refs[2 + n_after : -3]
-        k_ref, v_ref, sem = refs[-3:]
-        parts = count // PART
-        copies = []
-        for i in range(parts):
-            cols = pl.ds((first + i * PART) * DH, PART * DH)
-            to = pl.ds(i * PART * DH, PART * DH)
-            for j, (hbm_ref, ref) in enumerate(((k_hbm, k_ref), (v_hbm, v_ref))):
-                copy = pltpu.make_async_copy(hbm_ref.at[:, cols], ref.at[:, to], sem.at[2 * i + j])
-                copy.start()
-                copies.append(copy)
+
+    def kernel(ins, outs):
         for h in range(count):
-            if h % PART == 0:
-                copies[2 * (h // PART)].wait()
-                copies[2 * (h // PART) + 1].wait()
-            ka = silu(k_ref[:, head_cols(h)])
+            cols = head_cols(first + h)
+            ka = silu(ins[0][:, cols])
             outs[1][:, head_cols(h)] = ka
             outs[0][h] = lax.dot_general(
-                ka, v_ref[:, head_cols(h)], (((0,), (0,)), ((), ())),
-                preferred_element_type=F32,
+                ka, ins[1][:, cols], (((0,), (0,)), ((), ())), preferred_element_type=F32
             ).astype(BF16)
 
     outs = [states_of(count, DH), jax.ShapeDtypeStruct((rows, count * DH), BF16)]
-    hbm = pl.BlockSpec(memory_space=pltpu.HBM)
-    block = pltpu.VMEM((rows, count * DH), BF16)
-    return pl.pallas_call(
-        run,
-        in_specs=[hbm, hbm] + [ANY] * n_after,
-        out_specs=[VMEM] * len(outs),
-        out_shape=outs,
-        scratch_shapes=[block, block, pltpu.SemaphoreType.DMA((2 * (count // PART),))],
-        compiler_params=pltpu.CompilerParams(vmem_limit_bytes=limit),
-        cost_estimate=pl.CostEstimate(flops=10**6, bytes_accessed=1, transcendentals=0),
-        name="kv_states",
-    )(k_rows, v_rows, *after)
+    return call(kernel, "kv_states", [k_rows, v_rows], outs, after, EARLY)
 
 
 def local_scores(q_rows, ka, ka_first, first, count, after):
@@ -319,6 +292,7 @@
     def __init__(self, n, size):
         self.n, self.size = n, size
         self.own, self.other, self.x, self.a, self.b = {}, {}, {}, {}, {}
+        self.late, self.late_other = {}, {}
         self.couples = both_ways([(0, 1), (2, 3)])
         self.across = both_ways([(0, 2), (1, 3)])
         at = lambda z, c: 4 * z + c
@@ -335,7 +309,7 @@
 
     def cross(self, c, after):
         terms = [(*self.own[c], ()), (*self.other[c], ())]
-        send = combine("cross_sum", self.size, [terms], after)
+        send = combine("cross_sum", self.size, [terms], after, EARLY if c == LATE else COST)
         self.x[c] = (lax.ppermute(send, "ctx", self.across), 0)
         return [send]
 
@@ -370,7 +344,7 @@
             terms += also(self.mine(t), *(("outer",) if outwards else ()))
         if outwards:
             terms += also([*self.mirror(c), (*self.b[c], ())], *(("inner",) if inwards else ()))
-        send = combine("side_sum", self.size, [terms], after)
+        send = combine("side_sum", self.size, [terms], after, EARLY if t == 1 else COST)
         self.a[t] = (lax.ppermute(send, "head", both_ways([(0, 1), (3, 2)])), 0)
         return [send]
 
@@ -393,27 +367,25 @@
             (*self.a[c], ("right", "inner")),
         ]
 
-    def late_cross(self, after):
-        chunks = []
-        for c in range(LATE):
-            whole = [*self.lower(c), (*self.own[c], ()), (*self.other[c], ())]
-            chunks.append([*also(self.higher(c), "even"), *also(whole, "odd")])
-        send = combine("late_sum", self.size, chunks, after)
-        self.late = lax.ppermute(send, "ctx", self.across)
+    def late_cross(self, c, after):
+        whole = [*self.lower(c), (*self.own[c], ()), (*self.other[c], ())]
+        terms = [*also(self.higher(c), "even"), *also(whole, "odd")]
+        send = combine("late_sum", self.size, [terms], after)
+        self.late[c] = lax.ppermute(send, "ctx", self.across)
         return [send]
 
-    def late_swap(self, after):
-        self.late = lax.optimization_barrier((self.late, *after))[0]
-        self.late_other = lax.ppermute(self.late, "ctx", self.couples)
+    def late_swap(self, c, after):
+        self.late[c] = lax.optimization_barrier((self.late[c], *after))[0]
+        self.late_other[c] = lax.ppermute(self.late[c], "ctx", self.couples)
+        return [self.late[c]]
 
     def state(self, c):
         if c < LATE:
-            at = c * self.size
             return [
                 *self.lower(c),
                 *also([*self.higher(c), (*self.other[c], ())], "odd"),
-                (self.late, at, ("later",)),
-                (self.late_other, at, ("later",)),
+                (self.late[c], 0, ("later",)),
+                (self.late_other[c], 0, ("later",)),
             ]
         return [
             *self.early(c),
@@ -440,8 +412,13 @@
     both, attns, squares, ka = {}, {}, {}, {}
     scan = Scan(n, size)
 
-    def kv(first, count, after, limit=VMEM_LIMIT):
-        own, active = kv_states(k_rows, v_rows, first * size, count * size, after, limit)
+    def kv(first, count, after, cut=False):
+        at = first * size
+        k, v = k_rows, v_rows
+        if cut:
+            cols = slice(at * DH, (at + count * size) * DH)
+            k, v, at = k[:, cols], v[:, cols], 0
+        own, active = kv_states(k, v, at, count * size, after)
         scan.begin(first, own)
         for i in range(count):
             ka[first + i] = (active, i * size)
@@ -458,26 +435,32 @@
     fill = {
         1: [0], 2: [1], 3: [2], 4: [3], 5: [4], 6: [5], 7: [6], 8: [7],
     }
-    clock = kv(0, 2, [], 61 * 10**6)
-    clock = kv(2, 2, clock, 60 * 10**6)
+    clock = kv(0, 1, [], cut=True)
+    clock = kv(1, 1, clock, cut=True)
+    clock = kv(2, 1, clock, cut=True)
     for t in range(n + SKEW):
         clock = scan.side(t, clock)
         if t == 1:
+            clock = scan.cross(2, clock)
+            clock = kv(3, 1, clock)
             clock = kv(4, 4, clock)
+        if t == n + 1:
+            clock = scan.late_swap(1, clock)
         for c in fill.get(t, []):
             clock = scores(c, clock)
         if t > n:
             clock = attention(t - n - 1 + LATE, clock)
         if 0 <= t - 1 < n:
             clock = scan.middle(t - 1, clock)
-        if t + 2 < n:
+        if LATE < t + 2 < n:
             clock = scan.cross(t + 2, clock)
-        if t + 2 == n:
-            clock = scan.late_cross(clock)
-        if t == n + 1:
-            scan.late_swap(clock)
-    for c in [*range(LATE + 2, n - 2), *range(LATE), n - 2]:
-        clock = attention(c, clock)
+        if 0 <= t + 2 - n < LATE:
+            clock = scan.late_cross(t + 2 - n, clock)
+        if t == n:
+            clock = scan.late_swap(0, clock)
+    for c in [*range(LATE, n - 1), *range(LATE)]:
+        if c not in attns:
+            clock = attention(c, clock)
     return last_attend(
         both[n - 1], v_rows, (n - 1) * size, scan.state(n - 1),
         [attns[c] for c in range(n - 1)], [squares[c] for c in range(n - 1)], gain,

time: 78.3 us -> 74.4 us (0.950)
  Pallas kernels: 22.5 us -> 16.4 us
  starting transfers between devices: 39.4 us -> 41.5 us
    pallas_call x3 -> x0, Pallas kernels: 8.32 us -> none  [kv_states(): pl.pallas_call(run, in_specs=[hbm, hbm] + [ANY] * n_after, out_specs=[VME...]
    pallas_call x41 -> x47, Pallas kernels: 12.1 us -> 14.3 us  [call(): pl.pallas_call(run, in_specs=[VMEM] * n_in + [ANY] * n_after, out_specs=[...]
    ppermute x2 -> x4, starting transfers between devices: 1.64 us -> 3.48 us  [the longest x2 2.77 us: late_cross(): self.late[c] = lax.ppermute(send, 'ctx', self.across)]
    slice x0 -> x1, local copies, waits for them, and re-layouts: none -> 1.47 us  [kv(): k, v, at = (k[:, cols], v[:, cols], 0)]
    ppermute x11, starting transfers between devices: 27.3 us -> 26.1 us  [side(): self.a[t] = (lax.ppermute(send, 'head', both_ways([(0, 1), (3, 2)])), 0)]
    unnamed x18 -> x8, local copies, waits for them, and re-layouts: 1.09 us -> 0.03 us
    ppermute x3 -> x5, starting transfers between devices: 0.75 us -> 1.79 us  [begin(): other = lax.ppermute(own, 'ctx', self.couples)]
  transfers between devices with their start and end apart: 30 -> 34, of which waited for: 8 -> 10; matrix products, arithmetic and copies ran while one was open for 0% -> 0% of each run, Pallas kernels for 23% -> 19%
where the time goes in v5:
time: 74.4 us; the launch traced here: 74.2 us
  starting transfers between devices  41.5 us (56%)
  Pallas kernels  16.4 us (22%)
  waiting for transfers between devices  14.1 us (19%)
  local copies, waits for them, and re-layouts  1.51 us (2%)
    ppermute x11, starting transfers between devices, side(): self.a[t] = (lax.ppermute(send, 'head', both_ways([(0, 1), (3, 2)])), 0)  26.1 us
    pallas_call x47, Pallas kernels, call(): pl.pallas_call(run, in_specs=[VMEM] * n_in + [ANY] * n_after, out_specs=[...  14.3 us
    ppermute x6, starting transfers between devices, cross(): self.x[c] = (lax.ppermute(send, 'ctx', self.across), 0)  9.59 us
    ppermute x6, waiting for transfers between devices, cross(): self.x[c] = (lax.ppermute(send, 'ctx', self.across), 0)  7.06 us
    ppermute x11, waiting for transfers between devices, side(): self.a[t] = (lax.ppermute(send, 'head', both_ways([(0, 1), (3, 2)])), 0)  7.01 us
    ppermute x2, starting transfers between devices, late_cross(): self.late[c] = lax.ppermute(send, 'ctx', self.across)  2.77 us
    pallas_call x1, Pallas kernels, last_attend(): pl.pallas_call(kernel, in_specs=[VMEM] * len(operands), out_specs=pl.Bloc...  2.04 us
    ppermute x5, starting transfers between devices, begin(): other = lax.ppermute(own, 'ctx', self.couples)  1.79 us
  transfers between devices with their start and end apart: 34, of which 10 were waited for; matrix products, arithmetic and copies ran while one was open for 0% of the time, Pallas kernels for 19%

profile of v5, /device:TPU:0, one launch (start us, length us, event | category | flops | bytes accessed | tf_op | source)
XLA Modules:
  0.0 74.2 jit_solution(10558056140195912866)
XLA Ops:
  0.0 1.5 %fusion = (bf16[128,1024]{1,0:T(8,128)(2,1)S(1)}, bf16[128,1024]{1,0:T(8,128)(2,1)S(1)}, bf16[128,1024]{1,0:T(8,128)(2,1)S(1)}, bf16[128,1024]{1,0:T(8,128)(2,1)...) fusion(bf16[128,8192]{1,0:T(8,128)(2,1)} %bitcast.4, bf16[128,8192]{1,0:T(8,128)(2,1)} %bitcast.15), kind=kLoop, calls=%fused_computation | loop fusion | bytes 3145728 | tf_op jit(solution)/shard_map/slice | solution.py:420
  3.9 2.9 %collective-permute-start.6 = (bf16[8,128,128]{2,1,0:T(8,128)(2,1)S(1)}, bf16[8,128,128]{2,1,0:T(8,128)(2,1)S(1)}, u32[]{:S(2)}, u32[]{:S(2)}) collective-permute-start(bf16[8,128,128]{2,1,0:T(8,128)(2,1)S(1)} %side_sum.11.refs_4_), channel_id=1, source_target_pairs={{0,4},{12,8},{4,0},{8,12},{1,5},{13,9},{5,1},{9,13},{2,6},{14,10},... | collective-permute-start | bytes 786440 | tf_op jit(solution)/shard_map/ppermute | solution.py:348
  7.3 1.7 %collective-permute-start.4 = (bf16[8,128,128]{2,1,0:T(8,128)(2,1)S(1)}, bf16[8,128,128]{2,1,0:T(8,128)(2,1)S(1)}, u32[]{:S(2)}, u32[]{:S(2)}) collective-permute-start(bf16[8,128,128]{2,1,0:T(8,128)(2,1)S(1)} %cross_sum.6.refs_2_), channel_id=1, source_target_pairs={{0,2},{1,3},{2,0},{3,1},{4,6},{5,7},{6,4},{7,5},{8,10},{9,11},{10,... | collective-permute-start | bytes 786440 | tf_op jit(solution)/shard_map/ppermute | solution.py:313
  9.5 0.9 %kv_states.9 = (bf16[32,128,128]{2,1,0:T(8,128)(2,1)S(1)}, bf16[128,4096]{1,0:T(8,128)(2,1)S(1)}) custom-call(bf16[128,8192]{1,0:T(8,128)(2,1)S(1)} %bitcast.17, bf16[128,8192]{1,0:T(8,128)(2,1)S(1)} %bitcast.6, bf16[8,128,128]{2,1,0:T(8,128)(2,1)S(1)} %get-tuple-element.34.refs_2_.refs_0_.refs_5_), custom_call_target="tpu_custom_call" | custom-call | flops 1000000 | bytes 1 | tf_op jit(solution)/shard_map/kv_states/pallas_call | solution.py:31
  10.5 0.6 collective-permute-start.3
  11.3 2.5 %collective-permute-done.6.refs_4_.refs_2_.refs_3_.refs_7_ = bf16[8,128,128]{2,1,0:T(8,128)(2,1)S(1)} collective-permute-done((bf16[8,128,128]{2,1,0:T(8,128)(2,1)S(1)}, bf16[8,128,128]{2,1,0:T(8,128)(2,1)S(1)}, u32[]{:S(2)}, u32[]{:S(2)}) %collective-permute-start.6) | collective-permute-done | bytes 262176 | tf_op jit(solution)/shard_map/ppermute | solution.py:348
  14.2 2.0 %collective-permute-start.8 = (bf16[8,128,128]{2,1,0:T(8,128)(2,1)S(1)}, bf16[8,128,128]{2,1,0:T(8,128)(2,1)S(1)}, u32[]{:S(2)}, u32[]{:S(2)}) collective-permute-start(bf16[8,128,128]{2,1,0:T(8,128)(2,1)S(1)} %cross_sum.7.refs_3_), channel_id=1, source_target_pairs={{0,2},{1,3},{2,0},{3,1},{4,6},{5,7},{6,4},{7,5},{8,10},{9,11},{10,... | collective-permute-start | bytes 786440 | tf_op jit(solution)/shard_map/ppermute | solution.py:313
  16.4 3.2 %collective-permute-start.7 = (bf16[8,128,128]{2,1,0:T(8,128)(2,1)S(1)}, bf16[8,128,128]{2,1,0:T(8,128)(2,1)S(1)}, u32[]{:S(2)}, u32[]{:S(2)}) collective-permute-start(bf16[8,128,128]{2,1,0:T(8,128)(2,1)S(1)} %side_sum.13.refs_2_), channel_id=1, source_target_pairs={{0,4},{12,8},{4,0},{8,12},{1,5},{13,9},{5,1},{9,13},{2,6},{14,10},... | collective-permute-start | bytes 786440 | tf_op jit(solution)/shard_map/ppermute | solution.py:348
  20.3 1.5 %collective-permute-start.14 = (bf16[8,128,128]{2,1,0:T(8,128)(2,1)S(1)}, bf16[8,128,128]{2,1,0:T(8,128)(2,1)S(1)}, u32[]{:S(2)}, u32[]{:S(2)}) collective-permute-start(bf16[8,128,128]{2,1,0:T(8,128)(2,1)S(1)} %cross_sum.8.refs_8_), channel_id=1, source_target_pairs={{0,2},{1,3},{2,0},{3,1},{4,6},{5,7},{6,4},{7,5},{8,10},{9,11},{10,... | collective-permute-start | bytes 786440 | tf_op jit(solution)/shard_map/ppermute | solution.py:313
  21.9 1.3 %collective-permute-done.8.refs_1_.refs_4_.refs_3_ = bf16[8,128,128]{2,1,0:T(8,128)(2,1)S(1)} collective-permute-done((bf16[8,128,128]{2,1,0:T(8,128)(2,1)S(1)}, bf16[8,128,128]{2,1,0:T(8,128)(2,1)S(1)}, u32[]{:S(2)}, u32[]{:S(2)}) %collective-permute-start.8) | collective-permute-done | bytes 262176 | tf_op jit(solution)/shard_map/ppermute | solution.py:313
  23.6 1.9 %collective-permute-start.13 = (bf16[8,128,128]{2,1,0:T(8,128)(2,1)S(1)}, bf16[8,128,128]{2,1,0:T(8,128)(2,1)S(1)}, u32[]{:S(2)}, u32[]{:S(2)}) collective-permute-start(bf16[8,128,128]{2,1,0:T(8,128)(2,1)S(1)} %side_sum.14.refs_2_), channel_id=1, source_target_pairs={{0,4},{12,8},{4,0},{8,12},{1,5},{13,9},{5,1},{9,13},{2,6},{14,10},... | collective-permute-start | bytes 786440 | tf_op jit(solution)/shard_map/ppermute | solution.py:348
  26.2 1.2 %collective-permute-start.11 = (bf16[8,128,128]{2,1,0:T(8,128)(2,1)S(1)}, bf16[8,128,128]{2,1,0:T(8,128)(2,1)S(1)}, u32[]{:S(2)}, u32[]{:S(2)}) collective-permute-start(bf16[8,128,128]{2,1,0:T(8,128)(2,1)S(1)} %cross_sum.9.refs_8_), channel_id=1, source_target_pairs={{0,2},{1,3},{2,0},{3,1},{4,6},{5,7},{6,4},{7,5},{8,10},{9,11},{10,... | collective-permute-start | bytes 786440 | tf_op jit(solution)/shard_map/ppermute | solution.py:313
  27.4 1.7 %collective-permute-done.14.refs_1_.refs_4_.refs_3_ = bf16[8,128,128]{2,1,0:T(8,128)(2,1)S(1)} collective-permute-done((bf16[8,128,128]{2,1,0:T(8,128)(2,1)S(1)}, bf16[8,128,128]{2,1,0:T(8,128)(2,1)S(1)}, u32[]{:S(2)}, u32[]{:S(2)}) %collective-permute-start.14) | collective-permute-done | bytes 262176 | tf_op jit(solution)/shard_map/ppermute | solution.py:313
  29.5 1.9 %collective-permute-start.19 = (bf16[8,128,128]{2,1,0:T(8,128)(2,1)S(1)}, bf16[8,128,128]{2,1,0:T(8,128)(2,1)S(1)}, u32[]{:S(2)}, u32[]{:S(2)}) collective-permute-start(bf16[8,128,128]{2,1,0:T(8,128)(2,1)S(1)} %side_sum.15.refs_2_), channel_id=1, source_target_pairs={{0,4},{12,8},{4,0},{8,12},{1,5},{13,9},{5,1},{9,13},{2,6},{14,10},... | collective-permute-start | bytes 786440 | tf_op jit(solution)/shard_map/ppermute | solution.py:348
  32.1 1.7 %collective-permute-start.17 = (bf16[8,128,128]{2,1,0:T(8,128)(2,1)S(1)}, bf16[8,128,128]{2,1,0:T(8,128)(2,1)S(1)}, u32[]{:S(2)}, u32[]{:S(2)}) collective-permute-start(bf16[8,128,128]{2,1,0:T(8,128)(2,1)S(1)} %cross_sum.10.refs_7_), channel_id=1, source_target_pairs={{0,2},{1,3},{2,0},{3,1},{4,6},{5,7},{6,4},{7,5},{8,10},{9,11},{10,... | collective-permute-start | bytes 786440 | tf_op jit(solution)/shard_map/ppermute | solution.py:313
  33.8 1.2 %collective-permute-done.11.refs_1_.refs_3_ = bf16[8,128,128]{2,1,0:T(8,128)(2,1)S(1)} collective-permute-done((bf16[8,128,128]{2,1,0:T(8,128)(2,1)S(1)}, bf16[8,128,128]{2,1,0:T(8,128)(2,1)S(1)}, u32[]{:S(2)}, u32[]{:S(2)}) %collective-permute-start.11) | collective-permute-done | bytes 262176 | tf_op jit(solution)/shard_map/ppermute | solution.py:313
  35.3 2.0 %collective-permute-start.16 = (bf16[8,128,128]{2,1,0:T(8,128)(2,1)S(1)}, bf16[8,128,128]{2,1,0:T(8,128)(2,1)S(1)}, u32[]{:S(2)}, u32[]{:S(2)}) collective-permute-start(bf16[8,128,128]{2,1,0:T(8,128)(2,1)S(1)} %side_sum.16.refs_2_), channel_id=1, source_target_pairs={{0,4},{12,8},{4,0},{8,12},{1,5},{13,9},{5,1},{9,13},{2,6},{14,10},... | collective-permute-start | bytes 786440 | tf_op jit(solution)/shard_map/ppermute | solution.py:348
  38.0 1.4 %collective-permute-start.22 = (bf16[8,128,128]{2,1,0:T(8,128)(2,1)S(1)}, bf16[8,128,128]{2,1,0:T(8,128)(2,1)S(1)}, u32[]{:S(2)}, u32[]{:S(2)}) collective-permute-start(bf16[8,128,128]{2,1,0:T(8,128)(2,1)S(1)} %cross_sum.11.refs_7_), channel_id=1, source_target_pairs={{0,2},{1,3},{2,0},{3,1},{4,6},{5,7},{6,4},{7,5},{8,10},{9,11},{10,... | collective-permute-start | bytes 786440 | tf_op jit(solution)/shard_map/ppermute | solution.py:313
  39.4 1.5 %collective-permute-done.17.refs_1_.refs_3_ = bf16[8,128,128]{2,1,0:T(8,128)(2,1)S(1)} collective-permute-done((bf16[8,128,128]{2,1,0:T(8,128)(2,1)S(1)}, bf16[8,128,128]{2,1,0:T(8,128)(2,1)S(1)}, u32[]{:S(2)}, u32[]{:S(2)}) %collective-permute-start.17) | collective-permute-done | bytes 262176 | tf_op jit(solution)/shard_map/ppermute | solution.py:313
  41.3 1.8 %collective-permute-start.21 = (bf16[8,128,128]{2,1,0:T(8,128)(2,1)S(1)}, bf16[8,128,128]{2,1,0:T(8,128)(2,1)S(1)}, u32[]{:S(2)}, u32[]{:S(2)}) collective-permute-start(bf16[8,128,128]{2,1,0:T(8,128)(2,1)S(1)} %side_sum.17.refs_2_), channel_id=1, source_target_pairs={{0,4},{12,8},{4,0},{8,12},{1,5},{13,9},{5,1},{9,13},{2,6},{14,10},... | collective-permute-start | bytes 786440 | tf_op jit(solution)/shard_map/ppermute | solution.py:348
  44.0 1.4 %collective-permute-start.28 = (bf16[8,128,128]{2,1,0:T(8,128)(2,1)S(1)}, bf16[8,128,128]{2,1,0:T(8,128)(2,1)S(1)}, u32[]{:S(2)}, u32[]{:S(2)}) collective-permute-start(bf16[8,128,128]{2,1,0:T(8,128)(2,1)S(1)} %late_sum.2.refs_7_), channel_id=1, source_target_pairs={{0,2},{1,3},{2,0},{3,1},{4,6},{5,7},{6,4},{7,5},{8,10},{9,11},{10,... | collective-permute-start | bytes 786440 | tf_op jit(solution)/shard_map/ppermute | solution.py:374
  45.4 1.4 %collective-permute-done.22.refs_1_.refs_3_ = bf16[8,128,128]{2,1,0:T(8,128)(2,1)S(1)} collective-permute-done((bf16[8,128,128]{2,1,0:T(8,128)(2,1)S(1)}, bf16[8,128,128]{2,1,0:T(8,128)(2,1)S(1)}, u32[]{:S(2)}, u32[]{:S(2)}) %collective-permute-start.22) | collective-permute-done | bytes 262176 | tf_op jit(solution)/shard_map/ppermute | solution.py:313
  47.2 2.0 %collective-permute-start.24 = (bf16[8,128,128]{2,1,0:T(8,128)(2,1)S(1)}, bf16[8,128,128]{2,1,0:T(8,128)(2,1)S(1)}, u32[]{:S(2)}, u32[]{:S(2)}) collective-permute-start(bf16[8,128,128]{2,1,0:T(8,128)(2,1)S(1)} %side_sum.18.refs_2_), channel_id=1, source_target_pairs={{0,4},{12,8},{4,0},{8,12},{1,5},{13,9},{5,1},{9,13},{2,6},{14,10},... | collective-permute-start | bytes 786440 | tf_op jit(solution)/shard_map/ppermute | solution.py:348
  50.2 1.4 %collective-permute-start.26 = (bf16[8,128,128]{2,1,0:T(8,128)(2,1)S(1)}, bf16[8,128,128]{2,1,0:T(8,128)(2,1)S(1)}, u32[]{:S(2)}, u32[]{:S(2)}) collective-permute-start(bf16[8,128,128]{2,1,0:T(8,128)(2,1)S(1)} %late_sum.3.refs_4_), channel_id=1, source_target_pairs={{0,2},{1,3},{2,0},{3,1},{4,6},{5,7},{6,4},{7,5},{8,10},{9,11},{10,... | collective-permute-start | bytes 786440 | tf_op jit(solution)/shard_map/ppermute | solution.py:374
  52.1 3.0 %collective-permute-start.32 = (bf16[8,128,128]{2,1,0:T(8,128)(2,1)S(1)}, bf16[8,128,128]{2,1,0:T(8,128)(2,1)S(1)}, u32[]{:S(2)}, u32[]{:S(2)}) collective-permute-start(bf16[8,128,128]{2,1,0:T(8,128)(2,1)S(1)} %side_sum.19.refs_2_), channel_id=1, source_target_pairs={{0,4},{12,8},{4,0},{8,12},{1,5},{13,9},{5,1},{9,13},{2,6},{14,10},... | collective-permute-start | bytes 786440 | tf_op jit(solution)/shard_map/ppermute | solution.py:348
  56.4 2.6 %collective-permute-start.31 = (bf16[8,128,128]{2,1,0:T(8,128)(2,1)S(1)}, bf16[8,128,128]{2,1,0:T(8,128)(2,1)S(1)}, u32[]{:S(2)}, u32[]{:S(2)}) collective-permute-start(bf16[8,128,128]{2,1,0:T(8,128)(2,1)S(1)} %side_sum.20), channel_id=1, source_target_pairs={{0,4},{12,8},{4,0},{8,12},{1,5},{13,9},{5,1},{9,13},{2,6},{14,10},... | collective-permute-start | bytes 786440 | tf_op jit(solution)/shard_map/ppermute | solution.py:348
  59.9 4.6 %collective-permute-start.29 = (bf16[8,128,128]{2,1,0:T(8,128)(2,1)S(1)}, bf16[8,128,128]{2,1,0:T(8,128)(2,1)S(1)}, u32[]{:S(2)}, u32[]{:S(2)}) collective-permute-start(bf16[8,128,128]{2,1,0:T(8,128)(2,1)S(1)} %side_sum.21.refs_7_), channel_id=1, source_target_pairs={{0,4},{12,8},{4,0},{8,12},{1,5},{13,9},{5,1},{9,13},{2,6},{14,10},... | collective-permute-start | bytes 786440 | tf_op jit(solution)/shard_map/ppermute | solution.py:348
  65.9 0.8 %collective-permute-done.31.refs_6_ = bf16[8,128,128]{2,1,0:T(8,128)(2,1)S(1)} collective-permute-done((bf16[8,128,128]{2,1,0:T(8,128)(2,1)S(1)}, bf16[8,128,128]{2,1,0:T(8,128)(2,1)S(1)}, u32[]{:S(2)}, u32[]{:S(2)}) %collective-permute-start.31) | collective-permute-done | bytes 262176 | tf_op jit(solution)/shard_map/ppermute | solution.py:348
  67.2 0.7 attend.12
  67.9 0.7 attend.13
  68.5 3.5 %collective-permute-done.29.refs_6_ = bf16[8,128,128]{2,1,0:T(8,128)(2,1)S(1)} collective-permute-done((bf16[8,128,128]{2,1,0:T(8,128)(2,1)S(1)}, bf16[8,128,128]{2,1,0:T(8,128)(2,1)S(1)}, u32[]{:S(2)}, u32[]{:S(2)}) %collective-permute-start.29) | collective-permute-done | bytes 262176 | tf_op jit(solution)/shard_map/ppermute | solution.py:348
  72.0 2.0 %last_attend.1 = bf16[1,128,8192]{2,1,0:T(8,128)(2,1)} custom-call(bf16[128,2048]{1,0:T(8,128)(2,1)S(1)} %local_scores.15.refs_4_.refs_0_, bf16[128,8192]{1,0:T(8,128)(2,1)S(1)} %bitcast.14, bf16[32,128,128]{2,1,0:T(8,128)(2,1)S(1)} %collective-permute-done.3.refs_1_.refs_0_.refs_3_.refs_2_, ...), custom_call_target="tpu_custom_call" | custom-call | flops 2000000000 | bytes 1 | tf_op jit(solution)/shard_map/last_attend/pallas_call | solution.py:215
  (93 shorter events, 15.2 us)
Async XLA Ops:
  3.1 4.1 %collective-permute-start = (bf16[8,128,128]{2,1,0:T(8,128)(2,1)S(1)}, bf16[8,128,128]{2,1,0:T(8,128)(2,1)S(1)}, u32[]{:S(2)}, u32[]{:S(2)}) collective-permute-start(bf16[8,128,128]{2,1,0:T(8,128)(2,1)S(1)} %get-tuple-element.33.refs_4_.refs_0_.refs_2_.refs_5_), channel_id=1, source_target_pairs={{0,1},{2,3},{1,0},{3,2},{4,5},{6,7},{5,4},{7,6},{8,9},{10,11},{9,8... | collective-permute-start | bytes 786440 | tf_op jit(solution)/shard_map/ppermute | solution.py:305
  3.9 9.9 %collective-permute-start.6 = (bf16[8,128,128]{2,1,0:T(8,128)(2,1)S(1)}, bf16[8,128,128]{2,1,0:T(8,128)(2,1)S(1)}, u32[]{:S(2)}, u32[]{:S(2)}) collective-permute-start(bf16[8,128,128]{2,1,0:T(8,128)(2,1)S(1)} %side_sum.11.refs_4_), channel_id=1, source_target_pairs={{0,4},{12,8},{4,0},{8,12},{1,5},{13,9},{5,1},{9,13},{2,6},{14,10},... | collective-permute-start | bytes 786440 | tf_op jit(solution)/shard_map/ppermute | solution.py:348
  7.0 13.0 %collective-permute-start.10 = (bf16[8,128,128]{2,1,0:T(8,128)(2,1)S(1)}, bf16[8,128,128]{2,1,0:T(8,128)(2,1)S(1)}, u32[]{:S(2)}, u32[]{:S(2)}) collective-permute-start(bf16[8,128,128]{2,1,0:T(8,128)(2,1)S(1)} %side_sum.12.refs_2_), channel_id=1, source_target_pairs={{0,4},{12,8},{4,0},{8,12},{1,5},{13,9},{5,1},{9,13},{2,6},{14,10},... | collective-permute-start | bytes 786440 | tf_op jit(solution)/shard_map/ppermute | solution.py:348
  7.3 8.9 %collective-permute-start.4 = (bf16[8,128,128]{2,1,0:T(8,128)(2,1)S(1)}, bf16[8,128,128]{2,1,0:T(8,128)(2,1)S(1)}, u32[]{:S(2)}, u32[]{:S(2)}) collective-permute-start(bf16[8,128,128]{2,1,0:T(8,128)(2,1)S(1)} %cross_sum.6.refs_2_), channel_id=1, source_target_pairs={{0,2},{1,3},{2,0},{3,1},{4,6},{5,7},{6,4},{7,5},{8,10},{9,11},{10,... | collective-permute-start | bytes 786440 | tf_op jit(solution)/shard_map/ppermute | solution.py:313
  9.5 4.7 %collective-permute-start.5 = (bf16[8,128,128]{2,1,0:T(8,128)(2,1)S(1)}, bf16[8,128,128]{2,1,0:T(8,128)(2,1)S(1)}, u32[]{:S(2)}, u32[]{:S(2)}) collective-permute-start(bf16[8,128,128]{2,1,0:T(8,128)(2,1)S(1)} %get-tuple-element.34.refs_2_.refs_0_.refs_5_), channel_id=1, source_target_pairs={{0,1},{2,3},{1,0},{3,2},{4,5},{6,7},{5,4},{7,6},{8,9},{10,11},{9,8... | collective-permute-start | bytes 786440 | tf_op jit(solution)/shard_map/ppermute | solution.py:305
  10.5 9.8 %collective-permute-start.3 = (bf16[32,128,128]{2,1,0:T(8,128)(2,1)S(1)}, bf16[32,128,128]{2,1,0:T(8,128)(2,1)S(1)}, u32[]{:S(2)}, u32[]{:S(2)}) collective-permute-start(bf16[32,128,128]{2,1,0:T(8,128)(2,1)S(1)} %get-tuple-element.36.refs_2_.refs_0_.refs_5_), channel_id=1, source_target_pairs={{0,1},{2,3},{1,0},{3,2},{4,5},{6,7},{5,4},{7,6},{8,9},{10,11},{9,8... | collective-permute-start | bytes 3145736 | tf_op jit(solution)/shard_map/ppermute | solution.py:305
  14.1 9.2 %collective-permute-start.9 = (bf16[8,128,128]{2,1,0:T(8,128)(2,1)S(1)}, bf16[8,128,128]{2,1,0:T(8,128)(2,1)S(1)}, u32[]{:S(2)}, u32[]{:S(2)}) collective-permute-start(bf16[8,128,128]{2,1,0:T(8,128)(2,1)S(1)} %middle_sum.8.refs_2_), channel_id=1, source_target_pairs={{4,8},{5,9},{6,10},{7,11},{0,1},{2,3},{12,13},{14,15},{8,4},{9,5},... | collective-permute-start | bytes 786440 | tf_op jit(solution)/shard_map/ppermute | solution.py:353
  14.2 9.0 %collective-permute-start.8 = (bf16[8,128,128]{2,1,0:T(8,128)(2,1)S(1)}, bf16[8,128,128]{2,1,0:T(8,128)(2,1)S(1)}, u32[]{:S(2)}, u32[]{:S(2)}) collective-permute-start(bf16[8,128,128]{2,1,0:T(8,128)(2,1)S(1)} %cross_sum.7.refs_3_), channel_id=1, source_target_pairs={{0,2},{1,3},{2,0},{3,1},{4,6},{5,7},{6,4},{7,5},{8,10},{9,11},{10,... | collective-permute-start | bytes 786440 | tf_op jit(solution)/shard_map/ppermute | solution.py:313
  16.4 9.4 %collective-permute-start.7 = (bf16[8,128,128]{2,1,0:T(8,128)(2,1)S(1)}, bf16[8,128,128]{2,1,0:T(8,128)(2,1)S(1)}, u32[]{:S(2)}, u32[]{:S(2)}) collective-permute-start(bf16[8,128,128]{2,1,0:T(8,128)(2,1)S(1)} %side_sum.13.refs_2_), channel_id=1, source_target_pairs={{0,4},{12,8},{4,0},{8,12},{1,5},{13,9},{5,1},{9,13},{2,6},{14,10},... | collective-permute-start | bytes 786440 | tf_op jit(solution)/shard_map/ppermute | solution.py:348
  20.2 7.2 %collective-permute-start.15 = (bf16[8,128,128]{2,1,0:T(8,128)(2,1)S(1)}, bf16[8,128,128]{2,1,0:T(8,128)(2,1)S(1)}, u32[]{:S(2)}, u32[]{:S(2)}) collective-permute-start(bf16[8,128,128]{2,1,0:T(8,128)(2,1)S(1)} %middle_sum.9.refs_2_), channel_id=1, source_target_pairs={{4,8},{5,9},{6,10},{7,11},{0,1},{2,3},{12,13},{14,15},{8,4},{9,5},... | collective-permute-start | bytes 786440 | tf_op jit(solution)/shard_map/ppermute | solution.py:353
  20.3 8.8 %collective-permute-start.14 = (bf16[8,128,128]{2,1,0:T(8,128)(2,1)S(1)}, bf16[8,128,128]{2,1,0:T(8,128)(2,1)S(1)}, u32[]{:S(2)}, u32[]{:S(2)}) collective-permute-start(bf16[8,128,128]{2,1,0:T(8,128)(2,1)S(1)} %cross_sum.8.refs_8_), channel_id=1, source_target_pairs={{0,2},{1,3},{2,0},{3,1},{4,6},{5,7},{6,4},{7,5},{8,10},{9,11},{10,... | collective-permute-start | bytes 786440 | tf_op jit(solution)/shard_map/ppermute | solution.py:313
  23.6 8.1 %collective-permute-start.13 = (bf16[8,128,128]{2,1,0:T(8,128)(2,1)S(1)}, bf16[8,128,128]{2,1,0:T(8,128)(2,1)S(1)}, u32[]{:S(2)}, u32[]{:S(2)}) collective-permute-start(bf16[8,128,128]{2,1,0:T(8,128)(2,1)S(1)} %side_sum.14.refs_2_), channel_id=1, source_target_pairs={{0,4},{12,8},{4,0},{8,12},{1,5},{13,9},{5,1},{9,13},{2,6},{14,10},... | collective-permute-start | bytes 786440 | tf_op jit(solution)/shard_map/ppermute | solution.py:348
  26.0 8.9 %collective-permute-start.12 = (bf16[8,128,128]{2,1,0:T(8,128)(2,1)S(1)}, bf16[8,128,128]{2,1,0:T(8,128)(2,1)S(1)}, u32[]{:S(2)}, u32[]{:S(2)}) collective-permute-start(bf16[8,128,128]{2,1,0:T(8,128)(2,1)S(1)} %middle_sum.10.refs_2_), channel_id=1, source_target_pairs={{4,8},{5,9},{6,10},{7,11},{0,1},{2,3},{12,13},{14,15},{8,4},{9,5},... | collective-permute-start | bytes 786440 | tf_op jit(solution)/shard_map/ppermute | solution.py:353
  26.2 8.8 %collective-permute-start.11 = (bf16[8,128,128]{2,1,0:T(8,128)(2,1)S(1)}, bf16[8,128,128]{2,1,0:T(8,128)(2,1)S(1)}, u32[]{:S(2)}, u32[]{:S(2)}) collective-permute-start(bf16[8,128,128]{2,1,0:T(8,128)(2,1)S(1)} %cross_sum.9.refs_8_), channel_id=1, source_target_pairs={{0,2},{1,3},{2,0},{3,1},{4,6},{5,7},{6,4},{7,5},{8,10},{9,11},{10,... | collective-permute-start | bytes 786440 | tf_op jit(solution)/shard_map/ppermute | solution.py:313
  29.5 8.1 %collective-permute-start.19 = (bf16[8,128,128]{2,1,0:T(8,128)(2,1)S(1)}, bf16[8,128,128]{2,1,0:T(8,128)(2,1)S(1)}, u32[]{:S(2)}, u32[]{:S(2)}) collective-permute-start(bf16[8,128,128]{2,1,0:T(8,128)(2,1)S(1)} %side_sum.15.refs_2_), channel_id=1, source_target_pairs={{0,4},{12,8},{4,0},{8,12},{1,5},{13,9},{5,1},{9,13},{2,6},{14,10},... | collective-permute-start | bytes 786440 | tf_op jit(solution)/shard_map/ppermute | solution.py:348
  32.0 8.9 %collective-permute-start.18 = (bf16[8,128,128]{2,1,0:T(8,128)(2,1)S(1)}, bf16[8,128,128]{2,1,0:T(8,128)(2,1)S(1)}, u32[]{:S(2)}, u32[]{:S(2)}) collective-permute-start(bf16[8,128,128]{2,1,0:T(8,128)(2,1)S(1)} %middle_sum.11.refs_2_), channel_id=1, source_target_pairs={{4,8},{5,9},{6,10},{7,11},{0,1},{2,3},{12,13},{14,15},{8,4},{9,5},... | collective-permute-start | bytes 786440 | tf_op jit(solution)/shard_map/ppermute | solution.py:353
  32.1 8.8 %collective-permute-start.17 = (bf16[8,128,128]{2,1,0:T(8,128)(2,1)S(1)}, bf16[8,128,128]{2,1,0:T(8,128)(2,1)S(1)}, u32[]{:S(2)}, u32[]{:S(2)}) collective-permute-start(bf16[8,128,128]{2,1,0:T(8,128)(2,1)S(1)} %cross_sum.10.refs_7_), channel_id=1, source_target_pairs={{0,2},{1,3},{2,0},{3,1},{4,6},{5,7},{6,4},{7,5},{8,10},{9,11},{10,... | collective-permute-start | bytes 786440 | tf_op jit(solution)/shard_map/ppermute | solution.py:313
  35.3 8.0 %collective-permute-start.16 = (bf16[8,128,128]{2,1,0:T(8,128)(2,1)S(1)}, bf16[8,128,128]{2,1,0:T(8,128)(2,1)S(1)}, u32[]{:S(2)}, u32[]{:S(2)}) collective-permute-start(bf16[8,128,128]{2,1,0:T(8,128)(2,1)S(1)} %side_sum.16.refs_2_), channel_id=1, source_target_pairs={{0,4},{12,8},{4,0},{8,12},{1,5},{13,9},{5,1},{9,13},{2,6},{14,10},... | collective-permute-start | bytes 786440 | tf_op jit(solution)/shard_map/ppermute | solution.py:348
  37.9 8.9 %collective-permute-start.23 = (bf16[8,128,128]{2,1,0:T(8,128)(2,1)S(1)}, bf16[8,128,128]{2,1,0:T(8,128)(2,1)S(1)}, u32[]{:S(2)}, u32[]{:S(2)}) collective-permute-start(bf16[8,128,128]{2,1,0:T(8,128)(2,1)S(1)} %middle_sum.12.refs_2_), channel_id=1, source_target_pairs={{4,8},{5,9},{6,10},{7,11},{0,1},{2,3},{12,13},{14,15},{8,4},{9,5},... | collective-permute-start | bytes 786440 | tf_op jit(solution)/shard_map/ppermute | solution.py:353
  38.0 8.8 %collective-permute-start.22 = (bf16[8,128,128]{2,1,0:T(8,128)(2,1)S(1)}, bf16[8,128,128]{2,1,0:T(8,128)(2,1)S(1)}, u32[]{:S(2)}, u32[]{:S(2)}) collective-permute-start(bf16[8,128,128]{2,1,0:T(8,128)(2,1)S(1)} %cross_sum.11.refs_7_), channel_id=1, source_target_pairs={{0,2},{1,3},{2,0},{3,1},{4,6},{5,7},{6,4},{7,5},{8,10},{9,11},{10,... | collective-permute-start | bytes 786440 | tf_op jit(solution)/shard_map/ppermute | solution.py:313
  41.3 8.2 %collective-permute-start.21 = (bf16[8,128,128]{2,1,0:T(8,128)(2,1)S(1)}, bf16[8,128,128]{2,1,0:T(8,128)(2,1)S(1)}, u32[]{:S(2)}, u32[]{:S(2)}) collective-permute-start(bf16[8,128,128]{2,1,0:T(8,128)(2,1)S(1)} %side_sum.17.refs_2_), channel_id=1, source_target_pairs={{0,4},{12,8},{4,0},{8,12},{1,5},{13,9},{5,1},{9,13},{2,6},{14,10},... | collective-permute-start | bytes 786440 | tf_op jit(solution)/shard_map/ppermute | solution.py:348
  43.5 8.1 %collective-permute-start.20 = (bf16[8,128,128]{2,1,0:T(8,128)(2,1)S(1)}, bf16[8,128,128]{2,1,0:T(8,128)(2,1)S(1)}, u32[]{:S(2)}, u32[]{:S(2)}) collective-permute-start(bf16[8,128,128]{2,1,0:T(8,128)(2,1)S(1)} %middle_sum.13.refs_8_), channel_id=1, source_target_pairs={{4,8},{5,9},{6,10},{7,11},{0,1},{2,3},{12,13},{14,15},{8,4},{9,5},... | collective-permute-start | bytes 786440 | tf_op jit(solution)/shard_map/ppermute | solution.py:353
  44.0 11.7 %collective-permute-start.28 = (bf16[8,128,128]{2,1,0:T(8,128)(2,1)S(1)}, bf16[8,128,128]{2,1,0:T(8,128)(2,1)S(1)}, u32[]{:S(2)}, u32[]{:S(2)}) collective-permute-start(bf16[8,128,128]{2,1,0:T(8,128)(2,1)S(1)} %late_sum.2.refs_7_), channel_id=1, source_target_pairs={{0,2},{1,3},{2,0},{3,1},{4,6},{5,7},{6,4},{7,5},{8,10},{9,11},{10,... | collective-permute-start | bytes 786440 | tf_op jit(solution)/shard_map/ppermute | solution.py:374
  47.2 8.1 %collective-permute-start.24 = (bf16[8,128,128]{2,1,0:T(8,128)(2,1)S(1)}, bf16[8,128,128]{2,1,0:T(8,128)(2,1)S(1)}, u32[]{:S(2)}, u32[]{:S(2)}) collective-permute-start(bf16[8,128,128]{2,1,0:T(8,128)(2,1)S(1)} %side_sum.18.refs_2_), channel_id=1, source_target_pairs={{0,4},{12,8},{4,0},{8,12},{1,5},{13,9},{5,1},{9,13},{2,6},{14,10},... | collective-permute-start | bytes 786440 | tf_op jit(solution)/shard_map/ppermute | solution.py:348
  49.7 6.5 %collective-permute-start.27 = (bf16[8,128,128]{2,1,0:T(8,128)(2,1)S(1)}, bf16[8,128,128]{2,1,0:T(8,128)(2,1)S(1)}, u32[]{:S(2)}, u32[]{:S(2)}) collective-permute-start(bf16[8,128,128]{2,1,0:T(8,128)(2,1)S(1)} %middle_sum.14.refs_8_), channel_id=1, source_target_pairs={{4,8},{5,9},{6,10},{7,11},{0,1},{2,3},{12,13},{14,15},{8,4},{9,5},... | collective-permute-start | bytes 786440 | tf_op jit(solution)/shard_map/ppermute | solution.py:353
  50.2 8.8 %collective-permute-start.26 = (bf16[8,128,128]{2,1,0:T(8,128)(2,1)S(1)}, bf16[8,128,128]{2,1,0:T(8,128)(2,1)S(1)}, u32[]{:S(2)}, u32[]{:S(2)}) collective-permute-start(bf16[8,128,128]{2,1,0:T(8,128)(2,1)S(1)} %late_sum.3.refs_4_), channel_id=1, source_target_pairs={{0,2},{1,3},{2,0},{3,1},{4,6},{5,7},{6,4},{7,5},{8,10},{9,11},{10,... | collective-permute-start | bytes 786440 | tf_op jit(solution)/shard_map/ppermute | solution.py:374
  52.1 13.3 %collective-permute-start.32 = (bf16[8,128,128]{2,1,0:T(8,128)(2,1)S(1)}, bf16[8,128,128]{2,1,0:T(8,128)(2,1)S(1)}, u32[]{:S(2)}, u32[]{:S(2)}) collective-permute-start(bf16[8,128,128]{2,1,0:T(8,128)(2,1)S(1)} %side_sum.19.refs_2_), channel_id=1, source_target_pairs={{0,4},{12,8},{4,0},{8,12},{1,5},{13,9},{5,1},{9,13},{2,6},{14,10},... | collective-permute-start | bytes 786440 | tf_op jit(solution)/shard_map/ppermute | solution.py:348
  55.6 4.1 %collective-permute-start.25 = (bf16[8,128,128]{2,1,0:T(8,128)(2,1)S(1)}, bf16[8,128,128]{2,1,0:T(8,128)(2,1)S(1)}, u32[]{:S(2)}, u32[]{:S(2)}) collective-permute-start(bf16[8,128,128]{2,1,0:T(8,128)(2,1)S(1)} %middle_sum.15), channel_id=1, source_target_pairs={{4,8},{5,9},{6,10},{7,11},{0,1},{2,3},{12,13},{14,15},{8,4},{9,5},... | collective-permute-start | bytes 786440 | tf_op jit(solution)/shard_map/ppermute | solution.py:353
  55.7 11.4 %collective-permute-start.30 = (bf16[8,128,128]{2,1,0:T(8,128)(2,1)S(1)}, bf16[8,128,128]{2,1,0:T(8,128)(2,1)S(1)}, u32[]{:S(2)}, u32[]{:S(2)}) collective-permute-start(bf16[8,128,128]{2,1,0:T(8,128)(2,1)S(1)} %collective-permute-done.28.refs_4_.refs_9_), channel_id=1, source_target_pairs={{0,1},{2,3},{1,0},{3,2},{4,5},{6,7},{5,4},{7,6},{8,9},{10,11},{9,8... | collective-permute-start | bytes 786440 | tf_op jit(solution)/shard_map/ppermute | solution.py:379
  56.4 10.3 %collective-permute-start.31 = (bf16[8,128,128]{2,1,0:T(8,128)(2,1)S(1)}, bf16[8,128,128]{2,1,0:T(8,128)(2,1)S(1)}, u32[]{:S(2)}, u32[]{:S(2)}) collective-permute-start(bf16[8,128,128]{2,1,0:T(8,128)(2,1)S(1)} %side_sum.20), channel_id=1, source_target_pairs={{0,4},{12,8},{4,0},{8,12},{1,5},{13,9},{5,1},{9,13},{2,6},{14,10},... | collective-permute-start | bytes 786440 | tf_op jit(solution)/shard_map/ppermute | solution.py:348
  59.0 8.8 %collective-permute-start.33 = (bf16[8,128,128]{2,1,0:T(8,128)(2,1)S(1)}, bf16[8,128,128]{2,1,0:T(8,128)(2,1)S(1)}, u32[]{:S(2)}, u32[]{:S(2)}) collective-permute-start(bf16[8,128,128]{2,1,0:T(8,128)(2,1)S(1)} %collective-permute-done.26.refs_7_.refs_9_), channel_id=1, source_target_pairs={{0,1},{2,3},{1,0},{3,2},{4,5},{6,7},{5,4},{7,6},{8,9},{10,11},{9,8... | collective-permute-start | bytes 786440 | tf_op jit(solution)/shard_map/ppermute | solution.py:379
  59.9 12.1 %collective-permute-start.29 = (bf16[8,128,128]{2,1,0:T(8,128)(2,1)S(1)}, bf16[8,128,128]{2,1,0:T(8,128)(2,1)S(1)}, u32[]{:S(2)}, u32[]{:S(2)}) collective-permute-start(bf16[8,128,128]{2,1,0:T(8,128)(2,1)S(1)} %side_sum.21.refs_7_), channel_id=1, source_target_pairs={{0,4},{12,8},{4,0},{8,12},{1,5},{13,9},{5,1},{9,13},{2,6},{14,10},... | collective-permute-start | bytes 786440 | tf_op jit(solution)/shard_map/ppermute | solution.py:348
  (6 other events, 22.3 us)

commit v6 on v5

--- a/solution.py
+++ b/solution.py
@@ -292,7 +292,7 @@
     def __init__(self, n, size):
         self.n, self.size = n, size
         self.own, self.other, self.x, self.a, self.b = {}, {}, {}, {}, {}
-        self.late, self.late_other = {}, {}
+        self.late, self.late_other, self.whole = {}, {}, {}
         self.couples = both_ways([(0, 1), (2, 3)])
         self.across = both_ways([(0, 2), (1, 3)])
         at = lambda z, c: 4 * z + c
@@ -302,6 +302,9 @@
         )
 
     def begin(self, first, own):
+        if first < LATE:
+            self.own[first] = (own, 0)
+            return
         other = lax.ppermute(own, "ctx", self.couples)
         for i in range(own.shape[0] // self.size):
             self.own[first + i] = (own, i * self.size)
@@ -316,24 +319,14 @@
     def early(self, c):
         return [(*self.other[c], ("odd",)), (*self.x[c], ("later",))]
 
-    def to_right(self, c):
-        if c < LATE:
-            return [(*self.own[c], ()), (*self.other[c], ("odd",))]
-        return [*self.early(c), (*self.own[c], ())]
-
-    def to_left(self, c):
-        if c < LATE:
-            return [(*self.other[c], ()), (*self.own[c], ("even",))]
-        return self.early(c)
-
     def mine(self, c):
         if c < LATE:
-            return [*also(self.to_right(c), "left"), *also(self.to_left(c), "right")]
+            return [(*self.own[c], ())]
         return [*self.early(c), (*self.own[c], ("left",))]
 
     def mirror(self, c):
         if c < LATE:
-            return [*also(self.to_left(c), "left"), *also(self.to_right(c), "right")]
+            return [(*self.own[c], ())]
         return [*self.early(c), (*self.own[c], ("right",))]
 
     def side(self, t, after):
@@ -368,25 +361,21 @@
         ]
 
     def late_cross(self, c, after):
-        whole = [*self.lower(c), (*self.own[c], ()), (*self.other[c], ())]
-        terms = [*also(self.higher(c), "even"), *also(whole, "odd")]
-        send = combine("late_sum", self.size, [terms], after)
-        self.late[c] = lax.ppermute(send, "ctx", self.across)
+        terms = [*self.lower(c), (*self.own[c], ()), *self.higher(c)]
+        send = combine("late_sum", self.size, [terms], after, EARLY)
+        self.whole[c] = (send, 0)
+        self.late[c] = (lax.ppermute(send, "ctx", self.across), 0)
         return [send]
 
     def late_swap(self, c, after):
-        self.late[c] = lax.optimization_barrier((self.late[c], *after))[0]
-        self.late_other[c] = lax.ppermute(self.late[c], "ctx", self.couples)
-        return [self.late[c]]
+        terms = [(*self.late[c], ("later",)), (*self.whole[c], ("even",))]
+        send = combine("late_swap", self.size, [terms], after, EARLY)
+        self.late_other[c] = (lax.ppermute(send, "ctx", self.couples), 0)
+        return [send]
 
     def state(self, c):
         if c < LATE:
-            return [
-                *self.lower(c),
-                *also([*self.higher(c), (*self.other[c], ())], "odd"),
-                (self.late[c], 0, ("later",)),
-                (self.late_other[c], 0, ("later",)),
-            ]
+            return [*self.lower(c), (*self.late[c], ("later",)), (*self.late_other[c], ())]
         return [
             *self.early(c),
             (*self.a[c], ("inner",)),
@@ -435,11 +424,12 @@
     fill = {
         1: [0], 2: [1], 3: [2], 4: [3], 5: [4], 6: [5], 7: [6], 8: [7],
     }
-    clock = kv(0, 1, [], cut=True)
-    clock = kv(1, 1, clock, cut=True)
-    clock = kv(2, 1, clock, cut=True)
+    clock = kv(2, 1, [], cut=True)
+    clock = kv(0, 1, clock, cut=True)
     for t in range(n + SKEW):
         clock = scan.side(t, clock)
+        if t == 0:
+            clock = kv(1, 1, clock, cut=True)
         if t == 1:
             clock = scan.cross(2, clock)
             clock = kv(3, 1, clock)

time: 74.4 us -> 73 us (0.981)
  starting transfers between devices: 41.5 us -> 39.2 us
  waiting for transfers between devices: 14.1 us -> 16.3 us
  Pallas kernels: 16.4 us -> 15 us
    ppermute x11, starting transfers between devices: 26.1 us -> 23.4 us  [side(): self.a[t] = (lax.ppermute(send, 'head', both_ways([(0, 1), (3, 2)])), 0)]
    ppermute x11, waiting for transfers between devices: 7.01 us -> 9.23 us  [side(): self.a[t] = (lax.ppermute(send, 'head', both_ways([(0, 1), (3, 2)])), 0)]
    pallas_call x47 -> x49, Pallas kernels: 14.3 us -> 12.9 us  [call(): pl.pallas_call(run, in_specs=[VMEM] * n_in + [ANY] * n_after, out_specs=[...]
    ppermute x6, starting transfers between devices: 9.59 us -> 10.4 us  [cross(): self.x[c] = (lax.ppermute(send, 'ctx', self.across), 0)]
    ppermute x6, waiting for transfers between devices: 7.06 us -> 6.31 us  [cross(): self.x[c] = (lax.ppermute(send, 'ctx', self.across), 0)]
    ppermute x5 -> x3, starting transfers between devices: 1.79 us -> 1.15 us  [begin(): other = lax.ppermute(own, 'ctx', self.couples)]
  transfers between devices with their start and end apart: 34 -> 32, of which waited for: 10 -> 12; matrix products, arithmetic and copies ran while one was open for 0% -> 0% of each run, Pallas kernels for 19% -> 17%
where the time goes in v6:
time: 73 us; the launch traced here: 72.8 us
  starting transfers between devices  39.2 us (54%)
  waiting for transfers between devices  16.3 us (22%)
  Pallas kernels  15 us (21%)
  local copies, waits for them, and re-layouts  1.58 us (2%)
  between operations  0.73 us (1%)
    ppermute x11, starting transfers between devices, side(): self.a[t] = (lax.ppermute(send, 'head', both_ways([(0, 1), (3, 2)])), 0)  23.4 us
    pallas_call x49, Pallas kernels, call(): pl.pallas_call(run, in_specs=[VMEM] * n_in + [ANY] * n_after, out_specs=[...  12.9 us
    ppermute x6, starting transfers between devices, cross(): self.x[c] = (lax.ppermute(send, 'ctx', self.across), 0)  10.4 us
    ppermute x11, waiting for transfers between devices, side(): self.a[t] = (lax.ppermute(send, 'head', both_ways([(0, 1), (3, 2)])), 0)  9.23 us
    ppermute x6, waiting for transfers between devices, cross(): self.x[c] = (lax.ppermute(send, 'ctx', self.across), 0)  6.31 us
    ppermute x2, starting transfers between devices, late_cross(): self.late[c] = (lax.ppermute(send, 'ctx', self.across), 0)  3.05 us
    pallas_call x1, Pallas kernels, last_attend(): pl.pallas_call(kernel, in_specs=[VMEM] * len(operands), out_specs=pl.Bloc...  2.04 us
    slice x1, local copies, waits for them, and re-layouts, kv(): k, v, at = (k[:, cols], v[:, cols], 0)  1.55 us
  transfers between devices with their start and end apart: 32, of which 12 were waited for; matrix products, arithmetic and copies ran while one was open for 0% of the time, Pallas kernels for 17%

profile of v6, /device:TPU:0, one launch (start us, length us, event | category | flops | bytes accessed | tf_op | source)
XLA Modules:
  0.0 72.8 jit_solution(5455056634411934596)
XLA Ops:
  0.0 1.5 %fusion = (bf16[128,1024]{1,0:T(8,128)(2,1)S(1)}, bf16[128,1024]{1,0:T(8,128)(2,1)S(1)}, bf16[128,1024]{1,0:T(8,128)(2,1)S(1)}, bf16[128,1024]{1,0:T(8,128)(2,1)...) fusion(bf16[128,8192]{1,0:T(8,128)(2,1)} %bitcast.4, bf16[128,8192]{1,0:T(8,128)(2,1)} %bitcast.15), kind=kLoop, calls=%fused_computation | loop fusion | bytes 3145728 | tf_op jit(solution)/shard_map/slice | solution.py:409
  2.8 2.7 %collective-permute-start.4 = (bf16[8,128,128]{2,1,0:T(8,128)(2,1)S(1)}, bf16[8,128,128]{2,1,0:T(8,128)(2,1)S(1)}, u32[]{:S(2)}, u32[]{:S(2)}) collective-permute-start(bf16[8,128,128]{2,1,0:T(8,128)(2,1)S(1)} %side_sum.11.refs_2_), channel_id=1, source_target_pairs={{0,4},{12,8},{4,0},{8,12},{1,5},{13,9},{5,1},{9,13},{2,6},{14,10},... | collective-permute-start | bytes 786440 | tf_op jit(solution)/shard_map/ppermute | solution.py:341
  6.0 2.0 %collective-permute-start.2 = (bf16[8,128,128]{2,1,0:T(8,128)(2,1)S(1)}, bf16[8,128,128]{2,1,0:T(8,128)(2,1)S(1)}, u32[]{:S(2)}, u32[]{:S(2)}) collective-permute-start(bf16[8,128,128]{2,1,0:T(8,128)(2,1)S(1)} %cross_sum.6.refs_2_), channel_id=1, source_target_pairs={{0,2},{1,3},{2,0},{3,1},{4,6},{5,7},{6,4},{7,5},{8,10},{9,11},{10,... | collective-permute-start | bytes 786440 | tf_op jit(solution)/shard_map/ppermute | solution.py:316
  8.5 0.9 %kv_states.9 = (bf16[32,128,128]{2,1,0:T(8,128)(2,1)S(1)}, bf16[128,4096]{1,0:T(8,128)(2,1)S(1)}) custom-call(bf16[128,8192]{1,0:T(8,128)(2,1)S(1)} %bitcast.17, bf16[128,8192]{1,0:T(8,128)(2,1)S(1)} %bitcast.6, bf16[8,128,128]{2,1,0:T(8,128)(2,1)S(1)} %get-tuple-element.32.refs_2_.refs_0_.refs_5_), custom_call_target="tpu_custom_call" | custom-call | flops 1000000 | bytes 1 | tf_op jit(solution)/shard_map/kv_states/pallas_call | solution.py:31
  9.4 0.6 collective-permute-start.1
  10.3 2.4 %collective-permute-done.4.refs_1_.refs_0_.refs_6_.refs_2_ = bf16[8,128,128]{2,1,0:T(8,128)(2,1)S(1)} collective-permute-done((bf16[8,128,128]{2,1,0:T(8,128)(2,1)S(1)}, bf16[8,128,128]{2,1,0:T(8,128)(2,1)S(1)}, u32[]{:S(2)}, u32[]{:S(2)}) %collective-permute-start.4) | collective-permute-done | bytes 262176 | tf_op jit(solution)/shard_map/ppermute | solution.py:341
  12.9 1.9 %collective-permute-start.6 = (bf16[8,128,128]{2,1,0:T(8,128)(2,1)S(1)}, bf16[8,128,128]{2,1,0:T(8,128)(2,1)S(1)}, u32[]{:S(2)}, u32[]{:S(2)}) collective-permute-start(bf16[8,128,128]{2,1,0:T(8,128)(2,1)S(1)} %cross_sum.7.refs_3_), channel_id=1, source_target_pairs={{0,2},{1,3},{2,0},{3,1},{4,6},{5,7},{6,4},{7,5},{8,10},{9,11},{10,... | collective-permute-start | bytes 786440 | tf_op jit(solution)/shard_map/ppermute | solution.py:316
  15.0 3.2 %collective-permute-start.5 = (bf16[8,128,128]{2,1,0:T(8,128)(2,1)S(1)}, bf16[8,128,128]{2,1,0:T(8,128)(2,1)S(1)}, u32[]{:S(2)}, u32[]{:S(2)}) collective-permute-start(bf16[8,128,128]{2,1,0:T(8,128)(2,1)S(1)} %side_sum.13.refs_2_), channel_id=1, source_target_pairs={{0,4},{12,8},{4,0},{8,12},{1,5},{13,9},{5,1},{9,13},{2,6},{14,10},... | collective-permute-start | bytes 786440 | tf_op jit(solution)/shard_map/ppermute | solution.py:341
  18.7 1.7 %collective-permute-start.12 = (bf16[8,128,128]{2,1,0:T(8,128)(2,1)S(1)}, bf16[8,128,128]{2,1,0:T(8,128)(2,1)S(1)}, u32[]{:S(2)}, u32[]{:S(2)}) collective-permute-start(bf16[8,128,128]{2,1,0:T(8,128)(2,1)S(1)} %cross_sum.8.refs_5_), channel_id=1, source_target_pairs={{0,2},{1,3},{2,0},{3,1},{4,6},{5,7},{6,4},{7,5},{8,10},{9,11},{10,... | collective-permute-start | bytes 786440 | tf_op jit(solution)/shard_map/ppermute | solution.py:316
  20.4 1.3 %collective-permute-done.6.refs_1_.refs_4_.refs_3_ = bf16[8,128,128]{2,1,0:T(8,128)(2,1)S(1)} collective-permute-done((bf16[8,128,128]{2,1,0:T(8,128)(2,1)S(1)}, bf16[8,128,128]{2,1,0:T(8,128)(2,1)S(1)}, u32[]{:S(2)}, u32[]{:S(2)}) %collective-permute-start.6) | collective-permute-done | bytes 262176 | tf_op jit(solution)/shard_map/ppermute | solution.py:316
  22.0 2.0 %collective-permute-start.11 = (bf16[8,128,128]{2,1,0:T(8,128)(2,1)S(1)}, bf16[8,128,128]{2,1,0:T(8,128)(2,1)S(1)}, u32[]{:S(2)}, u32[]{:S(2)}) collective-permute-start(bf16[8,128,128]{2,1,0:T(8,128)(2,1)S(1)} %side_sum.14.refs_2_), channel_id=1, source_target_pairs={{0,4},{12,8},{4,0},{8,12},{1,5},{13,9},{5,1},{9,13},{2,6},{14,10},... | collective-permute-start | bytes 786440 | tf_op jit(solution)/shard_map/ppermute | solution.py:341
  24.7 1.6 %collective-permute-start.9 = (bf16[8,128,128]{2,1,0:T(8,128)(2,1)S(1)}, bf16[8,128,128]{2,1,0:T(8,128)(2,1)S(1)}, u32[]{:S(2)}, u32[]{:S(2)}) collective-permute-start(bf16[8,128,128]{2,1,0:T(8,128)(2,1)S(1)} %cross_sum.9.refs_5_), channel_id=1, source_target_pairs={{0,2},{1,3},{2,0},{3,1},{4,6},{5,7},{6,4},{7,5},{8,10},{9,11},{10,... | collective-permute-start | bytes 786440 | tf_op jit(solution)/shard_map/ppermute | solution.py:316
  26.2 1.2 %collective-permute-done.12.refs_1_.refs_4_.refs_3_ = bf16[8,128,128]{2,1,0:T(8,128)(2,1)S(1)} collective-permute-done((bf16[8,128,128]{2,1,0:T(8,128)(2,1)S(1)}, bf16[8,128,128]{2,1,0:T(8,128)(2,1)S(1)}, u32[]{:S(2)}, u32[]{:S(2)}) %collective-permute-start.12) | collective-permute-done | bytes 262176 | tf_op jit(solution)/shard_map/ppermute | solution.py:316
  27.7 1.9 %collective-permute-start.17 = (bf16[8,128,128]{2,1,0:T(8,128)(2,1)S(1)}, bf16[8,128,128]{2,1,0:T(8,128)(2,1)S(1)}, u32[]{:S(2)}, u32[]{:S(2)}) collective-permute-start(bf16[8,128,128]{2,1,0:T(8,128)(2,1)S(1)} %side_sum.15.refs_2_), channel_id=1, source_target_pairs={{0,4},{12,8},{4,0},{8,12},{1,5},{13,9},{5,1},{9,13},{2,6},{14,10},... | collective-permute-start | bytes 786440 | tf_op jit(solution)/shard_map/ppermute | solution.py:341
  30.5 1.7 %collective-permute-start.15 = (bf16[8,128,128]{2,1,0:T(8,128)(2,1)S(1)}, bf16[8,128,128]{2,1,0:T(8,128)(2,1)S(1)}, u32[]{:S(2)}, u32[]{:S(2)}) collective-permute-start(bf16[8,128,128]{2,1,0:T(8,128)(2,1)S(1)} %cross_sum.10.refs_7_), channel_id=1, source_target_pairs={{0,2},{1,3},{2,0},{3,1},{4,6},{5,7},{6,4},{7,5},{8,10},{9,11},{10,... | collective-permute-start | bytes 786440 | tf_op jit(solution)/shard_map/ppermute | solution.py:316
  32.1 1.3 %collective-permute-done.9.refs_1_.refs_3_ = bf16[8,128,128]{2,1,0:T(8,128)(2,1)S(1)} collective-permute-done((bf16[8,128,128]{2,1,0:T(8,128)(2,1)S(1)}, bf16[8,128,128]{2,1,0:T(8,128)(2,1)S(1)}, u32[]{:S(2)}, u32[]{:S(2)}) %collective-permute-start.9) | collective-permute-done | bytes 262176 | tf_op jit(solution)/shard_map/ppermute | solution.py:316
  33.8 1.7 %collective-permute-start.14 = (bf16[8,128,128]{2,1,0:T(8,128)(2,1)S(1)}, bf16[8,128,128]{2,1,0:T(8,128)(2,1)S(1)}, u32[]{:S(2)}, u32[]{:S(2)}) collective-permute-start(bf16[8,128,128]{2,1,0:T(8,128)(2,1)S(1)} %side_sum.16.refs_2_), channel_id=1, source_target_pairs={{0,4},{12,8},{4,0},{8,12},{1,5},{13,9},{5,1},{9,13},{2,6},{14,10},... | collective-permute-start | bytes 786440 | tf_op jit(solution)/shard_map/ppermute | solution.py:341
  36.2 1.6 %collective-permute-start.20 = (bf16[8,128,128]{2,1,0:T(8,128)(2,1)S(1)}, bf16[8,128,128]{2,1,0:T(8,128)(2,1)S(1)}, u32[]{:S(2)}, u32[]{:S(2)}) collective-permute-start(bf16[8,128,128]{2,1,0:T(8,128)(2,1)S(1)} %cross_sum.11.refs_7_), channel_id=1, source_target_pairs={{0,2},{1,3},{2,0},{3,1},{4,6},{5,7},{6,4},{7,5},{8,10},{9,11},{10,... | collective-permute-start | bytes 786440 | tf_op jit(solution)/shard_map/ppermute | solution.py:316
  37.8 1.4 %collective-permute-done.15.refs_1_.refs_3_ = bf16[8,128,128]{2,1,0:T(8,128)(2,1)S(1)} collective-permute-done((bf16[8,128,128]{2,1,0:T(8,128)(2,1)S(1)}, bf16[8,128,128]{2,1,0:T(8,128)(2,1)S(1)}, u32[]{:S(2)}, u32[]{:S(2)}) %collective-permute-start.15) | collective-permute-done | bytes 262176 | tf_op jit(solution)/shard_map/ppermute | solution.py:316
  39.6 1.6 %collective-permute-start.19 = (bf16[8,128,128]{2,1,0:T(8,128)(2,1)S(1)}, bf16[8,128,128]{2,1,0:T(8,128)(2,1)S(1)}, u32[]{:S(2)}, u32[]{:S(2)}) collective-permute-start(bf16[8,128,128]{2,1,0:T(8,128)(2,1)S(1)} %side_sum.17.refs_2_), channel_id=1, source_target_pairs={{0,4},{12,8},{4,0},{8,12},{1,5},{13,9},{5,1},{9,13},{2,6},{14,10},... | collective-permute-start | bytes 786440 | tf_op jit(solution)/shard_map/ppermute | solution.py:341
  42.4 1.6 %collective-permute-start.26 = (bf16[8,128,128]{2,1,0:T(8,128)(2,1)S(1)}, bf16[8,128,128]{2,1,0:T(8,128)(2,1)S(1)}, u32[]{:S(2)}, u32[]{:S(2)}) collective-permute-start(bf16[8,128,128]{2,1,0:T(8,128)(2,1)S(1)} %late_sum.2.refs_7_.refs_1_), channel_id=1, source_target_pairs={{0,2},{1,3},{2,0},{3,1},{4,6},{5,7},{6,4},{7,5},{8,10},{9,11},{10,... | collective-permute-start | bytes 786440 | tf_op jit(solution)/shard_map/ppermute | solution.py:367
  44.0 1.0 %collective-permute-done.20.refs_1_.refs_3_ = bf16[8,128,128]{2,1,0:T(8,128)(2,1)S(1)} collective-permute-done((bf16[8,128,128]{2,1,0:T(8,128)(2,1)S(1)}, bf16[8,128,128]{2,1,0:T(8,128)(2,1)S(1)}, u32[]{:S(2)}, u32[]{:S(2)}) %collective-permute-start.20) | collective-permute-done | bytes 262176 | tf_op jit(solution)/shard_map/ppermute | solution.py:316
  45.4 2.1 %collective-permute-start.22 = (bf16[8,128,128]{2,1,0:T(8,128)(2,1)S(1)}, bf16[8,128,128]{2,1,0:T(8,128)(2,1)S(1)}, u32[]{:S(2)}, u32[]{:S(2)}) collective-permute-start(bf16[8,128,128]{2,1,0:T(8,128)(2,1)S(1)} %side_sum.18.refs_2_), channel_id=1, source_target_pairs={{0,4},{12,8},{4,0},{8,12},{1,5},{13,9},{5,1},{9,13},{2,6},{14,10},... | collective-permute-start | bytes 786440 | tf_op jit(solution)/shard_map/ppermute | solution.py:341
  48.9 3.0 %collective-permute-start.30 = (bf16[8,128,128]{2,1,0:T(8,128)(2,1)S(1)}, bf16[8,128,128]{2,1,0:T(8,128)(2,1)S(1)}, u32[]{:S(2)}, u32[]{:S(2)}) collective-permute-start(bf16[8,128,128]{2,1,0:T(8,128)(2,1)S(1)} %side_sum.19.refs_2_), channel_id=1, source_target_pairs={{0,4},{12,8},{4,0},{8,12},{1,5},{13,9},{5,1},{9,13},{2,6},{14,10},... | collective-permute-start | bytes 786440 | tf_op jit(solution)/shard_map/ppermute | solution.py:341
  51.9 1.5 %collective-permute-start.24 = (bf16[8,128,128]{2,1,0:T(8,128)(2,1)S(1)}, bf16[8,128,128]{2,1,0:T(8,128)(2,1)S(1)}, u32[]{:S(2)}, u32[]{:S(2)}) collective-permute-start(bf16[8,128,128]{2,1,0:T(8,128)(2,1)S(1)} %late_sum.3.refs_4_.refs_1_), channel_id=1, source_target_pairs={{0,2},{1,3},{2,0},{3,1},{4,6},{5,7},{6,4},{7,5},{8,10},{9,11},{10,... | collective-permute-start | bytes 786440 | tf_op jit(solution)/shard_map/ppermute | solution.py:367
  53.4 1.2 %collective-permute-done.22.refs_3_.refs_6_.refs_4_ = bf16[8,128,128]{2,1,0:T(8,128)(2,1)S(1)} collective-permute-done((bf16[8,128,128]{2,1,0:T(8,128)(2,1)S(1)}, bf16[8,128,128]{2,1,0:T(8,128)(2,1)S(1)}, u32[]{:S(2)}, u32[]{:S(2)}) %collective-permute-start.22) | collective-permute-done | bytes 262176 | tf_op jit(solution)/shard_map/ppermute | solution.py:341
  55.7 2.3 %collective-permute-start.29 = (bf16[8,128,128]{2,1,0:T(8,128)(2,1)S(1)}, bf16[8,128,128]{2,1,0:T(8,128)(2,1)S(1)}, u32[]{:S(2)}, u32[]{:S(2)}) collective-permute-start(bf16[8,128,128]{2,1,0:T(8,128)(2,1)S(1)} %side_sum.20.refs_2_), channel_id=1, source_target_pairs={{0,4},{12,8},{4,0},{8,12},{1,5},{13,9},{5,1},{9,13},{2,6},{14,10},... | collective-permute-start | bytes 786440 | tf_op jit(solution)/shard_map/ppermute | solution.py:341
  58.0 0.7 collective-permute-done.24.refs_0_.refs_5_
  59.8 2.9 %collective-permute-start.27 = (bf16[8,128,128]{2,1,0:T(8,128)(2,1)S(1)}, bf16[8,128,128]{2,1,0:T(8,128)(2,1)S(1)}, u32[]{:S(2)}, u32[]{:S(2)}) collective-permute-start(bf16[8,128,128]{2,1,0:T(8,128)(2,1)S(1)} %side_sum.21.refs_7_), channel_id=1, source_target_pairs={{0,4},{12,8},{4,0},{8,12},{1,5},{13,9},{5,1},{9,13},{2,6},{14,10},... | collective-permute-start | bytes 786440 | tf_op jit(solution)/shard_map/ppermute | solution.py:341
  64.1 1.1 %collective-permute-done.29.refs_6_ = bf16[8,128,128]{2,1,0:T(8,128)(2,1)S(1)} collective-permute-done((bf16[8,128,128]{2,1,0:T(8,128)(2,1)S(1)}, bf16[8,128,128]{2,1,0:T(8,128)(2,1)S(1)}, u32[]{:S(2)}, u32[]{:S(2)}) %collective-permute-start.29) | collective-permute-done | bytes 262176 | tf_op jit(solution)/shard_map/ppermute | solution.py:341
  66.5 4.0 %collective-permute-done.27.refs_6_ = bf16[8,128,128]{2,1,0:T(8,128)(2,1)S(1)} collective-permute-done((bf16[8,128,128]{2,1,0:T(8,128)(2,1)S(1)}, bf16[8,128,128]{2,1,0:T(8,128)(2,1)S(1)}, u32[]{:S(2)}, u32[]{:S(2)}) %collective-permute-start.27) | collective-permute-done | bytes 262176 | tf_op jit(solution)/shard_map/ppermute | solution.py:341
  70.6 2.0 %last_attend.1 = bf16[1,128,8192]{2,1,0:T(8,128)(2,1)} custom-call(bf16[128,2048]{1,0:T(8,128)(2,1)S(1)} %local_scores.15.refs_4_.refs_0_, bf16[128,8192]{1,0:T(8,128)(2,1)S(1)} %bitcast.14, bf16[32,128,128]{2,1,0:T(8,128)(2,1)S(1)} %collective-permute-done.1.refs_1_.refs_0_.refs_3_.refs_2_, ...), custom_call_target="tpu_custom_call" | custom-call | flops 2000000000 | bytes 1 | tf_op jit(solution)/shard_map/last_attend/pallas_call | solution.py:215
  (91 shorter events, 14.5 us)
Async XLA Ops:
  1.9 4.1 %collective-permute-start = (bf16[8,128,128]{2,1,0:T(8,128)(2,1)S(1)}, bf16[8,128,128]{2,1,0:T(8,128)(2,1)S(1)}, u32[]{:S(2)}, u32[]{:S(2)}) collective-permute-start(bf16[8,128,128]{2,1,0:T(8,128)(2,1)S(1)} %get-tuple-element.29.refs_2_.refs_0_.refs_5_), channel_id=1, source_target_pairs={{0,1},{2,3},{1,0},{3,2},{4,5},{6,7},{5,4},{7,6},{8,9},{10,11},{9,8... | collective-permute-start | bytes 786440 | tf_op jit(solution)/shard_map/ppermute | solution.py:308
  2.8 9.8 %collective-permute-start.4 = (bf16[8,128,128]{2,1,0:T(8,128)(2,1)S(1)}, bf16[8,128,128]{2,1,0:T(8,128)(2,1)S(1)}, u32[]{:S(2)}, u32[]{:S(2)}) collective-permute-start(bf16[8,128,128]{2,1,0:T(8,128)(2,1)S(1)} %side_sum.11.refs_2_), channel_id=1, source_target_pairs={{0,4},{12,8},{4,0},{8,12},{1,5},{13,9},{5,1},{9,13},{2,6},{14,10},... | collective-permute-start | bytes 786440 | tf_op jit(solution)/shard_map/ppermute | solution.py:341
  5.9 12.6 %collective-permute-start.8 = (bf16[8,128,128]{2,1,0:T(8,128)(2,1)S(1)}, bf16[8,128,128]{2,1,0:T(8,128)(2,1)S(1)}, u32[]{:S(2)}, u32[]{:S(2)}) collective-permute-start(bf16[8,128,128]{2,1,0:T(8,128)(2,1)S(1)} %side_sum.12.refs_2_), channel_id=1, source_target_pairs={{0,4},{12,8},{4,0},{8,12},{1,5},{13,9},{5,1},{9,13},{2,6},{14,10},... | collective-permute-start | bytes 786440 | tf_op jit(solution)/shard_map/ppermute | solution.py:341
  6.0 8.8 %collective-permute-start.2 = (bf16[8,128,128]{2,1,0:T(8,128)(2,1)S(1)}, bf16[8,128,128]{2,1,0:T(8,128)(2,1)S(1)}, u32[]{:S(2)}, u32[]{:S(2)}) collective-permute-start(bf16[8,128,128]{2,1,0:T(8,128)(2,1)S(1)} %cross_sum.6.refs_2_), channel_id=1, source_target_pairs={{0,2},{1,3},{2,0},{3,1},{4,6},{5,7},{6,4},{7,5},{8,10},{9,11},{10,... | collective-permute-start | bytes 786440 | tf_op jit(solution)/shard_map/ppermute | solution.py:316
  8.4 4.4 %collective-permute-start.3 = (bf16[8,128,128]{2,1,0:T(8,128)(2,1)S(1)}, bf16[8,128,128]{2,1,0:T(8,128)(2,1)S(1)}, u32[]{:S(2)}, u32[]{:S(2)}) collective-permute-start(bf16[8,128,128]{2,1,0:T(8,128)(2,1)S(1)} %get-tuple-element.32.refs_2_.refs_0_.refs_5_), channel_id=1, source_target_pairs={{0,1},{2,3},{1,0},{3,2},{4,5},{6,7},{5,4},{7,6},{8,9},{10,11},{9,8... | collective-permute-start | bytes 786440 | tf_op jit(solution)/shard_map/ppermute | solution.py:308
  9.4 9.2 %collective-permute-start.1 = (bf16[32,128,128]{2,1,0:T(8,128)(2,1)S(1)}, bf16[32,128,128]{2,1,0:T(8,128)(2,1)S(1)}, u32[]{:S(2)}, u32[]{:S(2)}) collective-permute-start(bf16[32,128,128]{2,1,0:T(8,128)(2,1)S(1)} %get-tuple-element.34.refs_2_.refs_0_.refs_5_), channel_id=1, source_target_pairs={{0,1},{2,3},{1,0},{3,2},{4,5},{6,7},{5,4},{7,6},{8,9},{10,11},{9,8... | collective-permute-start | bytes 3145736 | tf_op jit(solution)/shard_map/ppermute | solution.py:308
  12.7 7.7 %collective-permute-start.7 = (bf16[8,128,128]{2,1,0:T(8,128)(2,1)S(1)}, bf16[8,128,128]{2,1,0:T(8,128)(2,1)S(1)}, u32[]{:S(2)}, u32[]{:S(2)}) collective-permute-start(bf16[8,128,128]{2,1,0:T(8,128)(2,1)S(1)} %middle_sum.8.refs_2_), channel_id=1, source_target_pairs={{4,8},{5,9},{6,10},{7,11},{0,1},{2,3},{12,13},{14,15},{8,4},{9,5},... | collective-permute-start | bytes 786440 | tf_op jit(solution)/shard_map/ppermute | solution.py:346
  12.9 8.9 %collective-permute-start.6 = (bf16[8,128,128]{2,1,0:T(8,128)(2,1)S(1)}, bf16[8,128,128]{2,1,0:T(8,128)(2,1)S(1)}, u32[]{:S(2)}, u32[]{:S(2)}) collective-permute-start(bf16[8,128,128]{2,1,0:T(8,128)(2,1)S(1)} %cross_sum.7.refs_3_), channel_id=1, source_target_pairs={{0,2},{1,3},{2,0},{3,1},{4,6},{5,7},{6,4},{7,5},{8,10},{9,11},{10,... | collective-permute-start | bytes 786440 | tf_op jit(solution)/shard_map/ppermute | solution.py:316
  15.0 9.4 %collective-permute-start.5 = (bf16[8,128,128]{2,1,0:T(8,128)(2,1)S(1)}, bf16[8,128,128]{2,1,0:T(8,128)(2,1)S(1)}, u32[]{:S(2)}, u32[]{:S(2)}) collective-permute-start(bf16[8,128,128]{2,1,0:T(8,128)(2,1)S(1)} %side_sum.13.refs_2_), channel_id=1, source_target_pairs={{0,4},{12,8},{4,0},{8,12},{1,5},{13,9},{5,1},{9,13},{2,6},{14,10},... | collective-permute-start | bytes 786440 | tf_op jit(solution)/shard_map/ppermute | solution.py:341
  18.5 7.7 %collective-permute-start.13 = (bf16[8,128,128]{2,1,0:T(8,128)(2,1)S(1)}, bf16[8,128,128]{2,1,0:T(8,128)(2,1)S(1)}, u32[]{:S(2)}, u32[]{:S(2)}) collective-permute-start(bf16[8,128,128]{2,1,0:T(8,128)(2,1)S(1)} %middle_sum.9.refs_2_), channel_id=1, source_target_pairs={{4,8},{5,9},{6,10},{7,11},{0,1},{2,3},{12,13},{14,15},{8,4},{9,5},... | collective-permute-start | bytes 786440 | tf_op jit(solution)/shard_map/ppermute | solution.py:346
  18.7 8.8 %collective-permute-start.12 = (bf16[8,128,128]{2,1,0:T(8,128)(2,1)S(1)}, bf16[8,128,128]{2,1,0:T(8,128)(2,1)S(1)}, u32[]{:S(2)}, u32[]{:S(2)}) collective-permute-start(bf16[8,128,128]{2,1,0:T(8,128)(2,1)S(1)} %cross_sum.8.refs_5_), channel_id=1, source_target_pairs={{0,2},{1,3},{2,0},{3,1},{4,6},{5,7},{6,4},{7,5},{8,10},{9,11},{10,... | collective-permute-start | bytes 786440 | tf_op jit(solution)/shard_map/ppermute | solution.py:316
  22.0 8.1 %collective-permute-start.11 = (bf16[8,128,128]{2,1,0:T(8,128)(2,1)S(1)}, bf16[8,128,128]{2,1,0:T(8,128)(2,1)S(1)}, u32[]{:S(2)}, u32[]{:S(2)}) collective-permute-start(bf16[8,128,128]{2,1,0:T(8,128)(2,1)S(1)} %side_sum.14.refs_2_), channel_id=1, source_target_pairs={{0,4},{12,8},{4,0},{8,12},{1,5},{13,9},{5,1},{9,13},{2,6},{14,10},... | collective-permute-start | bytes 786440 | tf_op jit(solution)/shard_map/ppermute | solution.py:341
  24.5 8.9 %collective-permute-start.10 = (bf16[8,128,128]{2,1,0:T(8,128)(2,1)S(1)}, bf16[8,128,128]{2,1,0:T(8,128)(2,1)S(1)}, u32[]{:S(2)}, u32[]{:S(2)}) collective-permute-start(bf16[8,128,128]{2,1,0:T(8,128)(2,1)S(1)} %middle_sum.10.refs_2_), channel_id=1, source_target_pairs={{4,8},{5,9},{6,10},{7,11},{0,1},{2,3},{12,13},{14,15},{8,4},{9,5},... | collective-permute-start | bytes 786440 | tf_op jit(solution)/shard_map/ppermute | solution.py:346
  24.7 8.8 %collective-permute-start.9 = (bf16[8,128,128]{2,1,0:T(8,128)(2,1)S(1)}, bf16[8,128,128]{2,1,0:T(8,128)(2,1)S(1)}, u32[]{:S(2)}, u32[]{:S(2)}) collective-permute-start(bf16[8,128,128]{2,1,0:T(8,128)(2,1)S(1)} %cross_sum.9.refs_5_), channel_id=1, source_target_pairs={{0,2},{1,3},{2,0},{3,1},{4,6},{5,7},{6,4},{7,5},{8,10},{9,11},{10,... | collective-permute-start | bytes 786440 | tf_op jit(solution)/shard_map/ppermute | solution.py:316
  27.7 8.1 %collective-permute-start.17 = (bf16[8,128,128]{2,1,0:T(8,128)(2,1)S(1)}, bf16[8,128,128]{2,1,0:T(8,128)(2,1)S(1)}, u32[]{:S(2)}, u32[]{:S(2)}) collective-permute-start(bf16[8,128,128]{2,1,0:T(8,128)(2,1)S(1)} %side_sum.15.refs_2_), channel_id=1, source_target_pairs={{0,4},{12,8},{4,0},{8,12},{1,5},{13,9},{5,1},{9,13},{2,6},{14,10},... | collective-permute-start | bytes 786440 | tf_op jit(solution)/shard_map/ppermute | solution.py:341
  30.3 8.9 %collective-permute-start.16 = (bf16[8,128,128]{2,1,0:T(8,128)(2,1)S(1)}, bf16[8,128,128]{2,1,0:T(8,128)(2,1)S(1)}, u32[]{:S(2)}, u32[]{:S(2)}) collective-permute-start(bf16[8,128,128]{2,1,0:T(8,128)(2,1)S(1)} %middle_sum.11.refs_2_), channel_id=1, source_target_pairs={{4,8},{5,9},{6,10},{7,11},{0,1},{2,3},{12,13},{14,15},{8,4},{9,5},... | collective-permute-start | bytes 786440 | tf_op jit(solution)/shard_map/ppermute | solution.py:346
  30.5 8.8 %collective-permute-start.15 = (bf16[8,128,128]{2,1,0:T(8,128)(2,1)S(1)}, bf16[8,128,128]{2,1,0:T(8,128)(2,1)S(1)}, u32[]{:S(2)}, u32[]{:S(2)}) collective-permute-start(bf16[8,128,128]{2,1,0:T(8,128)(2,1)S(1)} %cross_sum.10.refs_7_), channel_id=1, source_target_pairs={{0,2},{1,3},{2,0},{3,1},{4,6},{5,7},{6,4},{7,5},{8,10},{9,11},{10,... | collective-permute-start | bytes 786440 | tf_op jit(solution)/shard_map/ppermute | solution.py:316
  33.8 8.0 %collective-permute-start.14 = (bf16[8,128,128]{2,1,0:T(8,128)(2,1)S(1)}, bf16[8,128,128]{2,1,0:T(8,128)(2,1)S(1)}, u32[]{:S(2)}, u32[]{:S(2)}) collective-permute-start(bf16[8,128,128]{2,1,0:T(8,128)(2,1)S(1)} %side_sum.16.refs_2_), channel_id=1, source_target_pairs={{0,4},{12,8},{4,0},{8,12},{1,5},{13,9},{5,1},{9,13},{2,6},{14,10},... | collective-permute-start | bytes 786440 | tf_op jit(solution)/shard_map/ppermute | solution.py:341
  36.1 8.9 %collective-permute-start.21 = (bf16[8,128,128]{2,1,0:T(8,128)(2,1)S(1)}, bf16[8,128,128]{2,1,0:T(8,128)(2,1)S(1)}, u32[]{:S(2)}, u32[]{:S(2)}) collective-permute-start(bf16[8,128,128]{2,1,0:T(8,128)(2,1)S(1)} %middle_sum.12.refs_2_), channel_id=1, source_target_pairs={{4,8},{5,9},{6,10},{7,11},{0,1},{2,3},{12,13},{14,15},{8,4},{9,5},... | collective-permute-start | bytes 786440 | tf_op jit(solution)/shard_map/ppermute | solution.py:346
  36.2 8.8 %collective-permute-start.20 = (bf16[8,128,128]{2,1,0:T(8,128)(2,1)S(1)}, bf16[8,128,128]{2,1,0:T(8,128)(2,1)S(1)}, u32[]{:S(2)}, u32[]{:S(2)}) collective-permute-start(bf16[8,128,128]{2,1,0:T(8,128)(2,1)S(1)} %cross_sum.11.refs_7_), channel_id=1, source_target_pairs={{0,2},{1,3},{2,0},{3,1},{4,6},{5,7},{6,4},{7,5},{8,10},{9,11},{10,... | collective-permute-start | bytes 786440 | tf_op jit(solution)/shard_map/ppermute | solution.py:316
  39.6 8.2 %collective-permute-start.19 = (bf16[8,128,128]{2,1,0:T(8,128)(2,1)S(1)}, bf16[8,128,128]{2,1,0:T(8,128)(2,1)S(1)}, u32[]{:S(2)}, u32[]{:S(2)}) collective-permute-start(bf16[8,128,128]{2,1,0:T(8,128)(2,1)S(1)} %side_sum.17.refs_2_), channel_id=1, source_target_pairs={{0,4},{12,8},{4,0},{8,12},{1,5},{13,9},{5,1},{9,13},{2,6},{14,10},... | collective-permute-start | bytes 786440 | tf_op jit(solution)/shard_map/ppermute | solution.py:341
  42.0 6.4 %collective-permute-start.18 = (bf16[8,128,128]{2,1,0:T(8,128)(2,1)S(1)}, bf16[8,128,128]{2,1,0:T(8,128)(2,1)S(1)}, u32[]{:S(2)}, u32[]{:S(2)}) collective-permute-start(bf16[8,128,128]{2,1,0:T(8,128)(2,1)S(1)} %middle_sum.13.refs_7_), channel_id=1, source_target_pairs={{4,8},{5,9},{6,10},{7,11},{0,1},{2,3},{12,13},{14,15},{8,4},{9,5},... | collective-permute-start | bytes 786440 | tf_op jit(solution)/shard_map/ppermute | solution.py:346
  42.4 12.4 %collective-permute-start.26 = (bf16[8,128,128]{2,1,0:T(8,128)(2,1)S(1)}, bf16[8,128,128]{2,1,0:T(8,128)(2,1)S(1)}, u32[]{:S(2)}, u32[]{:S(2)}) collective-permute-start(bf16[8,128,128]{2,1,0:T(8,128)(2,1)S(1)} %late_sum.2.refs_7_.refs_1_), channel_id=1, source_target_pairs={{0,2},{1,3},{2,0},{3,1},{4,6},{5,7},{6,4},{7,5},{8,10},{9,11},{10,... | collective-permute-start | bytes 786440 | tf_op jit(solution)/shard_map/ppermute | solution.py:367
  45.4 9.2 %collective-permute-start.22 = (bf16[8,128,128]{2,1,0:T(8,128)(2,1)S(1)}, bf16[8,128,128]{2,1,0:T(8,128)(2,1)S(1)}, u32[]{:S(2)}, u32[]{:S(2)}) collective-permute-start(bf16[8,128,128]{2,1,0:T(8,128)(2,1)S(1)} %side_sum.18.refs_2_), channel_id=1, source_target_pairs={{0,4},{12,8},{4,0},{8,12},{1,5},{13,9},{5,1},{9,13},{2,6},{14,10},... | collective-permute-start | bytes 786440 | tf_op jit(solution)/shard_map/ppermute | solution.py:341
  48.0 7.5 %collective-permute-start.25 = (bf16[8,128,128]{2,1,0:T(8,128)(2,1)S(1)}, bf16[8,128,128]{2,1,0:T(8,128)(2,1)S(1)}, u32[]{:S(2)}, u32[]{:S(2)}) collective-permute-start(bf16[8,128,128]{2,1,0:T(8,128)(2,1)S(1)} %middle_sum.14.refs_7_), channel_id=1, source_target_pairs={{4,8},{5,9},{6,10},{7,11},{0,1},{2,3},{12,13},{14,15},{8,4},{9,5},... | collective-permute-start | bytes 786440 | tf_op jit(solution)/shard_map/ppermute | solution.py:346
  48.9 14.7 %collective-permute-start.30 = (bf16[8,128,128]{2,1,0:T(8,128)(2,1)S(1)}, bf16[8,128,128]{2,1,0:T(8,128)(2,1)S(1)}, u32[]{:S(2)}, u32[]{:S(2)}) collective-permute-start(bf16[8,128,128]{2,1,0:T(8,128)(2,1)S(1)} %side_sum.19.refs_2_), channel_id=1, source_target_pairs={{0,4},{12,8},{4,0},{8,12},{1,5},{13,9},{5,1},{9,13},{2,6},{14,10},... | collective-permute-start | bytes 786440 | tf_op jit(solution)/shard_map/ppermute | solution.py:341
  51.9 6.8 %collective-permute-start.24 = (bf16[8,128,128]{2,1,0:T(8,128)(2,1)S(1)}, bf16[8,128,128]{2,1,0:T(8,128)(2,1)S(1)}, u32[]{:S(2)}, u32[]{:S(2)}) collective-permute-start(bf16[8,128,128]{2,1,0:T(8,128)(2,1)S(1)} %late_sum.3.refs_4_.refs_1_), channel_id=1, source_target_pairs={{0,2},{1,3},{2,0},{3,1},{4,6},{5,7},{6,4},{7,5},{8,10},{9,11},{10,... | collective-permute-start | bytes 786440 | tf_op jit(solution)/shard_map/ppermute | solution.py:367
  54.8 4.6 %collective-permute-start.23 = (bf16[8,128,128]{2,1,0:T(8,128)(2,1)S(1)}, bf16[8,128,128]{2,1,0:T(8,128)(2,1)S(1)}, u32[]{:S(2)}, u32[]{:S(2)}) collective-permute-start(bf16[8,128,128]{2,1,0:T(8,128)(2,1)S(1)} %middle_sum.15.refs_2_), channel_id=1, source_target_pairs={{4,8},{5,9},{6,10},{7,11},{0,1},{2,3},{12,13},{14,15},{8,4},{9,5},... | collective-permute-start | bytes 786440 | tf_op jit(solution)/shard_map/ppermute | solution.py:346
  55.0 10.7 %collective-permute-start.28 = (bf16[8,128,128]{2,1,0:T(8,128)(2,1)S(1)}, bf16[8,128,128]{2,1,0:T(8,128)(2,1)S(1)}, u32[]{:S(2)}, u32[]{:S(2)}) collective-permute-start(bf16[8,128,128]{2,1,0:T(8,128)(2,1)S(1)} %late_swap.2.refs_4_), channel_id=1, source_target_pairs={{0,1},{2,3},{1,0},{3,2},{4,5},{6,7},{5,4},{7,6},{8,9},{10,11},{9,8... | collective-permute-start | bytes 786440 | tf_op jit(solution)/shard_map/ppermute | solution.py:373
  55.7 9.5 %collective-permute-start.29 = (bf16[8,128,128]{2,1,0:T(8,128)(2,1)S(1)}, bf16[8,128,128]{2,1,0:T(8,128)(2,1)S(1)}, u32[]{:S(2)}, u32[]{:S(2)}) collective-permute-start(bf16[8,128,128]{2,1,0:T(8,128)(2,1)S(1)} %side_sum.20.refs_2_), channel_id=1, source_target_pairs={{0,4},{12,8},{4,0},{8,12},{1,5},{13,9},{5,1},{9,13},{2,6},{14,10},... | collective-permute-start | bytes 786440 | tf_op jit(solution)/shard_map/ppermute | solution.py:341
  58.9 7.2 %collective-permute-start.31 = (bf16[8,128,128]{2,1,0:T(8,128)(2,1)S(1)}, bf16[8,128,128]{2,1,0:T(8,128)(2,1)S(1)}, u32[]{:S(2)}, u32[]{:S(2)}) collective-permute-start(bf16[8,128,128]{2,1,0:T(8,128)(2,1)S(1)} %late_swap.3.refs_7_), channel_id=1, source_target_pairs={{0,1},{2,3},{1,0},{3,2},{4,5},{6,7},{5,4},{7,6},{8,9},{10,11},{9,8... | collective-permute-start | bytes 786440 | tf_op jit(solution)/shard_map/ppermute | solution.py:373
  59.8 10.8 %collective-permute-start.27 = (bf16[8,128,128]{2,1,0:T(8,128)(2,1)S(1)}, bf16[8,128,128]{2,1,0:T(8,128)(2,1)S(1)}, u32[]{:S(2)}, u32[]{:S(2)}) collective-permute-start(bf16[8,128,128]{2,1,0:T(8,128)(2,1)S(1)} %side_sum.21.refs_7_), channel_id=1, source_target_pairs={{0,4},{12,8},{4,0},{8,12},{1,5},{13,9},{5,1},{9,13},{2,6},{14,10},... | collective-permute-start | bytes 786440 | tf_op jit(solution)/shard_map/ppermute | solution.py:341
  (4 other events, 16.6 us)

commit v7 on v6

--- a/solution.py
+++ b/solution.py
@@ -12,7 +12,7 @@
 BF16 = jnp.bfloat16
 VMEM_LIMIT = 8 << 20
 EARLY = 10**6
-COST = 2 * 10**9
+COST = 3 * 10**9
 VMEM = pl.BlockSpec(memory_space=pltpu.VMEM)
 ANY = pl.BlockSpec(memory_space=pl.ANY)
 
@@ -435,6 +435,8 @@
             clock = kv(3, 1, clock)
             clock = kv(4, 4, clock)
         if t == n + 1:
+            clock = scan.late_swap(0, clock)
+        if t == n + 2:
             clock = scan.late_swap(1, clock)
         for c in fill.get(t, []):
             clock = scores(c, clock)
@@ -446,8 +448,6 @@
             clock = scan.cross(t + 2, clock)
         if 0 <= t + 2 - n < LATE:
             clock = scan.late_cross(t + 2 - n, clock)
-        if t == n:
-            clock = scan.late_swap(0, clock)
     for c in [*range(LATE, n - 1), *range(LATE)]:
         if c not in attns:
             clock = attention(c, clock)

time: 73 us -> 72.8 us (level)
    ppermute x11, starting transfers between devices: 23.4 us -> 24.8 us  [side(): self.a[t] = (lax.ppermute(send, 'head', both_ways([(0, 1), (3, 2)])), 0)]
    ppermute x6, waiting for transfers between devices: 6.31 us -> 7.72 us  [cross(): self.x[c] = (lax.ppermute(send, 'ctx', self.across), 0)]
    ppermute x11, waiting for transfers between devices: 9.23 us -> 7.92 us  [side(): self.a[t] = (lax.ppermute(send, 'head', both_ways([(0, 1), (3, 2)])), 0)]
where the time goes in v7:
time: 72.8 us; the launch traced here: 72.7 us
  starting transfers between devices  39.9 us (55%)
  waiting for transfers between devices  15.7 us (22%)
  Pallas kernels  14.8 us (20%)
  local copies, waits for them, and re-layouts  1.52 us (2%)
  between operations  0.74 us (1%)
    ppermute x11, starting transfers between devices, side(): self.a[t] = (lax.ppermute(send, 'head', both_ways([(0, 1), (3, 2)])), 0)  24.8 us
    pallas_call x49, Pallas kernels, call(): pl.pallas_call(run, in_specs=[VMEM] * n_in + [ANY] * n_after, out_specs=[...  12.8 us
    ppermute x6, starting transfers between devices, cross(): self.x[c] = (lax.ppermute(send, 'ctx', self.across), 0)  10.2 us
    ppermute x11, waiting for transfers between devices, side(): self.a[t] = (lax.ppermute(send, 'head', both_ways([(0, 1), (3, 2)])), 0)  7.92 us
    ppermute x6, waiting for transfers between devices, cross(): self.x[c] = (lax.ppermute(send, 'ctx', self.across), 0)  7.72 us
    ppermute x2, starting transfers between devices, late_cross(): self.late[c] = (lax.ppermute(send, 'ctx', self.across), 0)  3.2 us
    pallas_call x1, Pallas kernels, last_attend(): pl.pallas_call(kernel, in_specs=[VMEM] * len(operands), out_specs=pl.Bloc...  2.04 us
    slice x1, local copies, waits for them, and re-layouts, kv(): k, v, at = (k[:, cols], v[:, cols], 0)  1.49 us
  transfers between devices with their start and end apart: 32, of which 12 were waited for; matrix products, arithmetic and copies ran while one was open for 0% of the time, Pallas kernels for 17%

profile of v7, /device:TPU:0, one launch (start us, length us, event | category | flops | bytes accessed | tf_op | source)
XLA Modules:
  0.0 72.7 jit_solution(6031385193118545624)
XLA Ops:
  0.0 1.5 %fusion = (bf16[128,1024]{1,0:T(8,128)(2,1)S(1)}, bf16[128,1024]{1,0:T(8,128)(2,1)S(1)}, bf16[128,1024]{1,0:T(8,128)(2,1)S(1)}, bf16[128,1024]{1,0:T(8,128)(2,1)...) fusion(bf16[128,8192]{1,0:T(8,128)(2,1)} %bitcast.7, bf16[128,8192]{1,0:T(8,128)(2,1)} %bitcast.4), kind=kLoop, calls=%fused_computation | loop fusion | bytes 3145728 | tf_op jit(solution)/shard_map/slice | solution.py:409
  1.8 0.5 collective-permute-start
  2.8 2.7 %collective-permute-start.4 = (bf16[8,128,128]{2,1,0:T(8,128)(2,1)S(1)}, bf16[8,128,128]{2,1,0:T(8,128)(2,1)S(1)}, u32[]{:S(2)}, u32[]{:S(2)}) collective-permute-start(bf16[8,128,128]{2,1,0:T(8,128)(2,1)S(1)} %side_sum.11.refs_2_), channel_id=1, source_target_pairs={{0,4},{12,8},{4,0},{8,12},{1,5},{13,9},{5,1},{9,13},{2,6},{14,10},... | collective-permute-start | bytes 786440 | tf_op jit(solution)/shard_map/ppermute | solution.py:341
  6.4 0.9 %kv_states.9 = (bf16[32,128,128]{2,1,0:T(8,128)(2,1)S(1)}, bf16[128,4096]{1,0:T(8,128)(2,1)S(1)}) custom-call(bf16[128,8192]{1,0:T(8,128)(2,1)S(1)} %bitcast.6, bf16[128,8192]{1,0:T(8,128)(2,1)S(1)} %bitcast.9, bf16[8,128,128]{2,1,0:T(8,128)(2,1)S(1)} %get-tuple-element.32.refs_2_.refs_0_.refs_5_), custom_call_target="tpu_custom_call" | custom-call | flops 1000000 | bytes 1 | tf_op jit(solution)/shard_map/kv_states/pallas_call | solution.py:31
  7.6 1.8 %collective-permute-start.2 = (bf16[8,128,128]{2,1,0:T(8,128)(2,1)S(1)}, bf16[8,128,128]{2,1,0:T(8,128)(2,1)S(1)}, u32[]{:S(2)}, u32[]{:S(2)}) collective-permute-start(bf16[8,128,128]{2,1,0:T(8,128)(2,1)S(1)} %cross_sum.6.refs_2_), channel_id=1, source_target_pairs={{0,2},{1,3},{2,0},{3,1},{4,6},{5,7},{6,4},{7,5},{8,10},{9,11},{10,... | collective-permute-start | bytes 786440 | tf_op jit(solution)/shard_map/ppermute | solution.py:316
  9.8 2.8 %collective-permute-done.4.refs_1_.refs_0_.refs_6_.refs_2_ = bf16[8,128,128]{2,1,0:T(8,128)(2,1)S(1)} collective-permute-done((bf16[8,128,128]{2,1,0:T(8,128)(2,1)S(1)}, bf16[8,128,128]{2,1,0:T(8,128)(2,1)S(1)}, u32[]{:S(2)}, u32[]{:S(2)}) %collective-permute-start.4) | collective-permute-done | bytes 262176 | tf_op jit(solution)/shard_map/ppermute | solution.py:341
  12.8 1.9 %collective-permute-start.6 = (bf16[8,128,128]{2,1,0:T(8,128)(2,1)S(1)}, bf16[8,128,128]{2,1,0:T(8,128)(2,1)S(1)}, u32[]{:S(2)}, u32[]{:S(2)}) collective-permute-start(bf16[8,128,128]{2,1,0:T(8,128)(2,1)S(1)} %cross_sum.7.refs_3_), channel_id=1, source_target_pairs={{0,2},{1,3},{2,0},{3,1},{4,6},{5,7},{6,4},{7,5},{8,10},{9,11},{10,... | collective-permute-start | bytes 786440 | tf_op jit(solution)/shard_map/ppermute | solution.py:316
  14.7 1.6 %collective-permute-done.2.refs_1_.refs_4_.refs_3_ = bf16[8,128,128]{2,1,0:T(8,128)(2,1)S(1)} collective-permute-done((bf16[8,128,128]{2,1,0:T(8,128)(2,1)S(1)}, bf16[8,128,128]{2,1,0:T(8,128)(2,1)S(1)}, u32[]{:S(2)}, u32[]{:S(2)}) %collective-permute-start.2) | collective-permute-done | bytes 262176 | tf_op jit(solution)/shard_map/ppermute | solution.py:316
  16.5 1.8 %collective-permute-start.5 = (bf16[8,128,128]{2,1,0:T(8,128)(2,1)S(1)}, bf16[8,128,128]{2,1,0:T(8,128)(2,1)S(1)}, u32[]{:S(2)}, u32[]{:S(2)}) collective-permute-start(bf16[8,128,128]{2,1,0:T(8,128)(2,1)S(1)} %side_sum.13.refs_2_), channel_id=1, source_target_pairs={{0,4},{12,8},{4,0},{8,12},{1,5},{13,9},{5,1},{9,13},{2,6},{14,10},... | collective-permute-start | bytes 786440 | tf_op jit(solution)/shard_map/ppermute | solution.py:341
  18.9 1.6 %collective-permute-start.12 = (bf16[8,128,128]{2,1,0:T(8,128)(2,1)S(1)}, bf16[8,128,128]{2,1,0:T(8,128)(2,1)S(1)}, u32[]{:S(2)}, u32[]{:S(2)}) collective-permute-start(bf16[8,128,128]{2,1,0:T(8,128)(2,1)S(1)} %cross_sum.8.refs_5_), channel_id=1, source_target_pairs={{0,2},{1,3},{2,0},{3,1},{4,6},{5,7},{6,4},{7,5},{8,10},{9,11},{10,... | collective-permute-start | bytes 786440 | tf_op jit(solution)/shard_map/ppermute | solution.py:316
  20.4 1.4 %collective-permute-done.6.refs_1_.refs_4_.refs_3_ = bf16[8,128,128]{2,1,0:T(8,128)(2,1)S(1)} collective-permute-done((bf16[8,128,128]{2,1,0:T(8,128)(2,1)S(1)}, bf16[8,128,128]{2,1,0:T(8,128)(2,1)S(1)}, u32[]{:S(2)}, u32[]{:S(2)}) %collective-permute-start.6) | collective-permute-done | bytes 262176 | tf_op jit(solution)/shard_map/ppermute | solution.py:316
  22.1 1.9 %collective-permute-start.11 = (bf16[8,128,128]{2,1,0:T(8,128)(2,1)S(1)}, bf16[8,128,128]{2,1,0:T(8,128)(2,1)S(1)}, u32[]{:S(2)}, u32[]{:S(2)}) collective-permute-start(bf16[8,128,128]{2,1,0:T(8,128)(2,1)S(1)} %side_sum.14.refs_2_), channel_id=1, source_target_pairs={{0,4},{12,8},{4,0},{8,12},{1,5},{13,9},{5,1},{9,13},{2,6},{14,10},... | collective-permute-start | bytes 786440 | tf_op jit(solution)/shard_map/ppermute | solution.py:341
  24.9 1.7 %collective-permute-start.9 = (bf16[8,128,128]{2,1,0:T(8,128)(2,1)S(1)}, bf16[8,128,128]{2,1,0:T(8,128)(2,1)S(1)}, u32[]{:S(2)}, u32[]{:S(2)}) collective-permute-start(bf16[8,128,128]{2,1,0:T(8,128)(2,1)S(1)} %cross_sum.9.refs_5_), channel_id=1, source_target_pairs={{0,2},{1,3},{2,0},{3,1},{4,6},{5,7},{6,4},{7,5},{8,10},{9,11},{10,... | collective-permute-start | bytes 786440 | tf_op jit(solution)/shard_map/ppermute | solution.py:316
  26.6 1.1 %collective-permute-done.12.refs_1_.refs_4_.refs_3_ = bf16[8,128,128]{2,1,0:T(8,128)(2,1)S(1)} collective-permute-done((bf16[8,128,128]{2,1,0:T(8,128)(2,1)S(1)}, bf16[8,128,128]{2,1,0:T(8,128)(2,1)S(1)}, u32[]{:S(2)}, u32[]{:S(2)}) %collective-permute-start.12) | collective-permute-done | bytes 262176 | tf_op jit(solution)/shard_map/ppermute | solution.py:316
  27.9 2.1 %collective-permute-start.17 = (bf16[8,128,128]{2,1,0:T(8,128)(2,1)S(1)}, bf16[8,128,128]{2,1,0:T(8,128)(2,1)S(1)}, u32[]{:S(2)}, u32[]{:S(2)}) collective-permute-start(bf16[8,128,128]{2,1,0:T(8,128)(2,1)S(1)} %side_sum.15.refs_2_), channel_id=1, source_target_pairs={{0,4},{12,8},{4,0},{8,12},{1,5},{13,9},{5,1},{9,13},{2,6},{14,10},... | collective-permute-start | bytes 786440 | tf_op jit(solution)/shard_map/ppermute | solution.py:341
  30.7 1.7 %collective-permute-start.15 = (bf16[8,128,128]{2,1,0:T(8,128)(2,1)S(1)}, bf16[8,128,128]{2,1,0:T(8,128)(2,1)S(1)}, u32[]{:S(2)}, u32[]{:S(2)}) collective-permute-start(bf16[8,128,128]{2,1,0:T(8,128)(2,1)S(1)} %cross_sum.10.refs_7_), channel_id=1, source_target_pairs={{0,2},{1,3},{2,0},{3,1},{4,6},{5,7},{6,4},{7,5},{8,10},{9,11},{10,... | collective-permute-start | bytes 786440 | tf_op jit(solution)/shard_map/ppermute | solution.py:316
  32.4 1.2 %collective-permute-done.9.refs_1_.refs_3_ = bf16[8,128,128]{2,1,0:T(8,128)(2,1)S(1)} collective-permute-done((bf16[8,128,128]{2,1,0:T(8,128)(2,1)S(1)}, bf16[8,128,128]{2,1,0:T(8,128)(2,1)S(1)}, u32[]{:S(2)}, u32[]{:S(2)}) %collective-permute-start.9) | collective-permute-done | bytes 262176 | tf_op jit(solution)/shard_map/ppermute | solution.py:316
  34.0 1.8 %collective-permute-start.14 = (bf16[8,128,128]{2,1,0:T(8,128)(2,1)S(1)}, bf16[8,128,128]{2,1,0:T(8,128)(2,1)S(1)}, u32[]{:S(2)}, u32[]{:S(2)}) collective-permute-start(bf16[8,128,128]{2,1,0:T(8,128)(2,1)S(1)} %side_sum.16.refs_2_), channel_id=1, source_target_pairs={{0,4},{12,8},{4,0},{8,12},{1,5},{13,9},{5,1},{9,13},{2,6},{14,10},... | collective-permute-start | bytes 786440 | tf_op jit(solution)/shard_map/ppermute | solution.py:341
  36.5 1.6 %collective-permute-start.20 = (bf16[8,128,128]{2,1,0:T(8,128)(2,1)S(1)}, bf16[8,128,128]{2,1,0:T(8,128)(2,1)S(1)}, u32[]{:S(2)}, u32[]{:S(2)}) collective-permute-start(bf16[8,128,128]{2,1,0:T(8,128)(2,1)S(1)} %cross_sum.11.refs_7_), channel_id=1, source_target_pairs={{0,2},{1,3},{2,0},{3,1},{4,6},{5,7},{6,4},{7,5},{8,10},{9,11},{10,... | collective-permute-start | bytes 786440 | tf_op jit(solution)/shard_map/ppermute | solution.py:316
  38.0 1.4 %collective-permute-done.15.refs_1_.refs_3_ = bf16[8,128,128]{2,1,0:T(8,128)(2,1)S(1)} collective-permute-done((bf16[8,128,128]{2,1,0:T(8,128)(2,1)S(1)}, bf16[8,128,128]{2,1,0:T(8,128)(2,1)S(1)}, u32[]{:S(2)}, u32[]{:S(2)}) %collective-permute-start.15) | collective-permute-done | bytes 262176 | tf_op jit(solution)/shard_map/ppermute | solution.py:316
  39.8 1.7 %collective-permute-start.19 = (bf16[8,128,128]{2,1,0:T(8,128)(2,1)S(1)}, bf16[8,128,128]{2,1,0:T(8,128)(2,1)S(1)}, u32[]{:S(2)}, u32[]{:S(2)}) collective-permute-start(bf16[8,128,128]{2,1,0:T(8,128)(2,1)S(1)} %side_sum.17.refs_2_), channel_id=1, source_target_pairs={{0,4},{12,8},{4,0},{8,12},{1,5},{13,9},{5,1},{9,13},{2,6},{14,10},... | collective-permute-start | bytes 786440 | tf_op jit(solution)/shard_map/ppermute | solution.py:341
  42.6 1.7 %collective-permute-start.24 = (bf16[8,128,128]{2,1,0:T(8,128)(2,1)S(1)}, bf16[8,128,128]{2,1,0:T(8,128)(2,1)S(1)}, u32[]{:S(2)}, u32[]{:S(2)}) collective-permute-start(bf16[8,128,128]{2,1,0:T(8,128)(2,1)S(1)} %late_sum.2.refs_7_.refs_1_), channel_id=1, source_target_pairs={{0,2},{1,3},{2,0},{3,1},{4,6},{5,7},{6,4},{7,5},{8,10},{9,11},{10,... | collective-permute-start | bytes 786440 | tf_op jit(solution)/shard_map/ppermute | solution.py:367
  44.3 0.9 %collective-permute-done.20.refs_1_.refs_3_ = bf16[8,128,128]{2,1,0:T(8,128)(2,1)S(1)} collective-permute-done((bf16[8,128,128]{2,1,0:T(8,128)(2,1)S(1)}, bf16[8,128,128]{2,1,0:T(8,128)(2,1)S(1)}, u32[]{:S(2)}, u32[]{:S(2)}) %collective-permute-start.20) | collective-permute-done | bytes 262176 | tf_op jit(solution)/shard_map/ppermute | solution.py:316
  45.6 2.1 %collective-permute-start.22 = (bf16[8,128,128]{2,1,0:T(8,128)(2,1)S(1)}, bf16[8,128,128]{2,1,0:T(8,128)(2,1)S(1)}, u32[]{:S(2)}, u32[]{:S(2)}) collective-permute-start(bf16[8,128,128]{2,1,0:T(8,128)(2,1)S(1)} %side_sum.18.refs_2_), channel_id=1, source_target_pairs={{0,4},{12,8},{4,0},{8,12},{1,5},{13,9},{5,1},{9,13},{2,6},{14,10},... | collective-permute-start | bytes 786440 | tf_op jit(solution)/shard_map/ppermute | solution.py:341
  48.6 1.5 %collective-permute-start.30 = (bf16[8,128,128]{2,1,0:T(8,128)(2,1)S(1)}, bf16[8,128,128]{2,1,0:T(8,128)(2,1)S(1)}, u32[]{:S(2)}, u32[]{:S(2)}) collective-permute-start(bf16[8,128,128]{2,1,0:T(8,128)(2,1)S(1)} %late_sum.3.refs_4_.refs_1_), channel_id=1, source_target_pairs={{0,2},{1,3},{2,0},{3,1},{4,6},{5,7},{6,4},{7,5},{8,10},{9,11},{10,... | collective-permute-start | bytes 786440 | tf_op jit(solution)/shard_map/ppermute | solution.py:367
  50.4 3.0 %collective-permute-start.29 = (bf16[8,128,128]{2,1,0:T(8,128)(2,1)S(1)}, bf16[8,128,128]{2,1,0:T(8,128)(2,1)S(1)}, u32[]{:S(2)}, u32[]{:S(2)}) collective-permute-start(bf16[8,128,128]{2,1,0:T(8,128)(2,1)S(1)} %side_sum.19.refs_2_), channel_id=1, source_target_pairs={{0,4},{12,8},{4,0},{8,12},{1,5},{13,9},{5,1},{9,13},{2,6},{14,10},... | collective-permute-start | bytes 786440 | tf_op jit(solution)/shard_map/ppermute | solution.py:341
  54.4 3.0 %collective-permute-start.28 = (bf16[8,128,128]{2,1,0:T(8,128)(2,1)S(1)}, bf16[8,128,128]{2,1,0:T(8,128)(2,1)S(1)}, u32[]{:S(2)}, u32[]{:S(2)}) collective-permute-start(bf16[8,128,128]{2,1,0:T(8,128)(2,1)S(1)} %side_sum.20.refs_2_), channel_id=1, source_target_pairs={{0,4},{12,8},{4,0},{8,12},{1,5},{13,9},{5,1},{9,13},{2,6},{14,10},... | collective-permute-start | bytes 786440 | tf_op jit(solution)/shard_map/ppermute | solution.py:341
  58.2 4.7 %collective-permute-start.26 = (bf16[8,128,128]{2,1,0:T(8,128)(2,1)S(1)}, bf16[8,128,128]{2,1,0:T(8,128)(2,1)S(1)}, u32[]{:S(2)}, u32[]{:S(2)}) collective-permute-start(bf16[8,128,128]{2,1,0:T(8,128)(2,1)S(1)} %side_sum.21.refs_2_), channel_id=1, source_target_pairs={{0,4},{12,8},{4,0},{8,12},{1,5},{13,9},{5,1},{9,13},{2,6},{14,10},... | collective-permute-start | bytes 786440 | tf_op jit(solution)/shard_map/ppermute | solution.py:341
  63.6 0.5 attend.9
  64.5 1.7 %collective-permute-done.28.refs_6_ = bf16[8,128,128]{2,1,0:T(8,128)(2,1)S(1)} collective-permute-done((bf16[8,128,128]{2,1,0:T(8,128)(2,1)S(1)}, bf16[8,128,128]{2,1,0:T(8,128)(2,1)S(1)}, u32[]{:S(2)}, u32[]{:S(2)}) %collective-permute-start.28) | collective-permute-done | bytes 262176 | tf_op jit(solution)/shard_map/ppermute | solution.py:341
  67.6 2.9 %collective-permute-done.26.refs_6_ = bf16[8,128,128]{2,1,0:T(8,128)(2,1)S(1)} collective-permute-done((bf16[8,128,128]{2,1,0:T(8,128)(2,1)S(1)}, bf16[8,128,128]{2,1,0:T(8,128)(2,1)S(1)}, u32[]{:S(2)}, u32[]{:S(2)}) %collective-permute-start.26) | collective-permute-done | bytes 262176 | tf_op jit(solution)/shard_map/ppermute | solution.py:341
  70.5 2.0 %last_attend.1 = bf16[1,128,8192]{2,1,0:T(8,128)(2,1)} custom-call(bf16[128,2048]{1,0:T(8,128)(2,1)S(1)} %local_scores.15.refs_4_.refs_0_, bf16[128,8192]{1,0:T(8,128)(2,1)S(1)} %bitcast.17, bf16[32,128,128]{2,1,0:T(8,128)(2,1)S(1)} %collective-permute-done.1.refs_1_.refs_0_.refs_3_.refs_2_, ...), custom_call_target="tpu_custom_call" | custom-call | flops 3000000000 | bytes 1 | tf_op jit(solution)/shard_map/last_attend/pallas_call | solution.py:215
  (91 shorter events, 13.3 us)
Async XLA Ops:
  1.8 4.1 %collective-permute-start = (bf16[8,128,128]{2,1,0:T(8,128)(2,1)S(1)}, bf16[8,128,128]{2,1,0:T(8,128)(2,1)S(1)}, u32[]{:S(2)}, u32[]{:S(2)}) collective-permute-start(bf16[8,128,128]{2,1,0:T(8,128)(2,1)S(1)} %get-tuple-element.29.refs_2_.refs_0_.refs_5_), channel_id=1, source_target_pairs={{0,1},{2,3},{1,0},{3,2},{4,5},{6,7},{5,4},{7,6},{8,9},{10,11},{9,8... | collective-permute-start | bytes 786440 | tf_op jit(solution)/shard_map/ppermute | solution.py:308
  2.8 9.8 %collective-permute-start.4 = (bf16[8,128,128]{2,1,0:T(8,128)(2,1)S(1)}, bf16[8,128,128]{2,1,0:T(8,128)(2,1)S(1)}, u32[]{:S(2)}, u32[]{:S(2)}) collective-permute-start(bf16[8,128,128]{2,1,0:T(8,128)(2,1)S(1)} %side_sum.11.refs_2_), channel_id=1, source_target_pairs={{0,4},{12,8},{4,0},{8,12},{1,5},{13,9},{5,1},{9,13},{2,6},{14,10},... | collective-permute-start | bytes 786440 | tf_op jit(solution)/shard_map/ppermute | solution.py:341
  5.8 12.8 %collective-permute-start.8 = (bf16[8,128,128]{2,1,0:T(8,128)(2,1)S(1)}, bf16[8,128,128]{2,1,0:T(8,128)(2,1)S(1)}, u32[]{:S(2)}, u32[]{:S(2)}) collective-permute-start(bf16[8,128,128]{2,1,0:T(8,128)(2,1)S(1)} %side_sum.12.refs_2_), channel_id=1, source_target_pairs={{0,4},{12,8},{4,0},{8,12},{1,5},{13,9},{5,1},{9,13},{2,6},{14,10},... | collective-permute-start | bytes 786440 | tf_op jit(solution)/shard_map/ppermute | solution.py:341
  7.3 5.4 %collective-permute-start.3 = (bf16[8,128,128]{2,1,0:T(8,128)(2,1)S(1)}, bf16[8,128,128]{2,1,0:T(8,128)(2,1)S(1)}, u32[]{:S(2)}, u32[]{:S(2)}) collective-permute-start(bf16[8,128,128]{2,1,0:T(8,128)(2,1)S(1)} %get-tuple-element.32.refs_2_.refs_0_.refs_5_), channel_id=1, source_target_pairs={{0,1},{2,3},{1,0},{3,2},{4,5},{6,7},{5,4},{7,6},{8,9},{10,11},{9,8... | collective-permute-start | bytes 786440 | tf_op jit(solution)/shard_map/ppermute | solution.py:308
  7.6 8.8 %collective-permute-start.2 = (bf16[8,128,128]{2,1,0:T(8,128)(2,1)S(1)}, bf16[8,128,128]{2,1,0:T(8,128)(2,1)S(1)}, u32[]{:S(2)}, u32[]{:S(2)}) collective-permute-start(bf16[8,128,128]{2,1,0:T(8,128)(2,1)S(1)} %cross_sum.6.refs_2_), channel_id=1, source_target_pairs={{0,2},{1,3},{2,0},{3,1},{4,6},{5,7},{6,4},{7,5},{8,10},{9,11},{10,... | collective-permute-start | bytes 786440 | tf_op jit(solution)/shard_map/ppermute | solution.py:316
  9.3 9.4 %collective-permute-start.1 = (bf16[32,128,128]{2,1,0:T(8,128)(2,1)S(1)}, bf16[32,128,128]{2,1,0:T(8,128)(2,1)S(1)}, u32[]{:S(2)}, u32[]{:S(2)}) collective-permute-start(bf16[32,128,128]{2,1,0:T(8,128)(2,1)S(1)} %get-tuple-element.34.refs_2_.refs_0_.refs_5_), channel_id=1, source_target_pairs={{0,1},{2,3},{1,0},{3,2},{4,5},{6,7},{5,4},{7,6},{8,9},{10,11},{9,8... | collective-permute-start | bytes 3145736 | tf_op jit(solution)/shard_map/ppermute | solution.py:308
  12.7 7.8 %collective-permute-start.7 = (bf16[8,128,128]{2,1,0:T(8,128)(2,1)S(1)}, bf16[8,128,128]{2,1,0:T(8,128)(2,1)S(1)}, u32[]{:S(2)}, u32[]{:S(2)}) collective-permute-start(bf16[8,128,128]{2,1,0:T(8,128)(2,1)S(1)} %middle_sum.8.refs_2_), channel_id=1, source_target_pairs={{4,8},{5,9},{6,10},{7,11},{0,1},{2,3},{12,13},{14,15},{8,4},{9,5},... | collective-permute-start | bytes 786440 | tf_op jit(solution)/shard_map/ppermute | solution.py:346
  12.8 9.1 %collective-permute-start.6 = (bf16[8,128,128]{2,1,0:T(8,128)(2,1)S(1)}, bf16[8,128,128]{2,1,0:T(8,128)(2,1)S(1)}, u32[]{:S(2)}, u32[]{:S(2)}) collective-permute-start(bf16[8,128,128]{2,1,0:T(8,128)(2,1)S(1)} %cross_sum.7.refs_3_), channel_id=1, source_target_pairs={{0,2},{1,3},{2,0},{3,1},{4,6},{5,7},{6,4},{7,5},{8,10},{9,11},{10,... | collective-permute-start | bytes 786440 | tf_op jit(solution)/shard_map/ppermute | solution.py:316
  16.5 8.0 %collective-permute-start.5 = (bf16[8,128,128]{2,1,0:T(8,128)(2,1)S(1)}, bf16[8,128,128]{2,1,0:T(8,128)(2,1)S(1)}, u32[]{:S(2)}, u32[]{:S(2)}) collective-permute-start(bf16[8,128,128]{2,1,0:T(8,128)(2,1)S(1)} %side_sum.13.refs_2_), channel_id=1, source_target_pairs={{0,4},{12,8},{4,0},{8,12},{1,5},{13,9},{5,1},{9,13},{2,6},{14,10},... | collective-permute-start | bytes 786440 | tf_op jit(solution)/shard_map/ppermute | solution.py:341
  18.7 7.8 %collective-permute-start.13 = (bf16[8,128,128]{2,1,0:T(8,128)(2,1)S(1)}, bf16[8,128,128]{2,1,0:T(8,128)(2,1)S(1)}, u32[]{:S(2)}, u32[]{:S(2)}) collective-permute-start(bf16[8,128,128]{2,1,0:T(8,128)(2,1)S(1)} %middle_sum.9.refs_2_), channel_id=1, source_target_pairs={{4,8},{5,9},{6,10},{7,11},{0,1},{2,3},{12,13},{14,15},{8,4},{9,5},... | collective-permute-start | bytes 786440 | tf_op jit(solution)/shard_map/ppermute | solution.py:346
  18.9 8.8 %collective-permute-start.12 = (bf16[8,128,128]{2,1,0:T(8,128)(2,1)S(1)}, bf16[8,128,128]{2,1,0:T(8,128)(2,1)S(1)}, u32[]{:S(2)}, u32[]{:S(2)}) collective-permute-start(bf16[8,128,128]{2,1,0:T(8,128)(2,1)S(1)} %cross_sum.8.refs_5_), channel_id=1, source_target_pairs={{0,2},{1,3},{2,0},{3,1},{4,6},{5,7},{6,4},{7,5},{8,10},{9,11},{10,... | collective-permute-start | bytes 786440 | tf_op jit(solution)/shard_map/ppermute | solution.py:316
  22.1 8.2 %collective-permute-start.11 = (bf16[8,128,128]{2,1,0:T(8,128)(2,1)S(1)}, bf16[8,128,128]{2,1,0:T(8,128)(2,1)S(1)}, u32[]{:S(2)}, u32[]{:S(2)}) collective-permute-start(bf16[8,128,128]{2,1,0:T(8,128)(2,1)S(1)} %side_sum.14.refs_2_), channel_id=1, source_target_pairs={{0,4},{12,8},{4,0},{8,12},{1,5},{13,9},{5,1},{9,13},{2,6},{14,10},... | collective-permute-start | bytes 786440 | tf_op jit(solution)/shard_map/ppermute | solution.py:341
  24.7 8.9 %collective-permute-start.10 = (bf16[8,128,128]{2,1,0:T(8,128)(2,1)S(1)}, bf16[8,128,128]{2,1,0:T(8,128)(2,1)S(1)}, u32[]{:S(2)}, u32[]{:S(2)}) collective-permute-start(bf16[8,128,128]{2,1,0:T(8,128)(2,1)S(1)} %middle_sum.10.refs_2_), channel_id=1, source_target_pairs={{4,8},{5,9},{6,10},{7,11},{0,1},{2,3},{12,13},{14,15},{8,4},{9,5},... | collective-permute-start | bytes 786440 | tf_op jit(solution)/shard_map/ppermute | solution.py:346
  24.9 8.8 %collective-permute-start.9 = (bf16[8,128,128]{2,1,0:T(8,128)(2,1)S(1)}, bf16[8,128,128]{2,1,0:T(8,128)(2,1)S(1)}, u32[]{:S(2)}, u32[]{:S(2)}) collective-permute-start(bf16[8,128,128]{2,1,0:T(8,128)(2,1)S(1)} %cross_sum.9.refs_5_), channel_id=1, source_target_pairs={{0,2},{1,3},{2,0},{3,1},{4,6},{5,7},{6,4},{7,5},{8,10},{9,11},{10,... | collective-permute-start | bytes 786440 | tf_op jit(solution)/shard_map/ppermute | solution.py:316
  27.9 8.2 %collective-permute-start.17 = (bf16[8,128,128]{2,1,0:T(8,128)(2,1)S(1)}, bf16[8,128,128]{2,1,0:T(8,128)(2,1)S(1)}, u32[]{:S(2)}, u32[]{:S(2)}) collective-permute-start(bf16[8,128,128]{2,1,0:T(8,128)(2,1)S(1)} %side_sum.15.refs_2_), channel_id=1, source_target_pairs={{0,4},{12,8},{4,0},{8,12},{1,5},{13,9},{5,1},{9,13},{2,6},{14,10},... | collective-permute-start | bytes 786440 | tf_op jit(solution)/shard_map/ppermute | solution.py:341
  30.5 8.9 %collective-permute-start.16 = (bf16[8,128,128]{2,1,0:T(8,128)(2,1)S(1)}, bf16[8,128,128]{2,1,0:T(8,128)(2,1)S(1)}, u32[]{:S(2)}, u32[]{:S(2)}) collective-permute-start(bf16[8,128,128]{2,1,0:T(8,128)(2,1)S(1)} %middle_sum.11.refs_2_), channel_id=1, source_target_pairs={{4,8},{5,9},{6,10},{7,11},{0,1},{2,3},{12,13},{14,15},{8,4},{9,5},... | collective-permute-start | bytes 786440 | tf_op jit(solution)/shard_map/ppermute | solution.py:346
  30.7 8.8 %collective-permute-start.15 = (bf16[8,128,128]{2,1,0:T(8,128)(2,1)S(1)}, bf16[8,128,128]{2,1,0:T(8,128)(2,1)S(1)}, u32[]{:S(2)}, u32[]{:S(2)}) collective-permute-start(bf16[8,128,128]{2,1,0:T(8,128)(2,1)S(1)} %cross_sum.10.refs_7_), channel_id=1, source_target_pairs={{0,2},{1,3},{2,0},{3,1},{4,6},{5,7},{6,4},{7,5},{8,10},{9,11},{10,... | collective-permute-start | bytes 786440 | tf_op jit(solution)/shard_map/ppermute | solution.py:316
  34.0 8.0 %collective-permute-start.14 = (bf16[8,128,128]{2,1,0:T(8,128)(2,1)S(1)}, bf16[8,128,128]{2,1,0:T(8,128)(2,1)S(1)}, u32[]{:S(2)}, u32[]{:S(2)}) collective-permute-start(bf16[8,128,128]{2,1,0:T(8,128)(2,1)S(1)} %side_sum.16.refs_2_), channel_id=1, source_target_pairs={{0,4},{12,8},{4,0},{8,12},{1,5},{13,9},{5,1},{9,13},{2,6},{14,10},... | collective-permute-start | bytes 786440 | tf_op jit(solution)/shard_map/ppermute | solution.py:341
  36.3 8.9 %collective-permute-start.21 = (bf16[8,128,128]{2,1,0:T(8,128)(2,1)S(1)}, bf16[8,128,128]{2,1,0:T(8,128)(2,1)S(1)}, u32[]{:S(2)}, u32[]{:S(2)}) collective-permute-start(bf16[8,128,128]{2,1,0:T(8,128)(2,1)S(1)} %middle_sum.12.refs_2_), channel_id=1, source_target_pairs={{4,8},{5,9},{6,10},{7,11},{0,1},{2,3},{12,13},{14,15},{8,4},{9,5},... | collective-permute-start | bytes 786440 | tf_op jit(solution)/shard_map/ppermute | solution.py:346
  36.5 8.8 %collective-permute-start.20 = (bf16[8,128,128]{2,1,0:T(8,128)(2,1)S(1)}, bf16[8,128,128]{2,1,0:T(8,128)(2,1)S(1)}, u32[]{:S(2)}, u32[]{:S(2)}) collective-permute-start(bf16[8,128,128]{2,1,0:T(8,128)(2,1)S(1)} %cross_sum.11.refs_7_), channel_id=1, source_target_pairs={{0,2},{1,3},{2,0},{3,1},{4,6},{5,7},{6,4},{7,5},{8,10},{9,11},{10,... | collective-permute-start | bytes 786440 | tf_op jit(solution)/shard_map/ppermute | solution.py:316
  39.8 8.2 %collective-permute-start.19 = (bf16[8,128,128]{2,1,0:T(8,128)(2,1)S(1)}, bf16[8,128,128]{2,1,0:T(8,128)(2,1)S(1)}, u32[]{:S(2)}, u32[]{:S(2)}) collective-permute-start(bf16[8,128,128]{2,1,0:T(8,128)(2,1)S(1)} %side_sum.17.refs_2_), channel_id=1, source_target_pairs={{0,4},{12,8},{4,0},{8,12},{1,5},{13,9},{5,1},{9,13},{2,6},{14,10},... | collective-permute-start | bytes 786440 | tf_op jit(solution)/shard_map/ppermute | solution.py:341
  42.2 8.0 %collective-permute-start.18 = (bf16[8,128,128]{2,1,0:T(8,128)(2,1)S(1)}, bf16[8,128,128]{2,1,0:T(8,128)(2,1)S(1)}, u32[]{:S(2)}, u32[]{:S(2)}) collective-permute-start(bf16[8,128,128]{2,1,0:T(8,128)(2,1)S(1)} %middle_sum.13.refs_7_), channel_id=1, source_target_pairs={{4,8},{5,9},{6,10},{7,11},{0,1},{2,3},{12,13},{14,15},{8,4},{9,5},... | collective-permute-start | bytes 786440 | tf_op jit(solution)/shard_map/ppermute | solution.py:346
  42.6 14.8 %collective-permute-start.24 = (bf16[8,128,128]{2,1,0:T(8,128)(2,1)S(1)}, bf16[8,128,128]{2,1,0:T(8,128)(2,1)S(1)}, u32[]{:S(2)}, u32[]{:S(2)}) collective-permute-start(bf16[8,128,128]{2,1,0:T(8,128)(2,1)S(1)} %late_sum.2.refs_7_.refs_1_), channel_id=1, source_target_pairs={{0,2},{1,3},{2,0},{3,1},{4,6},{5,7},{6,4},{7,5},{8,10},{9,11},{10,... | collective-permute-start | bytes 786440 | tf_op jit(solution)/shard_map/ppermute | solution.py:367
  45.6 8.3 %collective-permute-start.22 = (bf16[8,128,128]{2,1,0:T(8,128)(2,1)S(1)}, bf16[8,128,128]{2,1,0:T(8,128)(2,1)S(1)}, u32[]{:S(2)}, u32[]{:S(2)}) collective-permute-start(bf16[8,128,128]{2,1,0:T(8,128)(2,1)S(1)} %side_sum.18.refs_2_), channel_id=1, source_target_pairs={{0,4},{12,8},{4,0},{8,12},{1,5},{13,9},{5,1},{9,13},{2,6},{14,10},... | collective-permute-start | bytes 786440 | tf_op jit(solution)/shard_map/ppermute | solution.py:341
  48.2 6.0 %collective-permute-start.25 = (bf16[8,128,128]{2,1,0:T(8,128)(2,1)S(1)}, bf16[8,128,128]{2,1,0:T(8,128)(2,1)S(1)}, u32[]{:S(2)}, u32[]{:S(2)}) collective-permute-start(bf16[8,128,128]{2,1,0:T(8,128)(2,1)S(1)} %middle_sum.14.refs_7_), channel_id=1, source_target_pairs={{4,8},{5,9},{6,10},{7,11},{0,1},{2,3},{12,13},{14,15},{8,4},{9,5},... | collective-permute-start | bytes 786440 | tf_op jit(solution)/shard_map/ppermute | solution.py:346
  48.6 14.3 %collective-permute-start.30 = (bf16[8,128,128]{2,1,0:T(8,128)(2,1)S(1)}, bf16[8,128,128]{2,1,0:T(8,128)(2,1)S(1)}, u32[]{:S(2)}, u32[]{:S(2)}) collective-permute-start(bf16[8,128,128]{2,1,0:T(8,128)(2,1)S(1)} %late_sum.3.refs_4_.refs_1_), channel_id=1, source_target_pairs={{0,2},{1,3},{2,0},{3,1},{4,6},{5,7},{6,4},{7,5},{8,10},{9,11},{10,... | collective-permute-start | bytes 786440 | tf_op jit(solution)/shard_map/ppermute | solution.py:367
  50.4 13.7 %collective-permute-start.29 = (bf16[8,128,128]{2,1,0:T(8,128)(2,1)S(1)}, bf16[8,128,128]{2,1,0:T(8,128)(2,1)S(1)}, u32[]{:S(2)}, u32[]{:S(2)}) collective-permute-start(bf16[8,128,128]{2,1,0:T(8,128)(2,1)S(1)} %side_sum.19.refs_2_), channel_id=1, source_target_pairs={{0,4},{12,8},{4,0},{8,12},{1,5},{13,9},{5,1},{9,13},{2,6},{14,10},... | collective-permute-start | bytes 786440 | tf_op jit(solution)/shard_map/ppermute | solution.py:341
  54.1 3.9 %collective-permute-start.23 = (bf16[8,128,128]{2,1,0:T(8,128)(2,1)S(1)}, bf16[8,128,128]{2,1,0:T(8,128)(2,1)S(1)}, u32[]{:S(2)}, u32[]{:S(2)}) collective-permute-start(bf16[8,128,128]{2,1,0:T(8,128)(2,1)S(1)} %middle_sum.15.refs_4_), channel_id=1, source_target_pairs={{4,8},{5,9},{6,10},{7,11},{0,1},{2,3},{12,13},{14,15},{8,4},{9,5},... | collective-permute-start | bytes 786440 | tf_op jit(solution)/shard_map/ppermute | solution.py:346
  54.4 11.8 %collective-permute-start.28 = (bf16[8,128,128]{2,1,0:T(8,128)(2,1)S(1)}, bf16[8,128,128]{2,1,0:T(8,128)(2,1)S(1)}, u32[]{:S(2)}, u32[]{:S(2)}) collective-permute-start(bf16[8,128,128]{2,1,0:T(8,128)(2,1)S(1)} %side_sum.20.refs_2_), channel_id=1, source_target_pairs={{0,4},{12,8},{4,0},{8,12},{1,5},{13,9},{5,1},{9,13},{2,6},{14,10},... | collective-permute-start | bytes 786440 | tf_op jit(solution)/shard_map/ppermute | solution.py:341
  57.5 9.2 %collective-permute-start.27 = (bf16[8,128,128]{2,1,0:T(8,128)(2,1)S(1)}, bf16[8,128,128]{2,1,0:T(8,128)(2,1)S(1)}, u32[]{:S(2)}, u32[]{:S(2)}) collective-permute-start(bf16[8,128,128]{2,1,0:T(8,128)(2,1)S(1)} %late_swap.2.refs_7_), channel_id=1, source_target_pairs={{0,1},{2,3},{1,0},{3,2},{4,5},{6,7},{5,4},{7,6},{8,9},{10,11},{9,8... | collective-permute-start | bytes 786440 | tf_op jit(solution)/shard_map/ppermute | solution.py:373
  58.2 12.2 %collective-permute-start.26 = (bf16[8,128,128]{2,1,0:T(8,128)(2,1)S(1)}, bf16[8,128,128]{2,1,0:T(8,128)(2,1)S(1)}, u32[]{:S(2)}, u32[]{:S(2)}) collective-permute-start(bf16[8,128,128]{2,1,0:T(8,128)(2,1)S(1)} %side_sum.21.refs_2_), channel_id=1, source_target_pairs={{0,4},{12,8},{4,0},{8,12},{1,5},{13,9},{5,1},{9,13},{2,6},{14,10},... | collective-permute-start | bytes 786440 | tf_op jit(solution)/shard_map/ppermute | solution.py:341
  63.0 4.1 %collective-permute-start.31 = (bf16[8,128,128]{2,1,0:T(8,128)(2,1)S(1)}, bf16[8,128,128]{2,1,0:T(8,128)(2,1)S(1)}, u32[]{:S(2)}, u32[]{:S(2)}) collective-permute-start(bf16[8,128,128]{2,1,0:T(8,128)(2,1)S(1)} %late_swap.3.refs_7_), channel_id=1, source_target_pairs={{0,1},{2,3},{1,0},{3,2},{4,5},{6,7},{5,4},{7,6},{8,9},{10,11},{9,8... | collective-permute-start | bytes 786440 | tf_op jit(solution)/shard_map/ppermute | solution.py:373
  (4 other events, 13.0 us)

commit v8 on v7

--- a/solution.py
+++ b/solution.py
@@ -196,18 +196,28 @@
         mean_sq = jnp.sum(squares, axis=1, keepdims=True) / width
         scale = jnp.broadcast_to(lax.rsqrt(mean_sq + 1e-06), (rows, DH))
         copies = []
+
+        def send(start, wide):
+            part = pl.ds(start, wide)
+            copy = pltpu.make_async_copy(
+                done_ref.at[:, part], out_hbm.at[0, :, part], sem.at[len(copies)]
+            )
+            copy.start()
+            copies.append(copy)
+
         for i, start in enumerate(starts):
             wide = count * DH if i == n else attn_refs[i].shape[1]
+            half = wide // DH // 2
             for h in range(wide // DH):
+                if i == n and h == half:
+                    send(start, half * DH)
                 cols = slice(start + h * DH, start + (h + 1) * DH)
                 attn = last[h] if i == n else attn_refs[i][:, head_cols(h)]
                 done_ref[:, cols] = (attn.astype(F32) * scale * gain_ref[:, cols]).astype(BF16)
-            part = pl.ds(start, wide)
-            copy = pltpu.make_async_copy(
-                done_ref.at[:, part], out_hbm.at[0, :, part], sem.at[i]
-            )
-            copy.start()
-            copies.append(copy)
+            if i == n:
+                send(start + half * DH, wide - half * DH)
+            else:
+                send(start, wide)
         for copy in copies:
             copy.wait()
 
@@ -217,7 +227,7 @@
         in_specs=[VMEM] * len(operands),
         out_specs=pl.BlockSpec(memory_space=pltpu.HBM),
         out_shape=jax.ShapeDtypeStruct((1, rows, width), BF16),
-        scratch_shapes=[pltpu.VMEM((rows, width), BF16), pltpu.SemaphoreType.DMA((n + 1,))],
+        scratch_shapes=[pltpu.VMEM((rows, width), BF16), pltpu.SemaphoreType.DMA((n + 2,))],
         compiler_params=pltpu.CompilerParams(vmem_limit_bytes=VMEM_LIMIT),
         cost_estimate=pl.CostEstimate(flops=COST, bytes_accessed=1, transcendentals=0),
         name="last_attend",

time: 72.8 us -> 72.8 us (level)
  no operation moved by 1% of the time
where the time goes in v8:
time: 72.8 us; the launch traced here: 72.7 us
  starting transfers between devices  39.9 us (55%)
  waiting for transfers between devices  15.7 us (22%)
  Pallas kernels  14.8 us (20%)
  local copies, waits for them, and re-layouts  1.52 us (2%)
  between operations  0.74 us (1%)
    ppermute x11, starting transfers between devices, side(): self.a[t] = (lax.ppermute(send, 'head', both_ways([(0, 1), (3, 2)])), 0)  24.8 us
    pallas_call x49, Pallas kernels, call(): pl.pallas_call(run, in_specs=[VMEM] * n_in + [ANY] * n_after, out_specs=[...  12.8 us
    ppermute x6, starting transfers between devices, cross(): self.x[c] = (lax.ppermute(send, 'ctx', self.across), 0)  10.2 us
    ppermute x11, waiting for transfers between devices, side(): self.a[t] = (lax.ppermute(send, 'head', both_ways([(0, 1), (3, 2)])), 0)  7.92 us
    ppermute x6, waiting for transfers between devices, cross(): self.x[c] = (lax.ppermute(send, 'ctx', self.across), 0)  7.72 us
    ppermute x2, starting transfers between devices, late_cross(): self.late[c] = (lax.ppermute(send, 'ctx', self.across), 0)  3.2 us
    pallas_call x1, Pallas kernels, last_attend(): pl.pallas_call(kernel, in_specs=[VMEM] * len(operands), out_specs=pl.Bloc...  2.05 us
    slice x1, local copies, waits for them, and re-layouts, kv(): k, v, at = (k[:, cols], v[:, cols], 0)  1.49 us
  transfers between devices with their start and end apart: 32, of which 12 were waited for; matrix products, arithmetic and copies ran while one was open for 0% of the time, Pallas kernels for 17%

profile of v8, /device:TPU:0, one launch (start us, length us, event | category | flops | bytes accessed | tf_op | source)
XLA Modules:
  0.0 72.7 jit_solution(10127093563677539510)
XLA Ops:
  0.0 1.5 %fusion = (bf16[128,1024]{1,0:T(8,128)(2,1)S(1)}, bf16[128,1024]{1,0:T(8,128)(2,1)S(1)}, bf16[128,1024]{1,0:T(8,128)(2,1)S(1)}, bf16[128,1024]{1,0:T(8,128)(2,1)...) fusion(bf16[128,8192]{1,0:T(8,128)(2,1)} %bitcast.7, bf16[128,8192]{1,0:T(8,128)(2,1)} %bitcast.4), kind=kLoop, calls=%fused_computation | loop fusion | bytes 3145728 | tf_op jit(solution)/shard_map/slice | solution.py:419
  1.8 0.5 collective-permute-start
  2.8 2.7 %collective-permute-start.4 = (bf16[8,128,128]{2,1,0:T(8,128)(2,1)S(1)}, bf16[8,128,128]{2,1,0:T(8,128)(2,1)S(1)}, u32[]{:S(2)}, u32[]{:S(2)}) collective-permute-start(bf16[8,128,128]{2,1,0:T(8,128)(2,1)S(1)} %side_sum.11.refs_2_), channel_id=1, source_target_pairs={{0,4},{12,8},{4,0},{8,12},{1,5},{13,9},{5,1},{9,13},{2,6},{14,10},... | collective-permute-start | bytes 786440 | tf_op jit(solution)/shard_map/ppermute | solution.py:351
  6.4 0.9 %kv_states.9 = (bf16[32,128,128]{2,1,0:T(8,128)(2,1)S(1)}, bf16[128,4096]{1,0:T(8,128)(2,1)S(1)}) custom-call(bf16[128,8192]{1,0:T(8,128)(2,1)S(1)} %bitcast.6, bf16[128,8192]{1,0:T(8,128)(2,1)S(1)} %bitcast.9, bf16[8,128,128]{2,1,0:T(8,128)(2,1)S(1)} %get-tuple-element.32.refs_2_.refs_0_.refs_5_), custom_call_target="tpu_custom_call" | custom-call | flops 1000000 | bytes 1 | tf_op jit(solution)/shard_map/kv_states/pallas_call | solution.py:31
  7.6 1.8 %collective-permute-start.2 = (bf16[8,128,128]{2,1,0:T(8,128)(2,1)S(1)}, bf16[8,128,128]{2,1,0:T(8,128)(2,1)S(1)}, u32[]{:S(2)}, u32[]{:S(2)}) collective-permute-start(bf16[8,128,128]{2,1,0:T(8,128)(2,1)S(1)} %cross_sum.6.refs_2_), channel_id=1, source_target_pairs={{0,2},{1,3},{2,0},{3,1},{4,6},{5,7},{6,4},{7,5},{8,10},{9,11},{10,... | collective-permute-start | bytes 786440 | tf_op jit(solution)/shard_map/ppermute | solution.py:326
  9.8 2.8 %collective-permute-done.4.refs_1_.refs_0_.refs_6_.refs_2_ = bf16[8,128,128]{2,1,0:T(8,128)(2,1)S(1)} collective-permute-done((bf16[8,128,128]{2,1,0:T(8,128)(2,1)S(1)}, bf16[8,128,128]{2,1,0:T(8,128)(2,1)S(1)}, u32[]{:S(2)}, u32[]{:S(2)}) %collective-permute-start.4) | collective-permute-done | bytes 262176 | tf_op jit(solution)/shard_map/ppermute | solution.py:351
  12.8 1.9 %collective-permute-start.6 = (bf16[8,128,128]{2,1,0:T(8,128)(2,1)S(1)}, bf16[8,128,128]{2,1,0:T(8,128)(2,1)S(1)}, u32[]{:S(2)}, u32[]{:S(2)}) collective-permute-start(bf16[8,128,128]{2,1,0:T(8,128)(2,1)S(1)} %cross_sum.7.refs_3_), channel_id=1, source_target_pairs={{0,2},{1,3},{2,0},{3,1},{4,6},{5,7},{6,4},{7,5},{8,10},{9,11},{10,... | collective-permute-start | bytes 786440 | tf_op jit(solution)/shard_map/ppermute | solution.py:326
  14.7 1.6 %collective-permute-done.2.refs_1_.refs_4_.refs_3_ = bf16[8,128,128]{2,1,0:T(8,128)(2,1)S(1)} collective-permute-done((bf16[8,128,128]{2,1,0:T(8,128)(2,1)S(1)}, bf16[8,128,128]{2,1,0:T(8,128)(2,1)S(1)}, u32[]{:S(2)}, u32[]{:S(2)}) %collective-permute-start.2) | collective-permute-done | bytes 262176 | tf_op jit(solution)/shard_map/ppermute | solution.py:326
  16.5 1.8 %collective-permute-start.5 = (bf16[8,128,128]{2,1,0:T(8,128)(2,1)S(1)}, bf16[8,128,128]{2,1,0:T(8,128)(2,1)S(1)}, u32[]{:S(2)}, u32[]{:S(2)}) collective-permute-start(bf16[8,128,128]{2,1,0:T(8,128)(2,1)S(1)} %side_sum.13.refs_2_), channel_id=1, source_target_pairs={{0,4},{12,8},{4,0},{8,12},{1,5},{13,9},{5,1},{9,13},{2,6},{14,10},... | collective-permute-start | bytes 786440 | tf_op jit(solution)/shard_map/ppermute | solution.py:351
  18.9 1.6 %collective-permute-start.12 = (bf16[8,128,128]{2,1,0:T(8,128)(2,1)S(1)}, bf16[8,128,128]{2,1,0:T(8,128)(2,1)S(1)}, u32[]{:S(2)}, u32[]{:S(2)}) collective-permute-start(bf16[8,128,128]{2,1,0:T(8,128)(2,1)S(1)} %cross_sum.8.refs_5_), channel_id=1, source_target_pairs={{0,2},{1,3},{2,0},{3,1},{4,6},{5,7},{6,4},{7,5},{8,10},{9,11},{10,... | collective-permute-start | bytes 786440 | tf_op jit(solution)/shard_map/ppermute | solution.py:326
  20.4 1.4 %collective-permute-done.6.refs_1_.refs_4_.refs_3_ = bf16[8,128,128]{2,1,0:T(8,128)(2,1)S(1)} collective-permute-done((bf16[8,128,128]{2,1,0:T(8,128)(2,1)S(1)}, bf16[8,128,128]{2,1,0:T(8,128)(2,1)S(1)}, u32[]{:S(2)}, u32[]{:S(2)}) %collective-permute-start.6) | collective-permute-done | bytes 262176 | tf_op jit(solution)/shard_map/ppermute | solution.py:326
  22.1 1.9 %collective-permute-start.11 = (bf16[8,128,128]{2,1,0:T(8,128)(2,1)S(1)}, bf16[8,128,128]{2,1,0:T(8,128)(2,1)S(1)}, u32[]{:S(2)}, u32[]{:S(2)}) collective-permute-start(bf16[8,128,128]{2,1,0:T(8,128)(2,1)S(1)} %side_sum.14.refs_2_), channel_id=1, source_target_pairs={{0,4},{12,8},{4,0},{8,12},{1,5},{13,9},{5,1},{9,13},{2,6},{14,10},... | collective-permute-start | bytes 786440 | tf_op jit(solution)/shard_map/ppermute | solution.py:351
  24.9 1.7 %collective-permute-start.9 = (bf16[8,128,128]{2,1,0:T(8,128)(2,1)S(1)}, bf16[8,128,128]{2,1,0:T(8,128)(2,1)S(1)}, u32[]{:S(2)}, u32[]{:S(2)}) collective-permute-start(bf16[8,128,128]{2,1,0:T(8,128)(2,1)S(1)} %cross_sum.9.refs_5_), channel_id=1, source_target_pairs={{0,2},{1,3},{2,0},{3,1},{4,6},{5,7},{6,4},{7,5},{8,10},{9,11},{10,... | collective-permute-start | bytes 786440 | tf_op jit(solution)/shard_map/ppermute | solution.py:326
  26.6 1.1 %collective-permute-done.12.refs_1_.refs_4_.refs_3_ = bf16[8,128,128]{2,1,0:T(8,128)(2,1)S(1)} collective-permute-done((bf16[8,128,128]{2,1,0:T(8,128)(2,1)S(1)}, bf16[8,128,128]{2,1,0:T(8,128)(2,1)S(1)}, u32[]{:S(2)}, u32[]{:S(2)}) %collective-permute-start.12) | collective-permute-done | bytes 262176 | tf_op jit(solution)/shard_map/ppermute | solution.py:326
  27.9 2.1 %collective-permute-start.17 = (bf16[8,128,128]{2,1,0:T(8,128)(2,1)S(1)}, bf16[8,128,128]{2,1,0:T(8,128)(2,1)S(1)}, u32[]{:S(2)}, u32[]{:S(2)}) collective-permute-start(bf16[8,128,128]{2,1,0:T(8,128)(2,1)S(1)} %side_sum.15.refs_2_), channel_id=1, source_target_pairs={{0,4},{12,8},{4,0},{8,12},{1,5},{13,9},{5,1},{9,13},{2,6},{14,10},... | collective-permute-start | bytes 786440 | tf_op jit(solution)/shard_map/ppermute | solution.py:351
  30.7 1.7 %collective-permute-start.15 = (bf16[8,128,128]{2,1,0:T(8,128)(2,1)S(1)}, bf16[8,128,128]{2,1,0:T(8,128)(2,1)S(1)}, u32[]{:S(2)}, u32[]{:S(2)}) collective-permute-start(bf16[8,128,128]{2,1,0:T(8,128)(2,1)S(1)} %cross_sum.10.refs_7_), channel_id=1, source_target_pairs={{0,2},{1,3},{2,0},{3,1},{4,6},{5,7},{6,4},{7,5},{8,10},{9,11},{10,... | collective-permute-start | bytes 786440 | tf_op jit(solution)/shard_map/ppermute | solution.py:326
  32.4 1.2 %collective-permute-done.9.refs_1_.refs_3_ = bf16[8,128,128]{2,1,0:T(8,128)(2,1)S(1)} collective-permute-done((bf16[8,128,128]{2,1,0:T(8,128)(2,1)S(1)}, bf16[8,128,128]{2,1,0:T(8,128)(2,1)S(1)}, u32[]{:S(2)}, u32[]{:S(2)}) %collective-permute-start.9) | collective-permute-done | bytes 262176 | tf_op jit(solution)/shard_map/ppermute | solution.py:326
  34.0 1.8 %collective-permute-start.14 = (bf16[8,128,128]{2,1,0:T(8,128)(2,1)S(1)}, bf16[8,128,128]{2,1,0:T(8,128)(2,1)S(1)}, u32[]{:S(2)}, u32[]{:S(2)}) collective-permute-start(bf16[8,128,128]{2,1,0:T(8,128)(2,1)S(1)} %side_sum.16.refs_2_), channel_id=1, source_target_pairs={{0,4},{12,8},{4,0},{8,12},{1,5},{13,9},{5,1},{9,13},{2,6},{14,10},... | collective-permute-start | bytes 786440 | tf_op jit(solution)/shard_map/ppermute | solution.py:351
  36.5 1.6 %collective-permute-start.20 = (bf16[8,128,128]{2,1,0:T(8,128)(2,1)S(1)}, bf16[8,128,128]{2,1,0:T(8,128)(2,1)S(1)}, u32[]{:S(2)}, u32[]{:S(2)}) collective-permute-start(bf16[8,128,128]{2,1,0:T(8,128)(2,1)S(1)} %cross_sum.11.refs_7_), channel_id=1, source_target_pairs={{0,2},{1,3},{2,0},{3,1},{4,6},{5,7},{6,4},{7,5},{8,10},{9,11},{10,... | collective-permute-start | bytes 786440 | tf_op jit(solution)/shard_map/ppermute | solution.py:326
  38.0 1.4 %collective-permute-done.15.refs_1_.refs_3_ = bf16[8,128,128]{2,1,0:T(8,128)(2,1)S(1)} collective-permute-done((bf16[8,128,128]{2,1,0:T(8,128)(2,1)S(1)}, bf16[8,128,128]{2,1,0:T(8,128)(2,1)S(1)}, u32[]{:S(2)}, u32[]{:S(2)}) %collective-permute-start.15) | collective-permute-done | bytes 262176 | tf_op jit(solution)/shard_map/ppermute | solution.py:326
  39.8 1.7 %collective-permute-start.19 = (bf16[8,128,128]{2,1,0:T(8,128)(2,1)S(1)}, bf16[8,128,128]{2,1,0:T(8,128)(2,1)S(1)}, u32[]{:S(2)}, u32[]{:S(2)}) collective-permute-start(bf16[8,128,128]{2,1,0:T(8,128)(2,1)S(1)} %side_sum.17.refs_2_), channel_id=1, source_target_pairs={{0,4},{12,8},{4,0},{8,12},{1,5},{13,9},{5,1},{9,13},{2,6},{14,10},... | collective-permute-start | bytes 786440 | tf_op jit(solution)/shard_map/ppermute | solution.py:351
  42.6 1.7 %collective-permute-start.24 = (bf16[8,128,128]{2,1,0:T(8,128)(2,1)S(1)}, bf16[8,128,128]{2,1,0:T(8,128)(2,1)S(1)}, u32[]{:S(2)}, u32[]{:S(2)}) collective-permute-start(bf16[8,128,128]{2,1,0:T(8,128)(2,1)S(1)} %late_sum.2.refs_7_.refs_1_), channel_id=1, source_target_pairs={{0,2},{1,3},{2,0},{3,1},{4,6},{5,7},{6,4},{7,5},{8,10},{9,11},{10,... | collective-permute-start | bytes 786440 | tf_op jit(solution)/shard_map/ppermute | solution.py:377
  44.3 0.9 %collective-permute-done.20.refs_1_.refs_3_ = bf16[8,128,128]{2,1,0:T(8,128)(2,1)S(1)} collective-permute-done((bf16[8,128,128]{2,1,0:T(8,128)(2,1)S(1)}, bf16[8,128,128]{2,1,0:T(8,128)(2,1)S(1)}, u32[]{:S(2)}, u32[]{:S(2)}) %collective-permute-start.20) | collective-permute-done | bytes 262176 | tf_op jit(solution)/shard_map/ppermute | solution.py:326
  45.6 2.1 %collective-permute-start.22 = (bf16[8,128,128]{2,1,0:T(8,128)(2,1)S(1)}, bf16[8,128,128]{2,1,0:T(8,128)(2,1)S(1)}, u32[]{:S(2)}, u32[]{:S(2)}) collective-permute-start(bf16[8,128,128]{2,1,0:T(8,128)(2,1)S(1)} %side_sum.18.refs_2_), channel_id=1, source_target_pairs={{0,4},{12,8},{4,0},{8,12},{1,5},{13,9},{5,1},{9,13},{2,6},{14,10},... | collective-permute-start | bytes 786440 | tf_op jit(solution)/shard_map/ppermute | solution.py:351
  48.6 1.5 %collective-permute-start.30 = (bf16[8,128,128]{2,1,0:T(8,128)(2,1)S(1)}, bf16[8,128,128]{2,1,0:T(8,128)(2,1)S(1)}, u32[]{:S(2)}, u32[]{:S(2)}) collective-permute-start(bf16[8,128,128]{2,1,0:T(8,128)(2,1)S(1)} %late_sum.3.refs_4_.refs_1_), channel_id=1, source_target_pairs={{0,2},{1,3},{2,0},{3,1},{4,6},{5,7},{6,4},{7,5},{8,10},{9,11},{10,... | collective-permute-start | bytes 786440 | tf_op jit(solution)/shard_map/ppermute | solution.py:377
  50.4 3.0 %collective-permute-start.29 = (bf16[8,128,128]{2,1,0:T(8,128)(2,1)S(1)}, bf16[8,128,128]{2,1,0:T(8,128)(2,1)S(1)}, u32[]{:S(2)}, u32[]{:S(2)}) collective-permute-start(bf16[8,128,128]{2,1,0:T(8,128)(2,1)S(1)} %side_sum.19.refs_2_), channel_id=1, source_target_pairs={{0,4},{12,8},{4,0},{8,12},{1,5},{13,9},{5,1},{9,13},{2,6},{14,10},... | collective-permute-start | bytes 786440 | tf_op jit(solution)/shard_map/ppermute | solution.py:351
  54.4 3.0 %collective-permute-start.28 = (bf16[8,128,128]{2,1,0:T(8,128)(2,1)S(1)}, bf16[8,128,128]{2,1,0:T(8,128)(2,1)S(1)}, u32[]{:S(2)}, u32[]{:S(2)}) collective-permute-start(bf16[8,128,128]{2,1,0:T(8,128)(2,1)S(1)} %side_sum.20.refs_2_), channel_id=1, source_target_pairs={{0,4},{12,8},{4,0},{8,12},{1,5},{13,9},{5,1},{9,13},{2,6},{14,10},... | collective-permute-start | bytes 786440 | tf_op jit(solution)/shard_map/ppermute | solution.py:351
  58.2 4.7 %collective-permute-start.26 = (bf16[8,128,128]{2,1,0:T(8,128)(2,1)S(1)}, bf16[8,128,128]{2,1,0:T(8,128)(2,1)S(1)}, u32[]{:S(2)}, u32[]{:S(2)}) collective-permute-start(bf16[8,128,128]{2,1,0:T(8,128)(2,1)S(1)} %side_sum.21.refs_2_), channel_id=1, source_target_pairs={{0,4},{12,8},{4,0},{8,12},{1,5},{13,9},{5,1},{9,13},{2,6},{14,10},... | collective-permute-start | bytes 786440 | tf_op jit(solution)/shard_map/ppermute | solution.py:351
  63.6 0.5 attend.9
  64.5 1.7 %collective-permute-done.28.refs_6_ = bf16[8,128,128]{2,1,0:T(8,128)(2,1)S(1)} collective-permute-done((bf16[8,128,128]{2,1,0:T(8,128)(2,1)S(1)}, bf16[8,128,128]{2,1,0:T(8,128)(2,1)S(1)}, u32[]{:S(2)}, u32[]{:S(2)}) %collective-permute-start.28) | collective-permute-done | bytes 262176 | tf_op jit(solution)/shard_map/ppermute | solution.py:351
  67.6 2.9 %collective-permute-done.26.refs_6_ = bf16[8,128,128]{2,1,0:T(8,128)(2,1)S(1)} collective-permute-done((bf16[8,128,128]{2,1,0:T(8,128)(2,1)S(1)}, bf16[8,128,128]{2,1,0:T(8,128)(2,1)S(1)}, u32[]{:S(2)}, u32[]{:S(2)}) %collective-permute-start.26) | collective-permute-done | bytes 262176 | tf_op jit(solution)/shard_map/ppermute | solution.py:351
  70.5 2.0 %last_attend.1 = bf16[1,128,8192]{2,1,0:T(8,128)(2,1)} custom-call(bf16[128,2048]{1,0:T(8,128)(2,1)S(1)} %local_scores.15.refs_4_.refs_0_, bf16[128,8192]{1,0:T(8,128)(2,1)S(1)} %bitcast.17, bf16[32,128,128]{2,1,0:T(8,128)(2,1)S(1)} %collective-permute-done.1.refs_1_.refs_0_.refs_3_.refs_2_, ...), custom_call_target="tpu_custom_call" | custom-call | flops 3000000000 | bytes 1 | tf_op jit(solution)/shard_map/last_attend/pallas_call | solution.py:225
  (91 shorter events, 13.3 us)
Async XLA Ops:
  1.8 4.1 %collective-permute-start = (bf16[8,128,128]{2,1,0:T(8,128)(2,1)S(1)}, bf16[8,128,128]{2,1,0:T(8,128)(2,1)S(1)}, u32[]{:S(2)}, u32[]{:S(2)}) collective-permute-start(bf16[8,128,128]{2,1,0:T(8,128)(2,1)S(1)} %get-tuple-element.29.refs_2_.refs_0_.refs_5_), channel_id=1, source_target_pairs={{0,1},{2,3},{1,0},{3,2},{4,5},{6,7},{5,4},{7,6},{8,9},{10,11},{9,8... | collective-permute-start | bytes 786440 | tf_op jit(solution)/shard_map/ppermute | solution.py:318
  2.8 9.8 %collective-permute-start.4 = (bf16[8,128,128]{2,1,0:T(8,128)(2,1)S(1)}, bf16[8,128,128]{2,1,0:T(8,128)(2,1)S(1)}, u32[]{:S(2)}, u32[]{:S(2)}) collective-permute-start(bf16[8,128,128]{2,1,0:T(8,128)(2,1)S(1)} %side_sum.11.refs_2_), channel_id=1, source_target_pairs={{0,4},{12,8},{4,0},{8,12},{1,5},{13,9},{5,1},{9,13},{2,6},{14,10},... | collective-permute-start | bytes 786440 | tf_op jit(solution)/shard_map/ppermute | solution.py:351
  5.8 12.8 %collective-permute-start.8 = (bf16[8,128,128]{2,1,0:T(8,128)(2,1)S(1)}, bf16[8,128,128]{2,1,0:T(8,128)(2,1)S(1)}, u32[]{:S(2)}, u32[]{:S(2)}) collective-permute-start(bf16[8,128,128]{2,1,0:T(8,128)(2,1)S(1)} %side_sum.12.refs_2_), channel_id=1, source_target_pairs={{0,4},{12,8},{4,0},{8,12},{1,5},{13,9},{5,1},{9,13},{2,6},{14,10},... | collective-permute-start | bytes 786440 | tf_op jit(solution)/shard_map/ppermute | solution.py:351
  7.3 5.4 %collective-permute-start.3 = (bf16[8,128,128]{2,1,0:T(8,128)(2,1)S(1)}, bf16[8,128,128]{2,1,0:T(8,128)(2,1)S(1)}, u32[]{:S(2)}, u32[]{:S(2)}) collective-permute-start(bf16[8,128,128]{2,1,0:T(8,128)(2,1)S(1)} %get-tuple-element.32.refs_2_.refs_0_.refs_5_), channel_id=1, source_target_pairs={{0,1},{2,3},{1,0},{3,2},{4,5},{6,7},{5,4},{7,6},{8,9},{10,11},{9,8... | collective-permute-start | bytes 786440 | tf_op jit(solution)/shard_map/ppermute | solution.py:318
  7.6 8.8 %collective-permute-start.2 = (bf16[8,128,128]{2,1,0:T(8,128)(2,1)S(1)}, bf16[8,128,128]{2,1,0:T(8,128)(2,1)S(1)}, u32[]{:S(2)}, u32[]{:S(2)}) collective-permute-start(bf16[8,128,128]{2,1,0:T(8,128)(2,1)S(1)} %cross_sum.6.refs_2_), channel_id=1, source_target_pairs={{0,2},{1,3},{2,0},{3,1},{4,6},{5,7},{6,4},{7,5},{8,10},{9,11},{10,... | collective-permute-start | bytes 786440 | tf_op jit(solution)/shard_map/ppermute | solution.py:326
  9.3 9.4 %collective-permute-start.1 = (bf16[32,128,128]{2,1,0:T(8,128)(2,1)S(1)}, bf16[32,128,128]{2,1,0:T(8,128)(2,1)S(1)}, u32[]{:S(2)}, u32[]{:S(2)}) collective-permute-start(bf16[32,128,128]{2,1,0:T(8,128)(2,1)S(1)} %get-tuple-element.34.refs_2_.refs_0_.refs_5_), channel_id=1, source_target_pairs={{0,1},{2,3},{1,0},{3,2},{4,5},{6,7},{5,4},{7,6},{8,9},{10,11},{9,8... | collective-permute-start | bytes 3145736 | tf_op jit(solution)/shard_map/ppermute | solution.py:318
  12.7 7.8 %collective-permute-start.7 = (bf16[8,128,128]{2,1,0:T(8,128)(2,1)S(1)}, bf16[8,128,128]{2,1,0:T(8,128)(2,1)S(1)}, u32[]{:S(2)}, u32[]{:S(2)}) collective-permute-start(bf16[8,128,128]{2,1,0:T(8,128)(2,1)S(1)} %middle_sum.8.refs_2_), channel_id=1, source_target_pairs={{4,8},{5,9},{6,10},{7,11},{0,1},{2,3},{12,13},{14,15},{8,4},{9,5},... | collective-permute-start | bytes 786440 | tf_op jit(solution)/shard_map/ppermute | solution.py:356
  12.8 9.1 %collective-permute-start.6 = (bf16[8,128,128]{2,1,0:T(8,128)(2,1)S(1)}, bf16[8,128,128]{2,1,0:T(8,128)(2,1)S(1)}, u32[]{:S(2)}, u32[]{:S(2)}) collective-permute-start(bf16[8,128,128]{2,1,0:T(8,128)(2,1)S(1)} %cross_sum.7.refs_3_), channel_id=1, source_target_pairs={{0,2},{1,3},{2,0},{3,1},{4,6},{5,7},{6,4},{7,5},{8,10},{9,11},{10,... | collective-permute-start | bytes 786440 | tf_op jit(solution)/shard_map/ppermute | solution.py:326
  16.5 8.0 %collective-permute-start.5 = (bf16[8,128,128]{2,1,0:T(8,128)(2,1)S(1)}, bf16[8,128,128]{2,1,0:T(8,128)(2,1)S(1)}, u32[]{:S(2)}, u32[]{:S(2)}) collective-permute-start(bf16[8,128,128]{2,1,0:T(8,128)(2,1)S(1)} %side_sum.13.refs_2_), channel_id=1, source_target_pairs={{0,4},{12,8},{4,0},{8,12},{1,5},{13,9},{5,1},{9,13},{2,6},{14,10},... | collective-permute-start | bytes 786440 | tf_op jit(solution)/shard_map/ppermute | solution.py:351
  18.7 7.8 %collective-permute-start.13 = (bf16[8,128,128]{2,1,0:T(8,128)(2,1)S(1)}, bf16[8,128,128]{2,1,0:T(8,128)(2,1)S(1)}, u32[]{:S(2)}, u32[]{:S(2)}) collective-permute-start(bf16[8,128,128]{2,1,0:T(8,128)(2,1)S(1)} %middle_sum.9.refs_2_), channel_id=1, source_target_pairs={{4,8},{5,9},{6,10},{7,11},{0,1},{2,3},{12,13},{14,15},{8,4},{9,5},... | collective-permute-start | bytes 786440 | tf_op jit(solution)/shard_map/ppermute | solution.py:356
  18.9 8.8 %collective-permute-start.12 = (bf16[8,128,128]{2,1,0:T(8,128)(2,1)S(1)}, bf16[8,128,128]{2,1,0:T(8,128)(2,1)S(1)}, u32[]{:S(2)}, u32[]{:S(2)}) collective-permute-start(bf16[8,128,128]{2,1,0:T(8,128)(2,1)S(1)} %cross_sum.8.refs_5_), channel_id=1, source_target_pairs={{0,2},{1,3},{2,0},{3,1},{4,6},{5,7},{6,4},{7,5},{8,10},{9,11},{10,... | collective-permute-start | bytes 786440 | tf_op jit(solution)/shard_map/ppermute | solution.py:326
  22.1 8.2 %collective-permute-start.11 = (bf16[8,128,128]{2,1,0:T(8,128)(2,1)S(1)}, bf16[8,128,128]{2,1,0:T(8,128)(2,1)S(1)}, u32[]{:S(2)}, u32[]{:S(2)}) collective-permute-start(bf16[8,128,128]{2,1,0:T(8,128)(2,1)S(1)} %side_sum.14.refs_2_), channel_id=1, source_target_pairs={{0,4},{12,8},{4,0},{8,12},{1,5},{13,9},{5,1},{9,13},{2,6},{14,10},... | collective-permute-start | bytes 786440 | tf_op jit(solution)/shard_map/ppermute | solution.py:351
  24.7 8.9 %collective-permute-start.10 = (bf16[8,128,128]{2,1,0:T(8,128)(2,1)S(1)}, bf16[8,128,128]{2,1,0:T(8,128)(2,1)S(1)}, u32[]{:S(2)}, u32[]{:S(2)}) collective-permute-start(bf16[8,128,128]{2,1,0:T(8,128)(2,1)S(1)} %middle_sum.10.refs_2_), channel_id=1, source_target_pairs={{4,8},{5,9},{6,10},{7,11},{0,1},{2,3},{12,13},{14,15},{8,4},{9,5},... | collective-permute-start | bytes 786440 | tf_op jit(solution)/shard_map/ppermute | solution.py:356
  24.9 8.8 %collective-permute-start.9 = (bf16[8,128,128]{2,1,0:T(8,128)(2,1)S(1)}, bf16[8,128,128]{2,1,0:T(8,128)(2,1)S(1)}, u32[]{:S(2)}, u32[]{:S(2)}) collective-permute-start(bf16[8,128,128]{2,1,0:T(8,128)(2,1)S(1)} %cross_sum.9.refs_5_), channel_id=1, source_target_pairs={{0,2},{1,3},{2,0},{3,1},{4,6},{5,7},{6,4},{7,5},{8,10},{9,11},{10,... | collective-permute-start | bytes 786440 | tf_op jit(solution)/shard_map/ppermute | solution.py:326
  27.9 8.2 %collective-permute-start.17 = (bf16[8,128,128]{2,1,0:T(8,128)(2,1)S(1)}, bf16[8,128,128]{2,1,0:T(8,128)(2,1)S(1)}, u32[]{:S(2)}, u32[]{:S(2)}) collective-permute-start(bf16[8,128,128]{2,1,0:T(8,128)(2,1)S(1)} %side_sum.15.refs_2_), channel_id=1, source_target_pairs={{0,4},{12,8},{4,0},{8,12},{1,5},{13,9},{5,1},{9,13},{2,6},{14,10},... | collective-permute-start | bytes 786440 | tf_op jit(solution)/shard_map/ppermute | solution.py:351
  30.5 8.9 %collective-permute-start.16 = (bf16[8,128,128]{2,1,0:T(8,128)(2,1)S(1)}, bf16[8,128,128]{2,1,0:T(8,128)(2,1)S(1)}, u32[]{:S(2)}, u32[]{:S(2)}) collective-permute-start(bf16[8,128,128]{2,1,0:T(8,128)(2,1)S(1)} %middle_sum.11.refs_2_), channel_id=1, source_target_pairs={{4,8},{5,9},{6,10},{7,11},{0,1},{2,3},{12,13},{14,15},{8,4},{9,5},... | collective-permute-start | bytes 786440 | tf_op jit(solution)/shard_map/ppermute | solution.py:356
  30.7 8.8 %collective-permute-start.15 = (bf16[8,128,128]{2,1,0:T(8,128)(2,1)S(1)}, bf16[8,128,128]{2,1,0:T(8,128)(2,1)S(1)}, u32[]{:S(2)}, u32[]{:S(2)}) collective-permute-start(bf16[8,128,128]{2,1,0:T(8,128)(2,1)S(1)} %cross_sum.10.refs_7_), channel_id=1, source_target_pairs={{0,2},{1,3},{2,0},{3,1},{4,6},{5,7},{6,4},{7,5},{8,10},{9,11},{10,... | collective-permute-start | bytes 786440 | tf_op jit(solution)/shard_map/ppermute | solution.py:326
  34.0 8.0 %collective-permute-start.14 = (bf16[8,128,128]{2,1,0:T(8,128)(2,1)S(1)}, bf16[8,128,128]{2,1,0:T(8,128)(2,1)S(1)}, u32[]{:S(2)}, u32[]{:S(2)}) collective-permute-start(bf16[8,128,128]{2,1,0:T(8,128)(2,1)S(1)} %side_sum.16.refs_2_), channel_id=1, source_target_pairs={{0,4},{12,8},{4,0},{8,12},{1,5},{13,9},{5,1},{9,13},{2,6},{14,10},... | collective-permute-start | bytes 786440 | tf_op jit(solution)/shard_map/ppermute | solution.py:351
  36.3 8.9 %collective-permute-start.21 = (bf16[8,128,128]{2,1,0:T(8,128)(2,1)S(1)}, bf16[8,128,128]{2,1,0:T(8,128)(2,1)S(1)}, u32[]{:S(2)}, u32[]{:S(2)}) collective-permute-start(bf16[8,128,128]{2,1,0:T(8,128)(2,1)S(1)} %middle_sum.12.refs_2_), channel_id=1, source_target_pairs={{4,8},{5,9},{6,10},{7,11},{0,1},{2,3},{12,13},{14,15},{8,4},{9,5},... | collective-permute-start | bytes 786440 | tf_op jit(solution)/shard_map/ppermute | solution.py:356
  36.5 8.8 %collective-permute-start.20 = (bf16[8,128,128]{2,1,0:T(8,128)(2,1)S(1)}, bf16[8,128,128]{2,1,0:T(8,128)(2,1)S(1)}, u32[]{:S(2)}, u32[]{:S(2)}) collective-permute-start(bf16[8,128,128]{2,1,0:T(8,128)(2,1)S(1)} %cross_sum.11.refs_7_), channel_id=1, source_target_pairs={{0,2},{1,3},{2,0},{3,1},{4,6},{5,7},{6,4},{7,5},{8,10},{9,11},{10,... | collective-permute-start | bytes 786440 | tf_op jit(solution)/shard_map/ppermute | solution.py:326
  39.8 8.2 %collective-permute-start.19 = (bf16[8,128,128]{2,1,0:T(8,128)(2,1)S(1)}, bf16[8,128,128]{2,1,0:T(8,128)(2,1)S(1)}, u32[]{:S(2)}, u32[]{:S(2)}) collective-permute-start(bf16[8,128,128]{2,1,0:T(8,128)(2,1)S(1)} %side_sum.17.refs_2_), channel_id=1, source_target_pairs={{0,4},{12,8},{4,0},{8,12},{1,5},{13,9},{5,1},{9,13},{2,6},{14,10},... | collective-permute-start | bytes 786440 | tf_op jit(solution)/shard_map/ppermute | solution.py:351
  42.2 8.0 %collective-permute-start.18 = (bf16[8,128,128]{2,1,0:T(8,128)(2,1)S(1)}, bf16[8,128,128]{2,1,0:T(8,128)(2,1)S(1)}, u32[]{:S(2)}, u32[]{:S(2)}) collective-permute-start(bf16[8,128,128]{2,1,0:T(8,128)(2,1)S(1)} %middle_sum.13.refs_7_), channel_id=1, source_target_pairs={{4,8},{5,9},{6,10},{7,11},{0,1},{2,3},{12,13},{14,15},{8,4},{9,5},... | collective-permute-start | bytes 786440 | tf_op jit(solution)/shard_map/ppermute | solution.py:356
  42.6 14.8 %collective-permute-start.24 = (bf16[8,128,128]{2,1,0:T(8,128)(2,1)S(1)}, bf16[8,128,128]{2,1,0:T(8,128)(2,1)S(1)}, u32[]{:S(2)}, u32[]{:S(2)}) collective-permute-start(bf16[8,128,128]{2,1,0:T(8,128)(2,1)S(1)} %late_sum.2.refs_7_.refs_1_), channel_id=1, source_target_pairs={{0,2},{1,3},{2,0},{3,1},{4,6},{5,7},{6,4},{7,5},{8,10},{9,11},{10,... | collective-permute-start | bytes 786440 | tf_op jit(solution)/shard_map/ppermute | solution.py:377
  45.6 8.3 %collective-permute-start.22 = (bf16[8,128,128]{2,1,0:T(8,128)(2,1)S(1)}, bf16[8,128,128]{2,1,0:T(8,128)(2,1)S(1)}, u32[]{:S(2)}, u32[]{:S(2)}) collective-permute-start(bf16[8,128,128]{2,1,0:T(8,128)(2,1)S(1)} %side_sum.18.refs_2_), channel_id=1, source_target_pairs={{0,4},{12,8},{4,0},{8,12},{1,5},{13,9},{5,1},{9,13},{2,6},{14,10},... | collective-permute-start | bytes 786440 | tf_op jit(solution)/shard_map/ppermute | solution.py:351
  48.2 6.0 %collective-permute-start.25 = (bf16[8,128,128]{2,1,0:T(8,128)(2,1)S(1)}, bf16[8,128,128]{2,1,0:T(8,128)(2,1)S(1)}, u32[]{:S(2)}, u32[]{:S(2)}) collective-permute-start(bf16[8,128,128]{2,1,0:T(8,128)(2,1)S(1)} %middle_sum.14.refs_7_), channel_id=1, source_target_pairs={{4,8},{5,9},{6,10},{7,11},{0,1},{2,3},{12,13},{14,15},{8,4},{9,5},... | collective-permute-start | bytes 786440 | tf_op jit(solution)/shard_map/ppermute | solution.py:356
  48.6 14.3 %collective-permute-start.30 = (bf16[8,128,128]{2,1,0:T(8,128)(2,1)S(1)}, bf16[8,128,128]{2,1,0:T(8,128)(2,1)S(1)}, u32[]{:S(2)}, u32[]{:S(2)}) collective-permute-start(bf16[8,128,128]{2,1,0:T(8,128)(2,1)S(1)} %late_sum.3.refs_4_.refs_1_), channel_id=1, source_target_pairs={{0,2},{1,3},{2,0},{3,1},{4,6},{5,7},{6,4},{7,5},{8,10},{9,11},{10,... | collective-permute-start | bytes 786440 | tf_op jit(solution)/shard_map/ppermute | solution.py:377
  50.4 13.7 %collective-permute-start.29 = (bf16[8,128,128]{2,1,0:T(8,128)(2,1)S(1)}, bf16[8,128,128]{2,1,0:T(8,128)(2,1)S(1)}, u32[]{:S(2)}, u32[]{:S(2)}) collective-permute-start(bf16[8,128,128]{2,1,0:T(8,128)(2,1)S(1)} %side_sum.19.refs_2_), channel_id=1, source_target_pairs={{0,4},{12,8},{4,0},{8,12},{1,5},{13,9},{5,1},{9,13},{2,6},{14,10},... | collective-permute-start | bytes 786440 | tf_op jit(solution)/shard_map/ppermute | solution.py:351
  54.1 3.9 %collective-permute-start.23 = (bf16[8,128,128]{2,1,0:T(8,128)(2,1)S(1)}, bf16[8,128,128]{2,1,0:T(8,128)(2,1)S(1)}, u32[]{:S(2)}, u32[]{:S(2)}) collective-permute-start(bf16[8,128,128]{2,1,0:T(8,128)(2,1)S(1)} %middle_sum.15.refs_4_), channel_id=1, source_target_pairs={{4,8},{5,9},{6,10},{7,11},{0,1},{2,3},{12,13},{14,15},{8,4},{9,5},... | collective-permute-start | bytes 786440 | tf_op jit(solution)/shard_map/ppermute | solution.py:356
  54.4 11.8 %collective-permute-start.28 = (bf16[8,128,128]{2,1,0:T(8,128)(2,1)S(1)}, bf16[8,128,128]{2,1,0:T(8,128)(2,1)S(1)}, u32[]{:S(2)}, u32[]{:S(2)}) collective-permute-start(bf16[8,128,128]{2,1,0:T(8,128)(2,1)S(1)} %side_sum.20.refs_2_), channel_id=1, source_target_pairs={{0,4},{12,8},{4,0},{8,12},{1,5},{13,9},{5,1},{9,13},{2,6},{14,10},... | collective-permute-start | bytes 786440 | tf_op jit(solution)/shard_map/ppermute | solution.py:351
  57.5 9.2 %collective-permute-start.27 = (bf16[8,128,128]{2,1,0:T(8,128)(2,1)S(1)}, bf16[8,128,128]{2,1,0:T(8,128)(2,1)S(1)}, u32[]{:S(2)}, u32[]{:S(2)}) collective-permute-start(bf16[8,128,128]{2,1,0:T(8,128)(2,1)S(1)} %late_swap.2.refs_7_), channel_id=1, source_target_pairs={{0,1},{2,3},{1,0},{3,2},{4,5},{6,7},{5,4},{7,6},{8,9},{10,11},{9,8... | collective-permute-start | bytes 786440 | tf_op jit(solution)/shard_map/ppermute | solution.py:383
  58.2 12.2 %collective-permute-start.26 = (bf16[8,128,128]{2,1,0:T(8,128)(2,1)S(1)}, bf16[8,128,128]{2,1,0:T(8,128)(2,1)S(1)}, u32[]{:S(2)}, u32[]{:S(2)}) collective-permute-start(bf16[8,128,128]{2,1,0:T(8,128)(2,1)S(1)} %side_sum.21.refs_2_), channel_id=1, source_target_pairs={{0,4},{12,8},{4,0},{8,12},{1,5},{13,9},{5,1},{9,13},{2,6},{14,10},... | collective-permute-start | bytes 786440 | tf_op jit(solution)/shard_map/ppermute | solution.py:351
  63.0 4.1 %collective-permute-start.31 = (bf16[8,128,128]{2,1,0:T(8,128)(2,1)S(1)}, bf16[8,128,128]{2,1,0:T(8,128)(2,1)S(1)}, u32[]{:S(2)}, u32[]{:S(2)}) collective-permute-start(bf16[8,128,128]{2,1,0:T(8,128)(2,1)S(1)} %late_swap.3.refs_7_), channel_id=1, source_target_pairs={{0,1},{2,3},{1,0},{3,2},{4,5},{6,7},{5,4},{7,6},{8,9},{10,11},{9,8... | collective-permute-start | bytes 786440 | tf_op jit(solution)/shard_map/ppermute | solution.py:383
  (4 other events, 13.0 us)
